TPU v7x, 512 devices: a whole 4x4x16 slice. The times are simulated.
512 devices in a mesh: tile: 64 (over x, z_lo, core), depth: 8 (over y, z_hi).
Axes of the slice: x: 4, y: 4, z: 16 (z_hi: 2, z_lo: 8; z = z_hi * 8 + z_lo), core: 2. Of those that a mesh axis runs over, the one named last changes fastest.
Arguments:
- displacement: float32 [128, 1024, 1024], P('depth', 'tile'), may hold values from -6 to 6
- damage: float32 [128, 1024, 1024], P('depth', 'tile'), may hold values from 0 to 0.6
- modulus: float32 [128, 1024, 1024], P('depth', 'tile'), may hold values from 0.5 to 2
- toughness: float32 [128, 1024, 1024], P('depth', 'tile'), may hold values from 0.5 to 2
- pressure: float32 [1024, 1024], P('tile'), may hold values from -6 to 6
- crack_mask: int32 [1024, 1024], P('tile'), may hold values 0 or 1
- wells: int32 [16], replicated, may hold values from 0 to 1048575
- rates: float32 [16], replicated, may hold values from 0.5 to 2
Outputs:
- new_pressure: float32 [1024, 1024], P('tile')
All inputs are finite; a program needn't handle non-finite values. No bound on the sum of `crack_mask` on one device may be relied on, other than what follows from the above.
Results may differ from a plain program's by a relative error of at most 0.00002.
Values sent between devices are 32-bit elements; how exact they have to be, the bound alone decides.
No kernel may reach another device: no remote copies, remote signals or barrier semaphores. Data moves between devices by JAX's collectives and lax.ppermute only.
A program may use at most 64 MiB of HBM per device.

v0:
```python
import jax
import jax.numpy as jnp
from jax import lax
from jax.sharding import PartitionSpec as P


def padded_2(cells, sides, width):
    for axis, dim in sides:
        count = lax.axis_size(axis)
        ends = count - 1
        head = lax.slice_in_dim(cells, 0, width, axis=dim)
        tail = lax.slice_in_dim(cells, cells.shape[dim] - width, cells.shape[dim], axis=dim)
        cells = jnp.concatenate(
            [
                lax.ppermute(tail, axis, [(i, (i + 1) % count) for i in range(ends)]),
                cells,
                lax.ppermute(head, axis, [((i + 1) % count, i) for i in range(ends)]),
            ],
            axis=dim,
        )
    return cells


def sides(padded):
    return [
        padded[2:, 1:-1, 1:-1],
        padded[:-2, 1:-1, 1:-1],
        padded[1:-1, 2:, 1:-1],
        padded[1:-1, :-2, 1:-1],
        padded[1:-1, 1:-1, 2:],
        padded[1:-1, 1:-1, :-2],
    ]


def flat_sides(padded):
    return [padded[2:, 1:-1], padded[:-2, 1:-1], padded[1:-1, 2:], padded[1:-1, :-2]]


def pad_last(stacked):
    widths = [(0, 0)] * (stacked.ndim - 1) + [(1, 1)]
    return jnp.pad(stacked, widths)


def plane_sweep(p_pad, k_pad, anchor, source, trans):
    coef = jnp.zeros_like(trans)
    flow = jnp.zeros_like(trans)
    for k_side, p_side in zip(flat_sides(k_pad), flat_sides(p_pad)):
        face = 0.5 * (trans + k_side)
        coef = coef + face
        flow = flow + face * p_side
    return (anchor + source + flow) / (1.0 + coef)


def well_source(wells, rates, row_start, rows, cols, width):
    row_ids = row_start + jnp.arange(rows, dtype=jnp.int32)
    col_ids = jnp.arange(cols, dtype=jnp.int32)
    flat = row_ids[:, None] * width + col_ids[None, :]
    hit = flat[:, :, None] == wells[None, None, :]
    return 4.0 * jnp.sum(jnp.where(hit, rates[None, None, :], jnp.float32(0.0)), axis=-1)


def relax_step(u_pad, c_pad, center_u, center_c):
    coef = jnp.zeros_like(center_c)
    flux = jnp.zeros_like(center_c)
    for c_side, u_side in zip(sides(c_pad), sides(u_pad)):
        face = 0.5 * (center_c + c_side)
        coef = coef + face
        flux = flux + face * (u_side - center_u)
    return (coef, flux)


def on_device(displacement, damage, modulus, toughness, pressure, crack_mask, wells, rates):
    depth_cells, tile_cells, width = displacement.shape
    total_depth = depth_cells * lax.axis_size("depth")
    depth_start = lax.axis_index("depth") * depth_cells
    tile_start = lax.axis_index("tile") * tile_cells
    stiff = ((1.0 - damage) ** 2 + 0.001) * modulus
    mask_f = crack_mask.astype(jnp.float32)
    layer = depth_start + jnp.arange(depth_cells, dtype=jnp.int32) == total_depth // 2
    load = 4.0 * mask_f * pressure
    force = jnp.where(layer[:, None, None], load[None, :, :], jnp.float32(0.0))
    framed = pad_last(
        padded_2(jnp.stack([displacement, stiff, damage]), (("depth", 1), ("tile", 2)), 1)
    )
    u_pad, c_pad, d_pad = (framed[0], framed[1], framed[2])
    coef, flux = relax_step(u_pad, c_pad, displacement, stiff)
    moved = displacement + 0.8 * (force + flux) / coef
    m_pad = pad_last(padded_2(moved, (("depth", 0), ("tile", 1)), 1))
    energy = jnp.zeros_like(moved)
    for m_side in sides(m_pad):
        energy = energy + (m_side - moved) ** 2
    energy = 0.25 * modulus * energy
    beside_all = jnp.zeros_like(damage)
    for d_side in sides(d_pad):
        beside_all = beside_all + d_side
    trial = (2.0 * energy + toughness * beside_all) / (7.0 * toughness + 2.0 * energy)
    new_damage = jnp.maximum(damage, trial)
    partial_open = 4.0 / total_depth * jnp.sum(new_damage * moved * moved, axis=0)
    aperture = 0.5 + lax.psum(partial_open, "depth")
    trans = mask_f * aperture**3
    source = well_source(wells, rates, tile_start, tile_cells, width, width)
    rimmed = pad_last(padded_2(jnp.stack([trans, pressure]), (("tile", 1),), 1))
    k_pad = rimmed[0]
    level = plane_sweep(rimmed[1], k_pad, pressure, source, trans)
    level_pad = pad_last(padded_2(level, (("tile", 0),), 1))
    return plane_sweep(level_pad, k_pad, pressure, source, trans)


def solution(mesh):
    return jax.shard_map(
        on_device,
        mesh=mesh,
        in_specs=(
            P("depth", "tile", None),
            P("depth", "tile", None),
            P("depth", "tile", None),
            P("depth", "tile", None),
            P("tile", None),
            P("tile", None),
            P(),
            P(),
        ),
        out_specs=P("tile", None),
        check_vma=False,
    )
```

profile of v0, /device:TPU:4, one launch (start us, length us, event | category | flops | bytes accessed | tf_op | source)
XLA Modules:
  0.0 338.5 jit_solution(16810384898599751062)
XLA Ops:
  6.5 3.7 %fusion.46 = (f32[1,16,16,1024]{3,1,2,0:T(8,128)S(1)}, f32[1,16,16,1024]{3,1,2,0:T(8,128)S(1)}, f32[1,16,16,1024]{3,1,2,0:T(8,128)S(1)}) fusion(f32[16,16,1024]{2,1,0:T(8,128)} %param.10, f32[16,16,1024]{2,1,0:T(8,128)} %param.9, f32[16,16,1024]{2,1,0:T(8,128)} %param.8), kind=kLoop, calls=%fused_computation.110 | loop fusion | flops 1048576 | bytes 6291456 | tf_op jit(solution)/shard_map/stack | solution.py:83
  10.3 1.1 pad_maximum_fusion.15
  11.4 15.7 %collective-permute-start = (f32[3,1,16,1024]{3,1,2,0:T(1,128)}, f32[3,1,16,1024]{3,1,2,0:T(1,128)S(1)}, u32[]{:S(2)}, u32[]{:S(2)}) collective-permute-start(f32[3,1,16,1024]{3,1,2,0:T(1,128)} %get-tuple-element.10), channel_id=1, source_target_pairs={{0,1},{1,2},{2,3},{3,4},{4,5},{5,6},{6,7},{8,9},{9,10},{10,11},{11... | collective-permute-start | bytes 589832 | tf_op jit(solution)/shard_map/ppermute | solution.py:15
  27.1 1.3 collective-permute-start.1
  28.5 3.3 collective-permute-done
  31.8 21.4 %collective-permute-done.1 = f32[3,1,16,1024]{3,1,2,0:T(1,128)} collective-permute-done((f32[3,1,16,1024]{3,1,2,0:T(1,128)}, f32[3,1,16,1024]{3,1,2,0:T(1,128)}, u32[]{:S(2)}, u32[]{:S(2)}) %collective-permute-start.1) | collective-permute-done | bytes 196640 | tf_op jit(solution)/shard_map/ppermute | solution.py:17
  53.3 0.8 pad_maximum_fusion.12
  54.1 1.9 collective-permute-start.2
  56.0 11.1 %collective-permute-start.3 = (f32[3,18,1,1024]{3,1,2,0:T(8,128)S(1)}, f32[3,18,1,1024]{3,1,2,0:T(8,128)S(1)}, u32[]{:S(2)}, u32[]{:S(2)}) collective-permute-start(f32[3,18,1,1024]{3,1,2,0:T(8,128)S(1)} %get-tuple-element.9), channel_id=1, source_target_pairs={{8,0},{16,8},{24,16},{32,24},{40,32},{48,40},{56,48},{64,56},{72,6... | collective-permute-start | bytes 663560 | tf_op jit(solution)/shard_map/ppermute | solution.py:17
  67.2 2.5 collective-permute-done.2
  69.7 2.7 collective-permute-done.3
  72.5 8.0 %select_maximum_fusion = f32[3,18,18,1026]{3,1,2,0:T(8,128)S(1)} fusion(f32[3,18,1,1024]{3,1,2,0:T(8,128)S(1)} %collective-permute-done.3, f32[3,18,1,1024]{3,1,2,0:T(8,128)S(1)} %collective-permute-done.2, f32[3,1,16,1024]{3,1,2,0:T(1,128)} %collective-permute-done.1, f32[3,1,16,1024]{3,1,2,0:T(1,128)S(1)} %collective-permute-done, ...), kind=kLoop, calls=%fused_computation.2 | loop fusion | flops 15956352 | bytes 7970400 | tf_op jit(solution)/shard_map/concatenate | solution.py:13
  80.9 0.8 copy-done
  82.3 5.2 %fusion.29 = f32[16,16,1024]{2,0,1:T(8,128)S(1)} fusion(f32[18,18,1026]{2,0,1:T(8,128)S(1)} %get-tuple-element.6, f32[18,18,1026]{2,0,1:T(8,128)S(1)} %get-tuple-element.7, f32[16,16,1024]{2,1,0:T(8,128)S(1)} %copy-done.4, f32[16,1024]{1,0:T(8,128)S(1)} %multiply_multiply_fusion.2, pred[16]{0:T(512)(128)(4,1)S(1)} %add_compare_fusion, ...), kind=kLoop, calls=%fused_computation.63 | loop fusion | flops 11272192 | bytes 16842768 | tf_op jit(solution)/shard_map/add | solution.py:87
  87.6 1.3 collective-permute-start.4
  88.9 14.0 %collective-permute-start.5 = (f32[1,16,1024]{2,0,1:T(1,128)S(1)}, f32[1,16,1024]{2,0,1:T(1,128)S(1)}, u32[]{:S(2)}, u32[]{:S(2)}) collective-permute-start(f32[1,16,1024]{2,0,1:T(1,128)S(1)} %get-tuple-element.14), channel_id=1, source_target_pairs={{0,1},{1,2},{2,3},{3,4},{4,5},{5,6},{6,7},{8,9},{9,10},{10,11},{11... | collective-permute-start | bytes 196616 | tf_op jit(solution)/shard_map/ppermute | solution.py:15
  103.3 1.8 collective-permute-done.5
  105.1 10.4 %collective-permute-start.6 = (f32[18,1,1024]{2,0,1:T(8,128)S(1)}, f32[18,1,1024]{2,0,1:T(8,128)S(1)}, u32[]{:S(2)}, u32[]{:S(2)}) collective-permute-start(f32[18,1,1024]{2,0,1:T(8,128)S(1)} %get-tuple-element.13), channel_id=1, source_target_pairs={{8,0},{16,8},{24,16},{32,24},{40,32},{48,40},{56,48},{64,56},{72,6... | collective-permute-start | bytes 221192 | tf_op jit(solution)/shard_map/ppermute | solution.py:17
  115.6 2.1 collective-permute-start.7
  117.8 11.2 %collective-permute-done.7 = f32[18,1,1024]{2,0,1:T(8,128)S(1)} collective-permute-done((f32[18,1,1024]{2,0,1:T(8,128)S(1)}, f32[18,1,1024]{2,0,1:T(8,128)S(1)}, u32[]{:S(2)}, u32[]{:S(2)}) %collective-permute-start.7) | collective-permute-done | bytes 73760 | tf_op jit(solution)/shard_map/ppermute | solution.py:15
  129.0 1.0 select_maximum_fusion.6
  130.0 5.8 %fusion.2 = f32[16,1024]{1,0:T(8,128)S(1)} fusion(f32[16,16,1024]{2,0,1:T(8,128)S(1)} %fusion.29, f32[18,18,1026]{2,0,1:T(8,128)S(1)} %get-tuple-element.5, f32[18,18,1026]{2,0,1:T(8,128)S(1)} %select_maximum_fusion.6, f32[1,16,1024]{2,0,1:T(1,128)S(1)} %collective-permute-done.4, f32[1,16,1024]{2,0,1:T(1,128)S(1)} %collective-permute-done.5, ...), kind=kLoop, calls=%fused_computation.20 | loop fusion | flops 10993664 | bytes 12926976 | tf_op jit(solution)/shard_map/reduce_sum | solution.py:98
  136.6 154.0 %all-reduce.6.cloned.1.call-done = f32[16,1024]{1,0:T(8,128)} async-done(((f32[16,1024]{1,0:T(8,128)}), f32[16,1024]{1,0:T(8,128)}) %all-reduce.6.cloned.1.call-update) | async-done | bytes 65552 | tf_op jit(solution)/shard_map/psum | solution.py:99
  290.5 0.9 fusion.65
  291.5 1.9 collective-permute-start.8
  293.4 11.1 %collective-permute-start.9 = (f32[2,1,1024]{2,1,0:T(1,128)S(1)}, f32[2,1,1024]{2,1,0:T(1,128)S(1)}, u32[]{:S(2)}, u32[]{:S(2)}) collective-permute-start(f32[2,1,1024]{2,1,0:T(1,128)S(1)} %get-tuple-element.21), channel_id=1, source_target_pairs={{8,0},{16,8},{24,16},{32,24},{40,32},{48,40},{56,48},{64,56},{72,6... | collective-permute-start | bytes 24584 | tf_op jit(solution)/shard_map/ppermute | solution.py:17
  304.9 1.0 collective-permute-done.9
  306.1 1.0 fusion.58
  307.1 11.1 %collective-permute-start.10 = (f32[1,1024]{1,0:T(1,128)S(1)}, f32[1,1024]{1,0:T(1,128)S(1)}, u32[]{:S(2)}, u32[]{:S(2)}) collective-permute-start(f32[1,1024]{1,0:T(1,128)S(1)} %get-tuple-element.23), channel_id=1, source_target_pairs={{8,0},{16,8},{24,16},{32,24},{40,32},{48,40},{56,48},{64,56},{72,6... | collective-permute-start | bytes 12296 | tf_op jit(solution)/shard_map/ppermute | solution.py:17
  318.3 1.9 collective-permute-start.11
  320.2 10.5 %collective-permute-done.11 = f32[1,1024]{1,0:T(1,128)S(1)} collective-permute-done((f32[1,1024]{1,0:T(1,128)S(1)}, f32[1,1024]{1,0:T(1,128)S(1)}, u32[]{:S(2)}, u32[]{:S(2)}) %collective-permute-start.11) | collective-permute-done | bytes 4128 | tf_op jit(solution)/shard_map/ppermute | solution.py:15
  330.8 0.8 fusion.51
  (41 shorter events, 3.0 us)
Async XLA Ops:
  6.5 284.0 %all-reduce.6.cloned.1.call-start = ((), (), s32[]{:S(2)}) async-start(), calls=%async_computation | async-start | bytes 131072 | tf_op jit(solution)/shard_map/psum | solution.py:99
  11.4 20.4 %collective-permute-start = (f32[3,1,16,1024]{3,1,2,0:T(1,128)}, f32[3,1,16,1024]{3,1,2,0:T(1,128)S(1)}, u32[]{:S(2)}, u32[]{:S(2)}) collective-permute-start(f32[3,1,16,1024]{3,1,2,0:T(1,128)} %get-tuple-element.10), channel_id=1, source_target_pairs={{0,1},{1,2},{2,3},{3,4},{4,5},{5,6},{6,7},{8,9},{9,10},{10,11},{11... | collective-permute-start | bytes 589832 | tf_op jit(solution)/shard_map/ppermute | solution.py:15
  27.1 26.1 %collective-permute-start.1 = (f32[3,1,16,1024]{3,1,2,0:T(1,128)}, f32[3,1,16,1024]{3,1,2,0:T(1,128)}, u32[]{:S(2)}, u32[]{:S(2)}) collective-permute-start(f32[3,1,16,1024]{3,1,2,0:T(1,128)} %get-tuple-element.11), channel_id=1, source_target_pairs={{1,0},{2,1},{3,2},{4,3},{5,4},{6,5},{7,6},{9,8},{10,9},{11,10},{12... | collective-permute-start | bytes 589832 | tf_op jit(solution)/shard_map/ppermute | solution.py:17
  28.5 38.7 %copy-start.5 = (f32[16,1024]{1,0:T(8,128)S(1)}, f32[16,1024]{1,0:T(8,128)}, u32[]{:S(2)}) copy-start(f32[16,1024]{1,0:T(8,128)} %param.12) | copy-start | bytes 196612
  28.5 38.7 %copy-start.7 = (s32[16,1024]{1,0:T(8,128)S(1)}, s32[16,1024]{1,0:T(8,128)}, u32[]{:S(2)}) copy-start(s32[16,1024]{1,0:T(8,128)} %param.13) | copy-start | bytes 196612
  54.1 15.7 %collective-permute-start.2 = (f32[3,18,1,1024]{3,1,2,0:T(8,128)S(1)}, f32[3,18,1,1024]{3,1,2,0:T(8,128)S(1)}, u32[]{:S(2)}, u32[]{:S(2)}) collective-permute-start(f32[3,18,1,1024]{3,1,2,0:T(8,128)S(1)} %get-tuple-element.8), channel_id=1, source_target_pairs={{0,8},{8,16},{16,24},{24,32},{32,40},{40,48},{48,56},{56,64},{64,7... | collective-permute-start | bytes 663560 | tf_op jit(solution)/shard_map/ppermute | solution.py:15
  56.0 16.5 %collective-permute-start.3 = (f32[3,18,1,1024]{3,1,2,0:T(8,128)S(1)}, f32[3,18,1,1024]{3,1,2,0:T(8,128)S(1)}, u32[]{:S(2)}, u32[]{:S(2)}) collective-permute-start(f32[3,18,1,1024]{3,1,2,0:T(8,128)S(1)} %get-tuple-element.9), channel_id=1, source_target_pairs={{8,0},{16,8},{24,16},{32,24},{40,32},{48,40},{56,48},{64,56},{72,6... | collective-permute-start | bytes 663560 | tf_op jit(solution)/shard_map/ppermute | solution.py:17
  80.4 1.2 copy-start
  80.5 1.5 copy-start.2
  80.5 1.8 copy-start.4
  87.6 15.7 %collective-permute-start.4 = (f32[1,16,1024]{2,0,1:T(1,128)S(1)}, f32[1,16,1024]{2,0,1:T(1,128)S(1)}, u32[]{:S(2)}, u32[]{:S(2)}) collective-permute-start(f32[1,16,1024]{2,0,1:T(1,128)S(1)} %get-tuple-element.15), channel_id=1, source_target_pairs={{1,0},{2,1},{3,2},{4,3},{5,4},{6,5},{7,6},{9,8},{10,9},{11,10},{12... | collective-permute-start | bytes 196616 | tf_op jit(solution)/shard_map/ppermute | solution.py:17
  88.9 16.1 %collective-permute-start.5 = (f32[1,16,1024]{2,0,1:T(1,128)S(1)}, f32[1,16,1024]{2,0,1:T(1,128)S(1)}, u32[]{:S(2)}, u32[]{:S(2)}) collective-permute-start(f32[1,16,1024]{2,0,1:T(1,128)S(1)} %get-tuple-element.14), channel_id=1, source_target_pairs={{0,1},{1,2},{2,3},{3,4},{4,5},{5,6},{6,7},{8,9},{9,10},{10,11},{11... | collective-permute-start | bytes 196616 | tf_op jit(solution)/shard_map/ppermute | solution.py:15
  105.1 24.9 %copy-start.1 = (f32[16,16,1024]{2,1,0:T(8,128)S(1)}, f32[16,16,1024]{2,1,0:T(8,128)}, u32[]{:S(2)}) copy-start(f32[16,16,1024]{2,1,0:T(8,128)} %param.10) | copy-start | bytes 3145732
  105.1 24.9 %copy-start.3 = (f32[16,16,1024]{2,1,0:T(8,128)S(1)}, f32[16,16,1024]{2,1,0:T(8,128)}, u32[]{:S(2)}) copy-start(f32[16,16,1024]{2,1,0:T(8,128)} %param.9) | copy-start | bytes 3145732
  105.1 24.9 %copy-start.6 = (f32[16,16,1024]{2,1,0:T(8,128)S(1)}, f32[16,16,1024]{2,1,0:T(8,128)}, u32[]{:S(2)}) copy-start(f32[16,16,1024]{2,1,0:T(8,128)} %param.11) | copy-start | bytes 3145732
  105.1 12.6 %collective-permute-start.6 = (f32[18,1,1024]{2,0,1:T(8,128)S(1)}, f32[18,1,1024]{2,0,1:T(8,128)S(1)}, u32[]{:S(2)}, u32[]{:S(2)}) collective-permute-start(f32[18,1,1024]{2,0,1:T(8,128)S(1)} %get-tuple-element.13), channel_id=1, source_target_pairs={{8,0},{16,8},{24,16},{32,24},{40,32},{48,40},{56,48},{64,56},{72,6... | collective-permute-start | bytes 221192 | tf_op jit(solution)/shard_map/ppermute | solution.py:17
  115.6 13.4 %collective-permute-start.7 = (f32[18,1,1024]{2,0,1:T(8,128)S(1)}, f32[18,1,1024]{2,0,1:T(8,128)S(1)}, u32[]{:S(2)}, u32[]{:S(2)}) collective-permute-start(f32[18,1,1024]{2,0,1:T(8,128)S(1)} %get-tuple-element.12), channel_id=1, source_target_pairs={{0,8},{8,16},{16,24},{24,32},{32,40},{40,48},{48,56},{56,64},{64,7... | collective-permute-start | bytes 221192 | tf_op jit(solution)/shard_map/ppermute | solution.py:15
  130.0 174.5 %copy-start.9 = (f32[16]{0:T(128)S(1)}, f32[16]{0:T(128)}, u32[]{:S(2)}) copy-start(f32[16]{0:T(128)} %param.15) | copy-start | bytes 196
  130.0 174.5 %copy-start.10 = (s32[16]{0:T(128)S(1)}, s32[16]{0:T(128)}, u32[]{:S(2)}) copy-start(s32[16]{0:T(128)} %param.14) | copy-start | bytes 196
  290.5 40.3 %copy-start.8 = (f32[16,1024]{1,0:T(8,128)S(1)}, f32[16,1024]{1,0:T(8,128)}, u32[]{:S(2)}) copy-start(f32[16,1024]{1,0:T(8,128)} %all-reduce.6.cloned.1.call-done) | copy-start | bytes 196612
  291.5 13.4 %collective-permute-start.8 = (f32[2,1,1024]{2,1,0:T(1,128)S(1)}, f32[2,1,1024]{2,1,0:T(1,128)S(1)}, u32[]{:S(2)}, u32[]{:S(2)}) collective-permute-start(f32[2,1,1024]{2,1,0:T(1,128)S(1)} %get-tuple-element.20), channel_id=1, source_target_pairs={{0,8},{8,16},{16,24},{24,32},{32,40},{40,48},{48,56},{56,64},{64,7... | collective-permute-start | bytes 24584 | tf_op jit(solution)/shard_map/ppermute | solution.py:15
  293.4 12.5 %collective-permute-start.9 = (f32[2,1,1024]{2,1,0:T(1,128)S(1)}, f32[2,1,1024]{2,1,0:T(1,128)S(1)}, u32[]{:S(2)}, u32[]{:S(2)}) collective-permute-start(f32[2,1,1024]{2,1,0:T(1,128)S(1)} %get-tuple-element.21), channel_id=1, source_target_pairs={{8,0},{16,8},{24,16},{32,24},{40,32},{48,40},{56,48},{64,56},{72,6... | collective-permute-start | bytes 24584 | tf_op jit(solution)/shard_map/ppermute | solution.py:17
  307.1 13.1 %collective-permute-start.10 = (f32[1,1024]{1,0:T(1,128)S(1)}, f32[1,1024]{1,0:T(1,128)S(1)}, u32[]{:S(2)}, u32[]{:S(2)}) collective-permute-start(f32[1,1024]{1,0:T(1,128)S(1)} %get-tuple-element.23), channel_id=1, source_target_pairs={{8,0},{16,8},{24,16},{32,24},{40,32},{48,40},{56,48},{64,56},{72,6... | collective-permute-start | bytes 12296 | tf_op jit(solution)/shard_map/ppermute | solution.py:17
  318.3 12.4 %collective-permute-start.11 = (f32[1,1024]{1,0:T(1,128)S(1)}, f32[1,1024]{1,0:T(1,128)S(1)}, u32[]{:S(2)}, u32[]{:S(2)}) collective-permute-start(f32[1,1024]{1,0:T(1,128)S(1)} %get-tuple-element.22), channel_id=1, source_target_pairs={{0,8},{8,16},{16,24},{24,32},{32,40},{40,48},{48,56},{56,64},{64,7... | collective-permute-start | bytes 12296 | tf_op jit(solution)/shard_map/ppermute | solution.py:15
Sparse Core Ops, SparseCore 0:
  136.6 153.8 all-reduce.5
where the time goes:
time: 339 us; the launch traced here: 338 us
  waiting for transfers between devices  209 us (62%)
  starting transfers between devices  84 us (25%)
  other arithmetic  29.6 us (9%)
  between operations  13.8 us (4%)
    psum x1, waiting for transfers between devices, on_device(): aperture = 0.5 + lax.psum(partial_open, 'depth')  154 us
    ppermute x6, starting transfers between devices, padded_2(): lax.ppermute(head, axis, [((i + 1) % count, i) for i in range(ends)])  46.4 us
    ppermute x6, starting transfers between devices, padded_2(): lax.ppermute(tail, axis, [(i, (i + 1) % count) for i in range(ends)])  37.6 us
    ppermute x6, waiting for transfers between devices, padded_2(): lax.ppermute(tail, axis, [(i, (i + 1) % count) for i in range(ends)])  29.4 us
    ppermute x6, waiting for transfers between devices, padded_2(): lax.ppermute(head, axis, [((i + 1) % count, i) for i in range(ends)])  25.7 us
    concatenate x5, other arithmetic, padded_2(): jnp.concatenate([lax.ppermute(tail, axis, [(i, (i + 1) % count) for i in...  9.26 us
  transfers between devices with their start and end apart: 13, of which 11 were waited for; matrix products, arithmetic and copies ran while one was open for 0% of the time, Pallas kernels for 0%

commit v1 on v0

--- a/solution.py
+++ b/solution.py
@@ -59,6 +59,16 @@
     return 4.0 * jnp.sum(jnp.where(hit, rates[None, None, :], jnp.float32(0.0)), axis=-1)
 
 
+def butterfly_sum(part, axis):
+    count = lax.axis_size(axis)
+    step = 1
+    while step < count:
+        pairs = [(i, i ^ step) for i in range(count)]
+        part = part + lax.ppermute(part, axis, pairs)
+        step *= 2
+    return part
+
+
 def relax_step(u_pad, c_pad, center_u, center_c):
     coef = jnp.zeros_like(center_c)
     flux = jnp.zeros_like(center_c)
@@ -96,7 +106,7 @@
     trial = (2.0 * energy + toughness * beside_all) / (7.0 * toughness + 2.0 * energy)
     new_damage = jnp.maximum(damage, trial)
     partial_open = 4.0 / total_depth * jnp.sum(new_damage * moved * moved, axis=0)
-    aperture = 0.5 + lax.psum(partial_open, "depth")
+    aperture = 0.5 + butterfly_sum(partial_open, "depth")
     trans = mask_f * aperture**3
     source = well_source(wells, rates, tile_start, tile_cells, width, width)
     rimmed = pad_last(padded_2(jnp.stack([trans, pressure]), (("tile", 1),), 1))

time: 339 us -> 209 us (0.62)
  the two profiles are of different devices: /device:TPU:4 before, /device:TPU:10 now
where the time goes in v1:
time: 209 us
  starting transfers between devices  98.9 us (47%)
  waiting for transfers between devices  80.2 us (38%)
  other arithmetic  27.3 us (13%)
    ppermute x6, starting transfers between devices, padded_2(): lax.ppermute(head, axis, [((i + 1) % count, i) for i in range(ends)])  59.4 us
    ppermute x6, waiting for transfers between devices, padded_2(): lax.ppermute(tail, axis, [(i, (i + 1) % count) for i in range(ends)])  42.2 us
    ppermute x6, starting transfers between devices, padded_2(): lax.ppermute(tail, axis, [(i, (i + 1) % count) for i in range(ends)])  29.9 us
    ppermute x3, waiting for transfers between devices, butterfly_sum(): part = part + lax.ppermute(part, axis, pairs)  19 us
    ppermute x6, waiting for transfers between devices, padded_2(): lax.ppermute(head, axis, [((i + 1) % count, i) for i in range(ends)])  18.9 us
    ppermute x3, starting transfers between devices, butterfly_sum(): part = part + lax.ppermute(part, axis, pairs)  9.55 us
    concatenate x5, other arithmetic, padded_2(): jnp.concatenate([lax.ppermute(tail, axis, [(i, (i + 1) % count) for i in...  9.27 us
    reduce_sum x1, other arithmetic, on_device(): jnp.sum(new_damage * moved * moved, axis=0)  5.77 us
  transfers between devices with their start and end apart: 15, of which 13 were waited for; matrix products, arithmetic and copies ran while one was open for 0% of the time, Pallas kernels for 0%

profile of v1, /device:TPU:10, one launch (start us, length us, event | category | flops | bytes accessed | tf_op | source)
XLA Modules:
  0.0 208.7 jit_solution(11677618848842095418)
XLA Ops:
  0.0 3.7 %fusion.46 = (f32[1,16,16,1024]{3,1,2,0:T(8,128)S(1)}, f32[1,16,16,1024]{3,1,2,0:T(8,128)S(1)}, f32[1,16,16,1024]{3,1,2,0:T(8,128)S(1)}) fusion(f32[16,16,1024]{2,1,0:T(8,128)} %param.10, f32[16,16,1024]{2,1,0:T(8,128)} %param.9, f32[16,16,1024]{2,1,0:T(8,128)} %param.8), kind=kLoop, calls=%fused_computation.110 | loop fusion | flops 1048576 | bytes 6291456 | tf_op jit(solution)/shard_map/stack | solution.py:93
  3.7 1.1 pad_maximum_fusion.15
  4.9 15.7 %collective-permute-start = (f32[3,1,16,1024]{3,1,2,0:T(1,128)}, f32[3,1,16,1024]{3,1,2,0:T(1,128)S(1)}, u32[]{:S(2)}, u32[]{:S(2)}) collective-permute-start(f32[3,1,16,1024]{3,1,2,0:T(1,128)} %get-tuple-element.10), channel_id=1, source_target_pairs={{0,1},{1,2},{2,3},{3,4},{4,5},{5,6},{6,7},{8,9},{9,10},{10,11},{11... | collective-permute-start | bytes 589832 | tf_op jit(solution)/shard_map/ppermute | solution.py:15
  20.6 1.9 collective-permute-start.1
  22.6 11.4 %collective-permute-done = f32[3,1,16,1024]{3,1,2,0:T(1,128)S(1)} collective-permute-done((f32[3,1,16,1024]{3,1,2,0:T(1,128)}, f32[3,1,16,1024]{3,1,2,0:T(1,128)S(1)}, u32[]{:S(2)}, u32[]{:S(2)}) %collective-permute-start) | collective-permute-done | bytes 196640 | tf_op jit(solution)/shard_map/ppermute | solution.py:15
  34.0 12.1 %collective-permute-done.1 = f32[3,1,16,1024]{3,1,2,0:T(1,128)} collective-permute-done((f32[3,1,16,1024]{3,1,2,0:T(1,128)}, f32[3,1,16,1024]{3,1,2,0:T(1,128)}, u32[]{:S(2)}, u32[]{:S(2)}) %collective-permute-start.1) | collective-permute-done | bytes 196640 | tf_op jit(solution)/shard_map/ppermute | solution.py:17
  46.8 1.9 collective-permute-start.2
  48.8 17.9 %collective-permute-start.3 = (f32[3,18,1,1024]{3,1,2,0:T(8,128)S(1)}, f32[3,18,1,1024]{3,1,2,0:T(8,128)S(1)}, u32[]{:S(2)}, u32[]{:S(2)}) collective-permute-start(f32[3,18,1,1024]{3,1,2,0:T(8,128)S(1)} %get-tuple-element.9), channel_id=1, source_target_pairs={{8,0},{16,8},{24,16},{32,24},{40,32},{48,40},{56,48},{64,56},{72,6... | collective-permute-start | bytes 663560 | tf_op jit(solution)/shard_map/ppermute | solution.py:17
  66.7 2.5 %collective-permute-done.2 = f32[3,18,1,1024]{3,1,2,0:T(8,128)S(1)} collective-permute-done((f32[3,18,1,1024]{3,1,2,0:T(8,128)S(1)}, f32[3,18,1,1024]{3,1,2,0:T(8,128)S(1)}, u32[]{:S(2)}, u32[]{:S(2)}) %collective-permute-start.2) | collective-permute-done | bytes 221216 | tf_op jit(solution)/shard_map/ppermute | solution.py:15
  69.3 1.6 collective-permute-done.3
  70.9 8.0 %select_maximum_fusion = f32[3,18,18,1026]{3,1,2,0:T(8,128)S(1)} fusion(f32[3,18,1,1024]{3,1,2,0:T(8,128)S(1)} %collective-permute-done.3, f32[3,18,1,1024]{3,1,2,0:T(8,128)S(1)} %collective-permute-done.2, f32[3,1,16,1024]{3,1,2,0:T(1,128)} %collective-permute-done.1, f32[3,1,16,1024]{3,1,2,0:T(1,128)S(1)} %collective-permute-done, ...), kind=kLoop, calls=%fused_computation.2 | loop fusion | flops 15956352 | bytes 7970400 | tf_op jit(solution)/shard_map/concatenate | solution.py:13
  80.8 5.2 %fusion.29 = f32[16,16,1024]{2,0,1:T(8,128)S(1)} fusion(f32[18,18,1026]{2,0,1:T(8,128)S(1)} %get-tuple-element.6, f32[18,18,1026]{2,0,1:T(8,128)S(1)} %get-tuple-element.7, f32[16,16,1024]{2,1,0:T(8,128)S(1)} %copy-done.2, f32[16,1024]{1,0:T(8,128)S(1)} %multiply_multiply_fusion.2, pred[16]{0:T(512)(128)(4,1)S(1)} %add_compare_fusion, ...), kind=kLoop, calls=%fused_computation.63 | loop fusion | flops 11272192 | bytes 16842768 | tf_op jit(solution)/shard_map/add | solution.py:97
  86.1 8.2 %collective-permute-start.4 = (f32[1,16,1024]{2,0,1:T(1,128)S(1)}, f32[1,16,1024]{2,0,1:T(1,128)S(1)}, u32[]{:S(2)}, u32[]{:S(2)}) collective-permute-start(f32[1,16,1024]{2,0,1:T(1,128)S(1)} %get-tuple-element.15), channel_id=1, source_target_pairs={{1,0},{2,1},{3,2},{4,3},{5,4},{6,5},{7,6},{9,8},{10,9},{11,10},{12... | collective-permute-start | bytes 196616 | tf_op jit(solution)/shard_map/ppermute | solution.py:17
  94.3 6.3 %collective-permute-start.5 = (f32[1,16,1024]{2,0,1:T(1,128)S(1)}, f32[1,16,1024]{2,0,1:T(1,128)S(1)}, u32[]{:S(2)}, u32[]{:S(2)}) collective-permute-start(f32[1,16,1024]{2,0,1:T(1,128)S(1)} %get-tuple-element.14), channel_id=1, source_target_pairs={{0,1},{1,2},{2,3},{3,4},{4,5},{5,6},{6,7},{8,9},{9,10},{10,11},{11... | collective-permute-start | bytes 196616 | tf_op jit(solution)/shard_map/ppermute | solution.py:15
  100.7 4.1 %collective-permute-done.4 = f32[1,16,1024]{2,0,1:T(1,128)S(1)} collective-permute-done((f32[1,16,1024]{2,0,1:T(1,128)S(1)}, f32[1,16,1024]{2,0,1:T(1,128)S(1)}, u32[]{:S(2)}, u32[]{:S(2)}) %collective-permute-start.4) | collective-permute-done | bytes 65568 | tf_op jit(solution)/shard_map/ppermute | solution.py:17
  104.8 6.4 %collective-permute-done.5 = f32[1,16,1024]{2,0,1:T(1,128)S(1)} collective-permute-done((f32[1,16,1024]{2,0,1:T(1,128)S(1)}, f32[1,16,1024]{2,0,1:T(1,128)S(1)}, u32[]{:S(2)}, u32[]{:S(2)}) %collective-permute-start.5) | collective-permute-done | bytes 65568 | tf_op jit(solution)/shard_map/ppermute | solution.py:15
  111.2 9.1 %collective-permute-start.6 = (f32[18,1,1024]{2,0,1:T(8,128)S(1)}, f32[18,1,1024]{2,0,1:T(8,128)S(1)}, u32[]{:S(2)}, u32[]{:S(2)}) collective-permute-start(f32[18,1,1024]{2,0,1:T(8,128)S(1)} %get-tuple-element.13), channel_id=1, source_target_pairs={{8,0},{16,8},{24,16},{32,24},{40,32},{48,40},{56,48},{64,56},{72,6... | collective-permute-start | bytes 221192 | tf_op jit(solution)/shard_map/ppermute | solution.py:17
  120.3 2.1 %collective-permute-start.7 = (f32[18,1,1024]{2,0,1:T(8,128)S(1)}, f32[18,1,1024]{2,0,1:T(8,128)S(1)}, u32[]{:S(2)}, u32[]{:S(2)}) collective-permute-start(f32[18,1,1024]{2,0,1:T(8,128)S(1)} %get-tuple-element.12), channel_id=1, source_target_pairs={{0,8},{8,16},{16,24},{24,32},{32,40},{40,48},{48,56},{56,64},{64,7... | collective-permute-start | bytes 221192 | tf_op jit(solution)/shard_map/ppermute | solution.py:15
  122.5 11.4 %collective-permute-done.7 = f32[18,1,1024]{2,0,1:T(8,128)S(1)} collective-permute-done((f32[18,1,1024]{2,0,1:T(8,128)S(1)}, f32[18,1,1024]{2,0,1:T(8,128)S(1)}, u32[]{:S(2)}, u32[]{:S(2)}) %collective-permute-start.7) | collective-permute-done | bytes 73760 | tf_op jit(solution)/shard_map/ppermute | solution.py:15
  134.9 5.8 %fusion.2 = f32[16,1024]{1,0:T(8,128)S(1)} fusion(f32[16,16,1024]{2,0,1:T(8,128)S(1)} %fusion.29, f32[18,18,1026]{2,0,1:T(8,128)S(1)} %get-tuple-element.5, f32[18,18,1026]{2,0,1:T(8,128)S(1)} %select_maximum_fusion.6, f32[1,16,1024]{2,0,1:T(1,128)S(1)} %collective-permute-done.4, f32[1,16,1024]{2,0,1:T(1,128)S(1)} %collective-permute-done.5, ...), kind=kLoop, calls=%fused_computation.20 | loop fusion | flops 10993664 | bytes 12926976 | tf_op jit(solution)/shard_map/reduce_sum | solution.py:108
  140.7 5.6 %collective-permute-start.8 = (f32[16,1024]{1,0:T(8,128)S(1)}, f32[16,1024]{1,0:T(8,128)S(1)}, u32[]{:S(2)}, u32[]{:S(2)}) collective-permute-start(f32[16,1024]{1,0:T(8,128)S(1)} %broadcast_multiply_fusion), channel_id=1, source_target_pairs={{0,1},{1,0},{2,3},{3,2},{4,5},{5,4},{6,7},{7,6},{8,9},{9,8},{10,11... | collective-permute-start | bytes 196616 | tf_op jit(solution)/shard_map/ppermute | solution.py:67
  146.3 9.3 %collective-permute-done.8 = f32[16,1024]{1,0:T(8,128)S(1)} collective-permute-done((f32[16,1024]{1,0:T(8,128)S(1)}, f32[16,1024]{1,0:T(8,128)S(1)}, u32[]{:S(2)}, u32[]{:S(2)}) %collective-permute-start.8) | collective-permute-done | bytes 65568 | tf_op jit(solution)/shard_map/ppermute | solution.py:67
  155.6 1.9 collective-permute-start.9
  157.5 4.2 %collective-permute-done.9 = f32[16,1024]{1,0:T(8,128)S(1)} collective-permute-done((f32[16,1024]{1,0:T(8,128)S(1)}, f32[16,1024]{1,0:T(8,128)S(1)}, u32[]{:S(2)}, u32[]{:S(2)}) %collective-permute-start.9) | collective-permute-done | bytes 65568 | tf_op jit(solution)/shard_map/ppermute | solution.py:67
  161.7 2.0 collective-permute-start.10
  163.9 5.5 %collective-permute-done.10 = f32[16,1024]{1,0:T(8,128)S(1)} collective-permute-done((f32[16,1024]{1,0:T(8,128)S(1)}, f32[16,1024]{1,0:T(8,128)S(1)}, u32[]{:S(2)}, u32[]{:S(2)}) %collective-permute-start.10) | collective-permute-done | bytes 65568 | tf_op jit(solution)/shard_map/ppermute | solution.py:67
  169.5 1.9 collective-permute-start.11
  171.4 11.1 %collective-permute-start.12 = (f32[2,1,1024]{2,1,0:T(1,128)S(1)}, f32[2,1,1024]{2,1,0:T(1,128)S(1)}, u32[]{:S(2)}, u32[]{:S(2)}) collective-permute-start(f32[2,1,1024]{2,1,0:T(1,128)S(1)} %get-tuple-element.21), channel_id=1, source_target_pairs={{8,0},{16,8},{24,16},{32,24},{40,32},{48,40},{56,48},{64,56},{72,6... | collective-permute-start | bytes 24584 | tf_op jit(solution)/shard_map/ppermute | solution.py:17
  182.8 1.0 collective-permute-done.12
  184.3 11.1 %collective-permute-start.13 = (f32[1,1024]{1,0:T(1,128)S(1)}, f32[1,1024]{1,0:T(1,128)S(1)}, u32[]{:S(2)}, u32[]{:S(2)}) collective-permute-start(f32[1,1024]{1,0:T(1,128)S(1)} %get-tuple-element.23), channel_id=1, source_target_pairs={{8,0},{16,8},{24,16},{32,24},{40,32},{48,40},{56,48},{64,56},{72,6... | collective-permute-start | bytes 12296 | tf_op jit(solution)/shard_map/ppermute | solution.py:17
  195.4 1.9 collective-permute-start.14
  197.3 10.5 %collective-permute-done.14 = f32[1,1024]{1,0:T(1,128)S(1)} collective-permute-done((f32[1,1024]{1,0:T(1,128)S(1)}, f32[1,1024]{1,0:T(1,128)S(1)}, u32[]{:S(2)}, u32[]{:S(2)}) %collective-permute-start.14) | collective-permute-done | bytes 4128 | tf_op jit(solution)/shard_map/ppermute | solution.py:15
  (40 shorter events, 5.6 us)
Async XLA Ops:
  4.9 29.1 %collective-permute-start = (f32[3,1,16,1024]{3,1,2,0:T(1,128)}, f32[3,1,16,1024]{3,1,2,0:T(1,128)S(1)}, u32[]{:S(2)}, u32[]{:S(2)}) collective-permute-start(f32[3,1,16,1024]{3,1,2,0:T(1,128)} %get-tuple-element.10), channel_id=1, source_target_pairs={{0,1},{1,2},{2,3},{3,4},{4,5},{5,6},{6,7},{8,9},{9,10},{10,11},{11... | collective-permute-start | bytes 589832 | tf_op jit(solution)/shard_map/ppermute | solution.py:15
  20.6 25.4 %collective-permute-start.1 = (f32[3,1,16,1024]{3,1,2,0:T(1,128)}, f32[3,1,16,1024]{3,1,2,0:T(1,128)}, u32[]{:S(2)}, u32[]{:S(2)}) collective-permute-start(f32[3,1,16,1024]{3,1,2,0:T(1,128)} %get-tuple-element.11), channel_id=1, source_target_pairs={{1,0},{2,1},{3,2},{4,3},{5,4},{6,5},{7,6},{9,8},{10,9},{11,10},{12... | collective-permute-start | bytes 589832 | tf_op jit(solution)/shard_map/ppermute | solution.py:17
  22.5 44.2 %copy-start.3 = (f32[16,1024]{1,0:T(8,128)S(1)}, f32[16,1024]{1,0:T(8,128)}, u32[]{:S(2)}) copy-start(f32[16,1024]{1,0:T(8,128)} %param.12) | copy-start | bytes 196612
  22.5 44.2 %copy-start.5 = (s32[16,1024]{1,0:T(8,128)S(1)}, s32[16,1024]{1,0:T(8,128)}, u32[]{:S(2)}) copy-start(s32[16,1024]{1,0:T(8,128)} %param.13) | copy-start | bytes 196612
  46.8 22.4 %collective-permute-start.2 = (f32[3,18,1,1024]{3,1,2,0:T(8,128)S(1)}, f32[3,18,1,1024]{3,1,2,0:T(8,128)S(1)}, u32[]{:S(2)}, u32[]{:S(2)}) collective-permute-start(f32[3,18,1,1024]{3,1,2,0:T(8,128)S(1)} %get-tuple-element.8), channel_id=1, source_target_pairs={{0,8},{8,16},{16,24},{24,32},{32,40},{40,48},{48,56},{56,64},{64,7... | collective-permute-start | bytes 663560 | tf_op jit(solution)/shard_map/ppermute | solution.py:15
  48.8 22.2 %collective-permute-start.3 = (f32[3,18,1,1024]{3,1,2,0:T(8,128)S(1)}, f32[3,18,1,1024]{3,1,2,0:T(8,128)S(1)}, u32[]{:S(2)}, u32[]{:S(2)}) collective-permute-start(f32[3,18,1,1024]{3,1,2,0:T(8,128)S(1)} %get-tuple-element.9), channel_id=1, source_target_pairs={{8,0},{16,8},{24,16},{32,24},{40,32},{48,40},{56,48},{64,56},{72,6... | collective-permute-start | bytes 663560 | tf_op jit(solution)/shard_map/ppermute | solution.py:17
  78.9 1.2 copy-start
  78.9 1.5 copy-start.1
  78.9 1.8 copy-start.2
  86.1 18.7 %collective-permute-start.4 = (f32[1,16,1024]{2,0,1:T(1,128)S(1)}, f32[1,16,1024]{2,0,1:T(1,128)S(1)}, u32[]{:S(2)}, u32[]{:S(2)}) collective-permute-start(f32[1,16,1024]{2,0,1:T(1,128)S(1)} %get-tuple-element.15), channel_id=1, source_target_pairs={{1,0},{2,1},{3,2},{4,3},{5,4},{6,5},{7,6},{9,8},{10,9},{11,10},{12... | collective-permute-start | bytes 196616 | tf_op jit(solution)/shard_map/ppermute | solution.py:17
  94.3 16.9 %collective-permute-start.5 = (f32[1,16,1024]{2,0,1:T(1,128)S(1)}, f32[1,16,1024]{2,0,1:T(1,128)S(1)}, u32[]{:S(2)}, u32[]{:S(2)}) collective-permute-start(f32[1,16,1024]{2,0,1:T(1,128)S(1)} %get-tuple-element.14), channel_id=1, source_target_pairs={{0,1},{1,2},{2,3},{3,4},{4,5},{5,6},{6,7},{8,9},{9,10},{10,11},{11... | collective-permute-start | bytes 196616 | tf_op jit(solution)/shard_map/ppermute | solution.py:15
  111.2 23.6 %copy-start.4 = (f32[16,16,1024]{2,1,0:T(8,128)S(1)}, f32[16,16,1024]{2,1,0:T(8,128)}, u32[]{:S(2)}) copy-start(f32[16,16,1024]{2,1,0:T(8,128)} %param.11) | copy-start | bytes 3145732
  111.2 11.3 %collective-permute-start.6 = (f32[18,1,1024]{2,0,1:T(8,128)S(1)}, f32[18,1,1024]{2,0,1:T(8,128)S(1)}, u32[]{:S(2)}, u32[]{:S(2)}) collective-permute-start(f32[18,1,1024]{2,0,1:T(8,128)S(1)} %get-tuple-element.13), channel_id=1, source_target_pairs={{8,0},{16,8},{24,16},{32,24},{40,32},{48,40},{56,48},{64,56},{72,6... | collective-permute-start | bytes 221192 | tf_op jit(solution)/shard_map/ppermute | solution.py:17
  120.3 13.6 %collective-permute-start.7 = (f32[18,1,1024]{2,0,1:T(8,128)S(1)}, f32[18,1,1024]{2,0,1:T(8,128)S(1)}, u32[]{:S(2)}, u32[]{:S(2)}) collective-permute-start(f32[18,1,1024]{2,0,1:T(8,128)S(1)} %get-tuple-element.12), channel_id=1, source_target_pairs={{0,8},{8,16},{16,24},{24,32},{32,40},{40,48},{48,56},{56,64},{64,7... | collective-permute-start | bytes 221192 | tf_op jit(solution)/shard_map/ppermute | solution.py:15
  134.9 47.7 %copy-start.6 = (f32[16]{0:T(128)S(1)}, f32[16]{0:T(128)}, u32[]{:S(2)}) copy-start(f32[16]{0:T(128)} %param.15) | copy-start | bytes 196
  134.9 47.7 %copy-start.7 = (s32[16]{0:T(128)S(1)}, s32[16]{0:T(128)}, u32[]{:S(2)}) copy-start(s32[16]{0:T(128)} %param.14) | copy-start | bytes 196
  140.7 14.9 %collective-permute-start.8 = (f32[16,1024]{1,0:T(8,128)S(1)}, f32[16,1024]{1,0:T(8,128)S(1)}, u32[]{:S(2)}, u32[]{:S(2)}) collective-permute-start(f32[16,1024]{1,0:T(8,128)S(1)} %broadcast_multiply_fusion), channel_id=1, source_target_pairs={{0,1},{1,0},{2,3},{3,2},{4,5},{5,4},{6,7},{7,6},{8,9},{9,8},{10,11... | collective-permute-start | bytes 196616 | tf_op jit(solution)/shard_map/ppermute | solution.py:67
  155.6 6.2 %collective-permute-start.9 = (f32[16,1024]{1,0:T(8,128)S(1)}, f32[16,1024]{1,0:T(8,128)S(1)}, u32[]{:S(2)}, u32[]{:S(2)}) collective-permute-start(f32[16,1024]{1,0:T(8,128)S(1)} %fusion.65), channel_id=1, source_target_pairs={{0,2},{1,3},{2,0},{3,1},{4,6},{5,7},{6,4},{7,5},{8,10},{9,11},{10,... | collective-permute-start | bytes 196616 | tf_op jit(solution)/shard_map/ppermute | solution.py:67
  161.7 7.7 %collective-permute-start.10 = (f32[16,1024]{1,0:T(8,128)S(1)}, f32[16,1024]{1,0:T(8,128)S(1)}, u32[]{:S(2)}, u32[]{:S(2)}) collective-permute-start(f32[16,1024]{1,0:T(8,128)S(1)} %add.254), channel_id=1, source_target_pairs={{0,4},{1,5},{2,6},{3,7},{4,0},{5,1},{6,2},{7,3},{8,12},{9,13},{10,... | collective-permute-start | bytes 196616 | tf_op jit(solution)/shard_map/ppermute | solution.py:67
  169.5 13.4 %collective-permute-start.11 = (f32[2,1,1024]{2,1,0:T(1,128)S(1)}, f32[2,1,1024]{2,1,0:T(1,128)S(1)}, u32[]{:S(2)}, u32[]{:S(2)}) collective-permute-start(f32[2,1,1024]{2,1,0:T(1,128)S(1)} %get-tuple-element.20), channel_id=1, source_target_pairs={{0,8},{8,16},{16,24},{24,32},{32,40},{40,48},{48,56},{56,64},{64,7... | collective-permute-start | bytes 24584 | tf_op jit(solution)/shard_map/ppermute | solution.py:15
  171.4 12.5 %collective-permute-start.12 = (f32[2,1,1024]{2,1,0:T(1,128)S(1)}, f32[2,1,1024]{2,1,0:T(1,128)S(1)}, u32[]{:S(2)}, u32[]{:S(2)}) collective-permute-start(f32[2,1,1024]{2,1,0:T(1,128)S(1)} %get-tuple-element.21), channel_id=1, source_target_pairs={{8,0},{16,8},{24,16},{32,24},{40,32},{48,40},{56,48},{64,56},{72,6... | collective-permute-start | bytes 24584 | tf_op jit(solution)/shard_map/ppermute | solution.py:17
  184.3 13.1 %collective-permute-start.13 = (f32[1,1024]{1,0:T(1,128)S(1)}, f32[1,1024]{1,0:T(1,128)S(1)}, u32[]{:S(2)}, u32[]{:S(2)}) collective-permute-start(f32[1,1024]{1,0:T(1,128)S(1)} %get-tuple-element.23), channel_id=1, source_target_pairs={{8,0},{16,8},{24,16},{32,24},{40,32},{48,40},{56,48},{64,56},{72,6... | collective-permute-start | bytes 12296 | tf_op jit(solution)/shard_map/ppermute | solution.py:17
  195.4 12.4 %collective-permute-start.14 = (f32[1,1024]{1,0:T(1,128)S(1)}, f32[1,1024]{1,0:T(1,128)S(1)}, u32[]{:S(2)}, u32[]{:S(2)}) collective-permute-start(f32[1,1024]{1,0:T(1,128)S(1)} %get-tuple-element.22), channel_id=1, source_target_pairs={{0,8},{8,16},{16,24},{24,32},{32,40},{40,48},{48,56},{56,64},{64,7... | collective-permute-start | bytes 12296 | tf_op jit(solution)/shard_map/ppermute | solution.py:15

commit v2 on v0

v2 whole, which is shorter than its diff:
```python
import jax
import jax.numpy as jnp
from jax import lax
from jax.sharding import PartitionSpec as P


def halo_swap(lo_face, hi_face, axis):
    count = lax.axis_size(axis)
    even = lax.axis_index(axis) % 2 == 0
    pairs_a = [(i, i ^ 1) for i in range(count)]
    pairs_b = [(i, i + 1) for i in range(1, count - 1, 2)] + [(i + 1, i) for i in range(1, count - 1, 2)]
    got_a = lax.ppermute(jnp.where(even, hi_face, lo_face), axis, pairs_a)
    got_b = lax.ppermute(jnp.where(even, lo_face, hi_face), axis, pairs_b)
    return jnp.where(even, got_b, got_a), jnp.where(even, got_a, got_b)


def butterfly_sum(part, axis):
    count = lax.axis_size(axis)
    order = [1 << k for k in range(1, count.bit_length() - 1)] + [1]
    for step in order:
        pairs = [(i, i ^ step) for i in range(lax.axis_size(axis))]
        part = part + lax.ppermute(part, axis, pairs)
    return part


def pad_last(stacked):
    widths = [(0, 0)] * (stacked.ndim - 1) + [(1, 1)]
    return jnp.pad(stacked, widths)


def flat_sides(padded):
    return [padded[2:, 1:-1], padded[:-2, 1:-1], padded[1:-1, 2:], padded[1:-1, :-2]]


def plane_sweep(p_pad, k_pad, anchor, source, trans):
    coef = jnp.zeros_like(trans)
    flow = jnp.zeros_like(trans)
    for k_side, p_side in zip(flat_sides(k_pad), flat_sides(p_pad)):
        face = 0.5 * (trans + k_side)
        coef = coef + face
        flow = flow + face * p_side
    return (anchor + source + flow) / (1.0 + coef)


def well_source(wells, rates, row_start, rows, cols, width):
    row_ids = row_start + jnp.arange(rows, dtype=jnp.int32)
    col_ids = jnp.arange(cols, dtype=jnp.int32)
    flat = row_ids[:, None] * width + col_ids[None, :]
    hit = flat[:, :, None] == wells[None, None, :]
    return 4.0 * jnp.sum(jnp.where(hit, rates[None, None, :], jnp.float32(0.0)), axis=-1)


def cube_sides(padded):
    return [
        padded[2:, 1:-1, 1:-1],
        padded[:-2, 1:-1, 1:-1],
        padded[1:-1, 2:, 1:-1],
        padded[1:-1, :-2, 1:-1],
        padded[1:-1, 1:-1, 2:],
        padded[1:-1, 1:-1, :-2],
    ]


def on_device(displacement, damage, modulus, toughness, pressure, crack_mask, wells, rates):
    depth_cells, tile_cells, width = displacement.shape
    total_depth = depth_cells * lax.axis_size("depth")
    total_rows = tile_cells * lax.axis_size("tile")
    depth_start = lax.axis_index("depth") * depth_cells
    tile_start = lax.axis_index("tile") * tile_cells
    stiff = ((1.0 - damage) ** 2 + 0.001) * modulus
    mask_f = crack_mask.astype(jnp.float32)

    lo_z, hi_z = halo_swap(
        jnp.concatenate([displacement[:2], stiff[:2], damage[:1]]),
        jnp.concatenate([displacement[-2:], stiff[-2:], damage[-1:]]),
        "depth",
    )
    u_z = jnp.concatenate([lo_z[0:2], displacement, hi_z[0:2]])
    c_z = jnp.concatenate([lo_z[2:4], stiff, hi_z[2:4]])
    d_lo, d_hi = lo_z[4:5], hi_z[4:5]

    ext = depth_cells + 4

    def tile_face(rows, edge):
        return jnp.concatenate(
            [
                u_z[:, rows].reshape(-1, width),
                c_z[:, rows].reshape(-1, width),
                damage[:, edge],
                pressure[rows],
                mask_f[rows],
            ]
        )

    lo_x, hi_x = halo_swap(tile_face(slice(0, 2), 0), tile_face(slice(tile_cells - 2, tile_cells), tile_cells - 1), "tile")

    def unpack(face):
        at = 0
        u_f = face[at:at + ext * 2].reshape(ext, 2, width)
        at += ext * 2
        c_f = face[at:at + ext * 2].reshape(ext, 2, width)
        at += ext * 2
        d_f = face[at:at + depth_cells].reshape(depth_cells, 1, width)
        at += depth_cells
        p_f = face[at:at + 2]
        m_f = face[at + 2:at + 4]
        return u_f, c_f, d_f, p_f, m_f

    u_lo, c_lo, dx_lo, p_lo, m_lo = unpack(lo_x)
    u_hi, c_hi, dx_hi, p_hi, m_hi = unpack(hi_x)
    u_p = pad_last(jnp.concatenate([u_lo, u_z, u_hi], axis=1))
    c_p = pad_last(jnp.concatenate([c_lo, c_z, c_hi], axis=1))

    u_c = u_p[1:-1, 1:-1, 1:-1]
    c_c = c_p[1:-1, 1:-1, 1:-1]
    coef = jnp.zeros_like(c_c)
    flux = jnp.zeros_like(c_c)
    for c_side, u_side in zip(cube_sides(c_p), cube_sides(u_p)):
        face = 0.5 * (c_c + c_side)
        coef = coef + face
        flux = flux + face * (u_side - u_c)
    p_ext = jnp.concatenate([p_lo, pressure, p_hi])
    m_ext = jnp.concatenate([m_lo, mask_f, m_hi])
    load = 4.0 * m_ext[1:-1] * p_ext[1:-1]
    z_ids = depth_start - 1 + jnp.arange(depth_cells + 2, dtype=jnp.int32)
    x_ids = tile_start - 1 + jnp.arange(tile_cells + 2, dtype=jnp.int32)
    force = jnp.where((z_ids == total_depth // 2)[:, None, None], load[None, :, :], jnp.float32(0.0))
    moved = u_c + 0.8 * (force + flux) / coef
    inside = ((z_ids >= 0) & (z_ids < total_depth))[:, None, None] & ((x_ids >= 0) & (x_ids < total_rows))[None, :, None]
    moved = jnp.where(inside, moved, jnp.float32(0.0))

    m_pad = pad_last(moved)
    own = moved[1:-1, 1:-1]
    energy = jnp.zeros_like(own)
    for m_side in cube_sides(m_pad):
        energy = energy + (m_side - own) ** 2
    energy = 0.25 * modulus * energy

    d_zx = jnp.concatenate([d_lo, damage, d_hi])
    d_x = jnp.concatenate([dx_lo, damage, dx_hi], axis=1)
    d_y = pad_last(damage)
    beside_all = (
        d_zx[2:] + d_zx[:-2] + d_x[:, 2:] + d_x[:, :-2] + d_y[:, :, 2:] + d_y[:, :, :-2]
    )
    trial = (2.0 * energy + toughness * beside_all) / (7.0 * toughness + 2.0 * energy)
    new_damage = jnp.maximum(damage, trial)
    partial_open = 4.0 / total_depth * jnp.sum(new_damage * own * own, axis=0)
    aperture = 0.5 + butterfly_sum(partial_open, "depth")
    trans = mask_f * aperture**3

    t_lo, t_hi = halo_swap(trans[:2], trans[-2:], "tile")
    t_ext = jnp.concatenate([t_lo, trans, t_hi])
    rows_in = ((x_ids >= 0) & (x_ids < total_rows))[:, None]
    src_ext = well_source(wells, rates, tile_start - 1, tile_cells + 2, width, width)
    k_pad = pad_last(t_ext)
    level = plane_sweep(pad_last(p_ext), k_pad, p_ext[1:-1], src_ext, t_ext[1:-1])
    level = jnp.where(rows_in, level, jnp.float32(0.0))
    return plane_sweep(pad_last(level), k_pad[1:-1], pressure, src_ext[1:-1], trans)


def solution(mesh):
    return jax.shard_map(
        on_device,
        mesh=mesh,
        in_specs=(
            P("depth", "tile", None),
            P("depth", "tile", None),
            P("depth", "tile", None),
            P("depth", "tile", None),
            P("tile", None),
            P("tile", None),
            P(),
            P(),
        ),
        out_specs=P("tile", None),
        check_vma=False,
    )
```

time: 339 us -> 191 us (0.56)
  waiting for transfers between devices: 209 us -> 31.8 us
  local copies, waits for them, and re-layouts: 2 us -> 42.1 us
  between operations: 13.8 us -> 0.54 us
  starting transfers between devices: 84 us -> 92.6 us
  other arithmetic: 29.6 us -> 22.9 us
    psum x1 -> x0, waiting for transfers between devices: 154 us -> none  [on_device(): aperture = 0.5 + lax.psum(partial_open, 'depth')]
    ppermute x12 -> x9, waiting for transfers between devices: 55.1 us -> 31.8 us  [the longest x3 17.2 us: butterfly_sum(): part = part + lax.ppermute(part, axis, pairs)]
    reshape x0 -> x12, local copies, waits for them, and re-layouts: none -> 17.8 us  [the longest x4 4.33 us: unpack(): d_f = face[at:at + depth_cells].reshape(depth_cells, 1, width)]
    concatenate x0 -> x2, local copies, waits for them, and re-layouts: none -> 11.3 us  [tile_face(): jnp.concatenate([u_z[:, rows].reshape(-1, width), c_z[:, rows].reshape(-1...]
    select_n x0 -> x7, other arithmetic: none -> 10.5 us  [the longest x1 7.26 us: on_device(): moved = jnp.where(inside, moved, jnp.float32(0.0))]
    slice x2 -> x12, local copies, waits for them, and re-layouts: 0.11 us -> 9.48 us  [the longest x2 2.93 us: on_device(): d_lo, d_hi = (lo_z[4:5], hi_z[4:5])]
    ppermute x12 -> x9, starting transfers between devices: 84 us -> 92.6 us  [the longest x3 36.7 us: halo_swap(): got_b = lax.ppermute(jnp.where(even, lo_face, hi_face), axis, pairs_b)]
    concatenate x5 -> x4, other arithmetic: 9.26 us -> 2.62 us  [the longest x1 1.41 us: on_device(): u_p = pad_last(jnp.concatenate([u_lo, u_z, u_hi], axis=1))]
  transfers between devices with their start and end apart: 13 -> 9, of which waited for: 11 -> 5; matrix products, arithmetic and copies ran while one was open for 0% -> 4% of each run, Pallas kernels for 0% -> 0%
where the time goes in v2:
time: 191 us; the launch traced here: 190 us
  starting transfers between devices  92.6 us (48%)
  local copies, waits for them, and re-layouts  42.1 us (22%)
  waiting for transfers between devices  31.8 us (17%)
  other arithmetic  22.9 us (12%)
    ppermute x3, starting transfers between devices, halo_swap(): got_b = lax.ppermute(jnp.where(even, lo_face, hi_face), axis, pairs_b)  36.7 us
    ppermute x3, starting transfers between devices, halo_swap(): got_a = lax.ppermute(jnp.where(even, hi_face, lo_face), axis, pairs_a)  34.5 us
    ppermute x3, starting transfers between devices, butterfly_sum(): part = part + lax.ppermute(part, axis, pairs)  21.5 us
    ppermute x3, waiting for transfers between devices, butterfly_sum(): part = part + lax.ppermute(part, axis, pairs)  17.2 us
    concatenate x2, local copies, waits for them, and re-layouts, tile_face(): jnp.concatenate([u_z[:, rows].reshape(-1, width), c_z[:, rows].reshape(-1...  11.3 us
    ppermute x3, waiting for transfers between devices, halo_swap(): got_a = lax.ppermute(jnp.where(even, hi_face, lo_face), axis, pairs_a)  10.1 us
    select_n x1, other arithmetic, on_device(): moved = jnp.where(inside, moved, jnp.float32(0.0))  7.26 us
    ppermute x3, waiting for transfers between devices, halo_swap(): got_b = lax.ppermute(jnp.where(even, lo_face, hi_face), axis, pairs_b)  4.54 us
  transfers between devices with their start and end apart: 9, of which 5 were waited for; matrix products, arithmetic and copies ran while one was open for 4% of the time, Pallas kernels for 0%

profile of v2, /device:TPU:4, one launch (start us, length us, event | category | flops | bytes accessed | tf_op | source)
XLA Modules:
  0.0 190.0 jit_solution(12345736096432875607)
XLA Ops:
  1.0 1.7 add_multiply_fusion
  5.0 16.2 %collective-permute-start.1 = (f32[5,16,1024]{2,1,0:T(8,128)S(1)}, f32[5,16,1024]{2,1,0:T(8,128)}, u32[]{:S(2)}, u32[]{:S(2)}) collective-permute-start(f32[5,16,1024]{2,1,0:T(8,128)S(1)} %get-tuple-element.24), channel_id=1, source_target_pairs={{0,1},{1,0},{2,3},{3,2},{4,5},{5,4},{6,7},{7,6},{8,9},{9,8},{10,11... | collective-permute-start | bytes 983048 | tf_op jit(solution)/shard_map/ppermute | solution.py:12
  24.0 1.5 copy_bitcast_fusion
  25.5 10.1 %collective-permute-done.1 = f32[5,16,1024]{2,1,0:T(8,128)} collective-permute-done((f32[5,16,1024]{2,1,0:T(8,128)S(1)}, f32[5,16,1024]{2,1,0:T(8,128)}, u32[]{:S(2)}, u32[]{:S(2)}) %collective-permute-start.1) | collective-permute-done | bytes 327712 | tf_op jit(solution)/shard_map/ppermute | solution.py:12
  39.0 1.7 reshape.114
  40.7 1.7 reshape.116
  42.4 1.7 pad_maximum_fusion.25
  44.1 1.7 reshape.113
  45.8 1.7 reshape.115
  47.5 6.0 %concatenate.77 = f32[100,1024]{1,0:T(8,128)} concatenate(f32[40,1024]{1,0:T(8,128)} %reshape.113, f32[40,1024]{1,0:T(8,128)} %reshape.114, f32[16,1024]{1,0:T(8,128)} %get-tuple-element.50, f32[2,1024]{1,0:T(2,128)} %get-tuple-element.52, f32[2,1024]{1,0:T(2,128)} %get-tuple-element.41), dimensions={0} | concatenate | bytes 819200 | tf_op jit(solution)/shard_map/concatenate | solution.py:85
  53.5 5.3 %concatenate.78 = f32[100,1024]{1,0:T(8,128)} concatenate(f32[40,1024]{1,0:T(8,128)} %reshape.115, f32[40,1024]{1,0:T(8,128)} %reshape.116, f32[16,1024]{1,0:T(8,128)} %get-tuple-element.49, f32[2,1024]{1,0:T(2,128)S(1)} %get-tuple-element.51, f32[2,1024]{1,0:T(2,128)S(1)} %get-tuple-element.42), dimensions={0} | concatenate | bytes 819200 | tf_op jit(solution)/shard_map/concatenate | solution.py:85
  60.0 29.6 %collective-permute-start.2 = (f32[100,1024]{1,0:T(8,128)S(1)}, f32[100,1024]{1,0:T(8,128)S(1)}, u32[]{:S(2)}, u32[]{:S(2)}) collective-permute-start(f32[100,1024]{1,0:T(8,128)S(1)} %get-tuple-element.19), channel_id=1, source_target_pairs={{8,16},{24,32},{40,48},{56,64},{72,80},{88,96},{104,112},{120,128}... | collective-permute-start | bytes 1228808 | tf_op jit(solution)/shard_map/ppermute | solution.py:13
  89.6 16.3 %collective-permute-start.3 = (f32[100,1024]{1,0:T(8,128)S(1)}, f32[100,1024]{1,0:T(8,128)S(1)}, u32[]{:S(2)}, u32[]{:S(2)}) collective-permute-start(f32[100,1024]{1,0:T(8,128)S(1)} %get-tuple-element.20), channel_id=1, source_target_pairs={{0,8},{8,0},{16,24},{24,16},{32,40},{40,32},{48,56},{56,48},{64,72... | collective-permute-start | bytes 1228808 | tf_op jit(solution)/shard_map/ppermute | solution.py:12
  107.1 1.5 slice.384
  108.6 1.5 slice.383
  114.2 1.7 reshape.119
  115.8 1.5 copy.20
  117.4 1.7 reshape.120
  119.0 1.5 copy.19
  120.6 1.7 reshape.118
  122.2 1.7 reshape.117
  127.4 7.3 %fusion.29 = f32[18,18,1024]{2,1,0:T(8,128)S(1)} fusion(f32[20,20,1024]{2,1,0:T(8,128)S(1)} %pad_maximum_fusion, f32[20,20,1024]{2,1,0:T(8,128)S(1)} %pad_maximum_fusion.1, f32[2,16,1024]{2,1,0:T(8,128)S(1)} %copy-done.3, f32[16,16,1024]{2,1,0:T(8,128)S(1)} %copy-done, f32[2,16,1024]{2,1,0:T(8,128)S(1)} %get-tuple-element.34, ...), kind=kLoop, calls=%fused_computation.53 | loop fusion | flops 17252352 | bytes 19254784 | tf_op jit(solution)/shard_map/jit(_where)/select_n | solution.py:130
  134.8 2.8 %fusion.54 = f32[16,1024]{1,0:T(8,128)S(1)} fusion(f32[16,16,1024]{2,1,0:T(8,128)S(1)} %copy-done.1, f32[16,16,1024]{2,1,0:T(8,128)S(1)} %copy-done.10, f32[16,1,1024]{2,1,0:T(1,128)S(1)} %copy-done.16, f32[16,1,1024]{2,1,0:T(1,128)S(1)} %copy-done.17, f32[1,16,1024]{2,1,0:T(8,128)S(1)} %copy-done.14, f32[1,16,1024]{2,1,0:T(8,128)S(1)} %copy-done.15, ...), kind=kLoop, calls=%fused_computation.91 | loop fusion | flops 9945088 | bytes 10485760 | tf_op jit(solution)/shard_map/reduce_sum | solution.py:147
  137.7 12.6 %collective-permute-start.4 = (f32[16,1024]{1,0:T(8,128)S(1)}, f32[16,1024]{1,0:T(8,128)S(1)}, u32[]{:S(2)}, u32[]{:S(2)}) collective-permute-start(f32[16,1024]{1,0:T(8,128)S(1)} %broadcast_multiply_fusion.1), channel_id=1, source_target_pairs={{0,2},{1,3},{2,0},{3,1},{4,6},{5,7},{6,4},{7,5},{8,10},{9,11},{10,... | collective-permute-start | bytes 196616 | tf_op jit(solution)/shard_map/ppermute | solution.py:22
  150.3 2.2 %collective-permute-done.4 = f32[16,1024]{1,0:T(8,128)S(1)} collective-permute-done((f32[16,1024]{1,0:T(8,128)S(1)}, f32[16,1024]{1,0:T(8,128)S(1)}, u32[]{:S(2)}, u32[]{:S(2)}) %collective-permute-start.4) | collective-permute-done | bytes 65568 | tf_op jit(solution)/shard_map/ppermute | solution.py:22
  152.5 2.2 %collective-permute-start.5 = (f32[16,1024]{1,0:T(8,128)S(1)}, f32[16,1024]{1,0:T(8,128)S(1)}, u32[]{:S(2)}, u32[]{:S(2)}) collective-permute-start(f32[16,1024]{1,0:T(8,128)S(1)} %fusion.95), channel_id=1, source_target_pairs={{0,4},{1,5},{2,6},{3,7},{4,0},{5,1},{6,2},{7,3},{8,12},{9,13},{10,... | collective-permute-start | bytes 196616 | tf_op jit(solution)/shard_map/ppermute | solution.py:22
  154.7 5.5 %collective-permute-done.5 = f32[16,1024]{1,0:T(8,128)S(1)} collective-permute-done((f32[16,1024]{1,0:T(8,128)S(1)}, f32[16,1024]{1,0:T(8,128)S(1)}, u32[]{:S(2)}, u32[]{:S(2)}) %collective-permute-start.5) | collective-permute-done | bytes 65568 | tf_op jit(solution)/shard_map/ppermute | solution.py:22
  160.2 6.7 %collective-permute-start.6 = (f32[16,1024]{1,0:T(8,128)S(1)}, f32[16,1024]{1,0:T(8,128)S(1)}, u32[]{:S(2)}, u32[]{:S(2)}) collective-permute-start(f32[16,1024]{1,0:T(8,128)S(1)} %add.308), channel_id=1, source_target_pairs={{0,1},{1,0},{2,3},{3,2},{4,5},{5,4},{6,7},{7,6},{8,9},{9,8},{10,11... | collective-permute-start | bytes 196616 | tf_op jit(solution)/shard_map/ppermute | solution.py:22
  167.0 9.5 %collective-permute-done.6 = f32[16,1024]{1,0:T(8,128)S(1)} collective-permute-done((f32[16,1024]{1,0:T(8,128)S(1)}, f32[16,1024]{1,0:T(8,128)S(1)}, u32[]{:S(2)}, u32[]{:S(2)}) %collective-permute-start.6) | collective-permute-done | bytes 65568 | tf_op jit(solution)/shard_map/ppermute | solution.py:22
  176.5 5.7 %collective-permute-start.8 = (f32[2,1024]{1,0:T(2,128)S(1)}, f32[2,1024]{1,0:T(2,128)S(1)}, u32[]{:S(2)}, u32[]{:S(2)}) collective-permute-start(f32[2,1024]{1,0:T(2,128)S(1)} %get-tuple-element.39), channel_id=1, source_target_pairs={{8,16},{24,32},{40,48},{56,64},{72,80},{88,96},{104,112},{120,128}... | collective-permute-start | bytes 24584 | tf_op jit(solution)/shard_map/ppermute | solution.py:13
  182.2 1.9 %collective-permute-start.7 = (f32[2,1024]{1,0:T(2,128)S(1)}, f32[2,1024]{1,0:T(2,128)S(1)}, u32[]{:S(2)}, u32[]{:S(2)}) collective-permute-start(f32[2,1024]{1,0:T(2,128)S(1)} %get-tuple-element.40), channel_id=1, source_target_pairs={{0,8},{8,0},{16,24},{24,16},{32,40},{40,32},{48,56},{56,48},{64,72... | collective-permute-start | bytes 24584 | tf_op jit(solution)/shard_map/ppermute | solution.py:12
  184.4 4.5 %collective-permute-done.8 = f32[2,1024]{1,0:T(2,128)S(1)} collective-permute-done((f32[2,1024]{1,0:T(2,128)S(1)}, f32[2,1024]{1,0:T(2,128)S(1)}, u32[]{:S(2)}, u32[]{:S(2)}) %collective-permute-start.8) | collective-permute-done | bytes 8224 | tf_op jit(solution)/shard_map/ppermute | solution.py:13
  (98 shorter events, 20.6 us)
Async XLA Ops:
  0.0 2.7 %copy-start = (f32[16,16,1024]{2,1,0:T(8,128)S(1)}, f32[16,16,1024]{2,1,0:T(8,128)}, u32[]{:S(2)}) copy-start(f32[16,16,1024]{2,1,0:T(8,128)} %param.8) | copy-start | bytes 3145732
  2.7 18.5 %copy-start.1 = (f32[16,16,1024]{2,1,0:T(8,128)S(1)}, f32[16,16,1024]{2,1,0:T(8,128)}, u32[]{:S(2)}) copy-start(f32[16,16,1024]{2,1,0:T(8,128)} %param.9) | copy-start | bytes 3145732
  2.7 19.2 %copy-start.18 = (s32[16,1024]{1,0:T(8,128)S(1)}, s32[16,1024]{1,0:T(8,128)}, u32[]{:S(2)}) copy-start(s32[16,1024]{1,0:T(8,128)} %param.13) | copy-start | bytes 196612
  3.6 21.9 %collective-permute-start = (f32[5,16,1024]{2,1,0:T(8,128)}, f32[5,16,1024]{2,1,0:T(8,128)}, u32[]{:S(2)}, u32[]{:S(2)}) collective-permute-start(f32[5,16,1024]{2,1,0:T(8,128)} %get-tuple-element.23), channel_id=1, source_target_pairs={{1,2},{3,4},{5,6},{2,1},{4,3},{6,5},{9,10},{11,12},{13,14},{10,9},... | collective-permute-start | bytes 983048 | tf_op jit(solution)/shard_map/ppermute | solution.py:13
  5.0 30.6 %collective-permute-start.1 = (f32[5,16,1024]{2,1,0:T(8,128)S(1)}, f32[5,16,1024]{2,1,0:T(8,128)}, u32[]{:S(2)}, u32[]{:S(2)}) collective-permute-start(f32[5,16,1024]{2,1,0:T(8,128)S(1)} %get-tuple-element.24), channel_id=1, source_target_pairs={{0,1},{1,0},{2,3},{3,2},{4,5},{5,4},{6,7},{7,6},{8,9},{9,8},{10,11... | collective-permute-start | bytes 983048 | tf_op jit(solution)/shard_map/ppermute | solution.py:12
  36.8 1.4 copy-start.9
  60.0 50.1 %collective-permute-start.2 = (f32[100,1024]{1,0:T(8,128)S(1)}, f32[100,1024]{1,0:T(8,128)S(1)}, u32[]{:S(2)}, u32[]{:S(2)}) collective-permute-start(f32[100,1024]{1,0:T(8,128)S(1)} %get-tuple-element.19), channel_id=1, source_target_pairs={{8,16},{24,32},{40,48},{56,64},{72,80},{88,96},{104,112},{120,128}... | collective-permute-start | bytes 1228808 | tf_op jit(solution)/shard_map/ppermute | solution.py:13
  89.6 20.4 %collective-permute-start.3 = (f32[100,1024]{1,0:T(8,128)S(1)}, f32[100,1024]{1,0:T(8,128)S(1)}, u32[]{:S(2)}, u32[]{:S(2)}) collective-permute-start(f32[100,1024]{1,0:T(8,128)S(1)} %get-tuple-element.20), channel_id=1, source_target_pairs={{0,8},{8,0},{16,24},{24,16},{32,40},{40,32},{48,56},{56,48},{64,72... | collective-permute-start | bytes 1228808 | tf_op jit(solution)/shard_map/ppermute | solution.py:12
  106.5 3.6 %copy-start.23 = (pred[18]{0:T(512)(128)(4,1)}, pred[18]{0:T(512)(128)(4,1)S(1)}, u32[]{:S(2)}) copy-start(pred[18]{0:T(512)(128)(4,1)S(1)} %get-tuple-element.53) | copy-start | bytes 58
  124.8 1.4 copy-start.4
  124.8 1.4 copy-start.5
  126.3 0.9 copy-start.3
  126.3 1.0 copy-start.6
  126.3 1.1 copy-start.7
  126.3 1.1 copy-start.22
  126.3 1.1 copy-start.25
  127.4 7.3 %copy-start.2 = (f32[16,16,1024]{2,1,0:T(8,128)S(1)}, f32[16,16,1024]{2,1,0:T(8,128)}, u32[]{:S(2)}) copy-start(f32[16,16,1024]{2,1,0:T(8,128)} %param.10) | copy-start | bytes 3145732
  127.4 7.3 %copy-start.10 = (f32[16,16,1024]{2,1,0:T(8,128)S(1)}, f32[16,16,1024]{2,1,0:T(8,128)}, u32[]{:S(2)}) copy-start(f32[16,16,1024]{2,1,0:T(8,128)} %param.11) | copy-start | bytes 3145732
  127.4 7.3 %copy-start.14 = (f32[1,16,1024]{2,1,0:T(8,128)S(1)}, f32[1,16,1024]{2,1,0:T(8,128)}, u32[]{:S(2)}) copy-start(f32[1,16,1024]{2,1,0:T(8,128)} %slice.384) | copy-start | bytes 196612
  127.4 7.3 %copy-start.15 = (f32[1,16,1024]{2,1,0:T(8,128)S(1)}, f32[1,16,1024]{2,1,0:T(8,128)}, u32[]{:S(2)}) copy-start(f32[1,16,1024]{2,1,0:T(8,128)} %slice.383) | copy-start | bytes 196612
  127.4 7.3 %copy-start.16 = (f32[16,1,1024]{2,1,0:T(1,128)S(1)}, f32[16,1,1024]{2,1,0:T(1,128)}, u32[]{:S(2)}) copy-start(f32[16,1,1024]{2,1,0:T(1,128)} %copy.20) | copy-start | bytes 196612
  127.4 7.3 %copy-start.17 = (f32[16,1,1024]{2,1,0:T(1,128)S(1)}, f32[16,1,1024]{2,1,0:T(1,128)}, u32[]{:S(2)}) copy-start(f32[16,1,1024]{2,1,0:T(1,128)} %copy.19) | copy-start | bytes 196612
  134.7 41.7 %copy-start.19 = (s32[16,1024]{1,0:T(8,128)S(1)}, s32[16,1024]{1,0:T(8,128)}, u32[]{:S(2)}) copy-start(s32[16,1024]{1,0:T(8,128)} %param.13) | copy-start | bytes 196612
  134.8 49.4 %copy-start.26 = (f32[16]{0:T(128)S(1)}, f32[16]{0:T(128)}, u32[]{:S(2)}) copy-start(f32[16]{0:T(128)} %param.15) | copy-start | bytes 196
  134.8 49.4 %copy-start.27 = (s32[16]{0:T(128)S(1)}, s32[16]{0:T(128)}, u32[]{:S(2)}) copy-start(s32[16]{0:T(128)} %param.14) | copy-start | bytes 196
  134.8 54.2 %copy-start.11 = (f32[16,1024]{1,0:T(8,128)S(1)}, f32[16,1024]{1,0:T(8,128)}, u32[]{:S(2)}) copy-start(f32[16,1024]{1,0:T(8,128)} %param.12) | copy-start | bytes 196612
  134.8 54.2 %copy-start.24 = (pred[18]{0:T(512)(128)(4,1)S(1)}, pred[18]{0:T(512)(128)(4,1)}, u32[]{:S(2)}) copy-start(pred[18]{0:T(512)(128)(4,1)} %copy-done.23) | copy-start | bytes 58
  137.7 14.8 %collective-permute-start.4 = (f32[16,1024]{1,0:T(8,128)S(1)}, f32[16,1024]{1,0:T(8,128)S(1)}, u32[]{:S(2)}, u32[]{:S(2)}) collective-permute-start(f32[16,1024]{1,0:T(8,128)S(1)} %broadcast_multiply_fusion.1), channel_id=1, source_target_pairs={{0,2},{1,3},{2,0},{3,1},{4,6},{5,7},{6,4},{7,5},{8,10},{9,11},{10,... | collective-permute-start | bytes 196616 | tf_op jit(solution)/shard_map/ppermute | solution.py:22
  152.5 7.7 %collective-permute-start.5 = (f32[16,1024]{1,0:T(8,128)S(1)}, f32[16,1024]{1,0:T(8,128)S(1)}, u32[]{:S(2)}, u32[]{:S(2)}) collective-permute-start(f32[16,1024]{1,0:T(8,128)S(1)} %fusion.95), channel_id=1, source_target_pairs={{0,4},{1,5},{2,6},{3,7},{4,0},{5,1},{6,2},{7,3},{8,12},{9,13},{10,... | collective-permute-start | bytes 196616 | tf_op jit(solution)/shard_map/ppermute | solution.py:22
  160.2 16.3 %collective-permute-start.6 = (f32[16,1024]{1,0:T(8,128)S(1)}, f32[16,1024]{1,0:T(8,128)S(1)}, u32[]{:S(2)}, u32[]{:S(2)}) collective-permute-start(f32[16,1024]{1,0:T(8,128)S(1)} %add.308), channel_id=1, source_target_pairs={{0,1},{1,0},{2,3},{3,2},{4,5},{5,4},{6,7},{7,6},{8,9},{9,8},{10,11... | collective-permute-start | bytes 196616 | tf_op jit(solution)/shard_map/ppermute | solution.py:22
  176.5 12.5 %collective-permute-start.8 = (f32[2,1024]{1,0:T(2,128)S(1)}, f32[2,1024]{1,0:T(2,128)S(1)}, u32[]{:S(2)}, u32[]{:S(2)}) collective-permute-start(f32[2,1024]{1,0:T(2,128)S(1)} %get-tuple-element.39), channel_id=1, source_target_pairs={{8,16},{24,32},{40,48},{56,64},{72,80},{88,96},{104,112},{120,128}... | collective-permute-start | bytes 24584 | tf_op jit(solution)/shard_map/ppermute | solution.py:13
  182.2 6.8 %collective-permute-start.7 = (f32[2,1024]{1,0:T(2,128)S(1)}, f32[2,1024]{1,0:T(2,128)S(1)}, u32[]{:S(2)}, u32[]{:S(2)}) collective-permute-start(f32[2,1024]{1,0:T(2,128)S(1)} %get-tuple-element.40), channel_id=1, source_target_pairs={{0,8},{8,0},{16,24},{24,16},{32,40},{40,32},{48,56},{56,48},{64,72... | collective-permute-start | bytes 24584 | tf_op jit(solution)/shard_map/ppermute | solution.py:12
  (5 other events, 3.9 us)

commit v3 on v2

--- a/solution.py
+++ b/solution.py
@@ -1,6 +1,10 @@
+import functools
+
 import jax
 import jax.numpy as jnp
 from jax import lax
+from jax.experimental import pallas as pl
+from jax.experimental.pallas import tpu as pltpu
 from jax.sharding import PartitionSpec as P
 
 
@@ -61,31 +65,163 @@
     ]
 
 
+X0 = 8
+
+
+def stencil_kernel(total_depth, total_rows, ids_ref, u_ref, dmg_ref, mod_ref, tgh_ref, zlo_ref, zhi_ref, xlo_ref,
+                   xhi_ref, load_ref, out_ref, u_s, c_s, d_s, m_s):
+    depth_cells, tile_cells, width = u_ref.shape
+    rows_all = u_s.shape[1]
+    ext = depth_cells + 4
+    own = slice(X0, X0 + tile_cells)
+    zero = jnp.zeros((rows_all, width), jnp.float32)
+
+    def clear(k, carry):
+        u_s[k] = zero
+        c_s[k] = zero
+        return carry
+
+    lax.fori_loop(0, ext, clear, 0)
+
+    def clear_d(k, carry):
+        d_s[k] = zero
+        return carry
+
+    lax.fori_loop(0, depth_cells + 2, clear_d, 0)
+
+    def place(k, carry):
+        dk = dmg_ref[k]
+        u_s[k + 2, own] = u_ref[k]
+        c_s[k + 2, own] = ((1.0 - dk) ** 2 + 0.001) * mod_ref[k]
+        d_s[k + 1, own] = dk
+        return carry
+
+    lax.fori_loop(0, depth_cells, place, 0)
+    u_s[0:2, own] = zlo_ref[0:2]
+    c_s[0:2, own] = zlo_ref[2:4]
+    d_s[0, own] = zlo_ref[4]
+    u_s[ext - 2:ext, own] = zhi_ref[0:2]
+    c_s[ext - 2:ext, own] = zhi_ref[2:4]
+    d_s[depth_cells + 1, own] = zhi_ref[4]
+    for z in range(ext):
+        u_s[z, X0 - 2:X0] = xlo_ref[2 * z:2 * z + 2]
+        c_s[z, X0 - 2:X0] = xlo_ref[2 * ext + 2 * z:2 * ext + 2 * z + 2]
+        u_s[z, X0 + tile_cells:X0 + tile_cells + 2] = xhi_ref[2 * z:2 * z + 2]
+        c_s[z, X0 + tile_cells:X0 + tile_cells + 2] = xhi_ref[2 * ext + 2 * z:2 * ext + 2 * z + 2]
+    for z in range(depth_cells):
+        d_s[z + 1, X0 - 1:X0] = xlo_ref[4 * ext + z:4 * ext + z + 1]
+        d_s[z + 1, X0 + tile_cells:X0 + tile_cells + 1] = xhi_ref[4 * ext + z:4 * ext + z + 1]
+
+    col = lax.broadcasted_iota(jnp.int32, (rows_all, width), 1)
+    row = lax.broadcasted_iota(jnp.int32, (rows_all, width), 0)
+    has_next = col < width - 1
+    has_prev = col > 0
+    depth_start = ids_ref[0]
+    x_glob = ids_ref[1] + row - X0
+    x_in = (x_glob >= 0) & (x_glob < total_rows)
+    load = load_ref[...]
+
+    def y_next(a):
+        return jnp.where(has_next, pltpu.roll(a, width - 1, 1), 0.0)
+
+    def y_prev(a):
+        return jnp.where(has_prev, pltpu.roll(a, 1, 1), 0.0)
+
+    def x_next(a):
+        return pltpu.roll(a, rows_all - 1, 0)
+
+    def x_prev(a):
+        return pltpu.roll(a, 1, 0)
+
+    def moved_body(k, carry):
+        uc = u_s[k + 1]
+        cc = c_s[k + 1]
+        pairs = [
+            (c_s[k + 2], u_s[k + 2]),
+            (c_s[k], u_s[k]),
+            (x_next(cc), x_next(uc)),
+            (x_prev(cc), x_prev(uc)),
+            (y_next(cc), y_next(uc)),
+            (y_prev(cc), y_prev(uc)),
+        ]
+        coef = zero
+        flux = zero
+        for cn, un in pairs:
+            face = 0.5 * (cc + cn)
+            coef = coef + face
+            flux = flux + face * (un - uc)
+        z_glob = depth_start + k - 1
+        force = jnp.where(z_glob == total_depth // 2, load, 0.0)
+        moved = uc + 0.8 * (force + flux) / coef
+        keep = x_in & (z_glob >= 0) & (z_glob < total_depth)
+        m_s[k] = jnp.where(keep, moved, 0.0)
+        return carry
+
+    lax.fori_loop(0, depth_cells + 2, moved_body, 0)
+
+    def energy_body(k, acc):
+        mc = m_s[k + 1]
+        energy = (
+            (m_s[k + 2] - mc) ** 2 + (m_s[k] - mc) ** 2 + (x_next(mc) - mc) ** 2 + (x_prev(mc) - mc) ** 2
+            + (y_next(mc) - mc) ** 2 + (y_prev(mc) - mc) ** 2
+        )
+        dc = d_s[k + 1]
+        beside = d_s[k + 2] + d_s[k] + x_next(dc) + x_prev(dc) + y_next(dc) + y_prev(dc)
+        energy = 0.25 * mod_ref[k] * energy[own]
+        tough = tgh_ref[k]
+        trial = (2.0 * energy + tough * beside[own]) / (7.0 * tough + 2.0 * energy)
+        new_damage = jnp.maximum(dmg_ref[k], trial)
+        mo = mc[own]
+        return acc + new_damage * mo * mo
+
+    acc = lax.fori_loop(0, depth_cells, energy_body, jnp.zeros((tile_cells, width), jnp.float32))
+    out_ref[...] = (4.0 / total_depth) * acc
+
+
+def stencil_partial(ids, u, dmg, mod, tgh, zlo, zhi, xlo, xhi, load32, total_depth, total_rows):
+    depth_cells, tile_cells, width = u.shape
+    rows_all = tile_cells + 2 * X0
+    vmem = pl.BlockSpec(memory_space=pltpu.VMEM)
+    return pl.pallas_call(
+        functools.partial(stencil_kernel, total_depth, total_rows),
+        out_shape=jax.ShapeDtypeStruct((tile_cells, width), jnp.float32),
+        in_specs=[pl.BlockSpec(memory_space=pltpu.SMEM)] + [vmem] * 9,
+        out_specs=vmem,
+        scratch_shapes=[
+            pltpu.VMEM((depth_cells + 4, rows_all, width), jnp.float32),
+            pltpu.VMEM((depth_cells + 4, rows_all, width), jnp.float32),
+            pltpu.VMEM((depth_cells + 2, rows_all, width), jnp.float32),
+            pltpu.VMEM((depth_cells + 2, rows_all, width), jnp.float32),
+        ],
+    )(ids, u, dmg, mod, tgh, zlo, zhi, xlo, xhi, load32)
+
+
 def on_device(displacement, damage, modulus, toughness, pressure, crack_mask, wells, rates):
     depth_cells, tile_cells, width = displacement.shape
     total_depth = depth_cells * lax.axis_size("depth")
     total_rows = tile_cells * lax.axis_size("tile")
     depth_start = lax.axis_index("depth") * depth_cells
     tile_start = lax.axis_index("tile") * tile_cells
-    stiff = ((1.0 - damage) ** 2 + 0.001) * modulus
     mask_f = crack_mask.astype(jnp.float32)
 
+    def stiff_of(dmg, mod):
+        return ((1.0 - dmg) ** 2 + 0.001) * mod
+
     lo_z, hi_z = halo_swap(
-        jnp.concatenate([displacement[:2], stiff[:2], damage[:1]]),
-        jnp.concatenate([displacement[-2:], stiff[-2:], damage[-1:]]),
+        jnp.concatenate([displacement[:2], stiff_of(damage[:2], modulus[:2]), damage[:1]]),
+        jnp.concatenate([displacement[-2:], stiff_of(damage[-2:], modulus[-2:]), damage[-1:]]),
         "depth",
     )
-    u_z = jnp.concatenate([lo_z[0:2], displacement, hi_z[0:2]])
-    c_z = jnp.concatenate([lo_z[2:4], stiff, hi_z[2:4]])
-    d_lo, d_hi = lo_z[4:5], hi_z[4:5]
 
     ext = depth_cells + 4
 
     def tile_face(rows, edge):
         return jnp.concatenate(
             [
-                u_z[:, rows].reshape(-1, width),
-                c_z[:, rows].reshape(-1, width),
+                jnp.concatenate([lo_z[0:2, rows], displacement[:, rows], hi_z[0:2, rows]]).reshape(-1, width),
+                jnp.concatenate(
+                    [lo_z[2:4, rows], stiff_of(damage[:, rows], modulus[:, rows]), hi_z[2:4, rows]]
+                ).reshape(-1, width),
                 damage[:, edge],
                 pressure[rows],
                 mask_f[rows],
@@ -94,57 +230,16 @@
 
     lo_x, hi_x = halo_swap(tile_face(slice(0, 2), 0), tile_face(slice(tile_cells - 2, tile_cells), tile_cells - 1), "tile")
 
-    def unpack(face):
-        at = 0
-        u_f = face[at:at + ext * 2].reshape(ext, 2, width)
-        at += ext * 2
-        c_f = face[at:at + ext * 2].reshape(ext, 2, width)
-        at += ext * 2
-        d_f = face[at:at + depth_cells].reshape(depth_cells, 1, width)
-        at += depth_cells
-        p_f = face[at:at + 2]
-        m_f = face[at + 2:at + 4]
-        return u_f, c_f, d_f, p_f, m_f
-
-    u_lo, c_lo, dx_lo, p_lo, m_lo = unpack(lo_x)
-    u_hi, c_hi, dx_hi, p_hi, m_hi = unpack(hi_x)
-    u_p = pad_last(jnp.concatenate([u_lo, u_z, u_hi], axis=1))
-    c_p = pad_last(jnp.concatenate([c_lo, c_z, c_hi], axis=1))
-
-    u_c = u_p[1:-1, 1:-1, 1:-1]
-    c_c = c_p[1:-1, 1:-1, 1:-1]
-    coef = jnp.zeros_like(c_c)
-    flux = jnp.zeros_like(c_c)
-    for c_side, u_side in zip(cube_sides(c_p), cube_sides(u_p)):
-        face = 0.5 * (c_c + c_side)
-        coef = coef + face
-        flux = flux + face * (u_side - u_c)
+    p_lo, m_lo = lo_x[-4:-2], lo_x[-2:]
+    p_hi, m_hi = hi_x[-4:-2], hi_x[-2:]
     p_ext = jnp.concatenate([p_lo, pressure, p_hi])
     m_ext = jnp.concatenate([m_lo, mask_f, m_hi])
-    load = 4.0 * m_ext[1:-1] * p_ext[1:-1]
-    z_ids = depth_start - 1 + jnp.arange(depth_cells + 2, dtype=jnp.int32)
+    load32 = jnp.pad(4.0 * m_ext[1:-1] * p_ext[1:-1], ((X0 - 1, X0 - 1), (0, 0)))
     x_ids = tile_start - 1 + jnp.arange(tile_cells + 2, dtype=jnp.int32)
-    force = jnp.where((z_ids == total_depth // 2)[:, None, None], load[None, :, :], jnp.float32(0.0))
-    moved = u_c + 0.8 * (force + flux) / coef
-    inside = ((z_ids >= 0) & (z_ids < total_depth))[:, None, None] & ((x_ids >= 0) & (x_ids < total_rows))[None, :, None]
-    moved = jnp.where(inside, moved, jnp.float32(0.0))
-
-    m_pad = pad_last(moved)
-    own = moved[1:-1, 1:-1]
-    energy = jnp.zeros_like(own)
-    for m_side in cube_sides(m_pad):
-        energy = energy + (m_side - own) ** 2
-    energy = 0.25 * modulus * energy
-
-    d_zx = jnp.concatenate([d_lo, damage, d_hi])
-    d_x = jnp.concatenate([dx_lo, damage, dx_hi], axis=1)
-    d_y = pad_last(damage)
-    beside_all = (
-        d_zx[2:] + d_zx[:-2] + d_x[:, 2:] + d_x[:, :-2] + d_y[:, :, 2:] + d_y[:, :, :-2]
+    ids = jnp.stack([depth_start, tile_start]).astype(jnp.int32)
+    partial_open = stencil_partial(
+        ids, displacement, damage, modulus, toughness, lo_z, hi_z, lo_x, hi_x, load32, total_depth, total_rows
     )
-    trial = (2.0 * energy + toughness * beside_all) / (7.0 * toughness + 2.0 * energy)
-    new_damage = jnp.maximum(damage, trial)
-    partial_open = 4.0 / total_depth * jnp.sum(new_damage * own * own, axis=0)
     aperture = 0.5 + butterfly_sum(partial_open, "depth")
     trans = mask_f * aperture**3
 

time: 191 us -> 155 us (0.81)
  the two profiles are of different devices: /device:TPU:4 before, /device:TPU:14 now
where the time goes in v3:
time: 155 us; the launch traced here: 154 us
  starting transfers between devices  78.2 us (50%)
  waiting for transfers between devices  51.9 us (33%)
  Pallas kernels  12 us (8%)
  other arithmetic  6.52 us (4%)
  local copies, waits for them, and re-layouts  5.18 us (3%)
    ppermute x3, starting transfers between devices, halo_swap(): got_b = lax.ppermute(jnp.where(even, lo_face, hi_face), axis, pairs_b)  62.9 us
    ppermute x3, waiting for transfers between devices, butterfly_sum(): part = part + lax.ppermute(part, axis, pairs)  20.3 us
    ppermute x3, waiting for transfers between devices, halo_swap(): got_b = lax.ppermute(jnp.where(even, lo_face, hi_face), axis, pairs_b)  19.3 us
    ppermute x3, waiting for transfers between devices, halo_swap(): got_a = lax.ppermute(jnp.where(even, hi_face, lo_face), axis, pairs_a)  12.3 us
    pallas_call x1, Pallas kernels, stencil_partial(): pl.pallas_call(functools.partial(stencil_kernel, total_depth, total_rows)...  12 us
    ppermute x3, starting transfers between devices, butterfly_sum(): part = part + lax.ppermute(part, axis, pairs)  9.51 us
    ppermute x3, starting transfers between devices, halo_swap(): got_a = lax.ppermute(jnp.where(even, hi_face, lo_face), axis, pairs_a)  5.88 us
  transfers between devices with their start and end apart: 9, of which 7 were waited for; matrix products, arithmetic and copies ran while one was open for 4% of the time, Pallas kernels for 0%

profile of v3, /device:TPU:14, one launch (start us, length us, event | category | flops | bytes accessed | tf_op | source)
XLA Modules:
  0.0 154.2 jit_solution(9848769914225365899)
XLA Ops:
  0.0 0.9 fusion.42
  0.9 1.3 slice_multiply_fusion.3
  2.2 15.6 %collective-permute-start = (f32[5,16,1024]{2,1,0:T(8,128)S(1)}, f32[5,16,1024]{2,1,0:T(8,128)S(1)}, u32[]{:S(2)}, u32[]{:S(2)}) collective-permute-start(f32[5,16,1024]{2,1,0:T(8,128)S(1)} %get-tuple-element.23), channel_id=1, source_target_pairs={{1,2},{3,4},{5,6},{2,1},{4,3},{6,5},{9,10},{11,12},{13,14},{10,9},... | collective-permute-start | bytes 983048 | tf_op jit(solution)/shard_map/ppermute | solution.py:17
  17.9 2.0 %collective-permute-start.1 = (f32[5,16,1024]{2,1,0:T(8,128)S(1)}, f32[5,16,1024]{2,1,0:T(8,128)S(1)}, u32[]{:S(2)}, u32[]{:S(2)}) collective-permute-start(f32[5,16,1024]{2,1,0:T(8,128)S(1)} %get-tuple-element.24), channel_id=1, source_target_pairs={{0,1},{1,0},{2,3},{3,2},{4,5},{5,4},{6,7},{7,6},{8,9},{9,8},{10,11... | collective-permute-start | bytes 983048 | tf_op jit(solution)/shard_map/ppermute | solution.py:16
  19.9 1.3 fusion.40
  21.2 1.3 fusion.39
  22.6 1.8 %slice_multiply_fusion.1 = (f32[16,2,1024]{2,1,0:T(2,128)S(1)}, f32[16,2,1024]{2,1,0:T(2,128)S(1)}) fusion(f32[16,16,1024]{2,1,0:T(8,128)} %mod_ref.1, f32[16,16,1024]{2,1,0:T(8,128)} %dmg_ref.1), kind=kLoop, calls=%fused_computation.20 | loop fusion | flops 262144 | bytes 786432 | tf_op jit(solution)/shard_map/mul | solution.py:208
  24.4 6.6 %collective-permute-done = f32[5,16,1024]{2,1,0:T(8,128)S(1)} collective-permute-done((f32[5,16,1024]{2,1,0:T(8,128)S(1)}, f32[5,16,1024]{2,1,0:T(8,128)S(1)}, u32[]{:S(2)}, u32[]{:S(2)}) %collective-permute-start) | collective-permute-done | bytes 327712 | tf_op jit(solution)/shard_map/ppermute | solution.py:17
  31.0 12.3 %collective-permute-done.1 = f32[5,16,1024]{2,1,0:T(8,128)S(1)} collective-permute-done((f32[5,16,1024]{2,1,0:T(8,128)S(1)}, f32[5,16,1024]{2,1,0:T(8,128)S(1)}, u32[]{:S(2)}, u32[]{:S(2)}) %collective-permute-start.1) | collective-permute-done | bytes 327712 | tf_op jit(solution)/shard_map/ppermute | solution.py:16
  43.5 0.1 reshape.48
  43.7 0.1 reshape.47
  44.1 0.1 copy-done.3
  44.3 0.1 reshape.45
  44.6 41.5 %collective-permute-start.2 = (f32[100,1024]{1,0:T(8,128)S(1)}, f32[100,1024]{1,0:T(8,128)S(1)}, u32[]{:S(2)}, u32[]{:S(2)}) collective-permute-start(f32[100,1024]{1,0:T(8,128)S(1)} %get-tuple-element.19), channel_id=1, source_target_pairs={{8,16},{24,32},{40,48},{56,64},{72,80},{88,96},{104,112},{120,128}... | collective-permute-start | bytes 1228808 | tf_op jit(solution)/shard_map/ppermute | solution.py:17
  86.1 1.9 %collective-permute-start.3 = (f32[100,1024]{1,0:T(8,128)S(1)}, f32[100,1024]{1,0:T(8,128)S(1)}, u32[]{:S(2)}, u32[]{:S(2)}) collective-permute-start(f32[100,1024]{1,0:T(8,128)S(1)} %get-tuple-element.20), channel_id=1, source_target_pairs={{0,8},{8,0},{16,24},{24,16},{32,40},{40,32},{48,56},{56,48},{64,72... | collective-permute-start | bytes 1228808 | tf_op jit(solution)/shard_map/ppermute | solution.py:16
  88.1 0.6 pad_add_fusion.ids_ref
  88.7 6.0 %collective-permute-done.2 = f32[100,1024]{1,0:T(8,128)S(1)} collective-permute-done((f32[100,1024]{1,0:T(8,128)S(1)}, f32[100,1024]{1,0:T(8,128)S(1)}, u32[]{:S(2)}, u32[]{:S(2)}) %collective-permute-start.2) | collective-permute-done | bytes 409632 | tf_op jit(solution)/shard_map/ppermute | solution.py:17
  94.9 0.8 pad.15.load_ref
  95.7 12.0 %shard_map.82 = f32[16,1024]{1,0:T(8,128)} custom-call(s32[2]{0:T(128)} %pad_add_fusion.ids_ref, f32[16,16,1024]{2,1,0:T(8,128)} %u_ref.1, f32[16,16,1024]{2,1,0:T(8,128)} %dmg_ref.1, f32[16,16,1024]{2,1,0:T(8,128)} %mod_ref.1, f32[16,16,1024]{2,1,0:T(8,128)} %tgh_ref.1, f32[5,16,1024]{2,1,0:T(8,128)} %copy-done.2, f32[5,16,1024]{2,1,0:T(8,128)} %copy-done.3, ...), custom_call_target="tpu_custom_call" | custom-call | tf_op jit(solution)/shard_map/pallas_call | solution.py:185
  107.7 1.9 %collective-permute-start.4 = (f32[16,1024]{1,0:T(8,128)}, f32[16,1024]{1,0:T(8,128)S(1)}, u32[]{:S(2)}, u32[]{:S(2)}) collective-permute-start(f32[16,1024]{1,0:T(8,128)} %shard_map.82), channel_id=1, source_target_pairs={{0,2},{1,3},{2,0},{3,1},{4,6},{5,7},{6,4},{7,5},{8,10},{9,11},{10,... | collective-permute-start | bytes 196616 | tf_op jit(solution)/shard_map/ppermute | solution.py:26
  109.6 5.1 %collective-permute-done.4 = f32[16,1024]{1,0:T(8,128)S(1)} collective-permute-done((f32[16,1024]{1,0:T(8,128)}, f32[16,1024]{1,0:T(8,128)S(1)}, u32[]{:S(2)}, u32[]{:S(2)}) %collective-permute-start.4) | collective-permute-done | bytes 65568 | tf_op jit(solution)/shard_map/ppermute | solution.py:26
  114.7 0.8 add.169
  115.6 1.9 %collective-permute-start.5 = (f32[16,1024]{1,0:T(8,128)S(1)}, f32[16,1024]{1,0:T(8,128)S(1)}, u32[]{:S(2)}, u32[]{:S(2)}) collective-permute-start(f32[16,1024]{1,0:T(8,128)S(1)} %add.169), channel_id=1, source_target_pairs={{0,4},{1,5},{2,6},{3,7},{4,0},{5,1},{6,2},{7,3},{8,12},{9,13},{10,... | collective-permute-start | bytes 196616 | tf_op jit(solution)/shard_map/ppermute | solution.py:26
  117.6 5.7 %collective-permute-done.5 = f32[16,1024]{1,0:T(8,128)S(1)} collective-permute-done((f32[16,1024]{1,0:T(8,128)S(1)}, f32[16,1024]{1,0:T(8,128)S(1)}, u32[]{:S(2)}, u32[]{:S(2)}) %collective-permute-start.5) | collective-permute-done | bytes 65568 | tf_op jit(solution)/shard_map/ppermute | solution.py:26
  123.2 5.7 %collective-permute-start.6 = (f32[16,1024]{1,0:T(8,128)S(1)}, f32[16,1024]{1,0:T(8,128)S(1)}, u32[]{:S(2)}, u32[]{:S(2)}) collective-permute-start(f32[16,1024]{1,0:T(8,128)S(1)} %add.170), channel_id=1, source_target_pairs={{0,1},{1,0},{2,3},{3,2},{4,5},{5,4},{6,7},{7,6},{8,9},{9,8},{10,11... | collective-permute-start | bytes 196616 | tf_op jit(solution)/shard_map/ppermute | solution.py:26
  129.0 0.3 select_reduce_fusion
  129.3 9.5 %collective-permute-done.6 = f32[16,1024]{1,0:T(8,128)S(1)} collective-permute-done((f32[16,1024]{1,0:T(8,128)S(1)}, f32[16,1024]{1,0:T(8,128)S(1)}, u32[]{:S(2)}, u32[]{:S(2)}) %collective-permute-start.6) | collective-permute-done | bytes 65568 | tf_op jit(solution)/shard_map/ppermute | solution.py:26
  138.8 1.9 %collective-permute-start.7 = (f32[2,1024]{1,0:T(2,128)S(1)}, f32[2,1024]{1,0:T(2,128)S(1)}, u32[]{:S(2)}, u32[]{:S(2)}) collective-permute-start(f32[2,1024]{1,0:T(2,128)S(1)} %get-tuple-element.40), channel_id=1, source_target_pairs={{0,8},{8,0},{16,24},{24,16},{32,40},{40,32},{48,56},{56,48},{64,72... | collective-permute-start | bytes 24584 | tf_op jit(solution)/shard_map/ppermute | solution.py:16
  140.7 5.7 %collective-permute-start.8 = (f32[2,1024]{1,0:T(2,128)S(1)}, f32[2,1024]{1,0:T(2,128)S(1)}, u32[]{:S(2)}, u32[]{:S(2)}) collective-permute-start(f32[2,1024]{1,0:T(2,128)S(1)} %get-tuple-element.39), channel_id=1, source_target_pairs={{8,16},{24,32},{40,48},{56,64},{72,80},{88,96},{104,112},{120,128}... | collective-permute-start | bytes 24584 | tf_op jit(solution)/shard_map/ppermute | solution.py:17
  146.5 6.7 %collective-permute-done.8 = f32[2,1024]{1,0:T(2,128)S(1)} collective-permute-done((f32[2,1024]{1,0:T(2,128)S(1)}, f32[2,1024]{1,0:T(2,128)S(1)}, u32[]{:S(2)}, u32[]{:S(2)}) %collective-permute-start.8) | collective-permute-done | bytes 8224 | tf_op jit(solution)/shard_map/ppermute | solution.py:17
  153.3 0.2 broadcast_multiply_fusion
  153.4 0.8 fusion.35
  (45 shorter events, 1.2 us)
Async XLA Ops:
  2.1 20.4 %copy-start.5 = (s32[16,1024]{1,0:T(8,128)S(1)}, s32[16,1024]{1,0:T(8,128)}, u32[]{:S(2)}) copy-start(s32[16,1024]{1,0:T(8,128)} %param.13) | copy-start | bytes 196612
  2.2 20.4 %copy-start.4 = (f32[16,1024]{1,0:T(8,128)S(1)}, f32[16,1024]{1,0:T(8,128)}, u32[]{:S(2)}) copy-start(f32[16,1024]{1,0:T(8,128)} %param.12) | copy-start | bytes 196612
  2.2 28.7 %collective-permute-start = (f32[5,16,1024]{2,1,0:T(8,128)S(1)}, f32[5,16,1024]{2,1,0:T(8,128)S(1)}, u32[]{:S(2)}, u32[]{:S(2)}) collective-permute-start(f32[5,16,1024]{2,1,0:T(8,128)S(1)} %get-tuple-element.23), channel_id=1, source_target_pairs={{1,2},{3,4},{5,6},{2,1},{4,3},{6,5},{9,10},{11,12},{13,14},{10,9},... | collective-permute-start | bytes 983048 | tf_op jit(solution)/shard_map/ppermute | solution.py:17
  17.9 25.4 %collective-permute-start.1 = (f32[5,16,1024]{2,1,0:T(8,128)S(1)}, f32[5,16,1024]{2,1,0:T(8,128)S(1)}, u32[]{:S(2)}, u32[]{:S(2)}) collective-permute-start(f32[5,16,1024]{2,1,0:T(8,128)S(1)} %get-tuple-element.24), channel_id=1, source_target_pairs={{0,1},{1,0},{2,3},{3,2},{4,5},{5,4},{6,7},{7,6},{8,9},{9,8},{10,11... | collective-permute-start | bytes 983048 | tf_op jit(solution)/shard_map/ppermute | solution.py:16
  43.4 0.7 copy-start.2
  43.4 0.8 copy-start.3
  44.6 50.1 %collective-permute-start.2 = (f32[100,1024]{1,0:T(8,128)S(1)}, f32[100,1024]{1,0:T(8,128)S(1)}, u32[]{:S(2)}, u32[]{:S(2)}) collective-permute-start(f32[100,1024]{1,0:T(8,128)S(1)} %get-tuple-element.19), channel_id=1, source_target_pairs={{8,16},{24,32},{40,48},{56,64},{72,80},{88,96},{104,112},{120,128}... | collective-permute-start | bytes 1228808 | tf_op jit(solution)/shard_map/ppermute | solution.py:17
  86.1 8.5 %collective-permute-start.3 = (f32[100,1024]{1,0:T(8,128)S(1)}, f32[100,1024]{1,0:T(8,128)S(1)}, u32[]{:S(2)}, u32[]{:S(2)}) collective-permute-start(f32[100,1024]{1,0:T(8,128)S(1)} %get-tuple-element.20), channel_id=1, source_target_pairs={{0,8},{8,0},{16,24},{24,16},{32,40},{40,32},{48,56},{56,48},{64,72... | collective-permute-start | bytes 1228808 | tf_op jit(solution)/shard_map/ppermute | solution.py:16
  94.7 0.9 copy-start
  94.8 0.9 copy-start.1
  95.7 33.2 %copy-start.6 = (f32[16]{0:T(128)S(1)}, f32[16]{0:T(128)}, u32[]{:S(2)}) copy-start(f32[16]{0:T(128)} %param.15) | copy-start | bytes 196
  95.7 33.2 %copy-start.7 = (s32[16]{0:T(128)S(1)}, s32[16]{0:T(128)}, u32[]{:S(2)}) copy-start(s32[16]{0:T(128)} %param.14) | copy-start | bytes 196
  107.7 7.0 %collective-permute-start.4 = (f32[16,1024]{1,0:T(8,128)}, f32[16,1024]{1,0:T(8,128)S(1)}, u32[]{:S(2)}, u32[]{:S(2)}) collective-permute-start(f32[16,1024]{1,0:T(8,128)} %shard_map.82), channel_id=1, source_target_pairs={{0,2},{1,3},{2,0},{3,1},{4,6},{5,7},{6,4},{7,5},{8,10},{9,11},{10,... | collective-permute-start | bytes 196616 | tf_op jit(solution)/shard_map/ppermute | solution.py:26
  115.6 7.7 %collective-permute-start.5 = (f32[16,1024]{1,0:T(8,128)S(1)}, f32[16,1024]{1,0:T(8,128)S(1)}, u32[]{:S(2)}, u32[]{:S(2)}) collective-permute-start(f32[16,1024]{1,0:T(8,128)S(1)} %add.169), channel_id=1, source_target_pairs={{0,4},{1,5},{2,6},{3,7},{4,0},{5,1},{6,2},{7,3},{8,12},{9,13},{10,... | collective-permute-start | bytes 196616 | tf_op jit(solution)/shard_map/ppermute | solution.py:26
  123.2 15.5 %collective-permute-start.6 = (f32[16,1024]{1,0:T(8,128)S(1)}, f32[16,1024]{1,0:T(8,128)S(1)}, u32[]{:S(2)}, u32[]{:S(2)}) collective-permute-start(f32[16,1024]{1,0:T(8,128)S(1)} %add.170), channel_id=1, source_target_pairs={{0,1},{1,0},{2,3},{3,2},{4,5},{5,4},{6,7},{7,6},{8,9},{9,8},{10,11... | collective-permute-start | bytes 196616 | tf_op jit(solution)/shard_map/ppermute | solution.py:26
  138.8 7.7 %collective-permute-start.7 = (f32[2,1024]{1,0:T(2,128)S(1)}, f32[2,1024]{1,0:T(2,128)S(1)}, u32[]{:S(2)}, u32[]{:S(2)}) collective-permute-start(f32[2,1024]{1,0:T(2,128)S(1)} %get-tuple-element.40), channel_id=1, source_target_pairs={{0,8},{8,0},{16,24},{24,16},{32,40},{40,32},{48,56},{56,48},{64,72... | collective-permute-start | bytes 24584 | tf_op jit(solution)/shard_map/ppermute | solution.py:16
  140.7 12.5 %collective-permute-start.8 = (f32[2,1024]{1,0:T(2,128)S(1)}, f32[2,1024]{1,0:T(2,128)S(1)}, u32[]{:S(2)}, u32[]{:S(2)}) collective-permute-start(f32[2,1024]{1,0:T(2,128)S(1)} %get-tuple-element.39), channel_id=1, source_target_pairs={{8,16},{24,32},{40,48},{56,64},{72,80},{88,96},{104,112},{120,128}... | collective-permute-start | bytes 24584 | tf_op jit(solution)/shard_map/ppermute | solution.py:17

commit v4 on v2

v4 whole, which is shorter than its diff:
```python
import functools

import jax
import jax.numpy as jnp
from jax import lax
from jax.experimental import pallas as pl
from jax.experimental.pallas import tpu as pltpu
from jax.sharding import PartitionSpec as P


def halo_swap(lo_face, hi_face, axis):
    count = lax.axis_size(axis)
    even = lax.axis_index(axis) % 2 == 0
    pairs_a = [(i, i ^ 1) for i in range(count)]
    pairs_b = [(i, i + 1) for i in range(1, count - 1, 2)] + [(i + 1, i) for i in range(1, count - 1, 2)]
    got_a = lax.ppermute(jnp.where(even, hi_face, lo_face), axis, pairs_a)
    got_b = lax.ppermute(jnp.where(even, lo_face, hi_face), axis, pairs_b)
    return jnp.where(even, got_b, got_a), jnp.where(even, got_a, got_b)


def butterfly_sum(part, axis):
    count = lax.axis_size(axis)
    order = [1 << k for k in range(1, count.bit_length() - 1)] + [1]
    for step in order:
        pairs = [(i, i ^ step) for i in range(lax.axis_size(axis))]
        part = part + lax.ppermute(part, axis, pairs)
    return part


def pad_last(stacked):
    widths = [(0, 0)] * (stacked.ndim - 1) + [(1, 1)]
    return jnp.pad(stacked, widths)


def flat_sides(padded):
    return [padded[2:, 1:-1], padded[:-2, 1:-1], padded[1:-1, 2:], padded[1:-1, :-2]]


def plane_sweep(p_pad, k_pad, anchor, source, trans):
    coef = jnp.zeros_like(trans)
    flow = jnp.zeros_like(trans)
    for k_side, p_side in zip(flat_sides(k_pad), flat_sides(p_pad)):
        face = 0.5 * (trans + k_side)
        coef = coef + face
        flow = flow + face * p_side
    return (anchor + source + flow) / (1.0 + coef)


def well_source(wells, rates, row_start, rows, cols, width):
    row_ids = row_start + jnp.arange(rows, dtype=jnp.int32)
    col_ids = jnp.arange(cols, dtype=jnp.int32)
    flat = row_ids[:, None] * width + col_ids[None, :]
    hit = flat[:, :, None] == wells[None, None, :]
    return 4.0 * jnp.sum(jnp.where(hit, rates[None, None, :], jnp.float32(0.0)), axis=-1)


def cube_sides(padded):
    return [
        padded[2:, 1:-1, 1:-1],
        padded[:-2, 1:-1, 1:-1],
        padded[1:-1, 2:, 1:-1],
        padded[1:-1, :-2, 1:-1],
        padded[1:-1, 1:-1, 2:],
        padded[1:-1, 1:-1, :-2],
    ]


X0 = 8


def neighbours(rows_all, width):
    col = lax.broadcasted_iota(jnp.int32, (rows_all, width), 1)
    has_next = col < width - 1
    has_prev = col > 0

    def y_next(a):
        return jnp.where(has_next, pltpu.roll(a, width - 1, 1), 0.0)

    def y_prev(a):
        return jnp.where(has_prev, pltpu.roll(a, 1, 1), 0.0)

    def x_next(a):
        return pltpu.roll(a, rows_all - 1, 0)

    def x_prev(a):
        return pltpu.roll(a, 1, 0)

    return x_next, x_prev, y_next, y_prev


def moved_at(uc, cc, up, down, nb, z_glob, load, x_in, total_depth):
    x_next, x_prev, y_next, y_prev = nb
    pairs = [
        up,
        down,
        (x_next(cc), x_next(uc)),
        (x_prev(cc), x_prev(uc)),
        (y_next(cc), y_next(uc)),
        (y_prev(cc), y_prev(uc)),
    ]
    coef = jnp.zeros_like(uc)
    flux = jnp.zeros_like(uc)
    for cn, un in pairs:
        face = 0.5 * (cc + cn)
        coef = coef + face
        flux = flux + face * (un - uc)
    force = jnp.where(z_glob == total_depth // 2, load, 0.0)
    moved = uc + 0.8 * (force + flux) / coef
    keep = x_in & (z_glob >= 0) & (z_glob < total_depth)
    return jnp.where(keep, moved, 0.0)


def opening_at(mc, m_up, m_down, dc, d_up, d_down, nb, mod, tough, dmg, own):
    x_next, x_prev, y_next, y_prev = nb
    energy = (
        (m_up - mc) ** 2 + (m_down - mc) ** 2 + (x_next(mc) - mc) ** 2 + (x_prev(mc) - mc) ** 2
        + (y_next(mc) - mc) ** 2 + (y_prev(mc) - mc) ** 2
    )
    beside = d_up + d_down + x_next(dc) + x_prev(dc) + y_next(dc) + y_prev(dc)
    energy = 0.25 * mod * energy[own]
    trial = (2.0 * energy + tough * beside[own]) / (7.0 * tough + 2.0 * energy)
    new_damage = jnp.maximum(dmg, trial)
    mo = mc[own]
    return new_damage * mo * mo


def x_frame(ids_ref, rows_all, width, total_rows):
    row = lax.broadcasted_iota(jnp.int32, (rows_all, width), 0)
    x_glob = ids_ref[1] + row - X0
    return (x_glob >= 0) & (x_glob < total_rows)


def interior_kernel(total_depth, total_rows, ids_ref, u_ref, dmg_ref, mod_ref, tgh_ref, xlo_ref, xhi_ref, load_ref,
                    part_ref, edge_ref, u_s, c_s, d_s, m_s):
    depth_cells, tile_cells, width = u_ref.shape
    rows_all = u_s.shape[1]
    own = slice(X0, X0 + tile_cells)
    top = X0 + tile_cells
    zero = jnp.zeros((rows_all, width), jnp.float32)

    def place(k, carry):
        dk = dmg_ref[k]
        u_s[k] = zero
        c_s[k] = zero
        d_s[k] = zero
        u_s[k, own] = u_ref[k]
        c_s[k, own] = ((1.0 - dk) ** 2 + 0.001) * mod_ref[k]
        d_s[k, own] = dk
        return carry

    lax.fori_loop(0, depth_cells, place, 0)
    dz = 4 * depth_cells
    for z in range(depth_cells):
        u_s[z, X0 - 2:X0] = xlo_ref[2 * z:2 * z + 2]
        c_s[z, X0 - 2:X0] = xlo_ref[2 * depth_cells + 2 * z:2 * depth_cells + 2 * z + 2]
        d_s[z, X0 - 1:X0] = xlo_ref[dz + z:dz + z + 1]
        u_s[z, top:top + 2] = xhi_ref[2 * z:2 * z + 2]
        c_s[z, top:top + 2] = xhi_ref[2 * depth_cells + 2 * z:2 * depth_cells + 2 * z + 2]
        d_s[z, top:top + 1] = xhi_ref[dz + z:dz + z + 1]

    nb = neighbours(rows_all, width)
    x_in = x_frame(ids_ref, rows_all, width, total_rows)
    load = load_ref[...]
    depth_start = ids_ref[0]

    def moved_body(k, carry):
        m_s[k] = moved_at(
            u_s[k], c_s[k], (c_s[k + 1], u_s[k + 1]), (c_s[k - 1], u_s[k - 1]), nb, depth_start + k, load, x_in,
            total_depth,
        )
        return carry

    lax.fori_loop(1, depth_cells - 1, moved_body, 0)

    def open_body(k, acc):
        return acc + opening_at(
            m_s[k], m_s[k + 1], m_s[k - 1], d_s[k], d_s[k + 1], d_s[k - 1], nb, mod_ref[k], tgh_ref[k], dmg_ref[k], own
        )

    acc = lax.fori_loop(2, depth_cells - 2, open_body, jnp.zeros((tile_cells, width), jnp.float32))
    part_ref[...] = acc
    edge_ref[0] = m_s[1]
    edge_ref[1] = m_s[2]
    edge_ref[2] = m_s[depth_cells - 3]
    edge_ref[3] = m_s[depth_cells - 2]


def boundary_kernel(total_depth, total_rows, ids_ref, u_ref, dmg_ref, mod_ref, tgh_ref, xlo_ref, xhi_ref, zlo_ref,
                    zhi_ref, edge_ref, part_ref, load_ref, out_ref, u_s, c_s, d_s, m_s):
    depth_cells, tile_cells, width = u_ref.shape
    rows_all = u_s.shape[1]
    own = slice(X0, X0 + tile_cells)
    wide = slice(X0 - 1, X0 + tile_cells + 1)
    top = X0 + tile_cells
    zero = jnp.zeros((rows_all, width), jnp.float32)
    for j in range(8):
        u_s[j] = zero
        c_s[j] = zero
        d_s[j] = zero
    ext = tile_cells + 2
    for side, ref, adj, sec in ((0, zlo_ref, 1, 0), (4, zhi_ref, 6, 7)):
        u_s[adj, wide] = ref[0:ext]
        c_s[adj, wide] = ref[ext:2 * ext]
        u_s[sec, own] = ref[2 * ext:2 * ext + tile_cells]
        c_s[sec, own] = ref[2 * ext + tile_cells:2 * ext + 2 * tile_cells]
    d_s[0, own] = zlo_ref[2 * ext + 2 * tile_cells:2 * ext + 3 * tile_cells]
    d_s[7, own] = zhi_ref[2 * ext + 2 * tile_cells:2 * ext + 3 * tile_cells]
    dz = 4 * depth_cells
    for slot, z in ((2, 0), (3, 1), (4, depth_cells - 2), (5, depth_cells - 1)):
        dk = dmg_ref[z]
        u_s[slot, own] = u_ref[z]
        c_s[slot, own] = ((1.0 - dk) ** 2 + 0.001) * mod_ref[z]
        u_s[slot, X0 - 2:X0] = xlo_ref[2 * z:2 * z + 2]
        c_s[slot, X0 - 2:X0] = xlo_ref[2 * depth_cells + 2 * z:2 * depth_cells + 2 * z + 2]
        u_s[slot, top:top + 2] = xhi_ref[2 * z:2 * z + 2]
        c_s[slot, top:top + 2] = xhi_ref[2 * depth_cells + 2 * z:2 * depth_cells + 2 * z + 2]
    for slot, z in ((1, 0), (2, 1), (5, depth_cells - 2), (6, depth_cells - 1)):
        d_s[slot, own] = dmg_ref[z]
        d_s[slot, X0 - 1:X0] = xlo_ref[dz + z:dz + z + 1]
        d_s[slot, top:top + 1] = xhi_ref[dz + z:dz + z + 1]
    d_s[3, own] = dmg_ref[2]
    d_s[4, own] = dmg_ref[depth_cells - 3]
    m_s[2] = edge_ref[0]
    m_s[3] = edge_ref[1]
    m_s[4] = edge_ref[2]
    m_s[5] = edge_ref[3]

    nb = neighbours(rows_all, width)
    x_in = x_frame(ids_ref, rows_all, width, total_rows)
    load = load_ref[...]
    depth_start = ids_ref[0]
    for us, ms, z in ((1, 0, -1), (2, 1, 0), (5, 6, depth_cells - 1), (6, 7, depth_cells)):
        m_s[ms] = moved_at(
            u_s[us], c_s[us], (c_s[us + 1], u_s[us + 1]), (c_s[us - 1], u_s[us - 1]), nb, depth_start + z, load, x_in,
            total_depth,
        )
    acc = part_ref[...]
    for ms, z in ((1, 0), (2, 1), (5, depth_cells - 2), (6, depth_cells - 1)):
        acc = acc + opening_at(
            m_s[ms], m_s[ms + 1], m_s[ms - 1], d_s[ms], d_s[ms + 1], d_s[ms - 1], nb, mod_ref[z], tgh_ref[z],
            dmg_ref[z], own,
        )
    out_ref[...] = (4.0 / total_depth) * acc


def on_device(displacement, damage, modulus, toughness, pressure, crack_mask, wells, rates):
    depth_cells, tile_cells, width = displacement.shape
    total_depth = depth_cells * lax.axis_size("depth")
    total_rows = tile_cells * lax.axis_size("tile")
    depth_start = lax.axis_index("depth") * depth_cells
    tile_start = lax.axis_index("tile") * tile_cells
    mask_f = crack_mask.astype(jnp.float32)
    rows_all = tile_cells + 2 * X0

    def stiff_of(dmg, mod):
        return ((1.0 - dmg) ** 2 + 0.001) * mod

    def tile_face(rows, edge):
        return jnp.concatenate(
            [
                displacement[:, rows].reshape(-1, width),
                stiff_of(damage[:, rows], modulus[:, rows]).reshape(-1, width),
                damage[:, edge],
                pressure[rows],
                mask_f[rows],
            ]
        )

    lo_x, hi_x = halo_swap(tile_face(slice(0, 2), 0), tile_face(slice(tile_cells - 2, tile_cells), tile_cells - 1), "tile")
    dz = 4 * depth_cells
    p_ext = jnp.concatenate([lo_x[dz + depth_cells:dz + depth_cells + 2], pressure, hi_x[dz + depth_cells:dz + depth_cells + 2]])
    m_ext = jnp.concatenate([lo_x[dz + depth_cells + 2:], mask_f, hi_x[dz + depth_cells + 2:]])
    load_all = jnp.pad(4.0 * m_ext[1:-1] * p_ext[1:-1], ((X0 - 1, X0 - 1), (0, 0)))
    ids = jnp.stack([depth_start, tile_start]).astype(jnp.int32)

    def depth_face(adj, sec):
        u_adj = jnp.concatenate([lo_x[2 * adj + 1:2 * adj + 2], displacement[adj], hi_x[2 * adj:2 * adj + 1]])
        c0 = 2 * depth_cells
        c_adj = jnp.concatenate(
            [lo_x[c0 + 2 * adj + 1:c0 + 2 * adj + 2], stiff_of(damage[adj], modulus[adj]), hi_x[c0 + 2 * adj:c0 + 2 * adj + 1]]
        )
        return jnp.concatenate([u_adj, c_adj, displacement[sec], stiff_of(damage[sec], modulus[sec]), damage[adj]])

    lo_z, hi_z = halo_swap(depth_face(0, 1), depth_face(depth_cells - 1, depth_cells - 2), "depth")

    vmem = pl.BlockSpec(memory_space=pltpu.VMEM)
    smem = pl.BlockSpec(memory_space=pltpu.SMEM)
    f32 = jnp.float32
    part_in, edge = pl.pallas_call(
        functools.partial(interior_kernel, total_depth, total_rows),
        out_shape=(
            jax.ShapeDtypeStruct((tile_cells, width), f32),
            jax.ShapeDtypeStruct((4, rows_all, width), f32),
        ),
        in_specs=[smem] + [vmem] * 7,
        out_specs=(vmem, vmem),
        scratch_shapes=[pltpu.VMEM((depth_cells, rows_all, width), f32)] * 4,
    )(ids, displacement, damage, modulus, toughness, lo_x, hi_x, load_all)
    partial_open = pl.pallas_call(
        functools.partial(boundary_kernel, total_depth, total_rows),
        out_shape=jax.ShapeDtypeStruct((tile_cells, width), f32),
        in_specs=[smem] + [vmem] * 11,
        out_specs=vmem,
        scratch_shapes=[pltpu.VMEM((8, rows_all, width), f32)] * 4,
    )(ids, displacement, damage, modulus, toughness, lo_x, hi_x, lo_z, hi_z, edge, part_in, load_all)

    aperture = 0.5 + butterfly_sum(partial_open, "depth")
    trans = mask_f * aperture**3

    t_lo, t_hi = halo_swap(trans[:2], trans[-2:], "tile")
    t_ext = jnp.concatenate([t_lo, trans, t_hi])
    x_ids = tile_start - 1 + jnp.arange(tile_cells + 2, dtype=jnp.int32)
    rows_in = ((x_ids >= 0) & (x_ids < total_rows))[:, None]
    src_ext = well_source(wells, rates, tile_start - 1, tile_cells + 2, width, width)
    k_pad = pad_last(t_ext)
    level = plane_sweep(pad_last(p_ext), k_pad, p_ext[1:-1], src_ext, t_ext[1:-1])
    level = jnp.where(rows_in, level, jnp.float32(0.0))
    return plane_sweep(pad_last(level), k_pad[1:-1], pressure, src_ext[1:-1], trans)


def solution(mesh):
    return jax.shard_map(
        on_device,
        mesh=mesh,
        in_specs=(
            P("depth", "tile", None),
            P("depth", "tile", None),
            P("depth", "tile", None),
            P("depth", "tile", None),
            P("tile", None),
            P("tile", None),
            P(),
            P(),
        ),
        out_specs=P("tile", None),
        check_vma=False,
    )
```

time: 191 us -> 150 us (0.79)
  the two profiles are of different devices: /device:TPU:4 before, /device:TPU:30 now
where the time goes in v4:
time: 150 us; the launch traced here: 149 us
  waiting for transfers between devices  78.4 us (52%)
  starting transfers between devices  42.9 us (29%)
  Pallas kernels  14.6 us (10%)
  other arithmetic  7.54 us (5%)
  local copies, waits for them, and re-layouts  5.44 us (4%)
    ppermute x3, waiting for transfers between devices, halo_swap(): got_b = lax.ppermute(jnp.where(even, lo_face, hi_face), axis, pairs_b)  39 us
    ppermute x3, waiting for transfers between devices, butterfly_sum(): part = part + lax.ppermute(part, axis, pairs)  20.5 us
    ppermute x3, starting transfers between devices, halo_swap(): got_b = lax.ppermute(jnp.where(even, lo_face, hi_face), axis, pairs_b)  19.7 us
    ppermute x3, waiting for transfers between devices, halo_swap(): got_a = lax.ppermute(jnp.where(even, hi_face, lo_face), axis, pairs_a)  18.9 us
    ppermute x3, starting transfers between devices, halo_swap(): got_a = lax.ppermute(jnp.where(even, hi_face, lo_face), axis, pairs_a)  14.9 us
    pallas_call x1, Pallas kernels, on_device(): pl.pallas_call(functools.partial(interior_kernel, total_depth, total_rows...  9.67 us
    ppermute x3, starting transfers between devices, butterfly_sum(): part = part + lax.ppermute(part, axis, pairs)  8.31 us
    pallas_call x1, Pallas kernels, on_device(): pl.pallas_call(functools.partial(boundary_kernel, total_depth, total_rows...  4.97 us
  transfers between devices with their start and end apart: 9, of which 7 were waited for; matrix products, arithmetic and copies ran while one was open for 2% of the time, Pallas kernels for 6%

profile of v4, /device:TPU:30, one launch (start us, length us, event | category | flops | bytes accessed | tf_op | source)
XLA Modules:
  0.0 149.4 jit_solution(1494984767074238352)
XLA Ops:
  0.0 1.4 fusion.38
  1.5 1.3 fusion.37
  2.8 1.5 slice_multiply_fusion.1
  4.9 12.9 %collective-permute-start = (f32[84,1024]{1,0:T(8,128)S(1)}, f32[84,1024]{1,0:T(8,128)S(1)}, u32[]{:S(2)}, u32[]{:S(2)}) collective-permute-start(f32[84,1024]{1,0:T(8,128)S(1)} %get-tuple-element.33), channel_id=1, source_target_pairs={{8,16},{24,32},{40,48},{56,64},{72,80},{88,96},{104,112},{120,128}... | collective-permute-start | bytes 1032200 | tf_op jit(solution)/shard_map/ppermute | solution.py:17
  17.8 1.9 %collective-permute-start.1 = (f32[84,1024]{1,0:T(8,128)S(1)}, f32[84,1024]{1,0:T(8,128)S(1)}, u32[]{:S(2)}, u32[]{:S(2)}) collective-permute-start(f32[84,1024]{1,0:T(8,128)S(1)} %get-tuple-element.34), channel_id=1, source_target_pairs={{0,8},{8,0},{16,24},{24,16},{32,40},{40,32},{48,56},{56,48},{64,72... | collective-permute-start | bytes 1032200 | tf_op jit(solution)/shard_map/ppermute | solution.py:16
  19.7 0.9 bitcast_multiply_fusion
  20.6 0.7 pad_add_fusion.ids_ref
  21.3 1.0 slice_bitcast_fusion
  22.3 3.6 %collective-permute-done = f32[84,1024]{1,0:T(8,128)S(1)} collective-permute-done((f32[84,1024]{1,0:T(8,128)S(1)}, f32[84,1024]{1,0:T(8,128)S(1)}, u32[]{:S(2)}, u32[]{:S(2)}) %collective-permute-start) | collective-permute-done | bytes 344096 | tf_op jit(solution)/shard_map/ppermute | solution.py:17
  26.0 0.7 concatenate.38
  26.8 0.7 concatenate.37
  27.6 11.1 %collective-permute-start.3 = (f32[84,1024]{1,0:T(8,128)S(1)}, f32[84,1024]{1,0:T(8,128)S(1)}, u32[]{:S(2)}, u32[]{:S(2)}) collective-permute-start(f32[84,1024]{1,0:T(8,128)S(1)} %get-tuple-element.29), channel_id=1, source_target_pairs={{0,1},{1,0},{2,3},{3,2},{4,5},{5,4},{6,7},{7,6},{8,9},{9,8},{10,11... | collective-permute-start | bytes 1032200 | tf_op jit(solution)/shard_map/ppermute | solution.py:16
  38.7 3.7 %collective-permute-start.2 = (f32[84,1024]{1,0:T(8,128)S(1)}, f32[84,1024]{1,0:T(8,128)S(1)}, u32[]{:S(2)}, u32[]{:S(2)}) collective-permute-start(f32[84,1024]{1,0:T(8,128)S(1)} %get-tuple-element.30), channel_id=1, source_target_pairs={{1,2},{3,4},{5,6},{2,1},{4,3},{6,5},{9,10},{11,12},{13,14},{10,9},... | collective-permute-start | bytes 1032200 | tf_op jit(solution)/shard_map/ppermute | solution.py:17
  42.5 0.7 pad.15.load_ref
  43.1 9.7 %shard_map.82 = (f32[16,1024]{1,0:T(8,128)}, f32[4,32,1024]{2,1,0:T(8,128)}) custom-call(s32[2]{0:T(128)} %pad_add_fusion.ids_ref, f32[16,16,1024]{2,1,0:T(8,128)} %u_ref.3, f32[16,16,1024]{2,1,0:T(8,128)} %dmg_ref.3, f32[16,16,1024]{2,1,0:T(8,128)} %mod_ref.3, f32[16,16,1024]{2,1,0:T(8,128)} %tgh_ref.3, f32[84,1024]{1,0:T(8,128)} %copy-done.1, ...), custom_call_target="tpu_custom_call" | custom-call | tf_op jit(solution)/shard_map/pallas_call | solution.py:289
  52.8 18.9 %collective-permute-done.3 = f32[84,1024]{1,0:T(8,128)S(1)} collective-permute-done((f32[84,1024]{1,0:T(8,128)S(1)}, f32[84,1024]{1,0:T(8,128)S(1)}, u32[]{:S(2)}, u32[]{:S(2)}) %collective-permute-start.3) | collective-permute-done | bytes 344096 | tf_op jit(solution)/shard_map/ppermute | solution.py:16
  71.7 28.1 %collective-permute-done.2 = f32[84,1024]{1,0:T(8,128)S(1)} collective-permute-done((f32[84,1024]{1,0:T(8,128)S(1)}, f32[84,1024]{1,0:T(8,128)S(1)}, u32[]{:S(2)}, u32[]{:S(2)}) %collective-permute-start.2) | collective-permute-done | bytes 344096 | tf_op jit(solution)/shard_map/ppermute | solution.py:17
  99.8 0.9 broadcast_select_fusion
  100.7 5.0 %shard_map.83 = f32[16,1024]{1,0:T(8,128)} custom-call(s32[2]{0:T(128)} %pad_add_fusion.ids_ref, f32[16,16,1024]{2,1,0:T(8,128)} %u_ref.3, f32[16,16,1024]{2,1,0:T(8,128)} %dmg_ref.3, f32[16,16,1024]{2,1,0:T(8,128)} %mod_ref.3, f32[16,16,1024]{2,1,0:T(8,128)} %tgh_ref.3, f32[84,1024]{1,0:T(8,128)} %copy-done.1, f32[84,1024]{1,0:T(8,128)} %copy-done.2, ...), custom_call_target="tpu_custom_call" | custom-call | tf_op jit(solution)/shard_map/pallas_call | solution.py:299
  105.7 2.3 %collective-permute-start.4 = (f32[16,1024]{1,0:T(8,128)}, f32[16,1024]{1,0:T(8,128)S(1)}, u32[]{:S(2)}, u32[]{:S(2)}) collective-permute-start(f32[16,1024]{1,0:T(8,128)} %shard_map.83), channel_id=1, source_target_pairs={{0,2},{1,3},{2,0},{3,1},{4,6},{5,7},{6,4},{7,5},{8,10},{9,11},{10,... | collective-permute-start | bytes 196616 | tf_op jit(solution)/shard_map/ppermute | solution.py:26
  108.1 4.0 %collective-permute-done.4 = f32[16,1024]{1,0:T(8,128)S(1)} collective-permute-done((f32[16,1024]{1,0:T(8,128)}, f32[16,1024]{1,0:T(8,128)S(1)}, u32[]{:S(2)}, u32[]{:S(2)}) %collective-permute-start.4) | collective-permute-done | bytes 65568 | tf_op jit(solution)/shard_map/ppermute | solution.py:26
  112.0 0.8 add.176
  112.9 1.9 %collective-permute-start.5 = (f32[16,1024]{1,0:T(8,128)S(1)}, f32[16,1024]{1,0:T(8,128)S(1)}, u32[]{:S(2)}, u32[]{:S(2)}) collective-permute-start(f32[16,1024]{1,0:T(8,128)S(1)} %add.176), channel_id=1, source_target_pairs={{0,4},{1,5},{2,6},{3,7},{4,0},{5,1},{6,2},{7,3},{8,12},{9,13},{10,... | collective-permute-start | bytes 196616 | tf_op jit(solution)/shard_map/ppermute | solution.py:26
  114.9 5.7 %collective-permute-done.5 = f32[16,1024]{1,0:T(8,128)S(1)} collective-permute-done((f32[16,1024]{1,0:T(8,128)S(1)}, f32[16,1024]{1,0:T(8,128)S(1)}, u32[]{:S(2)}, u32[]{:S(2)}) %collective-permute-start.5) | collective-permute-done | bytes 65568 | tf_op jit(solution)/shard_map/ppermute | solution.py:26
  120.6 4.0 %collective-permute-start.6 = (f32[16,1024]{1,0:T(8,128)S(1)}, f32[16,1024]{1,0:T(8,128)S(1)}, u32[]{:S(2)}, u32[]{:S(2)}) collective-permute-start(f32[16,1024]{1,0:T(8,128)S(1)} %add.177), channel_id=1, source_target_pairs={{0,1},{1,0},{2,3},{3,2},{4,5},{5,4},{6,7},{7,6},{8,9},{9,8},{10,11... | collective-permute-start | bytes 196616 | tf_op jit(solution)/shard_map/ppermute | solution.py:26
  124.6 0.3 select_reduce_fusion
  125.0 10.9 %collective-permute-done.6 = f32[16,1024]{1,0:T(8,128)S(1)} collective-permute-done((f32[16,1024]{1,0:T(8,128)S(1)}, f32[16,1024]{1,0:T(8,128)S(1)}, u32[]{:S(2)}, u32[]{:S(2)}) %collective-permute-start.6) | collective-permute-done | bytes 65568 | tf_op jit(solution)/shard_map/ppermute | solution.py:26
  135.9 3.2 %collective-permute-start.8 = (f32[2,1024]{1,0:T(2,128)S(1)}, f32[2,1024]{1,0:T(2,128)S(1)}, u32[]{:S(2)}, u32[]{:S(2)}) collective-permute-start(f32[2,1024]{1,0:T(2,128)S(1)} %get-tuple-element.49), channel_id=1, source_target_pairs={{8,16},{24,32},{40,48},{56,64},{72,80},{88,96},{104,112},{120,128}... | collective-permute-start | bytes 24584 | tf_op jit(solution)/shard_map/ppermute | solution.py:17
  139.1 1.9 %collective-permute-start.7 = (f32[2,1024]{1,0:T(2,128)S(1)}, f32[2,1024]{1,0:T(2,128)S(1)}, u32[]{:S(2)}, u32[]{:S(2)}) collective-permute-start(f32[2,1024]{1,0:T(2,128)S(1)} %get-tuple-element.50), channel_id=1, source_target_pairs={{0,8},{8,0},{16,24},{24,16},{32,40},{40,32},{48,56},{56,48},{64,72... | collective-permute-start | bytes 24584 | tf_op jit(solution)/shard_map/ppermute | solution.py:16
  141.0 7.3 %collective-permute-done.8 = f32[2,1024]{1,0:T(2,128)S(1)} collective-permute-done((f32[2,1024]{1,0:T(2,128)S(1)}, f32[2,1024]{1,0:T(2,128)S(1)}, u32[]{:S(2)}, u32[]{:S(2)}) %collective-permute-start.8) | collective-permute-done | bytes 8224 | tf_op jit(solution)/shard_map/ppermute | solution.py:17
  148.4 0.2 broadcast_multiply_fusion
  148.6 0.8 fusion.33
  (42 shorter events, 1.0 us)
Async XLA Ops:
  0.0 2.8 %copy-start = (f32[16,16,1024]{2,1,0:T(8,128)S(1)}, f32[16,16,1024]{2,1,0:T(8,128)}, u32[]{:S(2)}) copy-start(f32[16,16,1024]{2,1,0:T(8,128)} %dmg_ref.3) | copy-start | bytes 3145732
  0.0 4.4 %copy-start.4 = (s32[16,1024]{1,0:T(8,128)S(1)}, s32[16,1024]{1,0:T(8,128)}, u32[]{:S(2)}) copy-start(s32[16,1024]{1,0:T(8,128)} %param.13) | copy-start | bytes 196612
  2.8 1.9 %copy-start.3 = (f32[16,1024]{1,0:T(8,128)S(1)}, f32[16,1024]{1,0:T(8,128)}, u32[]{:S(2)}) copy-start(f32[16,1024]{1,0:T(8,128)} %param.12) | copy-start | bytes 196612
  4.9 21.0 %collective-permute-start = (f32[84,1024]{1,0:T(8,128)S(1)}, f32[84,1024]{1,0:T(8,128)S(1)}, u32[]{:S(2)}, u32[]{:S(2)}) collective-permute-start(f32[84,1024]{1,0:T(8,128)S(1)} %get-tuple-element.33), channel_id=1, source_target_pairs={{8,16},{24,32},{40,48},{56,64},{72,80},{88,96},{104,112},{120,128}... | collective-permute-start | bytes 1032200 | tf_op jit(solution)/shard_map/ppermute | solution.py:17
  17.8 8.1 %collective-permute-start.1 = (f32[84,1024]{1,0:T(8,128)S(1)}, f32[84,1024]{1,0:T(8,128)S(1)}, u32[]{:S(2)}, u32[]{:S(2)}) collective-permute-start(f32[84,1024]{1,0:T(8,128)S(1)} %get-tuple-element.34), channel_id=1, source_target_pairs={{0,8},{8,0},{16,24},{24,16},{32,40},{40,32},{48,56},{56,48},{64,72... | collective-permute-start | bytes 1032200 | tf_op jit(solution)/shard_map/ppermute | solution.py:16
  26.0 1.7 %copy-start.2 = (f32[84,1024]{1,0:T(8,128)}, f32[84,1024]{1,0:T(8,128)S(1)}, u32[]{:S(2)}) copy-start(f32[84,1024]{1,0:T(8,128)S(1)} %get-tuple-element.32.xhi_ref) | copy-start | bytes 1032196
  26.0 16.4 %copy-start.1 = (f32[84,1024]{1,0:T(8,128)}, f32[84,1024]{1,0:T(8,128)S(1)}, u32[]{:S(2)}) copy-start(f32[84,1024]{1,0:T(8,128)S(1)} %get-tuple-element.31.xlo_ref) | copy-start | bytes 1032196
  27.6 44.1 %collective-permute-start.3 = (f32[84,1024]{1,0:T(8,128)S(1)}, f32[84,1024]{1,0:T(8,128)S(1)}, u32[]{:S(2)}, u32[]{:S(2)}) collective-permute-start(f32[84,1024]{1,0:T(8,128)S(1)} %get-tuple-element.29), channel_id=1, source_target_pairs={{0,1},{1,0},{2,3},{3,2},{4,5},{5,4},{6,7},{7,6},{8,9},{9,8},{10,11... | collective-permute-start | bytes 1032200 | tf_op jit(solution)/shard_map/ppermute | solution.py:16
  38.7 61.1 %collective-permute-start.2 = (f32[84,1024]{1,0:T(8,128)S(1)}, f32[84,1024]{1,0:T(8,128)S(1)}, u32[]{:S(2)}, u32[]{:S(2)}) collective-permute-start(f32[84,1024]{1,0:T(8,128)S(1)} %get-tuple-element.30), channel_id=1, source_target_pairs={{1,2},{3,4},{5,6},{2,1},{4,3},{6,5},{9,10},{11,12},{13,14},{10,9},... | collective-permute-start | bytes 1032200 | tf_op jit(solution)/shard_map/ppermute | solution.py:17
  100.7 23.9 %copy-start.5 = (f32[16]{0:T(128)S(1)}, f32[16]{0:T(128)}, u32[]{:S(2)}) copy-start(f32[16]{0:T(128)} %param.15) | copy-start | bytes 196
  100.7 23.9 %copy-start.6 = (s32[16]{0:T(128)S(1)}, s32[16]{0:T(128)}, u32[]{:S(2)}) copy-start(s32[16]{0:T(128)} %param.14) | copy-start | bytes 196
  105.7 6.4 %collective-permute-start.4 = (f32[16,1024]{1,0:T(8,128)}, f32[16,1024]{1,0:T(8,128)S(1)}, u32[]{:S(2)}, u32[]{:S(2)}) collective-permute-start(f32[16,1024]{1,0:T(8,128)} %shard_map.83), channel_id=1, source_target_pairs={{0,2},{1,3},{2,0},{3,1},{4,6},{5,7},{6,4},{7,5},{8,10},{9,11},{10,... | collective-permute-start | bytes 196616 | tf_op jit(solution)/shard_map/ppermute | solution.py:26
  112.9 7.7 %collective-permute-start.5 = (f32[16,1024]{1,0:T(8,128)S(1)}, f32[16,1024]{1,0:T(8,128)S(1)}, u32[]{:S(2)}, u32[]{:S(2)}) collective-permute-start(f32[16,1024]{1,0:T(8,128)S(1)} %add.176), channel_id=1, source_target_pairs={{0,4},{1,5},{2,6},{3,7},{4,0},{5,1},{6,2},{7,3},{8,12},{9,13},{10,... | collective-permute-start | bytes 196616 | tf_op jit(solution)/shard_map/ppermute | solution.py:26
  120.6 15.3 %collective-permute-start.6 = (f32[16,1024]{1,0:T(8,128)S(1)}, f32[16,1024]{1,0:T(8,128)S(1)}, u32[]{:S(2)}, u32[]{:S(2)}) collective-permute-start(f32[16,1024]{1,0:T(8,128)S(1)} %add.177), channel_id=1, source_target_pairs={{0,1},{1,0},{2,3},{3,2},{4,5},{5,4},{6,7},{7,6},{8,9},{9,8},{10,11... | collective-permute-start | bytes 196616 | tf_op jit(solution)/shard_map/ppermute | solution.py:26
  135.9 12.5 %collective-permute-start.8 = (f32[2,1024]{1,0:T(2,128)S(1)}, f32[2,1024]{1,0:T(2,128)S(1)}, u32[]{:S(2)}, u32[]{:S(2)}) collective-permute-start(f32[2,1024]{1,0:T(2,128)S(1)} %get-tuple-element.49), channel_id=1, source_target_pairs={{8,16},{24,32},{40,48},{56,64},{72,80},{88,96},{104,112},{120,128}... | collective-permute-start | bytes 24584 | tf_op jit(solution)/shard_map/ppermute | solution.py:17
  139.1 9.3 %collective-permute-start.7 = (f32[2,1024]{1,0:T(2,128)S(1)}, f32[2,1024]{1,0:T(2,128)S(1)}, u32[]{:S(2)}, u32[]{:S(2)}) collective-permute-start(f32[2,1024]{1,0:T(2,128)S(1)} %get-tuple-element.50), channel_id=1, source_target_pairs={{0,8},{8,0},{16,24},{24,16},{32,40},{40,32},{48,56},{56,48},{64,72... | collective-permute-start | bytes 24584 | tf_op jit(solution)/shard_map/ppermute | solution.py:16

commit v5 on v4

--- a/solution.py
+++ b/solution.py
@@ -255,6 +255,25 @@
     def stiff_of(dmg, mod):
         return ((1.0 - dmg) ** 2 + 0.001) * mod
 
+    def corner_face(x):
+        return jnp.stack(
+            [
+                displacement[0, x],
+                stiff_of(damage[0, x], modulus[0, x]),
+                displacement[depth_cells - 1, x],
+                stiff_of(damage[depth_cells - 1, x], modulus[depth_cells - 1, x]),
+            ]
+        )
+
+    lo_c, hi_c = halo_swap(corner_face(0), corner_face(tile_cells - 1), "tile")
+
+    def depth_face(adj, sec, at):
+        u_adj = jnp.concatenate([lo_c[at:at + 1], displacement[adj], hi_c[at:at + 1]])
+        c_adj = jnp.concatenate([lo_c[at + 1:at + 2], stiff_of(damage[adj], modulus[adj]), hi_c[at + 1:at + 2]])
+        return jnp.concatenate([u_adj, c_adj, displacement[sec], stiff_of(damage[sec], modulus[sec]), damage[adj]])
+
+    lo_z, hi_z = halo_swap(depth_face(0, 1, 0), depth_face(depth_cells - 1, depth_cells - 2, 2), "depth")
+
     def tile_face(rows, edge):
         return jnp.concatenate(
             [
@@ -266,22 +285,15 @@
             ]
         )
 
-    lo_x, hi_x = halo_swap(tile_face(slice(0, 2), 0), tile_face(slice(tile_cells - 2, tile_cells), tile_cells - 1), "tile")
+    face_lo, face_hi, _ = lax.optimization_barrier(
+        (tile_face(slice(0, 2), 0), tile_face(slice(tile_cells - 2, tile_cells), tile_cells - 1), lo_c)
+    )
+    lo_x, hi_x = halo_swap(face_lo, face_hi, "tile")
     dz = 4 * depth_cells
     p_ext = jnp.concatenate([lo_x[dz + depth_cells:dz + depth_cells + 2], pressure, hi_x[dz + depth_cells:dz + depth_cells + 2]])
     m_ext = jnp.concatenate([lo_x[dz + depth_cells + 2:], mask_f, hi_x[dz + depth_cells + 2:]])
     load_all = jnp.pad(4.0 * m_ext[1:-1] * p_ext[1:-1], ((X0 - 1, X0 - 1), (0, 0)))
     ids = jnp.stack([depth_start, tile_start]).astype(jnp.int32)
-
-    def depth_face(adj, sec):
-        u_adj = jnp.concatenate([lo_x[2 * adj + 1:2 * adj + 2], displacement[adj], hi_x[2 * adj:2 * adj + 1]])
-        c0 = 2 * depth_cells
-        c_adj = jnp.concatenate(
-            [lo_x[c0 + 2 * adj + 1:c0 + 2 * adj + 2], stiff_of(damage[adj], modulus[adj]), hi_x[c0 + 2 * adj:c0 + 2 * adj + 1]]
-        )
-        return jnp.concatenate([u_adj, c_adj, displacement[sec], stiff_of(damage[sec], modulus[sec]), damage[adj]])
-
-    lo_z, hi_z = halo_swap(depth_face(0, 1), depth_face(depth_cells - 1, depth_cells - 2), "depth")
 
     vmem = pl.BlockSpec(memory_space=pltpu.VMEM)
     smem = pl.BlockSpec(memory_space=pltpu.SMEM)

time: 150 us -> 158 us (1.053)
  starting transfers between devices: 42.9 us -> 51.8 us
  other arithmetic: 7.54 us -> 10.6 us
  waiting for transfers between devices: 78.4 us -> 75.6 us
    ppermute x3 -> x4, starting transfers between devices: 19.7 us -> 27.7 us  [halo_swap(): got_b = lax.ppermute(jnp.where(even, lo_face, hi_face), axis, pairs_b)]
    ppermute x3 -> x4, waiting for transfers between devices: 39 us -> 35.2 us  [halo_swap(): got_b = lax.ppermute(jnp.where(even, lo_face, hi_face), axis, pairs_b)]
    ppermute x3 -> x4, waiting for transfers between devices: 18.9 us -> 21.4 us  [halo_swap(): got_a = lax.ppermute(jnp.where(even, hi_face, lo_face), axis, pairs_a)]
    mul x2 -> x3, other arithmetic: 2.38 us -> 3.73 us  [stiff_of(): return ((1.0 - dmg) ** 2 + 0.001) * mod]
    ppermute x3 -> x4, starting transfers between devices: 14.9 us -> 14.6 us  [halo_swap(): got_a = lax.ppermute(jnp.where(even, hi_face, lo_face), axis, pairs_a)]
  transfers between devices with their start and end apart: 9 -> 11, of which waited for: 7 -> 6; matrix products, arithmetic and copies ran while one was open for 2% -> 6% of each run, Pallas kernels for 6% -> 6%
where the time goes in v5:
time: 158 us; the launch traced here: 157 us
  waiting for transfers between devices  75.6 us (48%)
  starting transfers between devices  51.8 us (33%)
  Pallas kernels  14.6 us (9%)
  other arithmetic  10.6 us (7%)
  local copies, waits for them, and re-layouts  4.3 us (3%)
    ppermute x4, waiting for transfers between devices, halo_swap(): got_b = lax.ppermute(jnp.where(even, lo_face, hi_face), axis, pairs_b)  35.2 us
    ppermute x4, starting transfers between devices, halo_swap(): got_b = lax.ppermute(jnp.where(even, lo_face, hi_face), axis, pairs_b)  27.7 us
    ppermute x4, waiting for transfers between devices, halo_swap(): got_a = lax.ppermute(jnp.where(even, hi_face, lo_face), axis, pairs_a)  21.4 us
    ppermute x3, waiting for transfers between devices, butterfly_sum(): part = part + lax.ppermute(part, axis, pairs)  19 us
    ppermute x4, starting transfers between devices, halo_swap(): got_a = lax.ppermute(jnp.where(even, hi_face, lo_face), axis, pairs_a)  14.6 us
    pallas_call x1, Pallas kernels, on_device(): pl.pallas_call(functools.partial(interior_kernel, total_depth, total_rows...  9.65 us
    ppermute x3, starting transfers between devices, butterfly_sum(): part = part + lax.ppermute(part, axis, pairs)  9.49 us
    pallas_call x1, Pallas kernels, on_device(): pl.pallas_call(functools.partial(boundary_kernel, total_depth, total_rows...  4.97 us
  transfers between devices with their start and end apart: 11, of which 6 were waited for; matrix products, arithmetic and copies ran while one was open for 6% of the time, Pallas kernels for 6%

profile of v5, /device:TPU:30, one launch (start us, length us, event | category | flops | bytes accessed | tf_op | source)
XLA Modules:
  0.0 157.4 jit_solution(17064253749479528976)
XLA Ops:
  0.0 1.1 multiply_bitcast_fusion.5
  1.1 1.9 %collective-permute-start.1 = (f32[4,1024]{1,0:T(4,128)S(1)}, f32[4,1024]{1,0:T(4,128)S(1)}, u32[]{:S(2)}, u32[]{:S(2)}) collective-permute-start(f32[4,1024]{1,0:T(4,128)S(1)} %get-tuple-element.61), channel_id=1, source_target_pairs={{0,8},{8,0},{16,24},{24,16},{32,40},{40,32},{48,56},{56,48},{64,72... | collective-permute-start | bytes 49160 | tf_op jit(solution)/shard_map/ppermute | solution.py:16
  3.0 13.5 %collective-permute-start = (f32[4,1024]{1,0:T(4,128)S(1)}, f32[4,1024]{1,0:T(4,128)S(1)}, u32[]{:S(2)}, u32[]{:S(2)}) collective-permute-start(f32[4,1024]{1,0:T(4,128)S(1)} %get-tuple-element.62), channel_id=1, source_target_pairs={{8,16},{24,32},{40,48},{56,64},{72,80},{88,96},{104,112},{120,128}... | collective-permute-start | bytes 49160 | tf_op jit(solution)/shard_map/ppermute | solution.py:17
  16.6 1.3 fusion.38
  17.9 1.8 %slice_multiply_fusion = (f32[16,2,1024]{2,1,0:T(2,128)S(1)}, f32[16,2,1024]{2,1,0:T(2,128)S(1)}) fusion(f32[16,16,1024]{2,1,0:T(8,128)} %mod_ref.3, f32[16,16,1024]{2,1,0:T(8,128)} %dmg_ref.3), kind=kLoop, calls=%fused_computation.13 | loop fusion | flops 262144 | bytes 786432 | tf_op jit(solution)/shard_map/mul | solution.py:256
  19.8 1.1 slice_bitcast_fusion
  20.9 0.9 bitcast_multiply_fusion
  21.9 0.6 pad_add_fusion.ids_ref
  23.1 6.4 %collective-permute-start.2 = (f32[84,1024]{1,0:T(8,128)S(1)}, f32[84,1024]{1,0:T(8,128)S(1)}, u32[]{:S(2)}, u32[]{:S(2)}) collective-permute-start(f32[84,1024]{1,0:T(8,128)S(1)} %get-tuple-element.45), channel_id=1, source_target_pairs={{8,16},{24,32},{40,48},{56,64},{72,80},{88,96},{104,112},{120,128}... | collective-permute-start | bytes 1032200 | tf_op jit(solution)/shard_map/ppermute | solution.py:17
  29.5 1.9 %collective-permute-start.3 = (f32[84,1024]{1,0:T(8,128)S(1)}, f32[84,1024]{1,0:T(8,128)S(1)}, u32[]{:S(2)}, u32[]{:S(2)}) collective-permute-start(f32[84,1024]{1,0:T(8,128)S(1)} %get-tuple-element.46), channel_id=1, source_target_pairs={{0,8},{8,0},{16,24},{24,16},{32,40},{40,32},{48,56},{56,48},{64,72... | collective-permute-start | bytes 1032200 | tf_op jit(solution)/shard_map/ppermute | solution.py:16
  31.4 0.7 concatenate.38
  32.2 0.7 concatenate.37
  32.9 0.8 broadcast_select_fusion.2
  33.7 8.9 %collective-permute-start.5 = (f32[84,1024]{1,0:T(8,128)}, f32[84,1024]{1,0:T(8,128)S(1)}, u32[]{:S(2)}, u32[]{:S(2)}) collective-permute-start(f32[84,1024]{1,0:T(8,128)} %get-tuple-element.41), channel_id=1, source_target_pairs={{0,1},{1,0},{2,3},{3,2},{4,5},{5,4},{6,7},{7,6},{8,9},{9,8},{10,11... | collective-permute-start | bytes 1032200 | tf_op jit(solution)/shard_map/ppermute | solution.py:16
  42.6 5.9 %collective-permute-start.4 = (f32[84,1024]{1,0:T(8,128)S(1)}, f32[84,1024]{1,0:T(8,128)}, u32[]{:S(2)}, u32[]{:S(2)}) collective-permute-start(f32[84,1024]{1,0:T(8,128)S(1)} %get-tuple-element.42), channel_id=1, source_target_pairs={{1,2},{3,4},{5,6},{2,1},{4,3},{6,5},{9,10},{11,12},{13,14},{10,9},... | collective-permute-start | bytes 1032200 | tf_op jit(solution)/shard_map/ppermute | solution.py:17
  48.7 0.8 pad.15.load_ref
  49.5 9.7 %shard_map.82 = (f32[16,1024]{1,0:T(8,128)}, f32[4,32,1024]{2,1,0:T(8,128)}) custom-call(s32[2]{0:T(128)} %pad_add_fusion.ids_ref, f32[16,16,1024]{2,1,0:T(8,128)} %u_ref.3, f32[16,16,1024]{2,1,0:T(8,128)} %dmg_ref.3, f32[16,16,1024]{2,1,0:T(8,128)} %mod_ref.3, f32[16,16,1024]{2,1,0:T(8,128)} %tgh_ref.3, f32[84,1024]{1,0:T(8,128)} %copy-done.1, ...), custom_call_target="tpu_custom_call" | custom-call | tf_op jit(solution)/shard_map/pallas_call | solution.py:301
  59.2 21.3 %collective-permute-done.5 = f32[84,1024]{1,0:T(8,128)S(1)} collective-permute-done((f32[84,1024]{1,0:T(8,128)}, f32[84,1024]{1,0:T(8,128)S(1)}, u32[]{:S(2)}, u32[]{:S(2)}) %collective-permute-start.5) | collective-permute-done | bytes 344096 | tf_op jit(solution)/shard_map/ppermute | solution.py:16
  80.5 26.6 %collective-permute-done.4 = f32[84,1024]{1,0:T(8,128)} collective-permute-done((f32[84,1024]{1,0:T(8,128)S(1)}, f32[84,1024]{1,0:T(8,128)}, u32[]{:S(2)}, u32[]{:S(2)}) %collective-permute-start.4) | collective-permute-done | bytes 344096 | tf_op jit(solution)/shard_map/ppermute | solution.py:17
  107.1 1.9 %broadcast_select_fusion = (f32[84,1024]{1,0:T(8,128)}, f32[84,1024]{1,0:T(8,128)}) fusion(f32[84,1024]{1,0:T(8,128)S(1)} %collective-permute-done.5, f32[84,1024]{1,0:T(8,128)} %collective-permute-done.4, pred[]{:T(512)S(6)} %eq.30), kind=kLoop, calls=%fused_computation.1 | loop fusion | flops 172032 | bytes 1376257 | tf_op jit(solution)/shard_map/jit(_where)/select_n | solution.py:18
  109.0 5.0 %shard_map.83 = f32[16,1024]{1,0:T(8,128)} custom-call(s32[2]{0:T(128)} %pad_add_fusion.ids_ref, f32[16,16,1024]{2,1,0:T(8,128)} %u_ref.3, f32[16,16,1024]{2,1,0:T(8,128)} %dmg_ref.3, f32[16,16,1024]{2,1,0:T(8,128)} %mod_ref.3, f32[16,16,1024]{2,1,0:T(8,128)} %tgh_ref.3, f32[84,1024]{1,0:T(8,128)} %copy-done.1, f32[84,1024]{1,0:T(8,128)} %copy-done.2, ...), custom_call_target="tpu_custom_call" | custom-call | tf_op jit(solution)/shard_map/pallas_call | solution.py:311
  114.0 2.3 %collective-permute-start.6 = (f32[16,1024]{1,0:T(8,128)}, f32[16,1024]{1,0:T(8,128)S(1)}, u32[]{:S(2)}, u32[]{:S(2)}) collective-permute-start(f32[16,1024]{1,0:T(8,128)} %shard_map.83), channel_id=1, source_target_pairs={{0,2},{1,3},{2,0},{3,1},{4,6},{5,7},{6,4},{7,5},{8,10},{9,11},{10,... | collective-permute-start | bytes 196616 | tf_op jit(solution)/shard_map/ppermute | solution.py:26
  116.4 4.0 %collective-permute-done.6 = f32[16,1024]{1,0:T(8,128)S(1)} collective-permute-done((f32[16,1024]{1,0:T(8,128)}, f32[16,1024]{1,0:T(8,128)S(1)}, u32[]{:S(2)}, u32[]{:S(2)}) %collective-permute-start.6) | collective-permute-done | bytes 65568 | tf_op jit(solution)/shard_map/ppermute | solution.py:26
  120.4 0.8 add.225
  121.2 1.9 %collective-permute-start.7 = (f32[16,1024]{1,0:T(8,128)S(1)}, f32[16,1024]{1,0:T(8,128)S(1)}, u32[]{:S(2)}, u32[]{:S(2)}) collective-permute-start(f32[16,1024]{1,0:T(8,128)S(1)} %add.225), channel_id=1, source_target_pairs={{0,4},{1,5},{2,6},{3,7},{4,0},{5,1},{6,2},{7,3},{8,12},{9,13},{10,... | collective-permute-start | bytes 196616 | tf_op jit(solution)/shard_map/ppermute | solution.py:26
  123.2 5.7 %collective-permute-done.7 = f32[16,1024]{1,0:T(8,128)S(1)} collective-permute-done((f32[16,1024]{1,0:T(8,128)S(1)}, f32[16,1024]{1,0:T(8,128)S(1)}, u32[]{:S(2)}, u32[]{:S(2)}) %collective-permute-start.7) | collective-permute-done | bytes 65568 | tf_op jit(solution)/shard_map/ppermute | solution.py:26
  128.9 5.2 %collective-permute-start.8 = (f32[16,1024]{1,0:T(8,128)S(1)}, f32[16,1024]{1,0:T(8,128)S(1)}, u32[]{:S(2)}, u32[]{:S(2)}) collective-permute-start(f32[16,1024]{1,0:T(8,128)S(1)} %add.226), channel_id=1, source_target_pairs={{0,1},{1,0},{2,3},{3,2},{4,5},{5,4},{6,7},{7,6},{8,9},{9,8},{10,11... | collective-permute-start | bytes 196616 | tf_op jit(solution)/shard_map/ppermute | solution.py:26
  134.4 9.4 %collective-permute-done.8 = f32[16,1024]{1,0:T(8,128)S(1)} collective-permute-done((f32[16,1024]{1,0:T(8,128)S(1)}, f32[16,1024]{1,0:T(8,128)S(1)}, u32[]{:S(2)}, u32[]{:S(2)}) %collective-permute-start.8) | collective-permute-done | bytes 65568 | tf_op jit(solution)/shard_map/ppermute | solution.py:26
  143.9 1.9 %collective-permute-start.10 = (f32[2,1024]{1,0:T(2,128)S(1)}, f32[2,1024]{1,0:T(2,128)S(1)}, u32[]{:S(2)}, u32[]{:S(2)}) collective-permute-start(f32[2,1024]{1,0:T(2,128)S(1)} %get-tuple-element.53), channel_id=1, source_target_pairs={{8,16},{24,32},{40,48},{56,64},{72,80},{88,96},{104,112},{120,128}... | collective-permute-start | bytes 24584 | tf_op jit(solution)/shard_map/ppermute | solution.py:17
  145.8 1.9 %collective-permute-start.9 = (f32[2,1024]{1,0:T(2,128)S(1)}, f32[2,1024]{1,0:T(2,128)S(1)}, u32[]{:S(2)}, u32[]{:S(2)}) collective-permute-start(f32[2,1024]{1,0:T(2,128)S(1)} %get-tuple-element.54), channel_id=1, source_target_pairs={{0,8},{8,0},{16,24},{24,16},{32,40},{40,32},{48,56},{56,48},{64,72... | collective-permute-start | bytes 24584 | tf_op jit(solution)/shard_map/ppermute | solution.py:16
  147.7 8.6 %collective-permute-done.10 = f32[2,1024]{1,0:T(2,128)S(1)} collective-permute-done((f32[2,1024]{1,0:T(2,128)S(1)}, f32[2,1024]{1,0:T(2,128)S(1)}, u32[]{:S(2)}, u32[]{:S(2)}) %collective-permute-start.10) | collective-permute-done | bytes 8224 | tf_op jit(solution)/shard_map/ppermute | solution.py:17
  156.6 0.8 fusion.33
  (49 shorter events, 1.6 us)
Async XLA Ops:
  0.0 19.7 %copy-start = (f32[16,16,1024]{2,1,0:T(8,128)S(1)}, f32[16,16,1024]{2,1,0:T(8,128)}, u32[]{:S(2)}) copy-start(f32[16,16,1024]{2,1,0:T(8,128)} %dmg_ref.3) | copy-start | bytes 3145732
  1.1 21.9 %collective-permute-start.1 = (f32[4,1024]{1,0:T(4,128)S(1)}, f32[4,1024]{1,0:T(4,128)S(1)}, u32[]{:S(2)}, u32[]{:S(2)}) collective-permute-start(f32[4,1024]{1,0:T(4,128)S(1)} %get-tuple-element.61), channel_id=1, source_target_pairs={{0,8},{8,0},{16,24},{24,16},{32,40},{40,32},{48,56},{56,48},{64,72... | collective-permute-start | bytes 49160 | tf_op jit(solution)/shard_map/ppermute | solution.py:16
  3.0 19.9 %collective-permute-start = (f32[4,1024]{1,0:T(4,128)S(1)}, f32[4,1024]{1,0:T(4,128)S(1)}, u32[]{:S(2)}, u32[]{:S(2)}) collective-permute-start(f32[4,1024]{1,0:T(4,128)S(1)} %get-tuple-element.62), channel_id=1, source_target_pairs={{8,16},{24,32},{40,48},{56,64},{72,80},{88,96},{104,112},{120,128}... | collective-permute-start | bytes 49160 | tf_op jit(solution)/shard_map/ppermute | solution.py:17
  19.7 2.1 %copy-start.4 = (s32[16,1024]{1,0:T(8,128)S(1)}, s32[16,1024]{1,0:T(8,128)}, u32[]{:S(2)}) copy-start(s32[16,1024]{1,0:T(8,128)} %param.13) | copy-start | bytes 196612
  19.8 2.1 %copy-start.3 = (f32[16,1024]{1,0:T(8,128)S(1)}, f32[16,1024]{1,0:T(8,128)}, u32[]{:S(2)}) copy-start(f32[16,1024]{1,0:T(8,128)} %param.12) | copy-start | bytes 196612
  23.1 25.4 %collective-permute-start.2 = (f32[84,1024]{1,0:T(8,128)S(1)}, f32[84,1024]{1,0:T(8,128)S(1)}, u32[]{:S(2)}, u32[]{:S(2)}) collective-permute-start(f32[84,1024]{1,0:T(8,128)S(1)} %get-tuple-element.45), channel_id=1, source_target_pairs={{8,16},{24,32},{40,48},{56,64},{72,80},{88,96},{104,112},{120,128}... | collective-permute-start | bytes 1032200 | tf_op jit(solution)/shard_map/ppermute | solution.py:17
  29.5 19.0 %collective-permute-start.3 = (f32[84,1024]{1,0:T(8,128)S(1)}, f32[84,1024]{1,0:T(8,128)S(1)}, u32[]{:S(2)}, u32[]{:S(2)}) collective-permute-start(f32[84,1024]{1,0:T(8,128)S(1)} %get-tuple-element.46), channel_id=1, source_target_pairs={{0,8},{8,0},{16,24},{24,16},{32,40},{40,32},{48,56},{56,48},{64,72... | collective-permute-start | bytes 1032200 | tf_op jit(solution)/shard_map/ppermute | solution.py:16
  33.7 46.8 %collective-permute-start.5 = (f32[84,1024]{1,0:T(8,128)}, f32[84,1024]{1,0:T(8,128)S(1)}, u32[]{:S(2)}, u32[]{:S(2)}) collective-permute-start(f32[84,1024]{1,0:T(8,128)} %get-tuple-element.41), channel_id=1, source_target_pairs={{0,1},{1,0},{2,3},{3,2},{4,5},{5,4},{6,7},{7,6},{8,9},{9,8},{10,11... | collective-permute-start | bytes 1032200 | tf_op jit(solution)/shard_map/ppermute | solution.py:16
  42.6 64.5 %collective-permute-start.4 = (f32[84,1024]{1,0:T(8,128)S(1)}, f32[84,1024]{1,0:T(8,128)}, u32[]{:S(2)}, u32[]{:S(2)}) collective-permute-start(f32[84,1024]{1,0:T(8,128)S(1)} %get-tuple-element.42), channel_id=1, source_target_pairs={{1,2},{3,4},{5,6},{2,1},{4,3},{6,5},{9,10},{11,12},{13,14},{10,9},... | collective-permute-start | bytes 1032200 | tf_op jit(solution)/shard_map/ppermute | solution.py:17
  48.6 1.0 copy-start.1
  48.6 0.9 copy-start.2
  109.0 25.1 %copy-start.5 = (f32[16]{0:T(128)S(1)}, f32[16]{0:T(128)}, u32[]{:S(2)}) copy-start(f32[16]{0:T(128)} %param.15) | copy-start | bytes 196
  109.0 25.1 %copy-start.6 = (s32[16]{0:T(128)S(1)}, s32[16]{0:T(128)}, u32[]{:S(2)}) copy-start(s32[16]{0:T(128)} %param.14) | copy-start | bytes 196
  114.0 6.4 %collective-permute-start.6 = (f32[16,1024]{1,0:T(8,128)}, f32[16,1024]{1,0:T(8,128)S(1)}, u32[]{:S(2)}, u32[]{:S(2)}) collective-permute-start(f32[16,1024]{1,0:T(8,128)} %shard_map.83), channel_id=1, source_target_pairs={{0,2},{1,3},{2,0},{3,1},{4,6},{5,7},{6,4},{7,5},{8,10},{9,11},{10,... | collective-permute-start | bytes 196616 | tf_op jit(solution)/shard_map/ppermute | solution.py:26
  121.2 7.7 %collective-permute-start.7 = (f32[16,1024]{1,0:T(8,128)S(1)}, f32[16,1024]{1,0:T(8,128)S(1)}, u32[]{:S(2)}, u32[]{:S(2)}) collective-permute-start(f32[16,1024]{1,0:T(8,128)S(1)} %add.225), channel_id=1, source_target_pairs={{0,4},{1,5},{2,6},{3,7},{4,0},{5,1},{6,2},{7,3},{8,12},{9,13},{10,... | collective-permute-start | bytes 196616 | tf_op jit(solution)/shard_map/ppermute | solution.py:26
  128.9 15.0 %collective-permute-start.8 = (f32[16,1024]{1,0:T(8,128)S(1)}, f32[16,1024]{1,0:T(8,128)S(1)}, u32[]{:S(2)}, u32[]{:S(2)}) collective-permute-start(f32[16,1024]{1,0:T(8,128)S(1)} %add.226), channel_id=1, source_target_pairs={{0,1},{1,0},{2,3},{3,2},{4,5},{5,4},{6,7},{7,6},{8,9},{9,8},{10,11... | collective-permute-start | bytes 196616 | tf_op jit(solution)/shard_map/ppermute | solution.py:26
  143.9 12.5 %collective-permute-start.10 = (f32[2,1024]{1,0:T(2,128)S(1)}, f32[2,1024]{1,0:T(2,128)S(1)}, u32[]{:S(2)}, u32[]{:S(2)}) collective-permute-start(f32[2,1024]{1,0:T(2,128)S(1)} %get-tuple-element.53), channel_id=1, source_target_pairs={{8,16},{24,32},{40,48},{56,64},{72,80},{88,96},{104,112},{120,128}... | collective-permute-start | bytes 24584 | tf_op jit(solution)/shard_map/ppermute | solution.py:17
  145.8 10.5 %collective-permute-start.9 = (f32[2,1024]{1,0:T(2,128)S(1)}, f32[2,1024]{1,0:T(2,128)S(1)}, u32[]{:S(2)}, u32[]{:S(2)}) collective-permute-start(f32[2,1024]{1,0:T(2,128)S(1)} %get-tuple-element.54), channel_id=1, source_target_pairs={{0,8},{8,0},{16,24},{24,16},{32,40},{40,32},{48,56},{56,48},{64,72... | collective-permute-start | bytes 24584 | tf_op jit(solution)/shard_map/ppermute | solution.py:16

commit v6 on v4

--- a/solution.py
+++ b/solution.py
@@ -15,6 +15,21 @@
     pairs_b = [(i, i + 1) for i in range(1, count - 1, 2)] + [(i + 1, i) for i in range(1, count - 1, 2)]
     got_a = lax.ppermute(jnp.where(even, hi_face, lo_face), axis, pairs_a)
     got_b = lax.ppermute(jnp.where(even, lo_face, hi_face), axis, pairs_b)
+    return jnp.where(even, got_b, got_a), jnp.where(even, got_a, got_b)
+
+
+def diagonal_swap(lo_face, hi_face, flip):
+    tiles = lax.axis_size("tile")
+    depths = lax.axis_size("depth")
+    even = lax.axis_index("tile") % 2 == 0
+    pairs_a = [(t * depths + d, (t ^ 1) * depths + (d ^ flip)) for t in range(tiles) for d in range(depths)]
+    pairs_b = []
+    for t in range(1, tiles - 1, 2):
+        for d in range(depths):
+            pairs_b.append((t * depths + d, (t + 1) * depths + (d ^ flip)))
+            pairs_b.append(((t + 1) * depths + (d ^ flip), t * depths + d))
+    got_a = lax.ppermute(jnp.where(even, hi_face, lo_face), ("tile", "depth"), pairs_a)
+    got_b = lax.ppermute(jnp.where(even, lo_face, hi_face), ("tile", "depth"), pairs_b)
     return jnp.where(even, got_b, got_a), jnp.where(even, got_a, got_b)
 
 
@@ -304,12 +319,19 @@
         scratch_shapes=[pltpu.VMEM((8, rows_all, width), f32)] * 4,
     )(ids, displacement, damage, modulus, toughness, lo_x, hi_x, lo_z, hi_z, edge, part_in, load_all)
 
-    aperture = 0.5 + butterfly_sum(partial_open, "depth")
-    trans = mask_f * aperture**3
-
-    t_lo, t_hi = halo_swap(trans[:2], trans[-2:], "tile")
-    t_ext = jnp.concatenate([t_lo, trans, t_hi])
+    depths = lax.axis_size("depth")
+    part_y = partial_open
+    for step in [1 << k for k in range(1, depths.bit_length() - 1)]:
+        part_y = part_y + lax.ppermute(part_y, "depth", [(i, i ^ step) for i in range(depths)])
+    far = lax.ppermute(part_y, "depth", [(i, i ^ 1) for i in range(depths)])
+    n_lo, n_hi = halo_swap(part_y[:2], part_y[-2:], "tile")
+    g_lo, g_hi = diagonal_swap(part_y[:2], part_y[-2:], 1)
+    open_ext = jnp.concatenate([n_lo + g_lo, part_y + far, n_hi + g_hi])
     x_ids = tile_start - 1 + jnp.arange(tile_cells + 2, dtype=jnp.int32)
+    x_ids2 = tile_start - 2 + jnp.arange(tile_cells + 4, dtype=jnp.int32)
+    rows_in2 = ((x_ids2 >= 0) & (x_ids2 < total_rows))[:, None]
+    t_ext = jnp.where(rows_in2, m_ext * (0.5 + open_ext) ** 3, jnp.float32(0.0))
+    trans = t_ext[2:-2]
     rows_in = ((x_ids >= 0) & (x_ids < total_rows))[:, None]
     src_ext = well_source(wells, rates, tile_start - 1, tile_cells + 2, width, width)
     k_pad = pad_last(t_ext)

time: 150 us -> 159 us (1.060)
  the two profiles are of different devices: /device:TPU:30 before, /device:TPU:23 now
where the time goes in v6:
time: 159 us
  waiting for transfers between devices  68.3 us (43%)
  starting transfers between devices  62.3 us (39%)
  Pallas kernels  14.6 us (9%)
  other arithmetic  7.58 us (5%)
  local copies, waits for them, and re-layouts  5.42 us (3%)
    ppermute x3, waiting for transfers between devices, halo_swap(): got_a = lax.ppermute(jnp.where(even, hi_face, lo_face), axis, pairs_a)  42.7 us
    ppermute x3, starting transfers between devices, halo_swap(): got_a = lax.ppermute(jnp.where(even, hi_face, lo_face), axis, pairs_a)  21.2 us
    ppermute x3, starting transfers between devices, halo_swap(): got_b = lax.ppermute(jnp.where(even, lo_face, hi_face), axis, pairs_b)  12 us
    ppermute x1, waiting for transfers between devices, on_device(): far = lax.ppermute(part_y, 'depth', [(i, i ^ 1) for i in range(depths)])  11.6 us
    pallas_call x1, Pallas kernels, on_device(): pl.pallas_call(functools.partial(interior_kernel, total_depth, total_rows...  9.66 us
    ppermute x1, starting transfers between devices, diagonal_swap(): lax.ppermute(jnp.where(even, lo_face, hi_face), ('tile', 'depth'), pairs_b)  9.62 us
    ppermute x1, starting transfers between devices, diagonal_swap(): lax.ppermute(jnp.where(even, hi_face, lo_face), ('tile', 'depth'), pairs_a)  8.79 us
    ppermute x3, waiting for transfers between devices, halo_swap(): got_b = lax.ppermute(jnp.where(even, lo_face, hi_face), axis, pairs_b)  7.62 us
  transfers between devices with their start and end apart: 11, of which 5 were waited for; matrix products, arithmetic and copies ran while one was open for 2% of the time, Pallas kernels for 6%

profile of v6, /device:TPU:23, one launch (start us, length us, event | category | flops | bytes accessed | tf_op | source)
XLA Modules:
  0.0 158.6 jit_solution(14954889246463143479)
XLA Ops:
  0.0 1.4 fusion.32
  1.5 1.3 fusion.31
  2.8 1.5 slice_multiply_fusion.1
  4.9 4.1 %collective-permute-start = (f32[84,1024]{1,0:T(8,128)S(1)}, f32[84,1024]{1,0:T(8,128)S(1)}, u32[]{:S(2)}, u32[]{:S(2)}) collective-permute-start(f32[84,1024]{1,0:T(8,128)S(1)} %get-tuple-element.33), channel_id=1, source_target_pairs={{8,16},{24,32},{40,48},{56,64},{72,80},{88,96},{104,112},{120,128}... | collective-permute-start | bytes 1032200 | tf_op jit(solution)/shard_map/ppermute | solution.py:17
  9.0 11.3 %collective-permute-start.1 = (f32[84,1024]{1,0:T(8,128)S(1)}, f32[84,1024]{1,0:T(8,128)S(1)}, u32[]{:S(2)}, u32[]{:S(2)}) collective-permute-start(f32[84,1024]{1,0:T(8,128)S(1)} %get-tuple-element.34), channel_id=1, source_target_pairs={{0,8},{8,0},{16,24},{24,16},{32,40},{40,32},{48,56},{56,48},{64,72... | collective-permute-start | bytes 1032200 | tf_op jit(solution)/shard_map/ppermute | solution.py:16
  20.3 0.9 bitcast_multiply_fusion
  21.3 0.7 pad_add_fusion.ids_ref
  22.0 1.0 slice_bitcast_fusion
  23.2 0.7 concatenate.31
  24.0 0.7 concatenate.30
  24.8 7.9 %collective-permute-start.3 = (f32[84,1024]{1,0:T(8,128)S(1)}, f32[84,1024]{1,0:T(8,128)S(1)}, u32[]{:S(2)}, u32[]{:S(2)}) collective-permute-start(f32[84,1024]{1,0:T(8,128)S(1)} %get-tuple-element.29), channel_id=1, source_target_pairs={{0,1},{1,0},{2,3},{3,2},{4,5},{5,4},{6,7},{7,6},{8,9},{9,8},{10,11... | collective-permute-start | bytes 1032200 | tf_op jit(solution)/shard_map/ppermute | solution.py:16
  32.8 5.9 %collective-permute-start.2 = (f32[84,1024]{1,0:T(8,128)S(1)}, f32[84,1024]{1,0:T(8,128)S(1)}, u32[]{:S(2)}, u32[]{:S(2)}) collective-permute-start(f32[84,1024]{1,0:T(8,128)S(1)} %get-tuple-element.30), channel_id=1, source_target_pairs={{1,2},{3,4},{5,6},{2,1},{4,3},{6,5},{9,10},{11,12},{13,14},{10,9},... | collective-permute-start | bytes 1032200 | tf_op jit(solution)/shard_map/ppermute | solution.py:17
  38.8 0.7 pad.15.load_ref
  39.5 9.7 %shard_map.82 = (f32[16,1024]{1,0:T(8,128)}, f32[4,32,1024]{2,1,0:T(8,128)}) custom-call(s32[2]{0:T(128)} %pad_add_fusion.ids_ref, f32[16,16,1024]{2,1,0:T(8,128)} %u_ref.3, f32[16,16,1024]{2,1,0:T(8,128)} %dmg_ref.3, f32[16,16,1024]{2,1,0:T(8,128)} %mod_ref.3, f32[16,16,1024]{2,1,0:T(8,128)} %tgh_ref.3, f32[84,1024]{1,0:T(8,128)} %copy-done.1, ...), custom_call_target="tpu_custom_call" | custom-call | tf_op jit(solution)/shard_map/pallas_call | solution.py:304
  49.1 42.7 %collective-permute-done.3 = f32[84,1024]{1,0:T(8,128)S(1)} collective-permute-done((f32[84,1024]{1,0:T(8,128)S(1)}, f32[84,1024]{1,0:T(8,128)S(1)}, u32[]{:S(2)}, u32[]{:S(2)}) %collective-permute-start.3) | collective-permute-done | bytes 344096 | tf_op jit(solution)/shard_map/ppermute | solution.py:16
  91.9 7.6 %collective-permute-done.2 = f32[84,1024]{1,0:T(8,128)S(1)} collective-permute-done((f32[84,1024]{1,0:T(8,128)S(1)}, f32[84,1024]{1,0:T(8,128)S(1)}, u32[]{:S(2)}, u32[]{:S(2)}) %collective-permute-start.2) | collective-permute-done | bytes 344096 | tf_op jit(solution)/shard_map/ppermute | solution.py:17
  99.5 0.9 broadcast_select_fusion
  100.4 5.0 %shard_map.83 = f32[16,1024]{1,0:T(8,128)} custom-call(s32[2]{0:T(128)} %pad_add_fusion.ids_ref, f32[16,16,1024]{2,1,0:T(8,128)} %u_ref.3, f32[16,16,1024]{2,1,0:T(8,128)} %dmg_ref.3, f32[16,16,1024]{2,1,0:T(8,128)} %mod_ref.3, f32[16,16,1024]{2,1,0:T(8,128)} %tgh_ref.3, f32[84,1024]{1,0:T(8,128)} %copy-done.1, f32[84,1024]{1,0:T(8,128)} %copy-done.2, ...), custom_call_target="tpu_custom_call" | custom-call | tf_op jit(solution)/shard_map/pallas_call | solution.py:314
  105.4 3.2 %collective-permute-start.4 = (f32[16,1024]{1,0:T(8,128)}, f32[16,1024]{1,0:T(8,128)S(1)}, u32[]{:S(2)}, u32[]{:S(2)}) collective-permute-start(f32[16,1024]{1,0:T(8,128)} %shard_map.83), channel_id=1, source_target_pairs={{0,2},{1,3},{2,0},{3,1},{4,6},{5,7},{6,4},{7,5},{8,10},{9,11},{10,... | collective-permute-start | bytes 196616 | tf_op jit(solution)/shard_map/ppermute | solution.py:325
  108.6 0.3 select_reduce_fusion
  108.9 1.7 %collective-permute-done.4 = f32[16,1024]{1,0:T(8,128)S(1)} collective-permute-done((f32[16,1024]{1,0:T(8,128)}, f32[16,1024]{1,0:T(8,128)S(1)}, u32[]{:S(2)}, u32[]{:S(2)}) %collective-permute-start.4) | collective-permute-done | bytes 65568 | tf_op jit(solution)/shard_map/ppermute | solution.py:325
  110.6 0.8 add.199
  111.4 1.9 %collective-permute-start.5 = (f32[16,1024]{1,0:T(8,128)S(1)}, f32[16,1024]{1,0:T(8,128)S(1)}, u32[]{:S(2)}, u32[]{:S(2)}) collective-permute-start(f32[16,1024]{1,0:T(8,128)S(1)} %add.199), channel_id=1, source_target_pairs={{0,4},{1,5},{2,6},{3,7},{4,0},{5,1},{6,2},{7,3},{8,12},{9,13},{10,... | collective-permute-start | bytes 196616 | tf_op jit(solution)/shard_map/ppermute | solution.py:325
  113.4 4.6 %collective-permute-done.5 = f32[16,1024]{1,0:T(8,128)S(1)} collective-permute-done((f32[16,1024]{1,0:T(8,128)S(1)}, f32[16,1024]{1,0:T(8,128)S(1)}, u32[]{:S(2)}, u32[]{:S(2)}) %collective-permute-start.5) | collective-permute-done | bytes 65568 | tf_op jit(solution)/shard_map/ppermute | solution.py:325
  118.0 9.6 %collective-permute-start.8 = (f32[2,1024]{1,0:T(2,128)S(1)}, f32[2,1024]{1,0:T(2,128)S(1)}, u32[]{:S(2)}, u32[]{:S(2)}) collective-permute-start(f32[2,1024]{1,0:T(2,128)S(1)} %get-tuple-element.49), channel_id=1, source_target_pairs={{8,17},{17,8},{9,16},{16,9},{10,19},{19,10},{11,18},{18,11},{12,21... | collective-permute-start | bytes 24584 | tf_op jit(solution)/shard_map/ppermute | solution.py:32
  127.6 1.9 %collective-permute-start.6 = (f32[2,1024]{1,0:T(2,128)S(1)}, f32[2,1024]{1,0:T(2,128)S(1)}, u32[]{:S(2)}, u32[]{:S(2)}) collective-permute-start(f32[2,1024]{1,0:T(2,128)S(1)} %get-tuple-element.49), channel_id=1, source_target_pairs={{8,16},{24,32},{40,48},{56,64},{72,80},{88,96},{104,112},{120,128}... | collective-permute-start | bytes 24584 | tf_op jit(solution)/shard_map/ppermute | solution.py:17
  129.5 8.8 %collective-permute-start.9 = (f32[2,1024]{1,0:T(2,128)S(1)}, f32[2,1024]{1,0:T(2,128)S(1)}, u32[]{:S(2)}, u32[]{:S(2)}) collective-permute-start(f32[2,1024]{1,0:T(2,128)S(1)} %get-tuple-element.50), channel_id=1, source_target_pairs={{0,9},{1,8},{2,11},{3,10},{4,13},{5,12},{6,15},{7,14},{8,1},{9,0},... | collective-permute-start | bytes 24584 | tf_op jit(solution)/shard_map/ppermute | solution.py:31
  138.3 1.9 %collective-permute-start.7 = (f32[2,1024]{1,0:T(2,128)S(1)}, f32[2,1024]{1,0:T(2,128)S(1)}, u32[]{:S(2)}, u32[]{:S(2)}) collective-permute-start(f32[2,1024]{1,0:T(2,128)S(1)} %get-tuple-element.50), channel_id=1, source_target_pairs={{0,8},{8,0},{16,24},{24,16},{32,40},{40,32},{48,56},{56,48},{64,72... | collective-permute-start | bytes 24584 | tf_op jit(solution)/shard_map/ppermute | solution.py:16
  140.3 5.6 %collective-permute-start.10 = (f32[16,1024]{1,0:T(8,128)S(1)}, f32[16,1024]{1,0:T(8,128)S(1)}, u32[]{:S(2)}, u32[]{:S(2)}) collective-permute-start(f32[16,1024]{1,0:T(8,128)S(1)} %add.200), channel_id=1, source_target_pairs={{0,1},{1,0},{2,3},{3,2},{4,5},{5,4},{6,7},{7,6},{8,9},{9,8},{10,11... | collective-permute-start | bytes 196616 | tf_op jit(solution)/shard_map/ppermute | solution.py:326
  145.9 11.6 %collective-permute-done.10 = f32[16,1024]{1,0:T(8,128)S(1)} collective-permute-done((f32[16,1024]{1,0:T(8,128)S(1)}, f32[16,1024]{1,0:T(8,128)S(1)}, u32[]{:S(2)}, u32[]{:S(2)}) %collective-permute-start.10) | collective-permute-done | bytes 65568 | tf_op jit(solution)/shard_map/ppermute | solution.py:326
  157.7 0.2 broadcast_multiply_fusion
  157.9 0.8 fusion.25
  (48 shorter events, 1.1 us)
Async XLA Ops:
  0.0 2.8 %copy-start = (f32[16,16,1024]{2,1,0:T(8,128)S(1)}, f32[16,16,1024]{2,1,0:T(8,128)}, u32[]{:S(2)}) copy-start(f32[16,16,1024]{2,1,0:T(8,128)} %dmg_ref.3) | copy-start | bytes 3145732
  0.0 4.4 %copy-start.4 = (s32[16,1024]{1,0:T(8,128)S(1)}, s32[16,1024]{1,0:T(8,128)}, u32[]{:S(2)}) copy-start(s32[16,1024]{1,0:T(8,128)} %param.13) | copy-start | bytes 196612
  2.8 1.9 %copy-start.3 = (f32[16,1024]{1,0:T(8,128)S(1)}, f32[16,1024]{1,0:T(8,128)}, u32[]{:S(2)}) copy-start(f32[16,1024]{1,0:T(8,128)} %param.12) | copy-start | bytes 196612
  4.9 18.2 %collective-permute-start = (f32[84,1024]{1,0:T(8,128)S(1)}, f32[84,1024]{1,0:T(8,128)S(1)}, u32[]{:S(2)}, u32[]{:S(2)}) collective-permute-start(f32[84,1024]{1,0:T(8,128)S(1)} %get-tuple-element.33), channel_id=1, source_target_pairs={{8,16},{24,32},{40,48},{56,64},{72,80},{88,96},{104,112},{120,128}... | collective-permute-start | bytes 1032200 | tf_op jit(solution)/shard_map/ppermute | solution.py:17
  9.0 14.1 %collective-permute-start.1 = (f32[84,1024]{1,0:T(8,128)S(1)}, f32[84,1024]{1,0:T(8,128)S(1)}, u32[]{:S(2)}, u32[]{:S(2)}) collective-permute-start(f32[84,1024]{1,0:T(8,128)S(1)} %get-tuple-element.34), channel_id=1, source_target_pairs={{0,8},{8,0},{16,24},{24,16},{32,40},{40,32},{48,56},{56,48},{64,72... | collective-permute-start | bytes 1032200 | tf_op jit(solution)/shard_map/ppermute | solution.py:16
  23.1 1.7 %copy-start.1 = (f32[84,1024]{1,0:T(8,128)}, f32[84,1024]{1,0:T(8,128)S(1)}, u32[]{:S(2)}) copy-start(f32[84,1024]{1,0:T(8,128)S(1)} %get-tuple-element.31.xlo_ref) | copy-start | bytes 1032196
  23.1 1.7 %copy-start.2 = (f32[84,1024]{1,0:T(8,128)}, f32[84,1024]{1,0:T(8,128)S(1)}, u32[]{:S(2)}) copy-start(f32[84,1024]{1,0:T(8,128)S(1)} %get-tuple-element.32.xhi_ref) | copy-start | bytes 1032196
  24.8 67.0 %collective-permute-start.3 = (f32[84,1024]{1,0:T(8,128)S(1)}, f32[84,1024]{1,0:T(8,128)S(1)}, u32[]{:S(2)}, u32[]{:S(2)}) collective-permute-start(f32[84,1024]{1,0:T(8,128)S(1)} %get-tuple-element.29), channel_id=1, source_target_pairs={{0,1},{1,0},{2,3},{3,2},{4,5},{5,4},{6,7},{7,6},{8,9},{9,8},{10,11... | collective-permute-start | bytes 1032200 | tf_op jit(solution)/shard_map/ppermute | solution.py:16
  32.8 66.7 %collective-permute-start.2 = (f32[84,1024]{1,0:T(8,128)S(1)}, f32[84,1024]{1,0:T(8,128)S(1)}, u32[]{:S(2)}, u32[]{:S(2)}) collective-permute-start(f32[84,1024]{1,0:T(8,128)S(1)} %get-tuple-element.30), channel_id=1, source_target_pairs={{1,2},{3,4},{5,6},{2,1},{4,3},{6,5},{9,10},{11,12},{13,14},{10,9},... | collective-permute-start | bytes 1032200 | tf_op jit(solution)/shard_map/ppermute | solution.py:17
  100.4 8.2 %copy-start.5 = (f32[16]{0:T(128)S(1)}, f32[16]{0:T(128)}, u32[]{:S(2)}) copy-start(f32[16]{0:T(128)} %param.15) | copy-start | bytes 196
  100.4 8.2 %copy-start.6 = (s32[16]{0:T(128)S(1)}, s32[16]{0:T(128)}, u32[]{:S(2)}) copy-start(s32[16]{0:T(128)} %param.14) | copy-start | bytes 196
  105.4 5.2 %collective-permute-start.4 = (f32[16,1024]{1,0:T(8,128)}, f32[16,1024]{1,0:T(8,128)S(1)}, u32[]{:S(2)}, u32[]{:S(2)}) collective-permute-start(f32[16,1024]{1,0:T(8,128)} %shard_map.83), channel_id=1, source_target_pairs={{0,2},{1,3},{2,0},{3,1},{4,6},{5,7},{6,4},{7,5},{8,10},{9,11},{10,... | collective-permute-start | bytes 196616 | tf_op jit(solution)/shard_map/ppermute | solution.py:325
  111.4 6.5 %collective-permute-start.5 = (f32[16,1024]{1,0:T(8,128)S(1)}, f32[16,1024]{1,0:T(8,128)S(1)}, u32[]{:S(2)}, u32[]{:S(2)}) collective-permute-start(f32[16,1024]{1,0:T(8,128)S(1)} %add.199), channel_id=1, source_target_pairs={{0,4},{1,5},{2,6},{3,7},{4,0},{5,1},{6,2},{7,3},{8,12},{9,13},{10,... | collective-permute-start | bytes 196616 | tf_op jit(solution)/shard_map/ppermute | solution.py:325
  118.0 27.9 %collective-permute-start.8 = (f32[2,1024]{1,0:T(2,128)S(1)}, f32[2,1024]{1,0:T(2,128)S(1)}, u32[]{:S(2)}, u32[]{:S(2)}) collective-permute-start(f32[2,1024]{1,0:T(2,128)S(1)} %get-tuple-element.49), channel_id=1, source_target_pairs={{8,17},{17,8},{9,16},{16,9},{10,19},{19,10},{11,18},{18,11},{12,21... | collective-permute-start | bytes 24584 | tf_op jit(solution)/shard_map/ppermute | solution.py:32
  127.6 18.3 %collective-permute-start.6 = (f32[2,1024]{1,0:T(2,128)S(1)}, f32[2,1024]{1,0:T(2,128)S(1)}, u32[]{:S(2)}, u32[]{:S(2)}) collective-permute-start(f32[2,1024]{1,0:T(2,128)S(1)} %get-tuple-element.49), channel_id=1, source_target_pairs={{8,16},{24,32},{40,48},{56,64},{72,80},{88,96},{104,112},{120,128}... | collective-permute-start | bytes 24584 | tf_op jit(solution)/shard_map/ppermute | solution.py:17
  129.5 16.4 %collective-permute-start.9 = (f32[2,1024]{1,0:T(2,128)S(1)}, f32[2,1024]{1,0:T(2,128)S(1)}, u32[]{:S(2)}, u32[]{:S(2)}) collective-permute-start(f32[2,1024]{1,0:T(2,128)S(1)} %get-tuple-element.50), channel_id=1, source_target_pairs={{0,9},{1,8},{2,11},{3,10},{4,13},{5,12},{6,15},{7,14},{8,1},{9,0},... | collective-permute-start | bytes 24584 | tf_op jit(solution)/shard_map/ppermute | solution.py:31
  138.3 7.6 %collective-permute-start.7 = (f32[2,1024]{1,0:T(2,128)S(1)}, f32[2,1024]{1,0:T(2,128)S(1)}, u32[]{:S(2)}, u32[]{:S(2)}) collective-permute-start(f32[2,1024]{1,0:T(2,128)S(1)} %get-tuple-element.50), channel_id=1, source_target_pairs={{0,8},{8,0},{16,24},{24,16},{32,40},{40,32},{48,56},{56,48},{64,72... | collective-permute-start | bytes 24584 | tf_op jit(solution)/shard_map/ppermute | solution.py:16
  140.3 17.3 %collective-permute-start.10 = (f32[16,1024]{1,0:T(8,128)S(1)}, f32[16,1024]{1,0:T(8,128)S(1)}, u32[]{:S(2)}, u32[]{:S(2)}) collective-permute-start(f32[16,1024]{1,0:T(8,128)S(1)} %add.200), channel_id=1, source_target_pairs={{0,1},{1,0},{2,3},{3,2},{4,5},{5,4},{6,7},{7,6},{8,9},{9,8},{10,11... | collective-permute-start | bytes 196616 | tf_op jit(solution)/shard_map/ppermute | solution.py:326

commit v7 on v4

--- a/solution.py
+++ b/solution.py
@@ -185,62 +185,77 @@
     edge_ref[3] = m_s[depth_cells - 2]
 
 
-def boundary_kernel(total_depth, total_rows, ids_ref, u_ref, dmg_ref, mod_ref, tgh_ref, xlo_ref, xhi_ref, zlo_ref,
-                    zhi_ref, edge_ref, part_ref, load_ref, out_ref, u_s, c_s, d_s, m_s):
+def side_kernel(total_depth, total_rows, first, ids_ref, u_ref, dmg_ref, mod_ref, tgh_ref, xlo_ref, xhi_ref, halo_ref,
+                edge_ref, load_ref, out_ref, u_s, c_s, d_s, m_s):
     depth_cells, tile_cells, width = u_ref.shape
     rows_all = u_s.shape[1]
     own = slice(X0, X0 + tile_cells)
     wide = slice(X0 - 1, X0 + tile_cells + 1)
     top = X0 + tile_cells
+    ext = tile_cells + 2
+    dz = 4 * depth_cells
     zero = jnp.zeros((rows_all, width), jnp.float32)
-    for j in range(8):
-        u_s[j] = zero
-        c_s[j] = zero
-        d_s[j] = zero
-    ext = tile_cells + 2
-    for side, ref, adj, sec in ((0, zlo_ref, 1, 0), (4, zhi_ref, 6, 7)):
-        u_s[adj, wide] = ref[0:ext]
-        c_s[adj, wide] = ref[ext:2 * ext]
-        u_s[sec, own] = ref[2 * ext:2 * ext + tile_cells]
-        c_s[sec, own] = ref[2 * ext + tile_cells:2 * ext + 2 * tile_cells]
-    d_s[0, own] = zlo_ref[2 * ext + 2 * tile_cells:2 * ext + 3 * tile_cells]
-    d_s[7, own] = zhi_ref[2 * ext + 2 * tile_cells:2 * ext + 3 * tile_cells]
-    dz = 4 * depth_cells
-    for slot, z in ((2, 0), (3, 1), (4, depth_cells - 2), (5, depth_cells - 1)):
-        dk = dmg_ref[z]
-        u_s[slot, own] = u_ref[z]
-        c_s[slot, own] = ((1.0 - dk) ** 2 + 0.001) * mod_ref[z]
-        u_s[slot, X0 - 2:X0] = xlo_ref[2 * z:2 * z + 2]
-        c_s[slot, X0 - 2:X0] = xlo_ref[2 * depth_cells + 2 * z:2 * depth_cells + 2 * z + 2]
-        u_s[slot, top:top + 2] = xhi_ref[2 * z:2 * z + 2]
-        c_s[slot, top:top + 2] = xhi_ref[2 * depth_cells + 2 * z:2 * depth_cells + 2 * z + 2]
-    for slot, z in ((1, 0), (2, 1), (5, depth_cells - 2), (6, depth_cells - 1)):
-        d_s[slot, own] = dmg_ref[z]
-        d_s[slot, X0 - 1:X0] = xlo_ref[dz + z:dz + z + 1]
-        d_s[slot, top:top + 1] = xhi_ref[dz + z:dz + z + 1]
-    d_s[3, own] = dmg_ref[2]
-    d_s[4, own] = dmg_ref[depth_cells - 3]
-    m_s[2] = edge_ref[0]
-    m_s[3] = edge_ref[1]
-    m_s[4] = edge_ref[2]
-    m_s[5] = edge_ref[3]
-
-    nb = neighbours(rows_all, width)
-    x_in = x_frame(ids_ref, rows_all, width, total_rows)
-    load = load_ref[...]
-    depth_start = ids_ref[0]
-    for us, ms, z in ((1, 0, -1), (2, 1, 0), (5, 6, depth_cells - 1), (6, 7, depth_cells)):
-        m_s[ms] = moved_at(
-            u_s[us], c_s[us], (c_s[us + 1], u_s[us + 1]), (c_s[us - 1], u_s[us - 1]), nb, depth_start + z, load, x_in,
-            total_depth,
-        )
-    acc = part_ref[...]
-    for ms, z in ((1, 0), (2, 1), (5, depth_cells - 2), (6, depth_cells - 1)):
-        acc = acc + opening_at(
-            m_s[ms], m_s[ms + 1], m_s[ms - 1], d_s[ms], d_s[ms + 1], d_s[ms - 1], nb, mod_ref[z], tgh_ref[z],
-            dmg_ref[z], own,
-        )
-    out_ref[...] = (4.0 / total_depth) * acc
+    odd = ids_ref[2]
+
+    def run(is_top):
+        for j in range(4):
+            u_s[j] = zero
+            c_s[j] = zero
+            d_s[j] = zero
+        adj, sec, d_halo = (2, 3, 3) if is_top else (1, 0, 0)
+        u_s[adj, wide] = halo_ref[0:ext]
+        c_s[adj, wide] = halo_ref[ext:2 * ext]
+        u_s[sec, own] = halo_ref[2 * ext:2 * ext + tile_cells]
+        c_s[sec, own] = halo_ref[2 * ext + tile_cells:2 * ext + 2 * tile_cells]
+        d_s[d_halo, own] = halo_ref[2 * ext + 2 * tile_cells:2 * ext + 3 * tile_cells]
+        base = depth_cells - 2 if is_top else 0
+        u_slots = (0, 1) if is_top else (2, 3)
+        for slot, z in zip(u_slots, (base, base + 1)):
+            dk = dmg_ref[z]
+            u_s[slot, own] = u_ref[z]
+            c_s[slot, own] = ((1.0 - dk) ** 2 + 0.001) * mod_ref[z]
+            u_s[slot, X0 - 2:X0] = xlo_ref[2 * z:2 * z + 2]
+            c_s[slot, X0 - 2:X0] = xlo_ref[2 * depth_cells + 2 * z:2 * depth_cells + 2 * z + 2]
+            u_s[slot, top:top + 2] = xhi_ref[2 * z:2 * z + 2]
+            c_s[slot, top:top + 2] = xhi_ref[2 * depth_cells + 2 * z:2 * depth_cells + 2 * z + 2]
+        for slot, z in zip((1, 2), (base, base + 1)):
+            d_s[slot, own] = dmg_ref[z]
+            d_s[slot, X0 - 1:X0] = xlo_ref[dz + z:dz + z + 1]
+            d_s[slot, top:top + 1] = xhi_ref[dz + z:dz + z + 1]
+        if is_top:
+            d_s[0, own] = dmg_ref[depth_cells - 3]
+            m_s[0] = edge_ref[2]
+            m_s[1] = edge_ref[3]
+            moves = ((1, 2, depth_cells - 1), (2, 3, depth_cells))
+        else:
+            d_s[3, own] = dmg_ref[2]
+            m_s[2] = edge_ref[0]
+            m_s[3] = edge_ref[1]
+            moves = ((1, 0, -1), (2, 1, 0))
+        nb = neighbours(rows_all, width)
+        x_in = x_frame(ids_ref, rows_all, width, total_rows)
+        load = load_ref[...]
+        depth_start = ids_ref[0]
+        for us, ms, z in moves:
+            m_s[ms] = moved_at(
+                u_s[us], c_s[us], (c_s[us + 1], u_s[us + 1]), (c_s[us - 1], u_s[us - 1]), nb, depth_start + z, load,
+                x_in, total_depth,
+            )
+        acc = jnp.zeros((tile_cells, width), jnp.float32)
+        for ms, z in zip((1, 2), (base, base + 1)):
+            acc = acc + opening_at(
+                m_s[ms], m_s[ms + 1], m_s[ms - 1], d_s[ms], d_s[ms + 1], d_s[ms - 1], nb, mod_ref[z], tgh_ref[z],
+                dmg_ref[z], own,
+            )
+        out_ref[...] = acc
+
+    @pl.when(odd == (0 if first else 1))
+    def _():
+        run(True)
+
+    @pl.when(odd == (1 if first else 0))
+    def _():
+        run(False)
 
 
 def on_device(displacement, damage, modulus, toughness, pressure, crack_mask, wells, rates):
@@ -271,7 +286,7 @@
     p_ext = jnp.concatenate([lo_x[dz + depth_cells:dz + depth_cells + 2], pressure, hi_x[dz + depth_cells:dz + depth_cells + 2]])
     m_ext = jnp.concatenate([lo_x[dz + depth_cells + 2:], mask_f, hi_x[dz + depth_cells + 2:]])
     load_all = jnp.pad(4.0 * m_ext[1:-1] * p_ext[1:-1], ((X0 - 1, X0 - 1), (0, 0)))
-    ids = jnp.stack([depth_start, tile_start]).astype(jnp.int32)
+    ids = jnp.stack([depth_start, tile_start, lax.axis_index("depth") % 2]).astype(jnp.int32)
 
     def depth_face(adj, sec):
         u_adj = jnp.concatenate([lo_x[2 * adj + 1:2 * adj + 2], displacement[adj], hi_x[2 * adj:2 * adj + 1]])
@@ -281,7 +296,12 @@
         )
         return jnp.concatenate([u_adj, c_adj, displacement[sec], stiff_of(damage[sec], modulus[sec]), damage[adj]])
 
-    lo_z, hi_z = halo_swap(depth_face(0, 1), depth_face(depth_cells - 1, depth_cells - 2), "depth")
+    depths = lax.axis_size("depth")
+    even_z = lax.axis_index("depth") % 2 == 0
+    lo_face, hi_face = depth_face(0, 1), depth_face(depth_cells - 1, depth_cells - 2)
+    got_a = lax.ppermute(jnp.where(even_z, hi_face, lo_face), "depth", [(i, i ^ 1) for i in range(depths)])
+    pairs_b = [(i, i + 1) for i in range(1, depths - 1, 2)] + [(i + 1, i) for i in range(1, depths - 1, 2)]
+    got_b = lax.ppermute(jnp.where(even_z, lo_face, hi_face), "depth", pairs_b)
 
     vmem = pl.BlockSpec(memory_space=pltpu.VMEM)
     smem = pl.BlockSpec(memory_space=pltpu.SMEM)
@@ -296,14 +316,16 @@
         out_specs=(vmem, vmem),
         scratch_shapes=[pltpu.VMEM((depth_cells, rows_all, width), f32)] * 4,
     )(ids, displacement, damage, modulus, toughness, lo_x, hi_x, load_all)
-    partial_open = pl.pallas_call(
-        functools.partial(boundary_kernel, total_depth, total_rows),
-        out_shape=jax.ShapeDtypeStruct((tile_cells, width), f32),
-        in_specs=[smem] + [vmem] * 11,
-        out_specs=vmem,
-        scratch_shapes=[pltpu.VMEM((8, rows_all, width), f32)] * 4,
-    )(ids, displacement, damage, modulus, toughness, lo_x, hi_x, lo_z, hi_z, edge, part_in, load_all)
-
+    sides = []
+    for first, got in ((True, got_a), (False, got_b)):
+        sides.append(pl.pallas_call(
+            functools.partial(side_kernel, total_depth, total_rows, first),
+            out_shape=jax.ShapeDtypeStruct((tile_cells, width), f32),
+            in_specs=[smem] + [vmem] * 9,
+            out_specs=vmem,
+            scratch_shapes=[pltpu.VMEM((4, rows_all, width), f32)] * 4,
+        )(ids, displacement, damage, modulus, toughness, lo_x, hi_x, got, edge, load_all))
+    partial_open = (4.0 / total_depth) * ((part_in + sides[0]) + sides[1])
     aperture = 0.5 + butterfly_sum(partial_open, "depth")
     trans = mask_f * aperture**3
 

time: 150 us -> 150 us (level)
  the two profiles are of different devices: /device:TPU:30 before, /device:TPU:22 now
where the time goes in v7:
time: 150 us; the launch traced here: 149 us
  waiting for transfers between devices  72.9 us (49%)
  starting transfers between devices  43.6 us (29%)
  Pallas kernels  17.9 us (12%)
  other arithmetic  7.51 us (5%)
  local copies, waits for them, and re-layouts  6.8 us (5%)
    ppermute x1, waiting for transfers between devices, on_device(): got_b = lax.ppermute(jnp.where(even_z, lo_face, hi_face), 'depth', pairs_b)  38.8 us
    ppermute x3, waiting for transfers between devices, butterfly_sum(): part = part + lax.ppermute(part, axis, pairs)  19.5 us
    ppermute x2, starting transfers between devices, halo_swap(): got_b = lax.ppermute(jnp.where(even, lo_face, hi_face), axis, pairs_b)  15.1 us
    ppermute x2, waiting for transfers between devices, halo_swap(): got_b = lax.ppermute(jnp.where(even, lo_face, hi_face), axis, pairs_b)  11.8 us
    ppermute x1, starting transfers between devices, on_device(): got_b = lax.ppermute(jnp.where(even_z, lo_face, hi_face), 'depth', pairs_b)  11 us
    pallas_call x1, Pallas kernels, on_device(): pl.pallas_call(functools.partial(interior_kernel, total_depth, total_rows...  9.65 us
    ppermute x3, starting transfers between devices, butterfly_sum(): part = part + lax.ppermute(part, axis, pairs)  9.34 us
    pallas_call x2, Pallas kernels, on_device(): pl.pallas_call(functools.partial(side_kernel, total_depth, total_rows, fi...  8.29 us
  transfers between devices with their start and end apart: 9, of which 7 were waited for; matrix products, arithmetic and copies ran while one was open for 2% of the time, Pallas kernels for 9%

profile of v7, /device:TPU:22, one launch (start us, length us, event | category | flops | bytes accessed | tf_op | source)
XLA Modules:
  0.0 149.1 jit_solution(8456823505153927739)
XLA Ops:
  0.0 0.9 convert_element_type.10
  0.9 1.3 fusion.37
  2.2 1.3 fusion.38
  3.8 1.5 slice_multiply_fusion.1
  5.7 12.9 %collective-permute-start = (f32[84,1024]{1,0:T(8,128)S(1)}, f32[84,1024]{1,0:T(8,128)S(1)}, u32[]{:S(2)}, u32[]{:S(2)}) collective-permute-start(f32[84,1024]{1,0:T(8,128)S(1)} %get-tuple-element.31), channel_id=1, source_target_pairs={{8,16},{24,32},{40,48},{56,64},{72,80},{88,96},{104,112},{120,128}... | collective-permute-start | bytes 1032200 | tf_op jit(solution)/shard_map/ppermute | solution.py:17
  18.5 1.9 %collective-permute-start.1 = (f32[84,1024]{1,0:T(8,128)S(1)}, f32[84,1024]{1,0:T(8,128)S(1)}, u32[]{:S(2)}, u32[]{:S(2)}) collective-permute-start(f32[84,1024]{1,0:T(8,128)S(1)} %get-tuple-element.32), channel_id=1, source_target_pairs={{0,8},{8,0},{16,24},{24,16},{32,40},{40,32},{48,56},{56,48},{64,72... | collective-permute-start | bytes 1032200 | tf_op jit(solution)/shard_map/ppermute | solution.py:16
  20.5 0.9 bitcast_multiply_fusion.1
  22.0 1.0 slice_bitcast_fusion.3
  23.1 3.6 %collective-permute-done = f32[84,1024]{1,0:T(8,128)S(1)} collective-permute-done((f32[84,1024]{1,0:T(8,128)S(1)}, f32[84,1024]{1,0:T(8,128)S(1)}, u32[]{:S(2)}, u32[]{:S(2)}) %collective-permute-start) | collective-permute-done | bytes 344096 | tf_op jit(solution)/shard_map/ppermute | solution.py:17
  26.8 0.7 concatenate.39
  27.6 0.7 concatenate.40
  28.4 11.0 %collective-permute-start.3 = (f32[84,1024]{1,0:T(8,128)S(1)}, f32[84,1024]{1,0:T(8,128)S(1)}, u32[]{:S(2)}, u32[]{:S(2)}) collective-permute-start(f32[84,1024]{1,0:T(8,128)S(1)} %get-tuple-element.28), channel_id=1, source_target_pairs={{1,2},{3,4},{5,6},{2,1},{4,3},{6,5},{9,10},{11,12},{13,14},{10,9},... | collective-permute-start | bytes 1032200 | tf_op jit(solution)/shard_map/ppermute | solution.py:304
  39.4 4.3 %collective-permute-start.2 = (f32[84,1024]{1,0:T(8,128)S(1)}, f32[84,1024]{1,0:T(8,128)S(1)}, u32[]{:S(2)}, u32[]{:S(2)}) collective-permute-start(f32[84,1024]{1,0:T(8,128)S(1)} %get-tuple-element.27), channel_id=1, source_target_pairs={{0,1},{1,0},{2,3},{3,2},{4,5},{5,4},{6,7},{7,6},{8,9},{9,8},{10,11... | collective-permute-start | bytes 1032200 | tf_op jit(solution)/shard_map/ppermute | solution.py:302
  43.8 0.7 pad.15.load_ref
  44.5 9.6 %shard_map.82 = (f32[16,1024]{1,0:T(8,128)}, f32[4,32,1024]{2,1,0:T(8,128)}) custom-call(s32[3]{0:T(128)} %pad_add_fusion.ids_ref, f32[16,16,1024]{2,1,0:T(8,128)} %u_ref.5, f32[16,16,1024]{2,1,0:T(8,128)} %dmg_ref.5, f32[16,16,1024]{2,1,0:T(8,128)} %mod_ref.5, f32[16,16,1024]{2,1,0:T(8,128)} %tgh_ref.5, f32[84,1024]{1,0:T(8,128)} %copy-done.1, ...), custom_call_target="tpu_custom_call" | custom-call | tf_op jit(solution)/shard_map/pallas_call | solution.py:309
  54.1 38.8 %collective-permute-done.3.halo_ref = f32[84,1024]{1,0:T(8,128)S(1)} collective-permute-done((f32[84,1024]{1,0:T(8,128)S(1)}, f32[84,1024]{1,0:T(8,128)S(1)}, u32[]{:S(2)}, u32[]{:S(2)}) %collective-permute-start.3) | collective-permute-done | bytes 344096 | tf_op jit(solution)/shard_map/ppermute | solution.py:304
  92.8 0.7 copy-done.5
  93.6 4.2 %shard_map.84 = f32[16,1024]{1,0:T(8,128)} custom-call(s32[3]{0:T(128)} %pad_add_fusion.ids_ref, f32[16,16,1024]{2,1,0:T(8,128)} %u_ref.5, f32[16,16,1024]{2,1,0:T(8,128)} %dmg_ref.5, f32[16,16,1024]{2,1,0:T(8,128)} %mod_ref.5, f32[16,16,1024]{2,1,0:T(8,128)} %tgh_ref.5, f32[84,1024]{1,0:T(8,128)} %copy-done.1, f32[84,1024]{1,0:T(8,128)} %copy-done.2, ...), custom_call_target="tpu_custom_call" | custom-call | tf_op jit(solution)/shard_map/pallas_call | solution.py:321
  97.8 2.8 %collective-permute-done.2.halo_ref = f32[84,1024]{1,0:T(8,128)S(1)} collective-permute-done((f32[84,1024]{1,0:T(8,128)S(1)}, f32[84,1024]{1,0:T(8,128)S(1)}, u32[]{:S(2)}, u32[]{:S(2)}) %collective-permute-start.2) | collective-permute-done | bytes 344096 | tf_op jit(solution)/shard_map/ppermute | solution.py:302
  100.6 0.7 copy-done.4
  101.3 4.1 %shard_map.83 = f32[16,1024]{1,0:T(8,128)} custom-call(s32[3]{0:T(128)} %pad_add_fusion.ids_ref, f32[16,16,1024]{2,1,0:T(8,128)} %u_ref.5, f32[16,16,1024]{2,1,0:T(8,128)} %dmg_ref.5, f32[16,16,1024]{2,1,0:T(8,128)} %mod_ref.5, f32[16,16,1024]{2,1,0:T(8,128)} %tgh_ref.5, f32[84,1024]{1,0:T(8,128)} %copy-done.1, f32[84,1024]{1,0:T(8,128)} %copy-done.2, ...), custom_call_target="tpu_custom_call" | custom-call | tf_op jit(solution)/shard_map/pallas_call | solution.py:321
  105.5 0.9 add_multiply_fusion
  106.3 1.9 %collective-permute-start.4 = (f32[16,1024]{1,0:T(8,128)S(1)}, f32[16,1024]{1,0:T(8,128)S(1)}, u32[]{:S(2)}, u32[]{:S(2)}) collective-permute-start(f32[16,1024]{1,0:T(8,128)S(1)} %add_multiply_fusion), channel_id=1, source_target_pairs={{0,2},{1,3},{2,0},{3,1},{4,6},{5,7},{6,4},{7,5},{8,10},{9,11},{10,... | collective-permute-start | bytes 196616 | tf_op jit(solution)/shard_map/ppermute | solution.py:26
  108.3 4.2 %collective-permute-done.4 = f32[16,1024]{1,0:T(8,128)S(1)} collective-permute-done((f32[16,1024]{1,0:T(8,128)S(1)}, f32[16,1024]{1,0:T(8,128)S(1)}, u32[]{:S(2)}, u32[]{:S(2)}) %collective-permute-start.4) | collective-permute-done | bytes 65568 | tf_op jit(solution)/shard_map/ppermute | solution.py:26
  112.5 1.9 %collective-permute-start.5 = (f32[16,1024]{1,0:T(8,128)S(1)}, f32[16,1024]{1,0:T(8,128)S(1)}, u32[]{:S(2)}, u32[]{:S(2)}) collective-permute-start(f32[16,1024]{1,0:T(8,128)S(1)} %add.185), channel_id=1, source_target_pairs={{0,4},{1,5},{2,6},{3,7},{4,0},{5,1},{6,2},{7,3},{8,12},{9,13},{10,... | collective-permute-start | bytes 196616 | tf_op jit(solution)/shard_map/ppermute | solution.py:26
  114.5 5.7 %collective-permute-done.5 = f32[16,1024]{1,0:T(8,128)S(1)} collective-permute-done((f32[16,1024]{1,0:T(8,128)S(1)}, f32[16,1024]{1,0:T(8,128)S(1)}, u32[]{:S(2)}, u32[]{:S(2)}) %collective-permute-start.5) | collective-permute-done | bytes 65568 | tf_op jit(solution)/shard_map/ppermute | solution.py:26
  120.2 5.5 %collective-permute-start.6 = (f32[16,1024]{1,0:T(8,128)S(1)}, f32[16,1024]{1,0:T(8,128)S(1)}, u32[]{:S(2)}, u32[]{:S(2)}) collective-permute-start(f32[16,1024]{1,0:T(8,128)S(1)} %add.186), channel_id=1, source_target_pairs={{0,1},{1,0},{2,3},{3,2},{4,5},{5,4},{6,7},{7,6},{8,9},{9,8},{10,11... | collective-permute-start | bytes 196616 | tf_op jit(solution)/shard_map/ppermute | solution.py:26
  126.0 9.6 %collective-permute-done.6 = f32[16,1024]{1,0:T(8,128)S(1)} collective-permute-done((f32[16,1024]{1,0:T(8,128)S(1)}, f32[16,1024]{1,0:T(8,128)S(1)}, u32[]{:S(2)}, u32[]{:S(2)}) %collective-permute-start.6) | collective-permute-done | bytes 65568 | tf_op jit(solution)/shard_map/ppermute | solution.py:26
  135.6 2.3 %collective-permute-start.8 = (f32[2,1024]{1,0:T(2,128)S(1)}, f32[2,1024]{1,0:T(2,128)S(1)}, u32[]{:S(2)}, u32[]{:S(2)}) collective-permute-start(f32[2,1024]{1,0:T(2,128)S(1)} %get-tuple-element.47), channel_id=1, source_target_pairs={{8,16},{24,32},{40,48},{56,64},{72,80},{88,96},{104,112},{120,128}... | collective-permute-start | bytes 24584 | tf_op jit(solution)/shard_map/ppermute | solution.py:17
  137.9 1.9 %collective-permute-start.7 = (f32[2,1024]{1,0:T(2,128)S(1)}, f32[2,1024]{1,0:T(2,128)S(1)}, u32[]{:S(2)}, u32[]{:S(2)}) collective-permute-start(f32[2,1024]{1,0:T(2,128)S(1)} %get-tuple-element.48), channel_id=1, source_target_pairs={{0,8},{8,0},{16,24},{24,16},{32,40},{40,32},{48,56},{56,48},{64,72... | collective-permute-start | bytes 24584 | tf_op jit(solution)/shard_map/ppermute | solution.py:16
  139.9 8.3 %collective-permute-done.8 = f32[2,1024]{1,0:T(2,128)S(1)} collective-permute-done((f32[2,1024]{1,0:T(2,128)S(1)}, f32[2,1024]{1,0:T(2,128)S(1)}, u32[]{:S(2)}, u32[]{:S(2)}) %collective-permute-start.8) | collective-permute-done | bytes 8224 | tf_op jit(solution)/shard_map/ppermute | solution.py:17
  148.4 0.8 fusion.33
  (51 shorter events, 2.2 us)
Async XLA Ops:
  0.0 3.8 %copy-start = (f32[16,16,1024]{2,1,0:T(8,128)S(1)}, f32[16,16,1024]{2,1,0:T(8,128)}, u32[]{:S(2)}) copy-start(f32[16,16,1024]{2,1,0:T(8,128)} %dmg_ref.5) | copy-start | bytes 3145732
  3.5 1.9 %copy-start.3 = (f32[16,1024]{1,0:T(8,128)S(1)}, f32[16,1024]{1,0:T(8,128)}, u32[]{:S(2)}) copy-start(f32[16,1024]{1,0:T(8,128)} %param.12) | copy-start | bytes 196612
  5.7 21.0 %collective-permute-start = (f32[84,1024]{1,0:T(8,128)S(1)}, f32[84,1024]{1,0:T(8,128)S(1)}, u32[]{:S(2)}, u32[]{:S(2)}) collective-permute-start(f32[84,1024]{1,0:T(8,128)S(1)} %get-tuple-element.31), channel_id=1, source_target_pairs={{8,16},{24,32},{40,48},{56,64},{72,80},{88,96},{104,112},{120,128}... | collective-permute-start | bytes 1032200 | tf_op jit(solution)/shard_map/ppermute | solution.py:17
  18.5 8.1 %collective-permute-start.1 = (f32[84,1024]{1,0:T(8,128)S(1)}, f32[84,1024]{1,0:T(8,128)S(1)}, u32[]{:S(2)}, u32[]{:S(2)}) collective-permute-start(f32[84,1024]{1,0:T(8,128)S(1)} %get-tuple-element.32), channel_id=1, source_target_pairs={{0,8},{8,0},{16,24},{24,16},{32,40},{40,32},{48,56},{56,48},{64,72... | collective-permute-start | bytes 1032200 | tf_op jit(solution)/shard_map/ppermute | solution.py:16
  26.7 1.7 %copy-start.1 = (f32[84,1024]{1,0:T(8,128)}, f32[84,1024]{1,0:T(8,128)S(1)}, u32[]{:S(2)}) copy-start(f32[84,1024]{1,0:T(8,128)S(1)} %get-tuple-element.29.xlo_ref) | copy-start | bytes 1032196
  26.7 1.7 %copy-start.2 = (f32[84,1024]{1,0:T(8,128)}, f32[84,1024]{1,0:T(8,128)S(1)}, u32[]{:S(2)}) copy-start(f32[84,1024]{1,0:T(8,128)S(1)} %get-tuple-element.30.xhi_ref) | copy-start | bytes 1032196
  28.4 64.4 %collective-permute-start.3 = (f32[84,1024]{1,0:T(8,128)S(1)}, f32[84,1024]{1,0:T(8,128)S(1)}, u32[]{:S(2)}, u32[]{:S(2)}) collective-permute-start(f32[84,1024]{1,0:T(8,128)S(1)} %get-tuple-element.28), channel_id=1, source_target_pairs={{1,2},{3,4},{5,6},{2,1},{4,3},{6,5},{9,10},{11,12},{13,14},{10,9},... | collective-permute-start | bytes 1032200 | tf_op jit(solution)/shard_map/ppermute | solution.py:304
  39.4 61.2 %collective-permute-start.2 = (f32[84,1024]{1,0:T(8,128)S(1)}, f32[84,1024]{1,0:T(8,128)S(1)}, u32[]{:S(2)}, u32[]{:S(2)}) collective-permute-start(f32[84,1024]{1,0:T(8,128)S(1)} %get-tuple-element.27), channel_id=1, source_target_pairs={{0,1},{1,0},{2,3},{3,2},{4,5},{5,4},{6,7},{7,6},{8,9},{9,8},{10,11... | collective-permute-start | bytes 1032200 | tf_op jit(solution)/shard_map/ppermute | solution.py:302
  92.8 0.7 copy-start.5
  97.7 7.7 %copy-start.6 = (f32[16,1024]{1,0:T(8,128)S(1)}, f32[16,1024]{1,0:T(8,128)}, u32[]{:S(2)}) copy-start(f32[16,1024]{1,0:T(8,128)} %shard_map.84) | copy-start | bytes 196612
  97.7 7.7 %copy-start.8 = (f32[16,1024]{1,0:T(8,128)S(1)}, f32[16,1024]{1,0:T(8,128)}, u32[]{:S(2)}) copy-start(f32[16,1024]{1,0:T(8,128)} %get-tuple-element.7) | copy-start | bytes 196612
  97.7 27.9 %copy-start.9 = (f32[16]{0:T(128)S(1)}, f32[16]{0:T(128)}, u32[]{:S(2)}) copy-start(f32[16]{0:T(128)} %param.15) | copy-start | bytes 196
  97.7 27.9 %copy-start.10 = (s32[16]{0:T(128)S(1)}, s32[16]{0:T(128)}, u32[]{:S(2)}) copy-start(s32[16]{0:T(128)} %param.14) | copy-start | bytes 196
  97.8 37.8 %copy-start.7 = (s32[16,1024]{1,0:T(8,128)S(1)}, s32[16,1024]{1,0:T(8,128)}, u32[]{:S(2)}) copy-start(s32[16,1024]{1,0:T(8,128)} %param.13) | copy-start | bytes 196612
  100.6 0.7 copy-start.4
  106.3 6.2 %collective-permute-start.4 = (f32[16,1024]{1,0:T(8,128)S(1)}, f32[16,1024]{1,0:T(8,128)S(1)}, u32[]{:S(2)}, u32[]{:S(2)}) collective-permute-start(f32[16,1024]{1,0:T(8,128)S(1)} %add_multiply_fusion), channel_id=1, source_target_pairs={{0,2},{1,3},{2,0},{3,1},{4,6},{5,7},{6,4},{7,5},{8,10},{9,11},{10,... | collective-permute-start | bytes 196616 | tf_op jit(solution)/shard_map/ppermute | solution.py:26
  112.5 7.7 %collective-permute-start.5 = (f32[16,1024]{1,0:T(8,128)S(1)}, f32[16,1024]{1,0:T(8,128)S(1)}, u32[]{:S(2)}, u32[]{:S(2)}) collective-permute-start(f32[16,1024]{1,0:T(8,128)S(1)} %add.185), channel_id=1, source_target_pairs={{0,4},{1,5},{2,6},{3,7},{4,0},{5,1},{6,2},{7,3},{8,12},{9,13},{10,... | collective-permute-start | bytes 196616 | tf_op jit(solution)/shard_map/ppermute | solution.py:26
  120.2 15.4 %collective-permute-start.6 = (f32[16,1024]{1,0:T(8,128)S(1)}, f32[16,1024]{1,0:T(8,128)S(1)}, u32[]{:S(2)}, u32[]{:S(2)}) collective-permute-start(f32[16,1024]{1,0:T(8,128)S(1)} %add.186), channel_id=1, source_target_pairs={{0,1},{1,0},{2,3},{3,2},{4,5},{5,4},{6,7},{7,6},{8,9},{9,8},{10,11... | collective-permute-start | bytes 196616 | tf_op jit(solution)/shard_map/ppermute | solution.py:26
  135.6 12.5 %collective-permute-start.8 = (f32[2,1024]{1,0:T(2,128)S(1)}, f32[2,1024]{1,0:T(2,128)S(1)}, u32[]{:S(2)}, u32[]{:S(2)}) collective-permute-start(f32[2,1024]{1,0:T(2,128)S(1)} %get-tuple-element.47), channel_id=1, source_target_pairs={{8,16},{24,32},{40,48},{56,64},{72,80},{88,96},{104,112},{120,128}... | collective-permute-start | bytes 24584 | tf_op jit(solution)/shard_map/ppermute | solution.py:17
  137.9 10.2 %collective-permute-start.7 = (f32[2,1024]{1,0:T(2,128)S(1)}, f32[2,1024]{1,0:T(2,128)S(1)}, u32[]{:S(2)}, u32[]{:S(2)}) collective-permute-start(f32[2,1024]{1,0:T(2,128)S(1)} %get-tuple-element.48), channel_id=1, source_target_pairs={{0,8},{8,0},{16,24},{24,16},{32,40},{40,32},{48,56},{56,48},{64,72... | collective-permute-start | bytes 24584 | tf_op jit(solution)/shard_map/ppermute | solution.py:16

commit v8 on v7

--- a/solution.py
+++ b/solution.py
@@ -185,9 +185,13 @@
     edge_ref[3] = m_s[depth_cells - 2]
 
 
-def side_kernel(total_depth, total_rows, first, ids_ref, u_ref, dmg_ref, mod_ref, tgh_ref, xlo_ref, xhi_ref, halo_ref,
+def side_kernel(total_depth, total_rows, depth_cells, first, ids_ref, u_ref, dmg_ref, mod_ref, tgh_ref, xlo_ref, xhi_ref, halo_ref,
                 edge_ref, load_ref, out_ref, u_s, c_s, d_s, m_s):
-    depth_cells, tile_cells, width = u_ref.shape
+    _, tile_cells, width = u_ref.shape
+
+    def loc(z):
+        return z if z < 3 else z - depth_cells + 6
+
     rows_all = u_s.shape[1]
     own = slice(X0, X0 + tile_cells)
     wide = slice(X0 - 1, X0 + tile_cells + 1)
@@ -211,24 +215,24 @@
         base = depth_cells - 2 if is_top else 0
         u_slots = (0, 1) if is_top else (2, 3)
         for slot, z in zip(u_slots, (base, base + 1)):
-            dk = dmg_ref[z]
-            u_s[slot, own] = u_ref[z]
-            c_s[slot, own] = ((1.0 - dk) ** 2 + 0.001) * mod_ref[z]
+            dk = dmg_ref[loc(z)]
+            u_s[slot, own] = u_ref[loc(z)]
+            c_s[slot, own] = ((1.0 - dk) ** 2 + 0.001) * mod_ref[loc(z)]
             u_s[slot, X0 - 2:X0] = xlo_ref[2 * z:2 * z + 2]
             c_s[slot, X0 - 2:X0] = xlo_ref[2 * depth_cells + 2 * z:2 * depth_cells + 2 * z + 2]
             u_s[slot, top:top + 2] = xhi_ref[2 * z:2 * z + 2]
             c_s[slot, top:top + 2] = xhi_ref[2 * depth_cells + 2 * z:2 * depth_cells + 2 * z + 2]
         for slot, z in zip((1, 2), (base, base + 1)):
-            d_s[slot, own] = dmg_ref[z]
+            d_s[slot, own] = dmg_ref[loc(z)]
             d_s[slot, X0 - 1:X0] = xlo_ref[dz + z:dz + z + 1]
             d_s[slot, top:top + 1] = xhi_ref[dz + z:dz + z + 1]
         if is_top:
-            d_s[0, own] = dmg_ref[depth_cells - 3]
+            d_s[0, own] = dmg_ref[loc(depth_cells - 3)]
             m_s[0] = edge_ref[2]
             m_s[1] = edge_ref[3]
             moves = ((1, 2, depth_cells - 1), (2, 3, depth_cells))
         else:
-            d_s[3, own] = dmg_ref[2]
+            d_s[3, own] = dmg_ref[loc(2)]
             m_s[2] = edge_ref[0]
             m_s[3] = edge_ref[1]
             moves = ((1, 0, -1), (2, 1, 0))
@@ -244,8 +248,8 @@
         acc = jnp.zeros((tile_cells, width), jnp.float32)
         for ms, z in zip((1, 2), (base, base + 1)):
             acc = acc + opening_at(
-                m_s[ms], m_s[ms + 1], m_s[ms - 1], d_s[ms], d_s[ms + 1], d_s[ms - 1], nb, mod_ref[z], tgh_ref[z],
-                dmg_ref[z], own,
+                m_s[ms], m_s[ms + 1], m_s[ms - 1], d_s[ms], d_s[ms + 1], d_s[ms - 1], nb, mod_ref[loc(z)], tgh_ref[loc(z)],
+                dmg_ref[loc(z)], own,
             )
         out_ref[...] = acc
 
@@ -316,15 +320,16 @@
         out_specs=(vmem, vmem),
         scratch_shapes=[pltpu.VMEM((depth_cells, rows_all, width), f32)] * 4,
     )(ids, displacement, damage, modulus, toughness, lo_x, hi_x, load_all)
+    ends = [jnp.concatenate([a[:3], a[-3:]]) for a in (displacement, damage, modulus, toughness)]
     sides = []
     for first, got in ((True, got_a), (False, got_b)):
         sides.append(pl.pallas_call(
-            functools.partial(side_kernel, total_depth, total_rows, first),
+            functools.partial(side_kernel, total_depth, total_rows, depth_cells, first),
             out_shape=jax.ShapeDtypeStruct((tile_cells, width), f32),
             in_specs=[smem] + [vmem] * 9,
             out_specs=vmem,
             scratch_shapes=[pltpu.VMEM((4, rows_all, width), f32)] * 4,
-        )(ids, displacement, damage, modulus, toughness, lo_x, hi_x, got, edge, load_all))
+        )(ids, *ends, lo_x, hi_x, got, edge, load_all))
     partial_open = (4.0 / total_depth) * ((part_in + sides[0]) + sides[1])
     aperture = 0.5 + butterfly_sum(partial_open, "depth")
     trans = mask_f * aperture**3

time: 150 us -> 160 us (1.067)
  local copies, waits for them, and re-layouts: 6.8 us -> 13.5 us
  other arithmetic: 7.51 us -> 13.2 us
    slice x0 -> x4, local copies, waits for them, and re-layouts: none -> 3.35 us  [on_device(): a[:3]]
    ppermute x2, waiting for transfers between devices: 11.8 us -> 8.61 us  [halo_swap(): got_b = lax.ppermute(jnp.where(even, lo_face, hi_face), axis, pairs_b)]
    concatenate x0 -> x2, other arithmetic: none -> 3.21 us  [on_device(): jnp.concatenate([a[:3], a[-3:]])]
    concatenate x2, local copies, waits for them, and re-layouts: 0.1 us -> 2.59 us  [tile_face(): jnp.concatenate([displacement[:, rows].reshape(-1, width), stiff_of(damag...]
    ppermute x1, starting transfers between devices: 11 us -> 8.71 us  [on_device(): got_b = lax.ppermute(jnp.where(even_z, lo_face, hi_face), 'depth', pairs_b)]
    ppermute x1, starting transfers between devices: 4.31 us -> 6.56 us  [on_device(): lax.ppermute(jnp.where(even_z, hi_face, lo_face), 'depth', [(i, i ^ 1) fo...]
    ppermute x1, waiting for transfers between devices: 38.8 us -> 40.9 us  [on_device(): got_b = lax.ppermute(jnp.where(even_z, lo_face, hi_face), 'depth', pairs_b)]
    select_n x2, other arithmetic: 0.07 us -> 2.01 us  [halo_swap(): got_b = lax.ppermute(jnp.where(even, lo_face, hi_face), axis, pairs_b)]
  transfers between devices with their start and end apart: 9 -> 9, of which waited for: 7 -> 6; matrix products, arithmetic and copies ran while one was open for 2% -> 6% of each run, Pallas kernels for 9% -> 8%
where the time goes in v8:
time: 160 us
  waiting for transfers between devices  72.9 us (46%)
  starting transfers between devices  43.2 us (27%)
  Pallas kernels  16.4 us (10%)
  local copies, waits for them, and re-layouts  13.5 us (8%)
  other arithmetic  13.2 us (8%)
    ppermute x1, waiting for transfers between devices, on_device(): got_b = lax.ppermute(jnp.where(even_z, lo_face, hi_face), 'depth', pairs_b)  40.9 us
    ppermute x3, waiting for transfers between devices, butterfly_sum(): part = part + lax.ppermute(part, axis, pairs)  19.7 us
    ppermute x2, starting transfers between devices, halo_swap(): got_b = lax.ppermute(jnp.where(even, lo_face, hi_face), axis, pairs_b)  14.8 us
    pallas_call x1, Pallas kernels, on_device(): pl.pallas_call(functools.partial(interior_kernel, total_depth, total_rows...  9.66 us
    ppermute x3, starting transfers between devices, butterfly_sum(): part = part + lax.ppermute(part, axis, pairs)  9.32 us
    ppermute x1, starting transfers between devices, on_device(): got_b = lax.ppermute(jnp.where(even_z, lo_face, hi_face), 'depth', pairs_b)  8.71 us
    ppermute x2, waiting for transfers between devices, halo_swap(): got_b = lax.ppermute(jnp.where(even, lo_face, hi_face), axis, pairs_b)  8.61 us
    pallas_call x2, Pallas kernels, on_device(): pl.pallas_call(functools.partial(side_kernel, total_depth, total_rows, de...  6.73 us
  transfers between devices with their start and end apart: 9, of which 6 were waited for; matrix products, arithmetic and copies ran while one was open for 6% of the time, Pallas kernels for 8%

profile of v8, /device:TPU:22, one launch (start us, length us, event | category | flops | bytes accessed | tf_op | source)
XLA Modules:
  0.0 159.6 jit_solution(15638328003175808731)
XLA Ops:
  0.0 0.9 convert_element_type.10
  0.9 1.3 fusion.41
  2.3 1.3 fusion.42
  3.8 1.4 slice_multiply_fusion.1
  5.4 0.8 fusion.47
  6.3 2.5 %concatenate.48 = f32[84,1024]{1,0:T(8,128)} concatenate(f32[32,1024]{1,0:T(8,128)S(1)} %reshape.59, f32[32,1024]{1,0:T(8,128)S(1)} %reshape.60, f32[16,1024]{1,0:T(8,128)S(1)} %get-tuple-element.61, f32[2,1024]{1,0:T(2,128)S(1)} %get-tuple-element.63, f32[2,1024]{1,0:T(2,128)S(1)} %get-tuple-element.56), dimensions={0} | concatenate | bytes 688128 | tf_op jit(solution)/shard_map/concatenate | solution.py:278
  8.9 2.0 %broadcast_select_fusion.5 = (f32[84,1024]{1,0:T(8,128)}, f32[84,1024]{1,0:T(8,128)}) fusion(f32[84,1024]{1,0:T(8,128)S(1)} %concatenate.47, f32[84,1024]{1,0:T(8,128)} %concatenate.48, pred[]{:T(512)S(6)} %eq.28), kind=kLoop, calls=%fused_computation.10 | loop fusion | flops 172032 | bytes 1376257 | tf_op jit(solution)/shard_map/jit(_where)/select_n | solution.py:17
  10.9 12.9 %collective-permute-start = (f32[84,1024]{1,0:T(8,128)}, f32[84,1024]{1,0:T(8,128)}, u32[]{:S(2)}, u32[]{:S(2)}) collective-permute-start(f32[84,1024]{1,0:T(8,128)} %get-tuple-element.37), channel_id=1, source_target_pairs={{8,16},{24,32},{40,48},{56,64},{72,80},{88,96},{104,112},{120,128}... | collective-permute-start | bytes 1032200 | tf_op jit(solution)/shard_map/ppermute | solution.py:17
  23.7 1.9 %collective-permute-start.1 = (f32[84,1024]{1,0:T(8,128)}, f32[84,1024]{1,0:T(8,128)}, u32[]{:S(2)}, u32[]{:S(2)}) collective-permute-start(f32[84,1024]{1,0:T(8,128)} %get-tuple-element.38), channel_id=1, source_target_pairs={{0,8},{8,0},{16,24},{24,16},{32,40},{40,32},{48,56},{56,48},{64,72... | collective-permute-start | bytes 1032200 | tf_op jit(solution)/shard_map/ppermute | solution.py:16
  27.1 0.8 fusion.39
  27.9 1.8 %fusion.37 = (f32[3,16,1024]{2,1,0:T(8,128)}, f32[3,16,1024]{2,1,0:T(8,128)}) fusion(f32[16,16,1024]{2,1,0:T(8,128)} %tgh_ref.1), kind=kLoop, calls=%fused_computation.96 | loop fusion | bytes 786432 | tf_op jit(solution)/shard_map/slice | solution.py:323
  29.7 2.2 %pad_maximum_fusion.2 = (f32[6,16,1024]{2,1,0:T(8,128)}, f32[6,16,1024]{2,1,0:T(8,128)}) fusion(f32[3,16,1024]{2,1,0:T(8,128)} %get-tuple-element.24, f32[3,16,1024]{2,1,0:T(8,128)} %get-tuple-element.23, f32[3,16,1024]{2,1,0:T(8,128)} %get-tuple-element.22, f32[3,16,1024]{2,1,0:T(8,128)} %get-tuple-element.21), kind=kLoop, calls=%fused_computation.3 | loop fusion | flops 196608 | bytes 1572864 | tf_op jit(solution)/shard_map/concatenate | solution.py:323
  32.0 1.0 pad_maximum_fusion
  34.3 1.2 broadcast_select_fusion.3
  37.2 8.7 %collective-permute-start.3 = (f32[84,1024]{1,0:T(8,128)S(1)}, f32[84,1024]{1,0:T(8,128)S(1)}, u32[]{:S(2)}, u32[]{:S(2)}) collective-permute-start(f32[84,1024]{1,0:T(8,128)S(1)} %get-tuple-element.34), channel_id=1, source_target_pairs={{1,2},{3,4},{5,6},{2,1},{4,3},{6,5},{9,10},{11,12},{13,14},{10,9},... | collective-permute-start | bytes 1032200 | tf_op jit(solution)/shard_map/ppermute | solution.py:308
  45.9 6.6 %collective-permute-start.2 = (f32[84,1024]{1,0:T(8,128)S(1)}, f32[84,1024]{1,0:T(8,128)S(1)}, u32[]{:S(2)}, u32[]{:S(2)}) collective-permute-start(f32[84,1024]{1,0:T(8,128)S(1)} %get-tuple-element.33), channel_id=1, source_target_pairs={{0,1},{1,0},{2,3},{3,2},{4,5},{5,4},{6,7},{7,6},{8,9},{9,8},{10,11... | collective-permute-start | bytes 1032200 | tf_op jit(solution)/shard_map/ppermute | solution.py:306
  53.3 9.7 %shard_map.82 = (f32[16,1024]{1,0:T(8,128)}, f32[4,32,1024]{2,1,0:T(8,128)}) custom-call(s32[3]{0:T(128)} %pad_add_fusion.ids_ref, f32[16,16,1024]{2,1,0:T(8,128)} %u_ref.1, f32[16,16,1024]{2,1,0:T(8,128)} %dmg_ref.1, f32[16,16,1024]{2,1,0:T(8,128)} %mod_ref.1, f32[16,16,1024]{2,1,0:T(8,128)} %tgh_ref.1, f32[84,1024]{1,0:T(8,128)} %copy-done, ...), custom_call_target="tpu_custom_call" | custom-call | tf_op jit(solution)/shard_map/pallas_call | solution.py:313
  62.9 40.9 %collective-permute-done.3.halo_ref = f32[84,1024]{1,0:T(8,128)S(1)} collective-permute-done((f32[84,1024]{1,0:T(8,128)S(1)}, f32[84,1024]{1,0:T(8,128)S(1)}, u32[]{:S(2)}, u32[]{:S(2)}) %collective-permute-start.3) | collective-permute-done | bytes 344096 | tf_op jit(solution)/shard_map/ppermute | solution.py:308
  104.6 3.4 %shard_map.84 = f32[16,1024]{1,0:T(8,128)} custom-call(s32[3]{0:T(128)} %pad_add_fusion.ids_ref, f32[6,16,1024]{2,1,0:T(8,128)} %get-tuple-element.69.u_ref, f32[6,16,1024]{2,1,0:T(8,128)} %get-tuple-element.70.dmg_ref, f32[6,16,1024]{2,1,0:T(8,128)} %get-tuple-element.71.mod_ref, f32[6,16,1024]{2,1,0:T(8,128)} %get-tuple-element.72.tgh_ref, ...), custom_call_target="tpu_custom_call" | custom-call | tf_op jit(solution)/shard_map/pallas_call | solution.py:326
  108.0 3.7 %collective-permute-done.2.halo_ref = f32[84,1024]{1,0:T(8,128)S(1)} collective-permute-done((f32[84,1024]{1,0:T(8,128)S(1)}, f32[84,1024]{1,0:T(8,128)S(1)}, u32[]{:S(2)}, u32[]{:S(2)}) %collective-permute-start.2) | collective-permute-done | bytes 344096 | tf_op jit(solution)/shard_map/ppermute | solution.py:306
  112.4 3.4 %shard_map.83 = f32[16,1024]{1,0:T(8,128)} custom-call(s32[3]{0:T(128)} %pad_add_fusion.ids_ref, f32[6,16,1024]{2,1,0:T(8,128)} %get-tuple-element.69.u_ref, f32[6,16,1024]{2,1,0:T(8,128)} %get-tuple-element.70.dmg_ref, f32[6,16,1024]{2,1,0:T(8,128)} %get-tuple-element.71.mod_ref, f32[6,16,1024]{2,1,0:T(8,128)} %get-tuple-element.72.tgh_ref, ...), custom_call_target="tpu_custom_call" | custom-call | tf_op jit(solution)/shard_map/pallas_call | solution.py:326
  115.8 0.9 add_multiply_fusion
  116.6 1.9 %collective-permute-start.4 = (f32[16,1024]{1,0:T(8,128)S(1)}, f32[16,1024]{1,0:T(8,128)S(1)}, u32[]{:S(2)}, u32[]{:S(2)}) collective-permute-start(f32[16,1024]{1,0:T(8,128)S(1)} %add_multiply_fusion), channel_id=1, source_target_pairs={{0,2},{1,3},{2,0},{3,1},{4,6},{5,7},{6,4},{7,5},{8,10},{9,11},{10,... | collective-permute-start | bytes 196616 | tf_op jit(solution)/shard_map/ppermute | solution.py:26
  118.6 4.2 %collective-permute-done.4 = f32[16,1024]{1,0:T(8,128)S(1)} collective-permute-done((f32[16,1024]{1,0:T(8,128)S(1)}, f32[16,1024]{1,0:T(8,128)S(1)}, u32[]{:S(2)}, u32[]{:S(2)}) %collective-permute-start.4) | collective-permute-done | bytes 65568 | tf_op jit(solution)/shard_map/ppermute | solution.py:26
  122.8 1.9 %collective-permute-start.5 = (f32[16,1024]{1,0:T(8,128)S(1)}, f32[16,1024]{1,0:T(8,128)S(1)}, u32[]{:S(2)}, u32[]{:S(2)}) collective-permute-start(f32[16,1024]{1,0:T(8,128)S(1)} %add.185), channel_id=1, source_target_pairs={{0,4},{1,5},{2,6},{3,7},{4,0},{5,1},{6,2},{7,3},{8,12},{9,13},{10,... | collective-permute-start | bytes 196616 | tf_op jit(solution)/shard_map/ppermute | solution.py:26
  124.8 5.7 %collective-permute-done.5 = f32[16,1024]{1,0:T(8,128)S(1)} collective-permute-done((f32[16,1024]{1,0:T(8,128)S(1)}, f32[16,1024]{1,0:T(8,128)S(1)}, u32[]{:S(2)}, u32[]{:S(2)}) %collective-permute-start.5) | collective-permute-done | bytes 65568 | tf_op jit(solution)/shard_map/ppermute | solution.py:26
  130.5 5.5 %collective-permute-start.6 = (f32[16,1024]{1,0:T(8,128)S(1)}, f32[16,1024]{1,0:T(8,128)S(1)}, u32[]{:S(2)}, u32[]{:S(2)}) collective-permute-start(f32[16,1024]{1,0:T(8,128)S(1)} %add.186), channel_id=1, source_target_pairs={{0,1},{1,0},{2,3},{3,2},{4,5},{5,4},{6,7},{7,6},{8,9},{9,8},{10,11... | collective-permute-start | bytes 196616 | tf_op jit(solution)/shard_map/ppermute | solution.py:26
  136.3 9.8 %collective-permute-done.6 = f32[16,1024]{1,0:T(8,128)S(1)} collective-permute-done((f32[16,1024]{1,0:T(8,128)S(1)}, f32[16,1024]{1,0:T(8,128)S(1)}, u32[]{:S(2)}, u32[]{:S(2)}) %collective-permute-start.6) | collective-permute-done | bytes 65568 | tf_op jit(solution)/shard_map/ppermute | solution.py:26
  146.1 1.9 %collective-permute-start.8 = (f32[2,1024]{1,0:T(2,128)S(1)}, f32[2,1024]{1,0:T(2,128)S(1)}, u32[]{:S(2)}, u32[]{:S(2)}) collective-permute-start(f32[2,1024]{1,0:T(2,128)S(1)} %get-tuple-element.53), channel_id=1, source_target_pairs={{8,16},{24,32},{40,48},{56,64},{72,80},{88,96},{104,112},{120,128}... | collective-permute-start | bytes 24584 | tf_op jit(solution)/shard_map/ppermute | solution.py:17
  148.0 1.9 %collective-permute-start.7 = (f32[2,1024]{1,0:T(2,128)S(1)}, f32[2,1024]{1,0:T(2,128)S(1)}, u32[]{:S(2)}, u32[]{:S(2)}) collective-permute-start(f32[2,1024]{1,0:T(2,128)S(1)} %get-tuple-element.54), channel_id=1, source_target_pairs={{0,8},{8,0},{16,24},{24,16},{32,40},{40,32},{48,56},{56,48},{64,72... | collective-permute-start | bytes 24584 | tf_op jit(solution)/shard_map/ppermute | solution.py:16
  150.0 8.6 %collective-permute-done.8 = f32[2,1024]{1,0:T(2,128)S(1)} collective-permute-done((f32[2,1024]{1,0:T(2,128)S(1)}, f32[2,1024]{1,0:T(2,128)S(1)}, u32[]{:S(2)}, u32[]{:S(2)}) %collective-permute-start.8) | collective-permute-done | bytes 8224 | tf_op jit(solution)/shard_map/ppermute | solution.py:17
  158.8 0.8 fusion.33
  (77 shorter events, 7.7 us)
Async XLA Ops:
  0.0 3.8 %copy-start.2 = (f32[16,16,1024]{2,1,0:T(8,128)S(1)}, f32[16,16,1024]{2,1,0:T(8,128)}, u32[]{:S(2)}) copy-start(f32[16,16,1024]{2,1,0:T(8,128)} %dmg_ref.1) | copy-start | bytes 3145732
  0.9 4.5 %copy-start.10 = (f32[16,1024]{1,0:T(8,128)}, f32[16,1024]{1,0:T(8,128)S(1)}, u32[]{:S(2)}) copy-start(f32[16,1024]{1,0:T(8,128)S(1)} %convert_element_type.10) | copy-start | bytes 196612
  6.3 19.3 %copy-start.3 = (f32[16,16,1024]{2,1,0:T(8,128)S(1)}, f32[16,16,1024]{2,1,0:T(8,128)}, u32[]{:S(2)}) copy-start(f32[16,16,1024]{2,1,0:T(8,128)} %mod_ref.1) | copy-start | bytes 3145732
  8.9 17.5 %copy-start.4 = (f32[16,16,1024]{2,1,0:T(8,128)S(1)}, f32[16,16,1024]{2,1,0:T(8,128)}, u32[]{:S(2)}) copy-start(f32[16,16,1024]{2,1,0:T(8,128)} %u_ref.1) | copy-start | bytes 3145732
  10.9 23.4 %collective-permute-start = (f32[84,1024]{1,0:T(8,128)}, f32[84,1024]{1,0:T(8,128)}, u32[]{:S(2)}, u32[]{:S(2)}) collective-permute-start(f32[84,1024]{1,0:T(8,128)} %get-tuple-element.37), channel_id=1, source_target_pairs={{8,16},{24,32},{40,48},{56,64},{72,80},{88,96},{104,112},{120,128}... | collective-permute-start | bytes 1032200 | tf_op jit(solution)/shard_map/ppermute | solution.py:17
  23.7 10.5 %collective-permute-start.1 = (f32[84,1024]{1,0:T(8,128)}, f32[84,1024]{1,0:T(8,128)}, u32[]{:S(2)}, u32[]{:S(2)}) collective-permute-start(f32[84,1024]{1,0:T(8,128)} %get-tuple-element.38), channel_id=1, source_target_pairs={{0,8},{8,0},{16,24},{24,16},{32,40},{40,32},{48,56},{56,48},{64,72... | collective-permute-start | bytes 1032200 | tf_op jit(solution)/shard_map/ppermute | solution.py:16
  29.7 2.3 %copy-start.5 = (f32[3,16,1024]{2,1,0:T(8,128)S(1)}, f32[3,16,1024]{2,1,0:T(8,128)}, u32[]{:S(2)}) copy-start(f32[3,16,1024]{2,1,0:T(8,128)} %get-tuple-element.25) | copy-start | bytes 589828
  29.7 2.3 %copy-start.6 = (f32[3,16,1024]{2,1,0:T(8,128)S(1)}, f32[3,16,1024]{2,1,0:T(8,128)}, u32[]{:S(2)}) copy-start(f32[3,16,1024]{2,1,0:T(8,128)} %get-tuple-element.26) | copy-start | bytes 589828
  34.2 1.3 copy-start.14
  34.2 1.3 copy-start.15
  34.2 1.3 copy-start.17
  34.2 2.1 %copy-start.16 = (f32[16,1024]{1,0:T(8,128)S(1)}, f32[16,1024]{1,0:T(8,128)}, u32[]{:S(2)}) copy-start(f32[16,1024]{1,0:T(8,128)} %get-tuple-element.12) | copy-start | bytes 196612
  35.5 1.7 %copy-start = (f32[84,1024]{1,0:T(8,128)}, f32[84,1024]{1,0:T(8,128)S(1)}, u32[]{:S(2)}) copy-start(f32[84,1024]{1,0:T(8,128)S(1)} %get-tuple-element.35.xlo_ref) | copy-start | bytes 1032196
  35.5 10.4 %copy-start.1 = (f32[84,1024]{1,0:T(8,128)}, f32[84,1024]{1,0:T(8,128)S(1)}, u32[]{:S(2)}) copy-start(f32[84,1024]{1,0:T(8,128)S(1)} %get-tuple-element.36.xhi_ref) | copy-start | bytes 1032196
  36.3 16.2 %copy-start.7 = (f32[16,1024]{1,0:T(8,128)S(1)}, f32[16,1024]{1,0:T(8,128)}, u32[]{:S(2)}) copy-start(f32[16,1024]{1,0:T(8,128)} %param.12) | copy-start | bytes 196612
  36.4 16.2 %copy-start.11 = (f32[16,1024]{1,0:T(8,128)S(1)}, f32[16,1024]{1,0:T(8,128)}, u32[]{:S(2)}) copy-start(f32[16,1024]{1,0:T(8,128)} %copy-done.10) | copy-start | bytes 196612
  37.2 66.7 %collective-permute-start.3 = (f32[84,1024]{1,0:T(8,128)S(1)}, f32[84,1024]{1,0:T(8,128)S(1)}, u32[]{:S(2)}, u32[]{:S(2)}) collective-permute-start(f32[84,1024]{1,0:T(8,128)S(1)} %get-tuple-element.34), channel_id=1, source_target_pairs={{1,2},{3,4},{5,6},{2,1},{4,3},{6,5},{9,10},{11,12},{13,14},{10,9},... | collective-permute-start | bytes 1032200 | tf_op jit(solution)/shard_map/ppermute | solution.py:308
  45.9 65.7 %collective-permute-start.2 = (f32[84,1024]{1,0:T(8,128)S(1)}, f32[84,1024]{1,0:T(8,128)S(1)}, u32[]{:S(2)}, u32[]{:S(2)}) collective-permute-start(f32[84,1024]{1,0:T(8,128)S(1)} %get-tuple-element.33), channel_id=1, source_target_pairs={{0,1},{1,0},{2,3},{3,2},{4,5},{5,4},{6,7},{7,6},{8,9},{9,8},{10,11... | collective-permute-start | bytes 1032200 | tf_op jit(solution)/shard_map/ppermute | solution.py:306
  103.9 0.7 copy-start.9
  108.0 7.8 %copy-start.12 = (f32[16,1024]{1,0:T(8,128)S(1)}, f32[16,1024]{1,0:T(8,128)}, u32[]{:S(2)}) copy-start(f32[16,1024]{1,0:T(8,128)} %shard_map.84) | copy-start | bytes 196612
  108.0 7.8 %copy-start.18 = (f32[16,1024]{1,0:T(8,128)S(1)}, f32[16,1024]{1,0:T(8,128)}, u32[]{:S(2)}) copy-start(f32[16,1024]{1,0:T(8,128)} %get-tuple-element.7) | copy-start | bytes 196612
  108.0 28.0 %copy-start.19 = (f32[16]{0:T(128)S(1)}, f32[16]{0:T(128)}, u32[]{:S(2)}) copy-start(f32[16]{0:T(128)} %param.15) | copy-start | bytes 196
  108.0 28.0 %copy-start.20 = (s32[16]{0:T(128)S(1)}, s32[16]{0:T(128)}, u32[]{:S(2)}) copy-start(s32[16]{0:T(128)} %param.14) | copy-start | bytes 196
  108.0 38.1 %copy-start.13 = (s32[16,1024]{1,0:T(8,128)S(1)}, s32[16,1024]{1,0:T(8,128)}, u32[]{:S(2)}) copy-start(s32[16,1024]{1,0:T(8,128)} %param.13) | copy-start | bytes 196612
  111.7 0.7 copy-start.8
  116.6 6.2 %collective-permute-start.4 = (f32[16,1024]{1,0:T(8,128)S(1)}, f32[16,1024]{1,0:T(8,128)S(1)}, u32[]{:S(2)}, u32[]{:S(2)}) collective-permute-start(f32[16,1024]{1,0:T(8,128)S(1)} %add_multiply_fusion), channel_id=1, source_target_pairs={{0,2},{1,3},{2,0},{3,1},{4,6},{5,7},{6,4},{7,5},{8,10},{9,11},{10,... | collective-permute-start | bytes 196616 | tf_op jit(solution)/shard_map/ppermute | solution.py:26
  122.8 7.7 %collective-permute-start.5 = (f32[16,1024]{1,0:T(8,128)S(1)}, f32[16,1024]{1,0:T(8,128)S(1)}, u32[]{:S(2)}, u32[]{:S(2)}) collective-permute-start(f32[16,1024]{1,0:T(8,128)S(1)} %add.185), channel_id=1, source_target_pairs={{0,4},{1,5},{2,6},{3,7},{4,0},{5,1},{6,2},{7,3},{8,12},{9,13},{10,... | collective-permute-start | bytes 196616 | tf_op jit(solution)/shard_map/ppermute | solution.py:26
  130.5 15.6 %collective-permute-start.6 = (f32[16,1024]{1,0:T(8,128)S(1)}, f32[16,1024]{1,0:T(8,128)S(1)}, u32[]{:S(2)}, u32[]{:S(2)}) collective-permute-start(f32[16,1024]{1,0:T(8,128)S(1)} %add.186), channel_id=1, source_target_pairs={{0,1},{1,0},{2,3},{3,2},{4,5},{5,4},{6,7},{7,6},{8,9},{9,8},{10,11... | collective-permute-start | bytes 196616 | tf_op jit(solution)/shard_map/ppermute | solution.py:26
  146.1 12.5 %collective-permute-start.8 = (f32[2,1024]{1,0:T(2,128)S(1)}, f32[2,1024]{1,0:T(2,128)S(1)}, u32[]{:S(2)}, u32[]{:S(2)}) collective-permute-start(f32[2,1024]{1,0:T(2,128)S(1)} %get-tuple-element.53), channel_id=1, source_target_pairs={{8,16},{24,32},{40,48},{56,64},{72,80},{88,96},{104,112},{120,128}... | collective-permute-start | bytes 24584 | tf_op jit(solution)/shard_map/ppermute | solution.py:17
  148.0 10.5 %collective-permute-start.7 = (f32[2,1024]{1,0:T(2,128)S(1)}, f32[2,1024]{1,0:T(2,128)S(1)}, u32[]{:S(2)}, u32[]{:S(2)}) collective-permute-start(f32[2,1024]{1,0:T(2,128)S(1)} %get-tuple-element.54), channel_id=1, source_target_pairs={{0,8},{8,0},{16,24},{24,16},{32,40},{40,32},{48,56},{56,48},{64,72... | collective-permute-start | bytes 24584 | tf_op jit(solution)/shard_map/ppermute | solution.py:16

commit v9 on v8

--- a/solution.py
+++ b/solution.py
@@ -320,7 +320,8 @@
         out_specs=(vmem, vmem),
         scratch_shapes=[pltpu.VMEM((depth_cells, rows_all, width), f32)] * 4,
     )(ids, displacement, damage, modulus, toughness, lo_x, hi_x, load_all)
-    ends = [jnp.concatenate([a[:3], a[-3:]]) for a in (displacement, damage, modulus, toughness)]
+    late = lax.optimization_barrier((displacement, damage, modulus, toughness, lo_x))[:4]
+    ends = [jnp.concatenate([a[:3], a[-3:]]) for a in late]
     sides = []
     for first, got in ((True, got_a), (False, got_b)):
         sides.append(pl.pallas_call(

time: 160 us -> 165 us (1.031)
  the two profiles are of different devices: /device:TPU:22 before, /device:TPU:30 now
where the time goes in v9:
time: 165 us; the launch traced here: 164 us
  waiting for transfers between devices  73.7 us (45%)
  starting transfers between devices  43.7 us (26%)
  local copies, waits for them, and re-layouts  16.6 us (10%)
  Pallas kernels  16.4 us (10%)
  other arithmetic  13.1 us (8%)
    ppermute x1, waiting for transfers between devices, on_device(): got_b = lax.ppermute(jnp.where(even_z, lo_face, hi_face), 'depth', pairs_b)  42.1 us
    ppermute x3, waiting for transfers between devices, butterfly_sum(): part = part + lax.ppermute(part, axis, pairs)  20 us
    ppermute x2, starting transfers between devices, halo_swap(): got_b = lax.ppermute(jnp.where(even, lo_face, hi_face), axis, pairs_b)  16.2 us
    ppermute x2, waiting for transfers between devices, halo_swap(): got_b = lax.ppermute(jnp.where(even, lo_face, hi_face), axis, pairs_b)  11.5 us
    ppermute x1, starting transfers between devices, on_device(): lax.ppermute(jnp.where(even_z, hi_face, lo_face), 'depth', [(i, i ^ 1) fo...  11 us
    pallas_call x1, Pallas kernels, on_device(): pl.pallas_call(functools.partial(interior_kernel, total_depth, total_rows...  9.67 us
    ppermute x3, starting transfers between devices, butterfly_sum(): part = part + lax.ppermute(part, axis, pairs)  8.93 us
    pallas_call x2, Pallas kernels, on_device(): pl.pallas_call(functools.partial(side_kernel, total_depth, total_rows, de...  6.71 us
  transfers between devices with their start and end apart: 9, of which 6 were waited for; matrix products, arithmetic and copies ran while one was open for 5% of the time, Pallas kernels for 8%

profile of v9, /device:TPU:30, one launch (start us, length us, event | category | flops | bytes accessed | tf_op | source)
XLA Modules:
  0.0 164.0 jit_solution(13030543482911654184)
XLA Ops:
  0.0 0.9 convert_element_type.10
  0.9 1.3 fusion.41
  2.3 1.3 fusion.42
  3.8 1.4 slice_multiply_fusion.1
  5.4 0.8 fusion.47
  6.3 2.6 %concatenate.48 = f32[84,1024]{1,0:T(8,128)} concatenate(f32[32,1024]{1,0:T(8,128)S(1)} %reshape.59, f32[32,1024]{1,0:T(8,128)S(1)} %reshape.60, f32[16,1024]{1,0:T(8,128)S(1)} %get-tuple-element.69, f32[2,1024]{1,0:T(2,128)S(1)} %get-tuple-element.71, f32[2,1024]{1,0:T(2,128)S(1)} %get-tuple-element.64), dimensions={0} | concatenate | bytes 688128 | tf_op jit(solution)/shard_map/concatenate | solution.py:278
  8.9 2.0 %broadcast_select_fusion.5 = (f32[84,1024]{1,0:T(8,128)}, f32[84,1024]{1,0:T(8,128)}) fusion(f32[84,1024]{1,0:T(8,128)S(1)} %concatenate.47, f32[84,1024]{1,0:T(8,128)} %concatenate.48, pred[]{:T(512)S(6)} %eq.28), kind=kLoop, calls=%fused_computation.10 | loop fusion | flops 172032 | bytes 1376257 | tf_op jit(solution)/shard_map/jit(_where)/select_n | solution.py:17
  10.9 12.9 %collective-permute-start = (f32[84,1024]{1,0:T(8,128)}, f32[84,1024]{1,0:T(8,128)S(1)}, u32[]{:S(2)}, u32[]{:S(2)}) collective-permute-start(f32[84,1024]{1,0:T(8,128)} %get-tuple-element.45), channel_id=1, source_target_pairs={{8,16},{24,32},{40,48},{56,64},{72,80},{88,96},{104,112},{120,128}... | collective-permute-start | bytes 1032200 | tf_op jit(solution)/shard_map/ppermute | solution.py:17
  23.7 1.9 %collective-permute-start.1 = (f32[84,1024]{1,0:T(8,128)}, f32[84,1024]{1,0:T(8,128)}, u32[]{:S(2)}, u32[]{:S(2)}) collective-permute-start(f32[84,1024]{1,0:T(8,128)} %get-tuple-element.46), channel_id=1, source_target_pairs={{0,8},{8,0},{16,24},{24,16},{32,40},{40,32},{48,56},{56,48},{64,72... | collective-permute-start | bytes 1032200 | tf_op jit(solution)/shard_map/ppermute | solution.py:16
  27.8 4.3 %collective-permute-done = f32[84,1024]{1,0:T(8,128)S(1)} collective-permute-done((f32[84,1024]{1,0:T(8,128)}, f32[84,1024]{1,0:T(8,128)S(1)}, u32[]{:S(2)}, u32[]{:S(2)}) %collective-permute-start) | collective-permute-done | bytes 344096 | tf_op jit(solution)/shard_map/ppermute | solution.py:17
  32.1 1.0 broadcast_select_fusion.3
  36.7 2.8 %concatenate.55 = f32[84,1024]{1,0:T(8,128)S(1)} concatenate(f32[1,1024]{1,0:T(1,128)} %get-tuple-element.58, f32[16,1024]{1,0:T(8,128)S(1)} %copy-done.18, f32[1,1024]{1,0:T(1,128)} %get-tuple-element.54, f32[1,1024]{1,0:T(1,128)} %get-tuple-element.55, f32[16,1024]{1,0:T(8,128)S(1)} %copy-done.21, f32[1,1024]{1,0:T(1,128)} %get-tuple-element.51, f32[16,1024]{1,0:T(8,128)S(1)} %copy-done.19, ...), dimensions={0} | concatenate | bytes 688128 | tf_op jit(solution)/shard_map/concatenate | solution.py:301
  40.4 11.0 %collective-permute-start.2 = (f32[84,1024]{1,0:T(8,128)S(1)}, f32[84,1024]{1,0:T(8,128)S(1)}, u32[]{:S(2)}, u32[]{:S(2)}) collective-permute-start(f32[84,1024]{1,0:T(8,128)S(1)} %get-tuple-element.41), channel_id=1, source_target_pairs={{0,1},{1,0},{2,3},{3,2},{4,5},{5,4},{6,7},{7,6},{8,9},{9,8},{10,11... | collective-permute-start | bytes 1032200 | tf_op jit(solution)/shard_map/ppermute | solution.py:306
  51.4 3.8 %collective-permute-start.3 = (f32[84,1024]{1,0:T(8,128)S(1)}, f32[84,1024]{1,0:T(8,128)S(1)}, u32[]{:S(2)}, u32[]{:S(2)}) collective-permute-start(f32[84,1024]{1,0:T(8,128)S(1)} %get-tuple-element.42), channel_id=1, source_target_pairs={{1,2},{3,4},{5,6},{2,1},{4,3},{6,5},{9,10},{11,12},{13,14},{10,9},... | collective-permute-start | bytes 1032200 | tf_op jit(solution)/shard_map/ppermute | solution.py:308
  56.7 0.8 pad_maximum_fusion.1.dmg_ref
  57.5 0.8 pad_maximum_fusion.2.mod_ref
  58.3 9.7 %shard_map.82 = (f32[16,1024]{1,0:T(8,128)}, f32[4,32,1024]{2,1,0:T(8,128)}) custom-call(s32[3]{0:T(128)} %pad_add_fusion.ids_ref, f32[16,16,1024]{2,1,0:T(8,128)} %u_ref.1, f32[16,16,1024]{2,1,0:T(8,128)} %dmg_ref.1, f32[16,16,1024]{2,1,0:T(8,128)} %mod_ref.1, f32[16,16,1024]{2,1,0:T(8,128)} %tgh_ref.1, f32[84,1024]{1,0:T(8,128)} %copy-done, ...), custom_call_target="tpu_custom_call" | custom-call | tf_op jit(solution)/shard_map/pallas_call | solution.py:313
  68.0 1.0 fusion.37
  69.0 0.8 pad_maximum_fusion.3.tgh_ref
  69.8 42.1 %collective-permute-done.3.halo_ref = f32[84,1024]{1,0:T(8,128)S(1)} collective-permute-done((f32[84,1024]{1,0:T(8,128)S(1)}, f32[84,1024]{1,0:T(8,128)S(1)}, u32[]{:S(2)}, u32[]{:S(2)}) %collective-permute-start.3) | collective-permute-done | bytes 344096 | tf_op jit(solution)/shard_map/ppermute | solution.py:308
  112.7 3.4 %shard_map.84 = f32[16,1024]{1,0:T(8,128)} custom-call(s32[3]{0:T(128)} %pad_add_fusion.ids_ref, f32[6,16,1024]{2,1,0:T(8,128)} %pad_maximum_fusion.u_ref, f32[6,16,1024]{2,1,0:T(8,128)} %pad_maximum_fusion.1.dmg_ref, f32[6,16,1024]{2,1,0:T(8,128)} %pad_maximum_fusion.2.mod_ref, f32[6,16,1024]{2,1,0:T(8,128)} %pad_maximum_fusion.3.tgh_ref, ...), custom_call_target="tpu_custom_call" | custom-call | tf_op jit(solution)/shard_map/pallas_call | solution.py:327
  116.8 3.3 %shard_map.83 = f32[16,1024]{1,0:T(8,128)} custom-call(s32[3]{0:T(128)} %pad_add_fusion.ids_ref, f32[6,16,1024]{2,1,0:T(8,128)} %pad_maximum_fusion.u_ref, f32[6,16,1024]{2,1,0:T(8,128)} %pad_maximum_fusion.1.dmg_ref, f32[6,16,1024]{2,1,0:T(8,128)} %pad_maximum_fusion.2.mod_ref, f32[6,16,1024]{2,1,0:T(8,128)} %pad_maximum_fusion.3.tgh_ref, ...), custom_call_target="tpu_custom_call" | custom-call | tf_op jit(solution)/shard_map/pallas_call | solution.py:327
  120.2 0.9 add_multiply_fusion
  121.0 2.3 %collective-permute-start.4 = (f32[16,1024]{1,0:T(8,128)S(1)}, f32[16,1024]{1,0:T(8,128)S(1)}, u32[]{:S(2)}, u32[]{:S(2)}) collective-permute-start(f32[16,1024]{1,0:T(8,128)S(1)} %add_multiply_fusion), channel_id=1, source_target_pairs={{0,2},{1,3},{2,0},{3,1},{4,6},{5,7},{6,4},{7,5},{8,10},{9,11},{10,... | collective-permute-start | bytes 196616 | tf_op jit(solution)/shard_map/ppermute | solution.py:26
  123.4 3.8 %collective-permute-done.4 = f32[16,1024]{1,0:T(8,128)S(1)} collective-permute-done((f32[16,1024]{1,0:T(8,128)S(1)}, f32[16,1024]{1,0:T(8,128)S(1)}, u32[]{:S(2)}, u32[]{:S(2)}) %collective-permute-start.4) | collective-permute-done | bytes 65568 | tf_op jit(solution)/shard_map/ppermute | solution.py:26
  127.2 1.9 %collective-permute-start.5 = (f32[16,1024]{1,0:T(8,128)S(1)}, f32[16,1024]{1,0:T(8,128)S(1)}, u32[]{:S(2)}, u32[]{:S(2)}) collective-permute-start(f32[16,1024]{1,0:T(8,128)S(1)} %add.185), channel_id=1, source_target_pairs={{0,4},{1,5},{2,6},{3,7},{4,0},{5,1},{6,2},{7,3},{8,12},{9,13},{10,... | collective-permute-start | bytes 196616 | tf_op jit(solution)/shard_map/ppermute | solution.py:26
  129.2 5.7 %collective-permute-done.5 = f32[16,1024]{1,0:T(8,128)S(1)} collective-permute-done((f32[16,1024]{1,0:T(8,128)S(1)}, f32[16,1024]{1,0:T(8,128)S(1)}, u32[]{:S(2)}, u32[]{:S(2)}) %collective-permute-start.5) | collective-permute-done | bytes 65568 | tf_op jit(solution)/shard_map/ppermute | solution.py:26
  134.9 4.7 %collective-permute-start.6 = (f32[16,1024]{1,0:T(8,128)S(1)}, f32[16,1024]{1,0:T(8,128)S(1)}, u32[]{:S(2)}, u32[]{:S(2)}) collective-permute-start(f32[16,1024]{1,0:T(8,128)S(1)} %add.186), channel_id=1, source_target_pairs={{0,1},{1,0},{2,3},{3,2},{4,5},{5,4},{6,7},{7,6},{8,9},{9,8},{10,11... | collective-permute-start | bytes 196616 | tf_op jit(solution)/shard_map/ppermute | solution.py:26
  139.9 10.5 %collective-permute-done.6 = f32[16,1024]{1,0:T(8,128)S(1)} collective-permute-done((f32[16,1024]{1,0:T(8,128)S(1)}, f32[16,1024]{1,0:T(8,128)S(1)}, u32[]{:S(2)}, u32[]{:S(2)}) %collective-permute-start.6) | collective-permute-done | bytes 65568 | tf_op jit(solution)/shard_map/ppermute | solution.py:26
  150.5 3.3 %collective-permute-start.8 = (f32[2,1024]{1,0:T(2,128)S(1)}, f32[2,1024]{1,0:T(2,128)S(1)}, u32[]{:S(2)}, u32[]{:S(2)}) collective-permute-start(f32[2,1024]{1,0:T(2,128)S(1)} %get-tuple-element.61), channel_id=1, source_target_pairs={{8,16},{24,32},{40,48},{56,64},{72,80},{88,96},{104,112},{120,128}... | collective-permute-start | bytes 24584 | tf_op jit(solution)/shard_map/ppermute | solution.py:17
  153.8 1.9 %collective-permute-start.7 = (f32[2,1024]{1,0:T(2,128)S(1)}, f32[2,1024]{1,0:T(2,128)S(1)}, u32[]{:S(2)}, u32[]{:S(2)}) collective-permute-start(f32[2,1024]{1,0:T(2,128)S(1)} %get-tuple-element.62), channel_id=1, source_target_pairs={{0,8},{8,0},{16,24},{24,16},{32,40},{40,32},{48,56},{56,48},{64,72... | collective-permute-start | bytes 24584 | tf_op jit(solution)/shard_map/ppermute | solution.py:16
  155.8 7.2 %collective-permute-done.8 = f32[2,1024]{1,0:T(2,128)S(1)} collective-permute-done((f32[2,1024]{1,0:T(2,128)S(1)}, f32[2,1024]{1,0:T(2,128)S(1)}, u32[]{:S(2)}, u32[]{:S(2)}) %collective-permute-start.8) | collective-permute-done | bytes 8224 | tf_op jit(solution)/shard_map/ppermute | solution.py:17
  (99 shorter events, 11.3 us)
Async XLA Ops:
  0.0 3.8 %copy-start.2 = (f32[16,16,1024]{2,1,0:T(8,128)S(1)}, f32[16,16,1024]{2,1,0:T(8,128)}, u32[]{:S(2)}) copy-start(f32[16,16,1024]{2,1,0:T(8,128)} %dmg_ref.1) | copy-start | bytes 3145732
  0.9 4.5 %copy-start.8 = (f32[16,1024]{1,0:T(8,128)}, f32[16,1024]{1,0:T(8,128)S(1)}, u32[]{:S(2)}) copy-start(f32[16,1024]{1,0:T(8,128)S(1)} %convert_element_type.10) | copy-start | bytes 196612
  6.3 19.4 %copy-start.3 = (f32[16,16,1024]{2,1,0:T(8,128)S(1)}, f32[16,16,1024]{2,1,0:T(8,128)}, u32[]{:S(2)}) copy-start(f32[16,16,1024]{2,1,0:T(8,128)} %mod_ref.1) | copy-start | bytes 3145732
  8.9 18.1 %copy-start.4 = (f32[16,16,1024]{2,1,0:T(8,128)S(1)}, f32[16,16,1024]{2,1,0:T(8,128)}, u32[]{:S(2)}) copy-start(f32[16,16,1024]{2,1,0:T(8,128)} %u_ref.1) | copy-start | bytes 3145732
  10.9 21.2 %collective-permute-start = (f32[84,1024]{1,0:T(8,128)}, f32[84,1024]{1,0:T(8,128)S(1)}, u32[]{:S(2)}, u32[]{:S(2)}) collective-permute-start(f32[84,1024]{1,0:T(8,128)} %get-tuple-element.45), channel_id=1, source_target_pairs={{8,16},{24,32},{40,48},{56,64},{72,80},{88,96},{104,112},{120,128}... | collective-permute-start | bytes 1032200 | tf_op jit(solution)/shard_map/ppermute | solution.py:17
  23.7 8.3 %collective-permute-start.1 = (f32[84,1024]{1,0:T(8,128)}, f32[84,1024]{1,0:T(8,128)}, u32[]{:S(2)}, u32[]{:S(2)}) collective-permute-start(f32[84,1024]{1,0:T(8,128)} %get-tuple-element.46), channel_id=1, source_target_pairs={{0,8},{8,0},{16,24},{24,16},{32,40},{40,32},{48,56},{56,48},{64,72... | collective-permute-start | bytes 1032200 | tf_op jit(solution)/shard_map/ppermute | solution.py:16
  33.1 2.8 %copy-start = (f32[84,1024]{1,0:T(8,128)}, f32[84,1024]{1,0:T(8,128)S(1)}, u32[]{:S(2)}) copy-start(f32[84,1024]{1,0:T(8,128)S(1)} %get-tuple-element.43.xlo_ref) | copy-start | bytes 1032196
  35.8 3.7 %copy-start.12 = (f32[16,1024]{1,0:T(8,128)S(1)}, f32[16,1024]{1,0:T(8,128)}, u32[]{:S(2)}) copy-start(f32[16,1024]{1,0:T(8,128)} %get-tuple-element.18) | copy-start | bytes 196612
  35.8 3.7 %copy-start.13 = (f32[16,1024]{1,0:T(8,128)S(1)}, f32[16,1024]{1,0:T(8,128)}, u32[]{:S(2)}) copy-start(f32[16,1024]{1,0:T(8,128)} %get-tuple-element.24) | copy-start | bytes 196612
  35.8 3.7 %copy-start.14 = (f32[16,1024]{1,0:T(8,128)S(1)}, f32[16,1024]{1,0:T(8,128)}, u32[]{:S(2)}) copy-start(f32[16,1024]{1,0:T(8,128)} %get-tuple-element.73) | copy-start | bytes 196612
  35.8 3.7 %copy-start.15 = (f32[16,1024]{1,0:T(8,128)S(1)}, f32[16,1024]{1,0:T(8,128)}, u32[]{:S(2)}) copy-start(f32[16,1024]{1,0:T(8,128)} %get-tuple-element.74) | copy-start | bytes 196612
  35.8 3.7 %copy-start.20 = (f32[16,1024]{1,0:T(8,128)S(1)}, f32[16,1024]{1,0:T(8,128)}, u32[]{:S(2)}) copy-start(f32[16,1024]{1,0:T(8,128)} %get-tuple-element.20) | copy-start | bytes 196612
  35.9 3.7 %copy-start.25 = (f32[1,1024]{1,0:T(1,128)S(1)}, f32[1,1024]{1,0:T(1,128)}, u32[]{:S(2)}) copy-start(f32[1,1024]{1,0:T(1,128)} %get-tuple-element.52) | copy-start | bytes 12292
  35.9 3.7 %copy-start.26 = (f32[1,1024]{1,0:T(1,128)S(1)}, f32[1,1024]{1,0:T(1,128)}, u32[]{:S(2)}) copy-start(f32[1,1024]{1,0:T(1,128)} %get-tuple-element.53) | copy-start | bytes 12292
  35.9 3.7 %copy-start.27 = (f32[1,1024]{1,0:T(1,128)S(1)}, f32[1,1024]{1,0:T(1,128)}, u32[]{:S(2)}) copy-start(f32[1,1024]{1,0:T(1,128)} %get-tuple-element.56) | copy-start | bytes 12292
  35.9 3.7 %copy-start.28 = (f32[1,1024]{1,0:T(1,128)S(1)}, f32[1,1024]{1,0:T(1,128)}, u32[]{:S(2)}) copy-start(f32[1,1024]{1,0:T(1,128)} %get-tuple-element.57) | copy-start | bytes 12292
  39.6 15.6 %copy-start.5 = (f32[16,1024]{1,0:T(8,128)S(1)}, f32[16,1024]{1,0:T(8,128)}, u32[]{:S(2)}) copy-start(f32[16,1024]{1,0:T(8,128)} %param.12) | copy-start | bytes 196612
  39.6 15.6 %copy-start.9 = (f32[16,1024]{1,0:T(8,128)S(1)}, f32[16,1024]{1,0:T(8,128)}, u32[]{:S(2)}) copy-start(f32[16,1024]{1,0:T(8,128)} %copy-done.8) | copy-start | bytes 196612
  39.6 15.6 %copy-start.23 = (f32[2,1024]{1,0:T(2,128)S(1)}, f32[2,1024]{1,0:T(2,128)}, u32[]{:S(2)}) copy-start(f32[2,1024]{1,0:T(2,128)} %get-tuple-element.49) | copy-start | bytes 24580
  39.6 15.6 %copy-start.24 = (f32[2,1024]{1,0:T(2,128)S(1)}, f32[2,1024]{1,0:T(2,128)}, u32[]{:S(2)}) copy-start(f32[2,1024]{1,0:T(2,128)} %get-tuple-element.47) | copy-start | bytes 24580
  40.4 75.6 %collective-permute-start.2 = (f32[84,1024]{1,0:T(8,128)S(1)}, f32[84,1024]{1,0:T(8,128)S(1)}, u32[]{:S(2)}, u32[]{:S(2)}) collective-permute-start(f32[84,1024]{1,0:T(8,128)S(1)} %get-tuple-element.41), channel_id=1, source_target_pairs={{0,1},{1,0},{2,3},{3,2},{4,5},{5,4},{6,7},{7,6},{8,9},{9,8},{10,11... | collective-permute-start | bytes 1032200 | tf_op jit(solution)/shard_map/ppermute | solution.py:306
  51.4 60.5 %collective-permute-start.3 = (f32[84,1024]{1,0:T(8,128)S(1)}, f32[84,1024]{1,0:T(8,128)S(1)}, u32[]{:S(2)}, u32[]{:S(2)}) collective-permute-start(f32[84,1024]{1,0:T(8,128)S(1)} %get-tuple-element.42), channel_id=1, source_target_pairs={{1,2},{3,4},{5,6},{2,1},{4,3},{6,5},{9,10},{11,12},{13,14},{10,9},... | collective-permute-start | bytes 1032200 | tf_op jit(solution)/shard_map/ppermute | solution.py:308
  116.0 4.1 %copy-start.10 = (f32[16,1024]{1,0:T(8,128)S(1)}, f32[16,1024]{1,0:T(8,128)}, u32[]{:S(2)}) copy-start(f32[16,1024]{1,0:T(8,128)} %shard_map.84) | copy-start | bytes 196612
  116.0 4.1 %copy-start.22 = (f32[16,1024]{1,0:T(8,128)S(1)}, f32[16,1024]{1,0:T(8,128)}, u32[]{:S(2)}) copy-start(f32[16,1024]{1,0:T(8,128)} %get-tuple-element.11) | copy-start | bytes 196612
  116.0 23.6 %copy-start.29 = (f32[16]{0:T(128)S(1)}, f32[16]{0:T(128)}, u32[]{:S(2)}) copy-start(f32[16]{0:T(128)} %param.15) | copy-start | bytes 196
  116.0 23.6 %copy-start.30 = (s32[16]{0:T(128)S(1)}, s32[16]{0:T(128)}, u32[]{:S(2)}) copy-start(s32[16]{0:T(128)} %param.14) | copy-start | bytes 196
  116.1 34.4 %copy-start.11 = (s32[16,1024]{1,0:T(8,128)S(1)}, s32[16,1024]{1,0:T(8,128)}, u32[]{:S(2)}) copy-start(s32[16,1024]{1,0:T(8,128)} %param.13) | copy-start | bytes 196612
  121.0 6.2 %collective-permute-start.4 = (f32[16,1024]{1,0:T(8,128)S(1)}, f32[16,1024]{1,0:T(8,128)S(1)}, u32[]{:S(2)}, u32[]{:S(2)}) collective-permute-start(f32[16,1024]{1,0:T(8,128)S(1)} %add_multiply_fusion), channel_id=1, source_target_pairs={{0,2},{1,3},{2,0},{3,1},{4,6},{5,7},{6,4},{7,5},{8,10},{9,11},{10,... | collective-permute-start | bytes 196616 | tf_op jit(solution)/shard_map/ppermute | solution.py:26
  127.2 7.7 %collective-permute-start.5 = (f32[16,1024]{1,0:T(8,128)S(1)}, f32[16,1024]{1,0:T(8,128)S(1)}, u32[]{:S(2)}, u32[]{:S(2)}) collective-permute-start(f32[16,1024]{1,0:T(8,128)S(1)} %add.185), channel_id=1, source_target_pairs={{0,4},{1,5},{2,6},{3,7},{4,0},{5,1},{6,2},{7,3},{8,12},{9,13},{10,... | collective-permute-start | bytes 196616 | tf_op jit(solution)/shard_map/ppermute | solution.py:26
  134.9 15.6 %collective-permute-start.6 = (f32[16,1024]{1,0:T(8,128)S(1)}, f32[16,1024]{1,0:T(8,128)S(1)}, u32[]{:S(2)}, u32[]{:S(2)}) collective-permute-start(f32[16,1024]{1,0:T(8,128)S(1)} %add.186), channel_id=1, source_target_pairs={{0,1},{1,0},{2,3},{3,2},{4,5},{5,4},{6,7},{7,6},{8,9},{9,8},{10,11... | collective-permute-start | bytes 196616 | tf_op jit(solution)/shard_map/ppermute | solution.py:26
  150.5 12.5 %collective-permute-start.8 = (f32[2,1024]{1,0:T(2,128)S(1)}, f32[2,1024]{1,0:T(2,128)S(1)}, u32[]{:S(2)}, u32[]{:S(2)}) collective-permute-start(f32[2,1024]{1,0:T(2,128)S(1)} %get-tuple-element.61), channel_id=1, source_target_pairs={{8,16},{24,32},{40,48},{56,64},{72,80},{88,96},{104,112},{120,128}... | collective-permute-start | bytes 24584 | tf_op jit(solution)/shard_map/ppermute | solution.py:17
  153.8 9.2 %collective-permute-start.7 = (f32[2,1024]{1,0:T(2,128)S(1)}, f32[2,1024]{1,0:T(2,128)S(1)}, u32[]{:S(2)}, u32[]{:S(2)}) collective-permute-start(f32[2,1024]{1,0:T(2,128)S(1)} %get-tuple-element.62), channel_id=1, source_target_pairs={{0,8},{8,0},{16,24},{24,16},{32,40},{40,32},{48,56},{56,48},{64,72... | collective-permute-start | bytes 24584 | tf_op jit(solution)/shard_map/ppermute | solution.py:16
  (8 other events, 8.7 us)

commit v10 on v4

--- a/solution.py
+++ b/solution.py
@@ -185,9 +185,22 @@
     edge_ref[3] = m_s[depth_cells - 2]
 
 
-def boundary_kernel(total_depth, total_rows, ids_ref, u_ref, dmg_ref, mod_ref, tgh_ref, xlo_ref, xhi_ref, zlo_ref,
-                    zhi_ref, edge_ref, part_ref, load_ref, out_ref, u_s, c_s, d_s, m_s):
-    depth_cells, tile_cells, width = u_ref.shape
+class Ends:
+    def __init__(self, lo, hi, depth_cells):
+        self.lo, self.hi, self.depth_cells = lo, hi, depth_cells
+
+    def __getitem__(self, z):
+        return self.lo[z] if z < 4 else self.hi[z - self.depth_cells + 4]
+
+
+def boundary_kernel(total_depth, total_rows, depth_cells, ids_ref, u_lo, u_hi, d_lo, d_hi, mod_lo, mod_hi, tgh_lo,
+                    tgh_hi, xlo_ref, xhi_ref, zlo_ref, zhi_ref, edge_ref, part_ref, load_ref, out_ref, u_s, c_s, d_s,
+                    m_s):
+    u_ref = Ends(u_lo, u_hi, depth_cells)
+    dmg_ref = Ends(d_lo, d_hi, depth_cells)
+    mod_ref = Ends(mod_lo, mod_hi, depth_cells)
+    tgh_ref = Ends(tgh_lo, tgh_hi, depth_cells)
+    _, tile_cells, width = u_lo.shape
     rows_all = u_s.shape[1]
     own = slice(X0, X0 + tile_cells)
     wide = slice(X0 - 1, X0 + tile_cells + 1)
@@ -296,13 +309,17 @@
         out_specs=(vmem, vmem),
         scratch_shapes=[pltpu.VMEM((depth_cells, rows_all, width), f32)] * 4,
     )(ids, displacement, damage, modulus, toughness, lo_x, hi_x, load_all)
+    end_lo = pl.BlockSpec((4, tile_cells, width), lambda i: (0, 0, 0))
+    end_hi = pl.BlockSpec((4, tile_cells, width), lambda i: (depth_cells // 4 - 1, 0, 0))
     partial_open = pl.pallas_call(
-        functools.partial(boundary_kernel, total_depth, total_rows),
+        functools.partial(boundary_kernel, total_depth, total_rows, depth_cells),
         out_shape=jax.ShapeDtypeStruct((tile_cells, width), f32),
-        in_specs=[smem] + [vmem] * 11,
+        grid=(1,),
+        in_specs=[smem] + [end_lo, end_hi] * 4 + [vmem] * 7,
         out_specs=vmem,
         scratch_shapes=[pltpu.VMEM((8, rows_all, width), f32)] * 4,
-    )(ids, displacement, damage, modulus, toughness, lo_x, hi_x, lo_z, hi_z, edge, part_in, load_all)
+    )(ids, displacement, displacement, damage, damage, modulus, modulus, toughness, toughness, lo_x, hi_x, lo_z, hi_z,
+      edge, part_in, load_all)
 
     aperture = 0.5 + butterfly_sum(partial_open, "depth")
     trans = mask_f * aperture**3

time: 150 us -> 149 us (level)
  transfers between devices with their start and end apart: 9 -> 9, of which waited for: 7 -> 7; matrix products, arithmetic and copies ran while one was open for 2% -> 3% of each run, Pallas kernels for 6% -> 7%
where the time goes in v10:
time: 149 us
  waiting for transfers between devices  78.4 us (53%)
  starting transfers between devices  42.9 us (29%)
  Pallas kernels  14 us (9%)
  other arithmetic  7.54 us (5%)
  local copies, waits for them, and re-layouts  5.44 us (4%)
    ppermute x3, waiting for transfers between devices, halo_swap(): got_b = lax.ppermute(jnp.where(even, lo_face, hi_face), axis, pairs_b)  39 us
    ppermute x3, waiting for transfers between devices, butterfly_sum(): part = part + lax.ppermute(part, axis, pairs)  20.5 us
    ppermute x3, starting transfers between devices, halo_swap(): got_b = lax.ppermute(jnp.where(even, lo_face, hi_face), axis, pairs_b)  19.7 us
    ppermute x3, waiting for transfers between devices, halo_swap(): got_a = lax.ppermute(jnp.where(even, hi_face, lo_face), axis, pairs_a)  18.9 us
    ppermute x3, starting transfers between devices, halo_swap(): got_a = lax.ppermute(jnp.where(even, hi_face, lo_face), axis, pairs_a)  14.9 us
    pallas_call x1, Pallas kernels, on_device(): pl.pallas_call(functools.partial(interior_kernel, total_depth, total_rows...  9.67 us
    ppermute x3, starting transfers between devices, butterfly_sum(): part = part + lax.ppermute(part, axis, pairs)  8.31 us
    pallas_call x1, Pallas kernels, on_device(): pl.pallas_call(functools.partial(boundary_kernel, total_depth, total_rows...  4.35 us
  transfers between devices with their start and end apart: 9, of which 7 were waited for; matrix products, arithmetic and copies ran while one was open for 3% of the time, Pallas kernels for 7%

profile of v10, /device:TPU:30, one launch (start us, length us, event | category | flops | bytes accessed | tf_op | source)
XLA Modules:
  0.0 148.7 jit_solution(1234824381129343053)
XLA Ops:
  0.0 1.4 fusion.38
  1.5 1.3 fusion.37
  2.8 1.5 slice_multiply_fusion.1
  4.9 12.9 %collective-permute-start = (f32[84,1024]{1,0:T(8,128)S(1)}, f32[84,1024]{1,0:T(8,128)S(1)}, u32[]{:S(2)}, u32[]{:S(2)}) collective-permute-start(f32[84,1024]{1,0:T(8,128)S(1)} %get-tuple-element.33), channel_id=1, source_target_pairs={{8,16},{24,32},{40,48},{56,64},{72,80},{88,96},{104,112},{120,128}... | collective-permute-start | bytes 1032200 | tf_op jit(solution)/shard_map/ppermute | solution.py:17
  17.8 1.9 %collective-permute-start.1 = (f32[84,1024]{1,0:T(8,128)S(1)}, f32[84,1024]{1,0:T(8,128)S(1)}, u32[]{:S(2)}, u32[]{:S(2)}) collective-permute-start(f32[84,1024]{1,0:T(8,128)S(1)} %get-tuple-element.34), channel_id=1, source_target_pairs={{0,8},{8,0},{16,24},{24,16},{32,40},{40,32},{48,56},{56,48},{64,72... | collective-permute-start | bytes 1032200 | tf_op jit(solution)/shard_map/ppermute | solution.py:16
  19.7 0.9 bitcast_multiply_fusion
  20.6 0.7 pad_add_fusion.ids_ref
  21.3 1.0 slice_bitcast_fusion
  22.3 3.6 %collective-permute-done = f32[84,1024]{1,0:T(8,128)S(1)} collective-permute-done((f32[84,1024]{1,0:T(8,128)S(1)}, f32[84,1024]{1,0:T(8,128)S(1)}, u32[]{:S(2)}, u32[]{:S(2)}) %collective-permute-start) | collective-permute-done | bytes 344096 | tf_op jit(solution)/shard_map/ppermute | solution.py:17
  26.0 0.7 concatenate.38
  26.8 0.7 concatenate.37
  27.6 11.1 %collective-permute-start.3 = (f32[84,1024]{1,0:T(8,128)S(1)}, f32[84,1024]{1,0:T(8,128)S(1)}, u32[]{:S(2)}, u32[]{:S(2)}) collective-permute-start(f32[84,1024]{1,0:T(8,128)S(1)} %get-tuple-element.29), channel_id=1, source_target_pairs={{0,1},{1,0},{2,3},{3,2},{4,5},{5,4},{6,7},{7,6},{8,9},{9,8},{10,11... | collective-permute-start | bytes 1032200 | tf_op jit(solution)/shard_map/ppermute | solution.py:16
  38.7 3.7 %collective-permute-start.2 = (f32[84,1024]{1,0:T(8,128)S(1)}, f32[84,1024]{1,0:T(8,128)S(1)}, u32[]{:S(2)}, u32[]{:S(2)}) collective-permute-start(f32[84,1024]{1,0:T(8,128)S(1)} %get-tuple-element.30), channel_id=1, source_target_pairs={{1,2},{3,4},{5,6},{2,1},{4,3},{6,5},{9,10},{11,12},{13,14},{10,9},... | collective-permute-start | bytes 1032200 | tf_op jit(solution)/shard_map/ppermute | solution.py:17
  42.5 0.7 pad.15.load_ref
  43.1 9.7 %shard_map.82 = (f32[16,1024]{1,0:T(8,128)}, f32[4,32,1024]{2,1,0:T(8,128)}) custom-call(s32[2]{0:T(128)} %pad_add_fusion.ids_ref, f32[16,16,1024]{2,1,0:T(8,128)} %u_hi.1, f32[16,16,1024]{2,1,0:T(8,128)} %d_hi.1, f32[16,16,1024]{2,1,0:T(8,128)} %mod_hi.1, f32[16,16,1024]{2,1,0:T(8,128)} %tgh_hi.1, f32[84,1024]{1,0:T(8,128)} %copy-done.1, ...), custom_call_target="tpu_custom_call" | custom-call | tf_op jit(solution)/shard_map/pallas_call | solution.py:302
  52.8 18.9 %collective-permute-done.3 = f32[84,1024]{1,0:T(8,128)S(1)} collective-permute-done((f32[84,1024]{1,0:T(8,128)S(1)}, f32[84,1024]{1,0:T(8,128)S(1)}, u32[]{:S(2)}, u32[]{:S(2)}) %collective-permute-start.3) | collective-permute-done | bytes 344096 | tf_op jit(solution)/shard_map/ppermute | solution.py:16
  71.7 28.1 %collective-permute-done.2 = f32[84,1024]{1,0:T(8,128)S(1)} collective-permute-done((f32[84,1024]{1,0:T(8,128)S(1)}, f32[84,1024]{1,0:T(8,128)S(1)}, u32[]{:S(2)}, u32[]{:S(2)}) %collective-permute-start.2) | collective-permute-done | bytes 344096 | tf_op jit(solution)/shard_map/ppermute | solution.py:17
  99.8 0.9 broadcast_select_fusion
  100.7 4.4 %shard_map.83 = f32[16,1024]{1,0:T(8,128)} custom-call(s32[2]{0:T(128)} %pad_add_fusion.ids_ref, f32[16,16,1024]{2,1,0:T(8,128)} %u_hi.1, f32[16,16,1024]{2,1,0:T(8,128)} %u_hi.1, f32[16,16,1024]{2,1,0:T(8,128)} %d_hi.1, f32[16,16,1024]{2,1,0:T(8,128)} %d_hi.1, f32[16,16,1024]{2,1,0:T(8,128)} %mod_hi.1, f32[16,16,1024]{2,1,0:T(8,128)} %mod_hi.1, ...), custom_call_target="tpu_custom_call" | custom-call | tf_op jit(solution)/shard_map/pallas_call | solution.py:314
  105.1 2.3 %collective-permute-start.4 = (f32[16,1024]{1,0:T(8,128)}, f32[16,1024]{1,0:T(8,128)S(1)}, u32[]{:S(2)}, u32[]{:S(2)}) collective-permute-start(f32[16,1024]{1,0:T(8,128)} %shard_map.83), channel_id=1, source_target_pairs={{0,2},{1,3},{2,0},{3,1},{4,6},{5,7},{6,4},{7,5},{8,10},{9,11},{10,... | collective-permute-start | bytes 196616 | tf_op jit(solution)/shard_map/ppermute | solution.py:26
  107.4 4.0 %collective-permute-done.4 = f32[16,1024]{1,0:T(8,128)S(1)} collective-permute-done((f32[16,1024]{1,0:T(8,128)}, f32[16,1024]{1,0:T(8,128)S(1)}, u32[]{:S(2)}, u32[]{:S(2)}) %collective-permute-start.4) | collective-permute-done | bytes 65568 | tf_op jit(solution)/shard_map/ppermute | solution.py:26
  111.4 0.8 add.176
  112.3 1.9 %collective-permute-start.5 = (f32[16,1024]{1,0:T(8,128)S(1)}, f32[16,1024]{1,0:T(8,128)S(1)}, u32[]{:S(2)}, u32[]{:S(2)}) collective-permute-start(f32[16,1024]{1,0:T(8,128)S(1)} %add.176), channel_id=1, source_target_pairs={{0,4},{1,5},{2,6},{3,7},{4,0},{5,1},{6,2},{7,3},{8,12},{9,13},{10,... | collective-permute-start | bytes 196616 | tf_op jit(solution)/shard_map/ppermute | solution.py:26
  114.3 5.7 %collective-permute-done.5 = f32[16,1024]{1,0:T(8,128)S(1)} collective-permute-done((f32[16,1024]{1,0:T(8,128)S(1)}, f32[16,1024]{1,0:T(8,128)S(1)}, u32[]{:S(2)}, u32[]{:S(2)}) %collective-permute-start.5) | collective-permute-done | bytes 65568 | tf_op jit(solution)/shard_map/ppermute | solution.py:26
  120.0 4.0 %collective-permute-start.6 = (f32[16,1024]{1,0:T(8,128)S(1)}, f32[16,1024]{1,0:T(8,128)S(1)}, u32[]{:S(2)}, u32[]{:S(2)}) collective-permute-start(f32[16,1024]{1,0:T(8,128)S(1)} %add.177), channel_id=1, source_target_pairs={{0,1},{1,0},{2,3},{3,2},{4,5},{5,4},{6,7},{7,6},{8,9},{9,8},{10,11... | collective-permute-start | bytes 196616 | tf_op jit(solution)/shard_map/ppermute | solution.py:26
  124.0 0.3 select_reduce_fusion
  124.3 10.9 %collective-permute-done.6 = f32[16,1024]{1,0:T(8,128)S(1)} collective-permute-done((f32[16,1024]{1,0:T(8,128)S(1)}, f32[16,1024]{1,0:T(8,128)S(1)}, u32[]{:S(2)}, u32[]{:S(2)}) %collective-permute-start.6) | collective-permute-done | bytes 65568 | tf_op jit(solution)/shard_map/ppermute | solution.py:26
  135.3 3.2 %collective-permute-start.8 = (f32[2,1024]{1,0:T(2,128)S(1)}, f32[2,1024]{1,0:T(2,128)S(1)}, u32[]{:S(2)}, u32[]{:S(2)}) collective-permute-start(f32[2,1024]{1,0:T(2,128)S(1)} %get-tuple-element.49), channel_id=1, source_target_pairs={{8,16},{24,32},{40,48},{56,64},{72,80},{88,96},{104,112},{120,128}... | collective-permute-start | bytes 24584 | tf_op jit(solution)/shard_map/ppermute | solution.py:17
  138.4 1.9 %collective-permute-start.7 = (f32[2,1024]{1,0:T(2,128)S(1)}, f32[2,1024]{1,0:T(2,128)S(1)}, u32[]{:S(2)}, u32[]{:S(2)}) collective-permute-start(f32[2,1024]{1,0:T(2,128)S(1)} %get-tuple-element.50), channel_id=1, source_target_pairs={{0,8},{8,0},{16,24},{24,16},{32,40},{40,32},{48,56},{56,48},{64,72... | collective-permute-start | bytes 24584 | tf_op jit(solution)/shard_map/ppermute | solution.py:16
  140.4 7.3 %collective-permute-done.8 = f32[2,1024]{1,0:T(2,128)S(1)} collective-permute-done((f32[2,1024]{1,0:T(2,128)S(1)}, f32[2,1024]{1,0:T(2,128)S(1)}, u32[]{:S(2)}, u32[]{:S(2)}) %collective-permute-start.8) | collective-permute-done | bytes 8224 | tf_op jit(solution)/shard_map/ppermute | solution.py:17
  147.8 0.2 broadcast_multiply_fusion
  148.0 0.8 fusion.33
  (42 shorter events, 1.0 us)
Async XLA Ops:
  0.0 2.8 %copy-start = (f32[16,16,1024]{2,1,0:T(8,128)S(1)}, f32[16,16,1024]{2,1,0:T(8,128)}, u32[]{:S(2)}) copy-start(f32[16,16,1024]{2,1,0:T(8,128)} %d_hi.1) | copy-start | bytes 3145732
  0.0 4.4 %copy-start.4 = (s32[16,1024]{1,0:T(8,128)S(1)}, s32[16,1024]{1,0:T(8,128)}, u32[]{:S(2)}) copy-start(s32[16,1024]{1,0:T(8,128)} %param.13) | copy-start | bytes 196612
  2.8 1.9 %copy-start.3 = (f32[16,1024]{1,0:T(8,128)S(1)}, f32[16,1024]{1,0:T(8,128)}, u32[]{:S(2)}) copy-start(f32[16,1024]{1,0:T(8,128)} %param.12) | copy-start | bytes 196612
  4.9 21.0 %collective-permute-start = (f32[84,1024]{1,0:T(8,128)S(1)}, f32[84,1024]{1,0:T(8,128)S(1)}, u32[]{:S(2)}, u32[]{:S(2)}) collective-permute-start(f32[84,1024]{1,0:T(8,128)S(1)} %get-tuple-element.33), channel_id=1, source_target_pairs={{8,16},{24,32},{40,48},{56,64},{72,80},{88,96},{104,112},{120,128}... | collective-permute-start | bytes 1032200 | tf_op jit(solution)/shard_map/ppermute | solution.py:17
  17.8 8.1 %collective-permute-start.1 = (f32[84,1024]{1,0:T(8,128)S(1)}, f32[84,1024]{1,0:T(8,128)S(1)}, u32[]{:S(2)}, u32[]{:S(2)}) collective-permute-start(f32[84,1024]{1,0:T(8,128)S(1)} %get-tuple-element.34), channel_id=1, source_target_pairs={{0,8},{8,0},{16,24},{24,16},{32,40},{40,32},{48,56},{56,48},{64,72... | collective-permute-start | bytes 1032200 | tf_op jit(solution)/shard_map/ppermute | solution.py:16
  26.0 1.7 %copy-start.2 = (f32[84,1024]{1,0:T(8,128)}, f32[84,1024]{1,0:T(8,128)S(1)}, u32[]{:S(2)}) copy-start(f32[84,1024]{1,0:T(8,128)S(1)} %get-tuple-element.32.xhi_ref) | copy-start | bytes 1032196
  26.0 16.4 %copy-start.1 = (f32[84,1024]{1,0:T(8,128)}, f32[84,1024]{1,0:T(8,128)S(1)}, u32[]{:S(2)}) copy-start(f32[84,1024]{1,0:T(8,128)S(1)} %get-tuple-element.31.xlo_ref) | copy-start | bytes 1032196
  27.6 44.1 %collective-permute-start.3 = (f32[84,1024]{1,0:T(8,128)S(1)}, f32[84,1024]{1,0:T(8,128)S(1)}, u32[]{:S(2)}, u32[]{:S(2)}) collective-permute-start(f32[84,1024]{1,0:T(8,128)S(1)} %get-tuple-element.29), channel_id=1, source_target_pairs={{0,1},{1,0},{2,3},{3,2},{4,5},{5,4},{6,7},{7,6},{8,9},{9,8},{10,11... | collective-permute-start | bytes 1032200 | tf_op jit(solution)/shard_map/ppermute | solution.py:16
  38.7 61.1 %collective-permute-start.2 = (f32[84,1024]{1,0:T(8,128)S(1)}, f32[84,1024]{1,0:T(8,128)S(1)}, u32[]{:S(2)}, u32[]{:S(2)}) collective-permute-start(f32[84,1024]{1,0:T(8,128)S(1)} %get-tuple-element.30), channel_id=1, source_target_pairs={{1,2},{3,4},{5,6},{2,1},{4,3},{6,5},{9,10},{11,12},{13,14},{10,9},... | collective-permute-start | bytes 1032200 | tf_op jit(solution)/shard_map/ppermute | solution.py:17
  100.7 23.3 %copy-start.5 = (f32[16]{0:T(128)S(1)}, f32[16]{0:T(128)}, u32[]{:S(2)}) copy-start(f32[16]{0:T(128)} %param.15) | copy-start | bytes 196
  100.7 23.3 %copy-start.6 = (s32[16]{0:T(128)S(1)}, s32[16]{0:T(128)}, u32[]{:S(2)}) copy-start(s32[16]{0:T(128)} %param.14) | copy-start | bytes 196
  105.1 6.4 %collective-permute-start.4 = (f32[16,1024]{1,0:T(8,128)}, f32[16,1024]{1,0:T(8,128)S(1)}, u32[]{:S(2)}, u32[]{:S(2)}) collective-permute-start(f32[16,1024]{1,0:T(8,128)} %shard_map.83), channel_id=1, source_target_pairs={{0,2},{1,3},{2,0},{3,1},{4,6},{5,7},{6,4},{7,5},{8,10},{9,11},{10,... | collective-permute-start | bytes 196616 | tf_op jit(solution)/shard_map/ppermute | solution.py:26
  112.3 7.7 %collective-permute-start.5 = (f32[16,1024]{1,0:T(8,128)S(1)}, f32[16,1024]{1,0:T(8,128)S(1)}, u32[]{:S(2)}, u32[]{:S(2)}) collective-permute-start(f32[16,1024]{1,0:T(8,128)S(1)} %add.176), channel_id=1, source_target_pairs={{0,4},{1,5},{2,6},{3,7},{4,0},{5,1},{6,2},{7,3},{8,12},{9,13},{10,... | collective-permute-start | bytes 196616 | tf_op jit(solution)/shard_map/ppermute | solution.py:26
  120.0 15.3 %collective-permute-start.6 = (f32[16,1024]{1,0:T(8,128)S(1)}, f32[16,1024]{1,0:T(8,128)S(1)}, u32[]{:S(2)}, u32[]{:S(2)}) collective-permute-start(f32[16,1024]{1,0:T(8,128)S(1)} %add.177), channel_id=1, source_target_pairs={{0,1},{1,0},{2,3},{3,2},{4,5},{5,4},{6,7},{7,6},{8,9},{9,8},{10,11... | collective-permute-start | bytes 196616 | tf_op jit(solution)/shard_map/ppermute | solution.py:26
  135.3 12.5 %collective-permute-start.8 = (f32[2,1024]{1,0:T(2,128)S(1)}, f32[2,1024]{1,0:T(2,128)S(1)}, u32[]{:S(2)}, u32[]{:S(2)}) collective-permute-start(f32[2,1024]{1,0:T(2,128)S(1)} %get-tuple-element.49), channel_id=1, source_target_pairs={{8,16},{24,32},{40,48},{56,64},{72,80},{88,96},{104,112},{120,128}... | collective-permute-start | bytes 24584 | tf_op jit(solution)/shard_map/ppermute | solution.py:17
  138.4 9.3 %collective-permute-start.7 = (f32[2,1024]{1,0:T(2,128)S(1)}, f32[2,1024]{1,0:T(2,128)S(1)}, u32[]{:S(2)}, u32[]{:S(2)}) collective-permute-start(f32[2,1024]{1,0:T(2,128)S(1)} %get-tuple-element.50), channel_id=1, source_target_pairs={{0,8},{8,0},{16,24},{24,16},{32,40},{40,32},{48,56},{56,48},{64,72... | collective-permute-start | bytes 24584 | tf_op jit(solution)/shard_map/ppermute | solution.py:16

commit v11 on v10

--- a/solution.py
+++ b/solution.py
@@ -183,6 +183,22 @@
     edge_ref[1] = m_s[2]
     edge_ref[2] = m_s[depth_cells - 3]
     edge_ref[3] = m_s[depth_cells - 2]
+
+
+def face_kernel(u_lo, u_hi, d_lo, d_hi, m_lo, m_hi, p_ref, k_ref, lo_out, hi_out):
+    depth_cells = u_lo.shape[0]
+    tile_cells = p_ref.shape[0]
+    dz = 4 * depth_cells
+    for z in range(depth_cells):
+        for out, u_b, d_b, m_b, rows, edge in ((lo_out, u_lo, d_lo, m_lo, slice(0, 2), 0), (hi_out, u_hi, d_hi, m_hi, slice(6, 8), 7)):
+            out[2 * z:2 * z + 2] = u_b[z, rows]
+            dk = d_b[z, rows]
+            out[2 * depth_cells + 2 * z:2 * depth_cells + 2 * z + 2] = ((1.0 - dk) ** 2 + 0.001) * m_b[z, rows]
+            out[dz + z:dz + z + 1] = d_b[z, edge:edge + 1]
+    lo_out[dz + depth_cells:dz + depth_cells + 2] = p_ref[0:2]
+    lo_out[dz + depth_cells + 2:dz + depth_cells + 4] = k_ref[0:2].astype(jnp.float32)
+    hi_out[dz + depth_cells:dz + depth_cells + 2] = p_ref[tile_cells - 2:tile_cells]
+    hi_out[dz + depth_cells + 2:dz + depth_cells + 4] = k_ref[tile_cells - 2:tile_cells].astype(jnp.float32)
 
 
 class Ends:
@@ -268,18 +284,20 @@
     def stiff_of(dmg, mod):
         return ((1.0 - dmg) ** 2 + 0.001) * mod
 
-    def tile_face(rows, edge):
-        return jnp.concatenate(
-            [
-                displacement[:, rows].reshape(-1, width),
-                stiff_of(damage[:, rows], modulus[:, rows]).reshape(-1, width),
-                damage[:, edge],
-                pressure[rows],
-                mask_f[rows],
-            ]
-        )
-
-    lo_x, hi_x = halo_swap(tile_face(slice(0, 2), 0), tile_face(slice(tile_cells - 2, tile_cells), tile_cells - 1), "tile")
+    vmem = pl.BlockSpec(memory_space=pltpu.VMEM)
+    smem = pl.BlockSpec(memory_space=pltpu.SMEM)
+    f32 = jnp.float32
+    rows_lo = pl.BlockSpec((depth_cells, 8, width), lambda i: (0, 0, 0))
+    rows_hi = pl.BlockSpec((depth_cells, 8, width), lambda i: (0, tile_cells // 8 - 1, 0))
+    face_rows = 5 * depth_cells + 4
+    face_lo, face_hi = pl.pallas_call(
+        face_kernel,
+        out_shape=(jax.ShapeDtypeStruct((face_rows, width), f32),) * 2,
+        grid=(1,),
+        in_specs=[rows_lo, rows_hi] * 3 + [vmem, vmem],
+        out_specs=(vmem, vmem),
+    )(displacement, displacement, damage, damage, modulus, modulus, pressure, crack_mask)
+    lo_x, hi_x = halo_swap(face_lo, face_hi, "tile")
     dz = 4 * depth_cells
     p_ext = jnp.concatenate([lo_x[dz + depth_cells:dz + depth_cells + 2], pressure, hi_x[dz + depth_cells:dz + depth_cells + 2]])
     m_ext = jnp.concatenate([lo_x[dz + depth_cells + 2:], mask_f, hi_x[dz + depth_cells + 2:]])

time: 149 us -> 149 us (level)
  local copies, waits for them, and re-layouts: 5.44 us -> 2.22 us
  Pallas kernels: 14 us -> 17.1 us
    pallas_call x0 -> x1, Pallas kernels: none -> 3.08 us  [on_device(): pl.pallas_call(face_kernel, out_shape=(jax.ShapeDtypeStruct((face_rows, w...]
    slice x5 -> x0, local copies, waits for them, and re-layouts: 2.73 us -> none  [the longest x1 1.39 us: tile_face(): displacement[:, rows].reshape(-1, width)]
where the time goes in v11:
time: 149 us; the launch traced here: 148 us
  waiting for transfers between devices  78.6 us (53%)
  starting transfers between devices  42.6 us (29%)
  Pallas kernels  17.1 us (11%)
  other arithmetic  7.28 us (5%)
  local copies, waits for them, and re-layouts  2.22 us (1%)
    ppermute x3, waiting for transfers between devices, halo_swap(): got_b = lax.ppermute(jnp.where(even, lo_face, hi_face), axis, pairs_b)  39.1 us
    ppermute x3, waiting for transfers between devices, butterfly_sum(): part = part + lax.ppermute(part, axis, pairs)  20.5 us
    ppermute x3, starting transfers between devices, halo_swap(): got_b = lax.ppermute(jnp.where(even, lo_face, hi_face), axis, pairs_b)  19.5 us
    ppermute x3, waiting for transfers between devices, halo_swap(): got_a = lax.ppermute(jnp.where(even, hi_face, lo_face), axis, pairs_a)  19 us
    ppermute x3, starting transfers between devices, halo_swap(): got_a = lax.ppermute(jnp.where(even, hi_face, lo_face), axis, pairs_a)  14.9 us
    pallas_call x1, Pallas kernels, on_device(): pl.pallas_call(functools.partial(interior_kernel, total_depth, total_rows...  9.67 us
    ppermute x3, starting transfers between devices, butterfly_sum(): part = part + lax.ppermute(part, axis, pairs)  8.26 us
    pallas_call x1, Pallas kernels, on_device(): pl.pallas_call(functools.partial(boundary_kernel, total_depth, total_rows...  4.35 us
  transfers between devices with their start and end apart: 9, of which 7 were waited for; matrix products, arithmetic and copies ran while one was open for 3% of the time, Pallas kernels for 7%

profile of v11, /device:TPU:30, one launch (start us, length us, event | category | flops | bytes accessed | tf_op | source)
XLA Modules:
  0.0 148.1 jit_solution(10726855500877748950)
XLA Ops:
  0.0 3.1 %shard_map.82 = (f32[84,1024]{1,0:T(8,128)}, f32[84,1024]{1,0:T(8,128)}) custom-call(f32[16,16,1024]{2,1,0:T(8,128)} %u_hi.3, f32[16,16,1024]{2,1,0:T(8,128)} %u_hi.3, f32[16,16,1024]{2,1,0:T(8,128)} %d_hi.3, f32[16,16,1024]{2,1,0:T(8,128)} %d_hi.3, f32[16,16,1024]{2,1,0:T(8,128)} %mod_hi.1, f32[16,16,1024]{2,1,0:T(8,128)} %mod_hi.1, f32[16,1024]{1,0:T(8,128)} %p_ref.1, ...), custom_call_target="tpu_custom_call" | custom-call | tf_op jit(solution)/shard_map/pallas_call | solution.py:293
  3.1 1.2 broadcast_select_fusion.7
  4.3 12.9 %collective-permute-start = (f32[84,1024]{1,0:T(8,128)S(1)}, f32[84,1024]{1,0:T(8,128)S(1)}, u32[]{:S(2)}, u32[]{:S(2)}) collective-permute-start(f32[84,1024]{1,0:T(8,128)S(1)} %get-tuple-element.29), channel_id=1, source_target_pairs={{8,16},{24,32},{40,48},{56,64},{72,80},{88,96},{104,112},{120,128}... | collective-permute-start | bytes 1032200 | tf_op jit(solution)/shard_map/ppermute | solution.py:17
  17.1 1.9 %collective-permute-start.1 = (f32[84,1024]{1,0:T(8,128)S(1)}, f32[84,1024]{1,0:T(8,128)S(1)}, u32[]{:S(2)}, u32[]{:S(2)}) collective-permute-start(f32[84,1024]{1,0:T(8,128)S(1)} %get-tuple-element.30), channel_id=1, source_target_pairs={{0,8},{8,0},{16,24},{24,16},{32,40},{40,32},{48,56},{56,48},{64,72... | collective-permute-start | bytes 1032200 | tf_op jit(solution)/shard_map/ppermute | solution.py:16
  19.1 1.0 bitcast_multiply_fusion
  20.1 0.6 pad_add_fusion.ids_ref
  20.7 1.2 multiply_bitcast_fusion
  21.8 3.4 %collective-permute-done = f32[84,1024]{1,0:T(8,128)S(1)} collective-permute-done((f32[84,1024]{1,0:T(8,128)S(1)}, f32[84,1024]{1,0:T(8,128)S(1)}, u32[]{:S(2)}, u32[]{:S(2)}) %collective-permute-start) | collective-permute-done | bytes 344096 | tf_op jit(solution)/shard_map/ppermute | solution.py:17
  25.4 0.7 concatenate.30
  26.2 0.7 concatenate.29
  27.0 11.1 %collective-permute-start.3 = (f32[84,1024]{1,0:T(8,128)S(1)}, f32[84,1024]{1,0:T(8,128)S(1)}, u32[]{:S(2)}, u32[]{:S(2)}) collective-permute-start(f32[84,1024]{1,0:T(8,128)S(1)} %get-tuple-element.25), channel_id=1, source_target_pairs={{0,1},{1,0},{2,3},{3,2},{4,5},{5,4},{6,7},{7,6},{8,9},{9,8},{10,11... | collective-permute-start | bytes 1032200 | tf_op jit(solution)/shard_map/ppermute | solution.py:16
  38.1 3.7 %collective-permute-start.2 = (f32[84,1024]{1,0:T(8,128)S(1)}, f32[84,1024]{1,0:T(8,128)S(1)}, u32[]{:S(2)}, u32[]{:S(2)}) collective-permute-start(f32[84,1024]{1,0:T(8,128)S(1)} %get-tuple-element.26), channel_id=1, source_target_pairs={{1,2},{3,4},{5,6},{2,1},{4,3},{6,5},{9,10},{11,12},{13,14},{10,9},... | collective-permute-start | bytes 1032200 | tf_op jit(solution)/shard_map/ppermute | solution.py:17
  41.9 0.7 pad.15.load_ref
  42.5 9.7 %shard_map.83 = (f32[16,1024]{1,0:T(8,128)}, f32[4,32,1024]{2,1,0:T(8,128)}) custom-call(s32[2]{0:T(128)} %pad_add_fusion.ids_ref, f32[16,16,1024]{2,1,0:T(8,128)} %u_hi.3, f32[16,16,1024]{2,1,0:T(8,128)} %d_hi.3, f32[16,16,1024]{2,1,0:T(8,128)} %mod_hi.1, f32[16,16,1024]{2,1,0:T(8,128)} %tgh_hi.1, f32[84,1024]{1,0:T(8,128)} %copy-done, ...), custom_call_target="tpu_custom_call" | custom-call | tf_op jit(solution)/shard_map/pallas_call | solution.py:320
  52.2 19.0 %collective-permute-done.3 = f32[84,1024]{1,0:T(8,128)S(1)} collective-permute-done((f32[84,1024]{1,0:T(8,128)S(1)}, f32[84,1024]{1,0:T(8,128)S(1)}, u32[]{:S(2)}, u32[]{:S(2)}) %collective-permute-start.3) | collective-permute-done | bytes 344096 | tf_op jit(solution)/shard_map/ppermute | solution.py:16
  71.2 28.1 %collective-permute-done.2 = f32[84,1024]{1,0:T(8,128)S(1)} collective-permute-done((f32[84,1024]{1,0:T(8,128)S(1)}, f32[84,1024]{1,0:T(8,128)S(1)}, u32[]{:S(2)}, u32[]{:S(2)}) %collective-permute-start.2) | collective-permute-done | bytes 344096 | tf_op jit(solution)/shard_map/ppermute | solution.py:17
  99.3 0.9 broadcast_select_fusion
  100.2 4.4 %shard_map.84 = f32[16,1024]{1,0:T(8,128)} custom-call(s32[2]{0:T(128)} %pad_add_fusion.ids_ref, f32[16,16,1024]{2,1,0:T(8,128)} %u_hi.3, f32[16,16,1024]{2,1,0:T(8,128)} %u_hi.3, f32[16,16,1024]{2,1,0:T(8,128)} %d_hi.3, f32[16,16,1024]{2,1,0:T(8,128)} %d_hi.3, f32[16,16,1024]{2,1,0:T(8,128)} %mod_hi.1, f32[16,16,1024]{2,1,0:T(8,128)} %mod_hi.1, ...), custom_call_target="tpu_custom_call" | custom-call | tf_op jit(solution)/shard_map/pallas_call | solution.py:332
  104.6 2.3 %collective-permute-start.4 = (f32[16,1024]{1,0:T(8,128)}, f32[16,1024]{1,0:T(8,128)S(1)}, u32[]{:S(2)}, u32[]{:S(2)}) collective-permute-start(f32[16,1024]{1,0:T(8,128)} %shard_map.84), channel_id=1, source_target_pairs={{0,2},{1,3},{2,0},{3,1},{4,6},{5,7},{6,4},{7,5},{8,10},{9,11},{10,... | collective-permute-start | bytes 196616 | tf_op jit(solution)/shard_map/ppermute | solution.py:26
  106.9 4.0 %collective-permute-done.4 = f32[16,1024]{1,0:T(8,128)S(1)} collective-permute-done((f32[16,1024]{1,0:T(8,128)}, f32[16,1024]{1,0:T(8,128)S(1)}, u32[]{:S(2)}, u32[]{:S(2)}) %collective-permute-start.4) | collective-permute-done | bytes 65568 | tf_op jit(solution)/shard_map/ppermute | solution.py:26
  110.9 0.9 add.168
  111.8 1.9 %collective-permute-start.5 = (f32[16,1024]{1,0:T(8,128)S(1)}, f32[16,1024]{1,0:T(8,128)S(1)}, u32[]{:S(2)}, u32[]{:S(2)}) collective-permute-start(f32[16,1024]{1,0:T(8,128)S(1)} %add.168), channel_id=1, source_target_pairs={{0,4},{1,5},{2,6},{3,7},{4,0},{5,1},{6,2},{7,3},{8,12},{9,13},{10,... | collective-permute-start | bytes 196616 | tf_op jit(solution)/shard_map/ppermute | solution.py:26
  113.7 0.1 iota_add_fusion
  113.8 5.7 %collective-permute-done.5 = f32[16,1024]{1,0:T(8,128)S(1)} collective-permute-done((f32[16,1024]{1,0:T(8,128)S(1)}, f32[16,1024]{1,0:T(8,128)S(1)}, u32[]{:S(2)}, u32[]{:S(2)}) %collective-permute-start.5) | collective-permute-done | bytes 65568 | tf_op jit(solution)/shard_map/ppermute | solution.py:26
  119.4 4.0 %collective-permute-start.6 = (f32[16,1024]{1,0:T(8,128)S(1)}, f32[16,1024]{1,0:T(8,128)S(1)}, u32[]{:S(2)}, u32[]{:S(2)}) collective-permute-start(f32[16,1024]{1,0:T(8,128)S(1)} %add.169), channel_id=1, source_target_pairs={{0,1},{1,0},{2,3},{3,2},{4,5},{5,4},{6,7},{7,6},{8,9},{9,8},{10,11... | collective-permute-start | bytes 196616 | tf_op jit(solution)/shard_map/ppermute | solution.py:26
  123.5 0.3 select_reduce_fusion
  123.8 10.8 %collective-permute-done.6 = f32[16,1024]{1,0:T(8,128)S(1)} collective-permute-done((f32[16,1024]{1,0:T(8,128)S(1)}, f32[16,1024]{1,0:T(8,128)S(1)}, u32[]{:S(2)}, u32[]{:S(2)}) %collective-permute-start.6) | collective-permute-done | bytes 65568 | tf_op jit(solution)/shard_map/ppermute | solution.py:26
  134.6 3.0 %collective-permute-start.8 = (f32[2,1024]{1,0:T(2,128)S(1)}, f32[2,1024]{1,0:T(2,128)S(1)}, u32[]{:S(2)}, u32[]{:S(2)}) collective-permute-start(f32[2,1024]{1,0:T(2,128)S(1)} %get-tuple-element.45), channel_id=1, source_target_pairs={{8,16},{24,32},{40,48},{56,64},{72,80},{88,96},{104,112},{120,128}... | collective-permute-start | bytes 24584 | tf_op jit(solution)/shard_map/ppermute | solution.py:17
  137.6 1.9 %collective-permute-start.7 = (f32[2,1024]{1,0:T(2,128)S(1)}, f32[2,1024]{1,0:T(2,128)S(1)}, u32[]{:S(2)}, u32[]{:S(2)}) collective-permute-start(f32[2,1024]{1,0:T(2,128)S(1)} %get-tuple-element.46), channel_id=1, source_target_pairs={{0,8},{8,0},{16,24},{24,16},{32,40},{40,32},{48,56},{56,48},{64,72... | collective-permute-start | bytes 24584 | tf_op jit(solution)/shard_map/ppermute | solution.py:16
  139.5 7.6 %collective-permute-done.8 = f32[2,1024]{1,0:T(2,128)S(1)} collective-permute-done((f32[2,1024]{1,0:T(2,128)S(1)}, f32[2,1024]{1,0:T(2,128)S(1)}, u32[]{:S(2)}, u32[]{:S(2)}) %collective-permute-start.8) | collective-permute-done | bytes 8224 | tf_op jit(solution)/shard_map/ppermute | solution.py:17
  147.1 0.2 broadcast_multiply_fusion
  147.3 0.8 fusion.33
  (28 shorter events, 0.3 us)
Async XLA Ops:
  3.1 17.0 %copy-start.3 = (s32[16,1024]{1,0:T(8,128)S(1)}, s32[16,1024]{1,0:T(8,128)}, u32[]{:S(2)}) copy-start(s32[16,1024]{1,0:T(8,128)} %k_ref.1) | copy-start | bytes 196612
  4.3 21.0 %collective-permute-start = (f32[84,1024]{1,0:T(8,128)S(1)}, f32[84,1024]{1,0:T(8,128)S(1)}, u32[]{:S(2)}, u32[]{:S(2)}) collective-permute-start(f32[84,1024]{1,0:T(8,128)S(1)} %get-tuple-element.29), channel_id=1, source_target_pairs={{8,16},{24,32},{40,48},{56,64},{72,80},{88,96},{104,112},{120,128}... | collective-permute-start | bytes 1032200 | tf_op jit(solution)/shard_map/ppermute | solution.py:17
  17.1 8.1 %collective-permute-start.1 = (f32[84,1024]{1,0:T(8,128)S(1)}, f32[84,1024]{1,0:T(8,128)S(1)}, u32[]{:S(2)}, u32[]{:S(2)}) collective-permute-start(f32[84,1024]{1,0:T(8,128)S(1)} %get-tuple-element.30), channel_id=1, source_target_pairs={{0,8},{8,0},{16,24},{24,16},{32,40},{40,32},{48,56},{56,48},{64,72... | collective-permute-start | bytes 1032200 | tf_op jit(solution)/shard_map/ppermute | solution.py:16
  25.3 16.4 %copy-start = (f32[84,1024]{1,0:T(8,128)}, f32[84,1024]{1,0:T(8,128)S(1)}, u32[]{:S(2)}) copy-start(f32[84,1024]{1,0:T(8,128)S(1)} %get-tuple-element.27.xlo_ref) | copy-start | bytes 1032196
  25.4 16.4 %copy-start.1 = (f32[84,1024]{1,0:T(8,128)}, f32[84,1024]{1,0:T(8,128)S(1)}, u32[]{:S(2)}) copy-start(f32[84,1024]{1,0:T(8,128)S(1)} %get-tuple-element.28.xhi_ref) | copy-start | bytes 1032196
  26.1 15.6 %copy-start.2 = (f32[16,1024]{1,0:T(8,128)S(1)}, f32[16,1024]{1,0:T(8,128)}, u32[]{:S(2)}) copy-start(f32[16,1024]{1,0:T(8,128)} %p_ref.1) | copy-start | bytes 196612
  27.0 44.2 %collective-permute-start.3 = (f32[84,1024]{1,0:T(8,128)S(1)}, f32[84,1024]{1,0:T(8,128)S(1)}, u32[]{:S(2)}, u32[]{:S(2)}) collective-permute-start(f32[84,1024]{1,0:T(8,128)S(1)} %get-tuple-element.25), channel_id=1, source_target_pairs={{0,1},{1,0},{2,3},{3,2},{4,5},{5,4},{6,7},{7,6},{8,9},{9,8},{10,11... | collective-permute-start | bytes 1032200 | tf_op jit(solution)/shard_map/ppermute | solution.py:16
  38.1 61.2 %collective-permute-start.2 = (f32[84,1024]{1,0:T(8,128)S(1)}, f32[84,1024]{1,0:T(8,128)S(1)}, u32[]{:S(2)}, u32[]{:S(2)}) collective-permute-start(f32[84,1024]{1,0:T(8,128)S(1)} %get-tuple-element.26), channel_id=1, source_target_pairs={{1,2},{3,4},{5,6},{2,1},{4,3},{6,5},{9,10},{11,12},{13,14},{10,9},... | collective-permute-start | bytes 1032200 | tf_op jit(solution)/shard_map/ppermute | solution.py:17
  100.2 23.2 %copy-start.4 = (f32[16]{0:T(128)S(1)}, f32[16]{0:T(128)}, u32[]{:S(2)}) copy-start(f32[16]{0:T(128)} %param.15) | copy-start | bytes 196
  100.2 23.2 %copy-start.5 = (s32[16]{0:T(128)S(1)}, s32[16]{0:T(128)}, u32[]{:S(2)}) copy-start(s32[16]{0:T(128)} %param.14) | copy-start | bytes 196
  104.6 6.4 %collective-permute-start.4 = (f32[16,1024]{1,0:T(8,128)}, f32[16,1024]{1,0:T(8,128)S(1)}, u32[]{:S(2)}, u32[]{:S(2)}) collective-permute-start(f32[16,1024]{1,0:T(8,128)} %shard_map.84), channel_id=1, source_target_pairs={{0,2},{1,3},{2,0},{3,1},{4,6},{5,7},{6,4},{7,5},{8,10},{9,11},{10,... | collective-permute-start | bytes 196616 | tf_op jit(solution)/shard_map/ppermute | solution.py:26
  111.8 7.7 %collective-permute-start.5 = (f32[16,1024]{1,0:T(8,128)S(1)}, f32[16,1024]{1,0:T(8,128)S(1)}, u32[]{:S(2)}, u32[]{:S(2)}) collective-permute-start(f32[16,1024]{1,0:T(8,128)S(1)} %add.168), channel_id=1, source_target_pairs={{0,4},{1,5},{2,6},{3,7},{4,0},{5,1},{6,2},{7,3},{8,12},{9,13},{10,... | collective-permute-start | bytes 196616 | tf_op jit(solution)/shard_map/ppermute | solution.py:26
  119.4 15.2 %collective-permute-start.6 = (f32[16,1024]{1,0:T(8,128)S(1)}, f32[16,1024]{1,0:T(8,128)S(1)}, u32[]{:S(2)}, u32[]{:S(2)}) collective-permute-start(f32[16,1024]{1,0:T(8,128)S(1)} %add.169), channel_id=1, source_target_pairs={{0,1},{1,0},{2,3},{3,2},{4,5},{5,4},{6,7},{7,6},{8,9},{9,8},{10,11... | collective-permute-start | bytes 196616 | tf_op jit(solution)/shard_map/ppermute | solution.py:26
  134.6 12.5 %collective-permute-start.8 = (f32[2,1024]{1,0:T(2,128)S(1)}, f32[2,1024]{1,0:T(2,128)S(1)}, u32[]{:S(2)}, u32[]{:S(2)}) collective-permute-start(f32[2,1024]{1,0:T(2,128)S(1)} %get-tuple-element.45), channel_id=1, source_target_pairs={{8,16},{24,32},{40,48},{56,64},{72,80},{88,96},{104,112},{120,128}... | collective-permute-start | bytes 24584 | tf_op jit(solution)/shard_map/ppermute | solution.py:17
  137.6 9.5 %collective-permute-start.7 = (f32[2,1024]{1,0:T(2,128)S(1)}, f32[2,1024]{1,0:T(2,128)S(1)}, u32[]{:S(2)}, u32[]{:S(2)}) collective-permute-start(f32[2,1024]{1,0:T(2,128)S(1)} %get-tuple-element.46), channel_id=1, source_target_pairs={{0,8},{8,0},{16,24},{24,16},{32,40},{40,32},{48,56},{56,48},{64,72... | collective-permute-start | bytes 24584 | tf_op jit(solution)/shard_map/ppermute | solution.py:16

commit v12 on v11

--- a/solution.py
+++ b/solution.py
@@ -185,7 +185,17 @@
     edge_ref[3] = m_s[depth_cells - 2]
 
 
-def face_kernel(u_lo, u_hi, d_lo, d_hi, m_lo, m_hi, p_ref, k_ref, lo_out, hi_out):
+def face_kernel(par_ref, u_lo, u_hi, d_lo, d_hi, m_lo, m_hi, p_ref, k_ref, send_a, send_b):
+    @pl.when(par_ref[0] == 0)
+    def _():
+        pack_faces(u_lo, u_hi, d_lo, d_hi, m_lo, m_hi, p_ref, k_ref, send_b, send_a)
+
+    @pl.when(par_ref[0] == 1)
+    def _():
+        pack_faces(u_lo, u_hi, d_lo, d_hi, m_lo, m_hi, p_ref, k_ref, send_a, send_b)
+
+
+def pack_faces(u_lo, u_hi, d_lo, d_hi, m_lo, m_hi, p_ref, k_ref, lo_out, hi_out):
     depth_cells = u_lo.shape[0]
     tile_cells = p_ref.shape[0]
     dz = 4 * depth_cells
@@ -290,14 +300,21 @@
     rows_lo = pl.BlockSpec((depth_cells, 8, width), lambda i: (0, 0, 0))
     rows_hi = pl.BlockSpec((depth_cells, 8, width), lambda i: (0, tile_cells // 8 - 1, 0))
     face_rows = 5 * depth_cells + 4
-    face_lo, face_hi = pl.pallas_call(
+    parity = (lax.axis_index("tile") % 2).astype(jnp.int32).reshape(1)
+    send_a, send_b = pl.pallas_call(
         face_kernel,
         out_shape=(jax.ShapeDtypeStruct((face_rows, width), f32),) * 2,
         grid=(1,),
-        in_specs=[rows_lo, rows_hi] * 3 + [vmem, vmem],
+        in_specs=[smem] + [rows_lo, rows_hi] * 3 + [vmem, vmem],
         out_specs=(vmem, vmem),
-    )(displacement, displacement, damage, damage, modulus, modulus, pressure, crack_mask)
-    lo_x, hi_x = halo_swap(face_lo, face_hi, "tile")
+    )(parity, displacement, displacement, damage, damage, modulus, modulus, pressure, crack_mask)
+    tiles = lax.axis_size("tile")
+    even_x = lax.axis_index("tile") % 2 == 0
+    got_a = lax.ppermute(send_a, "tile", [(i, i ^ 1) for i in range(tiles)])
+    got_b = lax.ppermute(
+        send_b, "tile", [(i, i + 1) for i in range(1, tiles - 1, 2)] + [(i + 1, i) for i in range(1, tiles - 1, 2)]
+    )
+    lo_x, hi_x = jnp.where(even_x, got_b, got_a), jnp.where(even_x, got_a, got_b)
     dz = 4 * depth_cells
     p_ext = jnp.concatenate([lo_x[dz + depth_cells:dz + depth_cells + 2], pressure, hi_x[dz + depth_cells:dz + depth_cells + 2]])
     m_ext = jnp.concatenate([lo_x[dz + depth_cells + 2:], mask_f, hi_x[dz + depth_cells + 2:]])

time: 149 us -> 148 us (level)
    ppermute x0 -> x2, starting transfers between devices: none -> 14.8 us  [the longest x1 12.8 us: on_device(): lax.ppermute(send_b, 'tile', [(i, i + 1) for i in range(1, tiles - 1, 2)]...]
    ppermute x3 -> x2, starting transfers between devices: 19.5 us -> 6.94 us  [halo_swap(): got_b = lax.ppermute(jnp.where(even, lo_face, hi_face), axis, pairs_b)]
    ppermute x3 -> x2, waiting for transfers between devices: 39.1 us -> 35.3 us  [halo_swap(): got_b = lax.ppermute(jnp.where(even, lo_face, hi_face), axis, pairs_b)]
    ppermute x0 -> x2, waiting for transfers between devices: none -> 3.63 us  [the longest x1 3.62 us: on_device(): lax.ppermute(send_b, 'tile', [(i, i + 1) for i in range(1, tiles - 1, 2)]...]
    ppermute x3 -> x2, starting transfers between devices: 14.9 us -> 13 us  [halo_swap(): got_a = lax.ppermute(jnp.where(even, hi_face, lo_face), axis, pairs_a)]
    ppermute x3 -> x2, waiting for transfers between devices: 19 us -> 18.8 us  [halo_swap(): got_a = lax.ppermute(jnp.where(even, hi_face, lo_face), axis, pairs_a)]
where the time goes in v12:
time: 148 us; the launch traced here: 147 us
  waiting for transfers between devices  78.2 us (53%)
  starting transfers between devices  43.2 us (29%)
  Pallas kernels  17.2 us (12%)
  other arithmetic  6.13 us (4%)
  local copies, waits for them, and re-layouts  2.22 us (2%)
    ppermute x2, waiting for transfers between devices, halo_swap(): got_b = lax.ppermute(jnp.where(even, lo_face, hi_face), axis, pairs_b)  35.3 us
    ppermute x3, waiting for transfers between devices, butterfly_sum(): part = part + lax.ppermute(part, axis, pairs)  20.5 us
    ppermute x2, waiting for transfers between devices, halo_swap(): got_a = lax.ppermute(jnp.where(even, hi_face, lo_face), axis, pairs_a)  18.8 us
    ppermute x2, starting transfers between devices, halo_swap(): got_a = lax.ppermute(jnp.where(even, hi_face, lo_face), axis, pairs_a)  13 us
    ppermute x1, starting transfers between devices, on_device(): lax.ppermute(send_b, 'tile', [(i, i + 1) for i in range(1, tiles - 1, 2)]...  12.8 us
    pallas_call x1, Pallas kernels, on_device(): pl.pallas_call(functools.partial(interior_kernel, total_depth, total_rows...  9.67 us
    ppermute x3, starting transfers between devices, butterfly_sum(): part = part + lax.ppermute(part, axis, pairs)  8.44 us
    ppermute x2, starting transfers between devices, halo_swap(): got_b = lax.ppermute(jnp.where(even, lo_face, hi_face), axis, pairs_b)  6.94 us
  transfers between devices with their start and end apart: 9, of which 7 were waited for; matrix products, arithmetic and copies ran while one was open for 3% of the time, Pallas kernels for 7%

profile of v12, /device:TPU:30, one launch (start us, length us, event | category | flops | bytes accessed | tf_op | source)
XLA Modules:
  0.0 147.2 jit_solution(2529989750024181609)
XLA Ops:
  0.0 3.1 %shard_map.82 = (f32[84,1024]{1,0:T(8,128)}, f32[84,1024]{1,0:T(8,128)}) custom-call(s32[1]{0:T(128)} %bitcast.2.par_ref, f32[16,16,1024]{2,1,0:T(8,128)} %u_hi.3, f32[16,16,1024]{2,1,0:T(8,128)} %u_hi.3, f32[16,16,1024]{2,1,0:T(8,128)} %d_hi.3, f32[16,16,1024]{2,1,0:T(8,128)} %d_hi.3, f32[16,16,1024]{2,1,0:T(8,128)} %mod_hi.1, f32[16,16,1024]{2,1,0:T(8,128)} %mod_hi.1, ...), custom_call_target="tpu_custom_call" | custom-call | tf_op jit(solution)/shard_map/pallas_call | solution.py:304
  3.1 12.8 %collective-permute-start = (f32[84,1024]{1,0:T(8,128)}, f32[84,1024]{1,0:T(8,128)S(1)}, u32[]{:S(2)}, u32[]{:S(2)}) collective-permute-start(f32[84,1024]{1,0:T(8,128)} %get-tuple-element.9), channel_id=1, source_target_pairs={{8,16},{24,32},{40,48},{56,64},{72,80},{88,96},{104,112},{120,128}... | collective-permute-start | bytes 1032200 | tf_op jit(solution)/shard_map/ppermute | solution.py:314
  16.0 1.9 %collective-permute-start.1 = (f32[84,1024]{1,0:T(8,128)}, f32[84,1024]{1,0:T(8,128)S(1)}, u32[]{:S(2)}, u32[]{:S(2)}) collective-permute-start(f32[84,1024]{1,0:T(8,128)} %get-tuple-element.10), channel_id=1, source_target_pairs={{0,8},{8,0},{16,24},{24,16},{32,40},{40,32},{48,56},{56,48},{64,72... | collective-permute-start | bytes 1032200 | tf_op jit(solution)/shard_map/ppermute | solution.py:313
  17.9 1.0 bitcast_multiply_fusion
  18.9 0.6 pad_add_fusion.ids_ref
  19.5 1.2 multiply_bitcast_fusion
  20.7 3.6 %collective-permute-done = f32[84,1024]{1,0:T(8,128)S(1)} collective-permute-done((f32[84,1024]{1,0:T(8,128)}, f32[84,1024]{1,0:T(8,128)S(1)}, u32[]{:S(2)}, u32[]{:S(2)}) %collective-permute-start) | collective-permute-done | bytes 344096 | tf_op jit(solution)/shard_map/ppermute | solution.py:314
  24.4 0.7 concatenate.30
  25.2 0.7 concatenate.29
  26.0 0.1 broadcast_select_fusion.2
  26.0 11.1 %collective-permute-start.3 = (f32[84,1024]{1,0:T(8,128)S(1)}, f32[84,1024]{1,0:T(8,128)S(1)}, u32[]{:S(2)}, u32[]{:S(2)}) collective-permute-start(f32[84,1024]{1,0:T(8,128)S(1)} %get-tuple-element.25), channel_id=1, source_target_pairs={{0,1},{1,0},{2,3},{3,2},{4,5},{5,4},{6,7},{7,6},{8,9},{9,8},{10,11... | collective-permute-start | bytes 1032200 | tf_op jit(solution)/shard_map/ppermute | solution.py:16
  37.1 3.7 %collective-permute-start.2 = (f32[84,1024]{1,0:T(8,128)S(1)}, f32[84,1024]{1,0:T(8,128)S(1)}, u32[]{:S(2)}, u32[]{:S(2)}) collective-permute-start(f32[84,1024]{1,0:T(8,128)S(1)} %get-tuple-element.26), channel_id=1, source_target_pairs={{1,2},{3,4},{5,6},{2,1},{4,3},{6,5},{9,10},{11,12},{13,14},{10,9},... | collective-permute-start | bytes 1032200 | tf_op jit(solution)/shard_map/ppermute | solution.py:17
  40.9 0.7 pad.15.load_ref
  41.6 9.7 %shard_map.83 = (f32[16,1024]{1,0:T(8,128)}, f32[4,32,1024]{2,1,0:T(8,128)}) custom-call(s32[2]{0:T(128)} %pad_add_fusion.ids_ref, f32[16,16,1024]{2,1,0:T(8,128)} %u_hi.3, f32[16,16,1024]{2,1,0:T(8,128)} %d_hi.3, f32[16,16,1024]{2,1,0:T(8,128)} %mod_hi.1, f32[16,16,1024]{2,1,0:T(8,128)} %tgh_hi.1, f32[84,1024]{1,0:T(8,128)} %copy-done, ...), custom_call_target="tpu_custom_call" | custom-call | tf_op jit(solution)/shard_map/pallas_call | solution.py:337
  51.2 18.8 %collective-permute-done.3 = f32[84,1024]{1,0:T(8,128)S(1)} collective-permute-done((f32[84,1024]{1,0:T(8,128)S(1)}, f32[84,1024]{1,0:T(8,128)S(1)}, u32[]{:S(2)}, u32[]{:S(2)}) %collective-permute-start.3) | collective-permute-done | bytes 344096 | tf_op jit(solution)/shard_map/ppermute | solution.py:16
  70.1 28.1 %collective-permute-done.2 = f32[84,1024]{1,0:T(8,128)S(1)} collective-permute-done((f32[84,1024]{1,0:T(8,128)S(1)}, f32[84,1024]{1,0:T(8,128)S(1)}, u32[]{:S(2)}, u32[]{:S(2)}) %collective-permute-start.2) | collective-permute-done | bytes 344096 | tf_op jit(solution)/shard_map/ppermute | solution.py:17
  98.1 0.9 broadcast_select_fusion
  99.1 4.4 %shard_map.84 = f32[16,1024]{1,0:T(8,128)} custom-call(s32[2]{0:T(128)} %pad_add_fusion.ids_ref, f32[16,16,1024]{2,1,0:T(8,128)} %u_hi.3, f32[16,16,1024]{2,1,0:T(8,128)} %u_hi.3, f32[16,16,1024]{2,1,0:T(8,128)} %d_hi.3, f32[16,16,1024]{2,1,0:T(8,128)} %d_hi.3, f32[16,16,1024]{2,1,0:T(8,128)} %mod_hi.1, f32[16,16,1024]{2,1,0:T(8,128)} %mod_hi.1, ...), custom_call_target="tpu_custom_call" | custom-call | tf_op jit(solution)/shard_map/pallas_call | solution.py:349
  103.4 2.4 %collective-permute-start.4 = (f32[16,1024]{1,0:T(8,128)}, f32[16,1024]{1,0:T(8,128)S(1)}, u32[]{:S(2)}, u32[]{:S(2)}) collective-permute-start(f32[16,1024]{1,0:T(8,128)} %shard_map.84), channel_id=1, source_target_pairs={{0,2},{1,3},{2,0},{3,1},{4,6},{5,7},{6,4},{7,5},{8,10},{9,11},{10,... | collective-permute-start | bytes 196616 | tf_op jit(solution)/shard_map/ppermute | solution.py:26
  105.8 4.0 %collective-permute-done.4 = f32[16,1024]{1,0:T(8,128)S(1)} collective-permute-done((f32[16,1024]{1,0:T(8,128)}, f32[16,1024]{1,0:T(8,128)S(1)}, u32[]{:S(2)}, u32[]{:S(2)}) %collective-permute-start.4) | collective-permute-done | bytes 65568 | tf_op jit(solution)/shard_map/ppermute | solution.py:26
  109.8 0.9 add.169
  110.7 1.9 %collective-permute-start.5 = (f32[16,1024]{1,0:T(8,128)S(1)}, f32[16,1024]{1,0:T(8,128)S(1)}, u32[]{:S(2)}, u32[]{:S(2)}) collective-permute-start(f32[16,1024]{1,0:T(8,128)S(1)} %add.169), channel_id=1, source_target_pairs={{0,4},{1,5},{2,6},{3,7},{4,0},{5,1},{6,2},{7,3},{8,12},{9,13},{10,... | collective-permute-start | bytes 196616 | tf_op jit(solution)/shard_map/ppermute | solution.py:26
  112.6 0.1 iota_add_fusion
  112.6 5.7 %collective-permute-done.5 = f32[16,1024]{1,0:T(8,128)S(1)} collective-permute-done((f32[16,1024]{1,0:T(8,128)S(1)}, f32[16,1024]{1,0:T(8,128)S(1)}, u32[]{:S(2)}, u32[]{:S(2)}) %collective-permute-start.5) | collective-permute-done | bytes 65568 | tf_op jit(solution)/shard_map/ppermute | solution.py:26
  118.3 4.2 %collective-permute-start.6 = (f32[16,1024]{1,0:T(8,128)S(1)}, f32[16,1024]{1,0:T(8,128)S(1)}, u32[]{:S(2)}, u32[]{:S(2)}) collective-permute-start(f32[16,1024]{1,0:T(8,128)S(1)} %add.170), channel_id=1, source_target_pairs={{0,1},{1,0},{2,3},{3,2},{4,5},{5,4},{6,7},{7,6},{8,9},{9,8},{10,11... | collective-permute-start | bytes 196616 | tf_op jit(solution)/shard_map/ppermute | solution.py:26
  122.5 0.3 select_reduce_fusion
  122.8 10.8 %collective-permute-done.6 = f32[16,1024]{1,0:T(8,128)S(1)} collective-permute-done((f32[16,1024]{1,0:T(8,128)S(1)}, f32[16,1024]{1,0:T(8,128)S(1)}, u32[]{:S(2)}, u32[]{:S(2)}) %collective-permute-start.6) | collective-permute-done | bytes 65568 | tf_op jit(solution)/shard_map/ppermute | solution.py:26
  133.7 3.3 %collective-permute-start.8 = (f32[2,1024]{1,0:T(2,128)S(1)}, f32[2,1024]{1,0:T(2,128)S(1)}, u32[]{:S(2)}, u32[]{:S(2)}) collective-permute-start(f32[2,1024]{1,0:T(2,128)S(1)} %get-tuple-element.43), channel_id=1, source_target_pairs={{8,16},{24,32},{40,48},{56,64},{72,80},{88,96},{104,112},{120,128}... | collective-permute-start | bytes 24584 | tf_op jit(solution)/shard_map/ppermute | solution.py:17
  137.0 1.9 %collective-permute-start.7 = (f32[2,1024]{1,0:T(2,128)S(1)}, f32[2,1024]{1,0:T(2,128)S(1)}, u32[]{:S(2)}, u32[]{:S(2)}) collective-permute-start(f32[2,1024]{1,0:T(2,128)S(1)} %get-tuple-element.44), channel_id=1, source_target_pairs={{0,8},{8,0},{16,24},{24,16},{32,40},{40,32},{48,56},{56,48},{64,72... | collective-permute-start | bytes 24584 | tf_op jit(solution)/shard_map/ppermute | solution.py:16
  138.9 7.2 %collective-permute-done.8 = f32[2,1024]{1,0:T(2,128)S(1)} collective-permute-done((f32[2,1024]{1,0:T(2,128)S(1)}, f32[2,1024]{1,0:T(2,128)S(1)}, u32[]{:S(2)}, u32[]{:S(2)}) %collective-permute-start.8) | collective-permute-done | bytes 8224 | tf_op jit(solution)/shard_map/ppermute | solution.py:17
  146.2 0.2 broadcast_multiply_fusion
  146.4 0.8 fusion.33
  (27 shorter events, 0.3 us)
Async XLA Ops:
  0.0 18.9 %copy-start.3 = (s32[16,1024]{1,0:T(8,128)S(1)}, s32[16,1024]{1,0:T(8,128)}, u32[]{:S(2)}) copy-start(s32[16,1024]{1,0:T(8,128)} %k_ref.1) | copy-start | bytes 196612
  3.1 21.2 %collective-permute-start = (f32[84,1024]{1,0:T(8,128)}, f32[84,1024]{1,0:T(8,128)S(1)}, u32[]{:S(2)}, u32[]{:S(2)}) collective-permute-start(f32[84,1024]{1,0:T(8,128)} %get-tuple-element.9), channel_id=1, source_target_pairs={{8,16},{24,32},{40,48},{56,64},{72,80},{88,96},{104,112},{120,128}... | collective-permute-start | bytes 1032200 | tf_op jit(solution)/shard_map/ppermute | solution.py:314
  16.0 8.3 %collective-permute-start.1 = (f32[84,1024]{1,0:T(8,128)}, f32[84,1024]{1,0:T(8,128)S(1)}, u32[]{:S(2)}, u32[]{:S(2)}) collective-permute-start(f32[84,1024]{1,0:T(8,128)} %get-tuple-element.10), channel_id=1, source_target_pairs={{0,8},{8,0},{16,24},{24,16},{32,40},{40,32},{48,56},{56,48},{64,72... | collective-permute-start | bytes 1032200 | tf_op jit(solution)/shard_map/ppermute | solution.py:313
  24.4 16.4 %copy-start = (f32[84,1024]{1,0:T(8,128)}, f32[84,1024]{1,0:T(8,128)S(1)}, u32[]{:S(2)}) copy-start(f32[84,1024]{1,0:T(8,128)S(1)} %get-tuple-element.27.xlo_ref) | copy-start | bytes 1032196
  24.4 16.4 %copy-start.1 = (f32[84,1024]{1,0:T(8,128)}, f32[84,1024]{1,0:T(8,128)S(1)}, u32[]{:S(2)}) copy-start(f32[84,1024]{1,0:T(8,128)S(1)} %get-tuple-element.28.xhi_ref) | copy-start | bytes 1032196
  25.2 15.6 %copy-start.2 = (f32[16,1024]{1,0:T(8,128)S(1)}, f32[16,1024]{1,0:T(8,128)}, u32[]{:S(2)}) copy-start(f32[16,1024]{1,0:T(8,128)} %p_ref.1) | copy-start | bytes 196612
  26.0 44.0 %collective-permute-start.3 = (f32[84,1024]{1,0:T(8,128)S(1)}, f32[84,1024]{1,0:T(8,128)S(1)}, u32[]{:S(2)}, u32[]{:S(2)}) collective-permute-start(f32[84,1024]{1,0:T(8,128)S(1)} %get-tuple-element.25), channel_id=1, source_target_pairs={{0,1},{1,0},{2,3},{3,2},{4,5},{5,4},{6,7},{7,6},{8,9},{9,8},{10,11... | collective-permute-start | bytes 1032200 | tf_op jit(solution)/shard_map/ppermute | solution.py:16
  37.1 61.0 %collective-permute-start.2 = (f32[84,1024]{1,0:T(8,128)S(1)}, f32[84,1024]{1,0:T(8,128)S(1)}, u32[]{:S(2)}, u32[]{:S(2)}) collective-permute-start(f32[84,1024]{1,0:T(8,128)S(1)} %get-tuple-element.26), channel_id=1, source_target_pairs={{1,2},{3,4},{5,6},{2,1},{4,3},{6,5},{9,10},{11,12},{13,14},{10,9},... | collective-permute-start | bytes 1032200 | tf_op jit(solution)/shard_map/ppermute | solution.py:17
  99.1 23.4 %copy-start.4 = (f32[16]{0:T(128)S(1)}, f32[16]{0:T(128)}, u32[]{:S(2)}) copy-start(f32[16]{0:T(128)} %param.15) | copy-start | bytes 196
  99.1 23.4 %copy-start.5 = (s32[16]{0:T(128)S(1)}, s32[16]{0:T(128)}, u32[]{:S(2)}) copy-start(s32[16]{0:T(128)} %param.14) | copy-start | bytes 196
  103.4 6.4 %collective-permute-start.4 = (f32[16,1024]{1,0:T(8,128)}, f32[16,1024]{1,0:T(8,128)S(1)}, u32[]{:S(2)}, u32[]{:S(2)}) collective-permute-start(f32[16,1024]{1,0:T(8,128)} %shard_map.84), channel_id=1, source_target_pairs={{0,2},{1,3},{2,0},{3,1},{4,6},{5,7},{6,4},{7,5},{8,10},{9,11},{10,... | collective-permute-start | bytes 196616 | tf_op jit(solution)/shard_map/ppermute | solution.py:26
  110.7 7.7 %collective-permute-start.5 = (f32[16,1024]{1,0:T(8,128)S(1)}, f32[16,1024]{1,0:T(8,128)S(1)}, u32[]{:S(2)}, u32[]{:S(2)}) collective-permute-start(f32[16,1024]{1,0:T(8,128)S(1)} %add.169), channel_id=1, source_target_pairs={{0,4},{1,5},{2,6},{3,7},{4,0},{5,1},{6,2},{7,3},{8,12},{9,13},{10,... | collective-permute-start | bytes 196616 | tf_op jit(solution)/shard_map/ppermute | solution.py:26
  118.3 15.3 %collective-permute-start.6 = (f32[16,1024]{1,0:T(8,128)S(1)}, f32[16,1024]{1,0:T(8,128)S(1)}, u32[]{:S(2)}, u32[]{:S(2)}) collective-permute-start(f32[16,1024]{1,0:T(8,128)S(1)} %add.170), channel_id=1, source_target_pairs={{0,1},{1,0},{2,3},{3,2},{4,5},{5,4},{6,7},{7,6},{8,9},{9,8},{10,11... | collective-permute-start | bytes 196616 | tf_op jit(solution)/shard_map/ppermute | solution.py:26
  133.7 12.5 %collective-permute-start.8 = (f32[2,1024]{1,0:T(2,128)S(1)}, f32[2,1024]{1,0:T(2,128)S(1)}, u32[]{:S(2)}, u32[]{:S(2)}) collective-permute-start(f32[2,1024]{1,0:T(2,128)S(1)} %get-tuple-element.43), channel_id=1, source_target_pairs={{8,16},{24,32},{40,48},{56,64},{72,80},{88,96},{104,112},{120,128}... | collective-permute-start | bytes 24584 | tf_op jit(solution)/shard_map/ppermute | solution.py:17
  137.0 9.2 %collective-permute-start.7 = (f32[2,1024]{1,0:T(2,128)S(1)}, f32[2,1024]{1,0:T(2,128)S(1)}, u32[]{:S(2)}, u32[]{:S(2)}) collective-permute-start(f32[2,1024]{1,0:T(2,128)S(1)} %get-tuple-element.44), channel_id=1, source_target_pairs={{0,8},{8,0},{16,24},{24,16},{32,40},{40,32},{48,56},{56,48},{64,72... | collective-permute-start | bytes 24584 | tf_op jit(solution)/shard_map/ppermute | solution.py:16

commit v13 on v12

--- a/solution.py
+++ b/solution.py
@@ -209,6 +209,35 @@
     lo_out[dz + depth_cells + 2:dz + depth_cells + 4] = k_ref[0:2].astype(jnp.float32)
     hi_out[dz + depth_cells:dz + depth_cells + 2] = p_ref[tile_cells - 2:tile_cells]
     hi_out[dz + depth_cells + 2:dz + depth_cells + 4] = k_ref[tile_cells - 2:tile_cells].astype(jnp.float32)
+
+
+def depth_pack_kernel(depth_cells, par_ref, u_lo, u_hi, d_lo, d_hi, m_lo, m_hi, xlo_ref, xhi_ref, send_a, send_b):
+    @pl.when(par_ref[0] == 0)
+    def _():
+        pack_depth(depth_cells, u_lo, d_lo, m_lo, xlo_ref, xhi_ref, send_b, 0, 1, 0)
+        pack_depth(depth_cells, u_hi, d_hi, m_hi, xlo_ref, xhi_ref, send_a, 3, 2, depth_cells - 1)
+
+    @pl.when(par_ref[0] == 1)
+    def _():
+        pack_depth(depth_cells, u_lo, d_lo, m_lo, xlo_ref, xhi_ref, send_a, 0, 1, 0)
+        pack_depth(depth_cells, u_hi, d_hi, m_hi, xlo_ref, xhi_ref, send_b, 3, 2, depth_cells - 1)
+
+
+def pack_depth(depth_cells, u_b, d_b, m_b, xlo_ref, xhi_ref, out, adj, sec, adj_z):
+    tile_cells = u_b.shape[1]
+    ext = tile_cells + 2
+    c0 = 2 * depth_cells
+    d_adj = d_b[adj]
+    d_sec = d_b[sec]
+    out[0:1] = xlo_ref[2 * adj_z + 1:2 * adj_z + 2]
+    out[1:1 + tile_cells] = u_b[adj]
+    out[1 + tile_cells:ext] = xhi_ref[2 * adj_z:2 * adj_z + 1]
+    out[ext:ext + 1] = xlo_ref[c0 + 2 * adj_z + 1:c0 + 2 * adj_z + 2]
+    out[ext + 1:ext + 1 + tile_cells] = ((1.0 - d_adj) ** 2 + 0.001) * m_b[adj]
+    out[ext + 1 + tile_cells:2 * ext] = xhi_ref[c0 + 2 * adj_z:c0 + 2 * adj_z + 1]
+    out[2 * ext:2 * ext + tile_cells] = u_b[sec]
+    out[2 * ext + tile_cells:2 * ext + 2 * tile_cells] = ((1.0 - d_sec) ** 2 + 0.001) * m_b[sec]
+    out[2 * ext + 2 * tile_cells:2 * ext + 3 * tile_cells] = d_adj
 
 
 class Ends:
@@ -321,15 +350,23 @@
     load_all = jnp.pad(4.0 * m_ext[1:-1] * p_ext[1:-1], ((X0 - 1, X0 - 1), (0, 0)))
     ids = jnp.stack([depth_start, tile_start]).astype(jnp.int32)
 
-    def depth_face(adj, sec):
-        u_adj = jnp.concatenate([lo_x[2 * adj + 1:2 * adj + 2], displacement[adj], hi_x[2 * adj:2 * adj + 1]])
-        c0 = 2 * depth_cells
-        c_adj = jnp.concatenate(
-            [lo_x[c0 + 2 * adj + 1:c0 + 2 * adj + 2], stiff_of(damage[adj], modulus[adj]), hi_x[c0 + 2 * adj:c0 + 2 * adj + 1]]
-        )
-        return jnp.concatenate([u_adj, c_adj, displacement[sec], stiff_of(damage[sec], modulus[sec]), damage[adj]])
-
-    lo_z, hi_z = halo_swap(depth_face(0, 1), depth_face(depth_cells - 1, depth_cells - 2), "depth")
+    layers_lo = pl.BlockSpec((4, tile_cells, width), lambda i: (0, 0, 0))
+    layers_hi = pl.BlockSpec((4, tile_cells, width), lambda i: (depth_cells // 4 - 1, 0, 0))
+    depths = lax.axis_size("depth")
+    parity_z = (lax.axis_index("depth") % 2).astype(jnp.int32).reshape(1)
+    zsend_a, zsend_b = pl.pallas_call(
+        functools.partial(depth_pack_kernel, depth_cells),
+        out_shape=(jax.ShapeDtypeStruct((2 * (tile_cells + 2) + 3 * tile_cells, width), f32),) * 2,
+        grid=(1,),
+        in_specs=[smem] + [layers_lo, layers_hi] * 3 + [vmem, vmem],
+        out_specs=(vmem, vmem),
+    )(parity_z, displacement, displacement, damage, damage, modulus, modulus, lo_x, hi_x)
+    even_z = lax.axis_index("depth") % 2 == 0
+    zgot_a = lax.ppermute(zsend_a, "depth", [(i, i ^ 1) for i in range(depths)])
+    zgot_b = lax.ppermute(
+        zsend_b, "depth", [(i, i + 1) for i in range(1, depths - 1, 2)] + [(i + 1, i) for i in range(1, depths - 1, 2)]
+    )
+    lo_z, hi_z = jnp.where(even_z, zgot_b, zgot_a), jnp.where(even_z, zgot_a, zgot_b)
 
     vmem = pl.BlockSpec(memory_space=pltpu.VMEM)
     smem = pl.BlockSpec(memory_space=pltpu.SMEM)

time: 148 us -> 148 us (level)
  waiting for transfers between devices: 78.2 us -> 74.9 us
  starting transfers between devices: 43.2 us -> 46.1 us
  Pallas kernels: 17.2 us -> 19.7 us
    ppermute x0 -> x2, waiting for transfers between devices: none -> 44.9 us  [the longest x1 27.9 us: on_device(): lax.ppermute(zsend_b, 'depth', [(i, i + 1) for i in range(1, depths - 1,...]
    ppermute x2 -> x1, waiting for transfers between devices: 35.3 us -> 5.62 us  [halo_swap(): got_b = lax.ppermute(jnp.where(even, lo_face, hi_face), axis, pairs_b)]
    ppermute x2 -> x1, waiting for transfers between devices: 18.8 us -> 0.01 us  [halo_swap(): got_a = lax.ppermute(jnp.where(even, hi_face, lo_face), axis, pairs_a)]
    ppermute x0 -> x2, starting transfers between devices: none -> 14.7 us  [the longest x1 11 us: on_device(): zgot_a = lax.ppermute(zsend_a, 'depth', [(i, i ^ 1) for i in range(depths)])]
    ppermute x2 -> x1, starting transfers between devices: 13 us -> 1.92 us  [halo_swap(): got_a = lax.ppermute(jnp.where(even, hi_face, lo_face), axis, pairs_a)]
    pallas_call x0 -> x1, Pallas kernels: none -> 2.56 us  [on_device(): pl.pallas_call(functools.partial(depth_pack_kernel, depth_cells), out_sha...]
    mul x2 -> x0, other arithmetic: 2.12 us -> none  [stiff_of(): return ((1.0 - dmg) ** 2 + 0.001) * mod]
    ppermute x1, waiting for transfers between devices: 3.62 us -> 5.71 us  [on_device(): lax.ppermute(send_b, 'tile', [(i, i + 1) for i in range(1, tiles - 1, 2)]...]
  transfers between devices with their start and end apart: 9 -> 9, of which waited for: 7 -> 7; matrix products, arithmetic and copies ran while one was open for 3% -> 2% of each run, Pallas kernels for 7% -> 7%
where the time goes in v13:
time: 148 us; the launch traced here: 147 us
  waiting for transfers between devices  74.9 us (51%)
  starting transfers between devices  46.1 us (31%)
  Pallas kernels  19.7 us (13%)
  other arithmetic  4.84 us (3%)
  local copies, waits for them, and re-layouts  1.53 us (1%)
    ppermute x1, waiting for transfers between devices, on_device(): lax.ppermute(zsend_b, 'depth', [(i, i + 1) for i in range(1, depths - 1,...  27.9 us
    ppermute x3, waiting for transfers between devices, butterfly_sum(): part = part + lax.ppermute(part, axis, pairs)  18.7 us
    ppermute x1, waiting for transfers between devices, on_device(): zgot_a = lax.ppermute(zsend_a, 'depth', [(i, i ^ 1) for i in range(depths)])  17 us
    ppermute x1, starting transfers between devices, on_device(): lax.ppermute(send_b, 'tile', [(i, i + 1) for i in range(1, tiles - 1, 2)]...  12.8 us
    ppermute x1, starting transfers between devices, on_device(): zgot_a = lax.ppermute(zsend_a, 'depth', [(i, i ^ 1) for i in range(depths)])  11 us
    ppermute x3, starting transfers between devices, butterfly_sum(): part = part + lax.ppermute(part, axis, pairs)  9.8 us
    pallas_call x1, Pallas kernels, on_device(): pl.pallas_call(functools.partial(interior_kernel, total_depth, total_rows...  9.66 us
    ppermute x1, waiting for transfers between devices, on_device(): lax.ppermute(send_b, 'tile', [(i, i + 1) for i in range(1, tiles - 1, 2)]...  5.71 us
  transfers between devices with their start and end apart: 9, of which 7 were waited for; matrix products, arithmetic and copies ran while one was open for 2% of the time, Pallas kernels for 7%

profile of v13, /device:TPU:30, one launch (start us, length us, event | category | flops | bytes accessed | tf_op | source)
XLA Modules:
  0.0 147.3 jit_solution(2074281067478416087)
XLA Ops:
  0.0 3.2 %shard_map.82 = (f32[84,1024]{1,0:T(8,128)}, f32[84,1024]{1,0:T(8,128)}) custom-call(s32[1]{0:T(128)} %bitcast.2.par_ref, f32[16,16,1024]{2,1,0:T(8,128)} %u_hi.5, f32[16,16,1024]{2,1,0:T(8,128)} %u_hi.5, f32[16,16,1024]{2,1,0:T(8,128)} %d_hi.5, f32[16,16,1024]{2,1,0:T(8,128)} %d_hi.5, f32[16,16,1024]{2,1,0:T(8,128)} %mod_hi.1, f32[16,16,1024]{2,1,0:T(8,128)} %mod_hi.1, ...), custom_call_target="tpu_custom_call" | custom-call | tf_op jit(solution)/shard_map/pallas_call | solution.py:333
  3.2 12.8 %collective-permute-start = (f32[84,1024]{1,0:T(8,128)}, f32[84,1024]{1,0:T(8,128)S(1)}, u32[]{:S(2)}, u32[]{:S(2)}) collective-permute-start(f32[84,1024]{1,0:T(8,128)} %get-tuple-element.11), channel_id=1, source_target_pairs={{8,16},{24,32},{40,48},{56,64},{72,80},{88,96},{104,112},{120,128}... | collective-permute-start | bytes 1032200 | tf_op jit(solution)/shard_map/ppermute | solution.py:343
  16.0 1.9 %collective-permute-start.1 = (f32[84,1024]{1,0:T(8,128)}, f32[84,1024]{1,0:T(8,128)S(1)}, u32[]{:S(2)}, u32[]{:S(2)}) collective-permute-start(f32[84,1024]{1,0:T(8,128)} %get-tuple-element.12), channel_id=1, source_target_pairs={{0,8},{8,0},{16,24},{24,16},{32,40},{40,32},{48,56},{56,48},{64,72... | collective-permute-start | bytes 1032200 | tf_op jit(solution)/shard_map/ppermute | solution.py:342
  18.0 0.6 pad_add_fusion.ids_ref
  18.6 5.7 %collective-permute-done = f32[84,1024]{1,0:T(8,128)S(1)} collective-permute-done((f32[84,1024]{1,0:T(8,128)}, f32[84,1024]{1,0:T(8,128)S(1)}, u32[]{:S(2)}, u32[]{:S(2)}) %collective-permute-start) | collective-permute-done | bytes 344096 | tf_op jit(solution)/shard_map/ppermute | solution.py:343
  24.3 0.0 collective-permute-done.1
  24.3 0.9 broadcast_select_fusion.3
  25.3 2.6 %shard_map.83 = (f32[84,1024]{1,0:T(8,128)}, f32[84,1024]{1,0:T(8,128)}) custom-call(s32[1]{0:T(128)} %bitcast.3.par_ref, f32[16,16,1024]{2,1,0:T(8,128)} %u_hi.5, f32[16,16,1024]{2,1,0:T(8,128)} %u_hi.5, f32[16,16,1024]{2,1,0:T(8,128)} %d_hi.5, f32[16,16,1024]{2,1,0:T(8,128)} %d_hi.5, f32[16,16,1024]{2,1,0:T(8,128)} %mod_hi.1, f32[16,16,1024]{2,1,0:T(8,128)} %mod_hi.1, ...), custom_call_target="tpu_custom_call" | custom-call | tf_op jit(solution)/shard_map/pallas_call | solution.py:357
  27.9 11.0 %collective-permute-start.3 = (f32[84,1024]{1,0:T(8,128)}, f32[84,1024]{1,0:T(8,128)S(1)}, u32[]{:S(2)}, u32[]{:S(2)}) collective-permute-start(f32[84,1024]{1,0:T(8,128)} %get-tuple-element.14), channel_id=1, source_target_pairs={{0,1},{1,0},{2,3},{3,2},{4,5},{5,4},{6,7},{7,6},{8,9},{9,8},{10,11... | collective-permute-start | bytes 1032200 | tf_op jit(solution)/shard_map/ppermute | solution.py:365
  38.8 3.8 %collective-permute-start.2 = (f32[84,1024]{1,0:T(8,128)}, f32[84,1024]{1,0:T(8,128)S(1)}, u32[]{:S(2)}, u32[]{:S(2)}) collective-permute-start(f32[84,1024]{1,0:T(8,128)} %get-tuple-element.13), channel_id=1, source_target_pairs={{1,2},{3,4},{5,6},{2,1},{4,3},{6,5},{9,10},{11,12},{13,14},{10,9},... | collective-permute-start | bytes 1032200 | tf_op jit(solution)/shard_map/ppermute | solution.py:366
  42.6 0.9 fusion.37
  43.5 0.7 pad.15.load_ref
  44.2 9.7 %shard_map.84 = (f32[16,1024]{1,0:T(8,128)}, f32[4,32,1024]{2,1,0:T(8,128)}) custom-call(s32[2]{0:T(128)} %pad_add_fusion.ids_ref, f32[16,16,1024]{2,1,0:T(8,128)} %u_hi.5, f32[16,16,1024]{2,1,0:T(8,128)} %d_hi.5, f32[16,16,1024]{2,1,0:T(8,128)} %mod_hi.1, f32[16,16,1024]{2,1,0:T(8,128)} %tgh_hi.1, f32[84,1024]{1,0:T(8,128)} %get-tuple-element.19.xlo_ref, ...), custom_call_target="tpu_custom_call" | custom-call | tf_op jit(solution)/shard_map/pallas_call | solution.py:374
  53.9 17.0 %collective-permute-done.3 = f32[84,1024]{1,0:T(8,128)S(1)} collective-permute-done((f32[84,1024]{1,0:T(8,128)}, f32[84,1024]{1,0:T(8,128)S(1)}, u32[]{:S(2)}, u32[]{:S(2)}) %collective-permute-start.3) | collective-permute-done | bytes 344096 | tf_op jit(solution)/shard_map/ppermute | solution.py:365
  70.9 27.9 %collective-permute-done.2 = f32[84,1024]{1,0:T(8,128)S(1)} collective-permute-done((f32[84,1024]{1,0:T(8,128)}, f32[84,1024]{1,0:T(8,128)S(1)}, u32[]{:S(2)}, u32[]{:S(2)}) %collective-permute-start.2) | collective-permute-done | bytes 344096 | tf_op jit(solution)/shard_map/ppermute | solution.py:366
  98.7 0.9 broadcast_select_fusion
  99.7 4.3 %shard_map.85 = f32[16,1024]{1,0:T(8,128)} custom-call(s32[2]{0:T(128)} %pad_add_fusion.ids_ref, f32[16,16,1024]{2,1,0:T(8,128)} %u_hi.5, f32[16,16,1024]{2,1,0:T(8,128)} %u_hi.5, f32[16,16,1024]{2,1,0:T(8,128)} %d_hi.5, f32[16,16,1024]{2,1,0:T(8,128)} %d_hi.5, f32[16,16,1024]{2,1,0:T(8,128)} %mod_hi.1, f32[16,16,1024]{2,1,0:T(8,128)} %mod_hi.1, ...), custom_call_target="tpu_custom_call" | custom-call | tf_op jit(solution)/shard_map/pallas_call | solution.py:386
  104.0 2.4 %collective-permute-start.4 = (f32[16,1024]{1,0:T(8,128)}, f32[16,1024]{1,0:T(8,128)S(1)}, u32[]{:S(2)}, u32[]{:S(2)}) collective-permute-start(f32[16,1024]{1,0:T(8,128)} %shard_map.85), channel_id=1, source_target_pairs={{0,2},{1,3},{2,0},{3,1},{4,6},{5,7},{6,4},{7,5},{8,10},{9,11},{10,... | collective-permute-start | bytes 196616 | tf_op jit(solution)/shard_map/ppermute | solution.py:26
  106.4 4.0 %collective-permute-done.4 = f32[16,1024]{1,0:T(8,128)S(1)} collective-permute-done((f32[16,1024]{1,0:T(8,128)}, f32[16,1024]{1,0:T(8,128)S(1)}, u32[]{:S(2)}, u32[]{:S(2)}) %collective-permute-start.4) | collective-permute-done | bytes 65568 | tf_op jit(solution)/shard_map/ppermute | solution.py:26
  110.4 0.8 add.155
  111.2 1.9 %collective-permute-start.5 = (f32[16,1024]{1,0:T(8,128)S(1)}, f32[16,1024]{1,0:T(8,128)S(1)}, u32[]{:S(2)}, u32[]{:S(2)}) collective-permute-start(f32[16,1024]{1,0:T(8,128)S(1)} %add.155), channel_id=1, source_target_pairs={{0,4},{1,5},{2,6},{3,7},{4,0},{5,1},{6,2},{7,3},{8,12},{9,13},{10,... | collective-permute-start | bytes 196616 | tf_op jit(solution)/shard_map/ppermute | solution.py:26
  113.1 0.1 iota_add_fusion
  113.2 5.7 %collective-permute-done.5 = f32[16,1024]{1,0:T(8,128)S(1)} collective-permute-done((f32[16,1024]{1,0:T(8,128)S(1)}, f32[16,1024]{1,0:T(8,128)S(1)}, u32[]{:S(2)}, u32[]{:S(2)}) %collective-permute-start.5) | collective-permute-done | bytes 65568 | tf_op jit(solution)/shard_map/ppermute | solution.py:26
  118.9 5.5 %collective-permute-start.6 = (f32[16,1024]{1,0:T(8,128)S(1)}, f32[16,1024]{1,0:T(8,128)S(1)}, u32[]{:S(2)}, u32[]{:S(2)}) collective-permute-start(f32[16,1024]{1,0:T(8,128)S(1)} %add.156), channel_id=1, source_target_pairs={{0,1},{1,0},{2,3},{3,2},{4,5},{5,4},{6,7},{7,6},{8,9},{9,8},{10,11... | collective-permute-start | bytes 196616 | tf_op jit(solution)/shard_map/ppermute | solution.py:26
  124.4 0.3 select_reduce_fusion
  124.7 9.0 %collective-permute-done.6 = f32[16,1024]{1,0:T(8,128)S(1)} collective-permute-done((f32[16,1024]{1,0:T(8,128)S(1)}, f32[16,1024]{1,0:T(8,128)S(1)}, u32[]{:S(2)}, u32[]{:S(2)}) %collective-permute-start.6) | collective-permute-done | bytes 65568 | tf_op jit(solution)/shard_map/ppermute | solution.py:26
  133.8 4.9 %collective-permute-start.8 = (f32[2,1024]{1,0:T(2,128)S(1)}, f32[2,1024]{1,0:T(2,128)S(1)}, u32[]{:S(2)}, u32[]{:S(2)}) collective-permute-start(f32[2,1024]{1,0:T(2,128)S(1)} %get-tuple-element.27), channel_id=1, source_target_pairs={{8,16},{24,32},{40,48},{56,64},{72,80},{88,96},{104,112},{120,128}... | collective-permute-start | bytes 24584 | tf_op jit(solution)/shard_map/ppermute | solution.py:17
  138.7 1.9 %collective-permute-start.7 = (f32[2,1024]{1,0:T(2,128)S(1)}, f32[2,1024]{1,0:T(2,128)S(1)}, u32[]{:S(2)}, u32[]{:S(2)}) collective-permute-start(f32[2,1024]{1,0:T(2,128)S(1)} %get-tuple-element.28), channel_id=1, source_target_pairs={{0,8},{8,0},{16,24},{24,16},{32,40},{40,32},{48,56},{56,48},{64,72... | collective-permute-start | bytes 24584 | tf_op jit(solution)/shard_map/ppermute | solution.py:16
  140.7 5.6 %collective-permute-done.8 = f32[2,1024]{1,0:T(2,128)S(1)} collective-permute-done((f32[2,1024]{1,0:T(2,128)S(1)}, f32[2,1024]{1,0:T(2,128)S(1)}, u32[]{:S(2)}, u32[]{:S(2)}) %collective-permute-start.8) | collective-permute-done | bytes 8224 | tf_op jit(solution)/shard_map/ppermute | solution.py:17
  146.3 0.0 collective-permute-done.7
  146.3 0.2 broadcast_multiply_fusion
  146.5 0.8 fusion.33
  (18 shorter events, 0.2 us)
Async XLA Ops:
  0.0 18.0 %copy-start.1 = (s32[16,1024]{1,0:T(8,128)S(1)}, s32[16,1024]{1,0:T(8,128)}, u32[]{:S(2)}) copy-start(s32[16,1024]{1,0:T(8,128)} %k_ref.1) | copy-start | bytes 196612
  3.2 21.2 %collective-permute-start = (f32[84,1024]{1,0:T(8,128)}, f32[84,1024]{1,0:T(8,128)S(1)}, u32[]{:S(2)}, u32[]{:S(2)}) collective-permute-start(f32[84,1024]{1,0:T(8,128)} %get-tuple-element.11), channel_id=1, source_target_pairs={{8,16},{24,32},{40,48},{56,64},{72,80},{88,96},{104,112},{120,128}... | collective-permute-start | bytes 1032200 | tf_op jit(solution)/shard_map/ppermute | solution.py:343
  16.0 8.3 %collective-permute-start.1 = (f32[84,1024]{1,0:T(8,128)}, f32[84,1024]{1,0:T(8,128)S(1)}, u32[]{:S(2)}, u32[]{:S(2)}) collective-permute-start(f32[84,1024]{1,0:T(8,128)} %get-tuple-element.12), channel_id=1, source_target_pairs={{0,8},{8,0},{16,24},{24,16},{32,40},{40,32},{48,56},{56,48},{64,72... | collective-permute-start | bytes 1032200 | tf_op jit(solution)/shard_map/ppermute | solution.py:342
  25.3 18.2 %copy-start = (f32[16,1024]{1,0:T(8,128)S(1)}, f32[16,1024]{1,0:T(8,128)}, u32[]{:S(2)}) copy-start(f32[16,1024]{1,0:T(8,128)} %p_ref.1) | copy-start | bytes 196612
  27.9 43.0 %collective-permute-start.3 = (f32[84,1024]{1,0:T(8,128)}, f32[84,1024]{1,0:T(8,128)S(1)}, u32[]{:S(2)}, u32[]{:S(2)}) collective-permute-start(f32[84,1024]{1,0:T(8,128)} %get-tuple-element.14), channel_id=1, source_target_pairs={{0,1},{1,0},{2,3},{3,2},{4,5},{5,4},{6,7},{7,6},{8,9},{9,8},{10,11... | collective-permute-start | bytes 1032200 | tf_op jit(solution)/shard_map/ppermute | solution.py:365
  38.8 59.9 %collective-permute-start.2 = (f32[84,1024]{1,0:T(8,128)}, f32[84,1024]{1,0:T(8,128)S(1)}, u32[]{:S(2)}, u32[]{:S(2)}) collective-permute-start(f32[84,1024]{1,0:T(8,128)} %get-tuple-element.13), channel_id=1, source_target_pairs={{1,2},{3,4},{5,6},{2,1},{4,3},{6,5},{9,10},{11,12},{13,14},{10,9},... | collective-permute-start | bytes 1032200 | tf_op jit(solution)/shard_map/ppermute | solution.py:366
  99.7 24.8 %copy-start.2 = (f32[16]{0:T(128)S(1)}, f32[16]{0:T(128)}, u32[]{:S(2)}) copy-start(f32[16]{0:T(128)} %param.15) | copy-start | bytes 196
  99.7 24.8 %copy-start.3 = (s32[16]{0:T(128)S(1)}, s32[16]{0:T(128)}, u32[]{:S(2)}) copy-start(s32[16]{0:T(128)} %param.14) | copy-start | bytes 196
  104.0 6.4 %collective-permute-start.4 = (f32[16,1024]{1,0:T(8,128)}, f32[16,1024]{1,0:T(8,128)S(1)}, u32[]{:S(2)}, u32[]{:S(2)}) collective-permute-start(f32[16,1024]{1,0:T(8,128)} %shard_map.85), channel_id=1, source_target_pairs={{0,2},{1,3},{2,0},{3,1},{4,6},{5,7},{6,4},{7,5},{8,10},{9,11},{10,... | collective-permute-start | bytes 196616 | tf_op jit(solution)/shard_map/ppermute | solution.py:26
  111.2 7.7 %collective-permute-start.5 = (f32[16,1024]{1,0:T(8,128)S(1)}, f32[16,1024]{1,0:T(8,128)S(1)}, u32[]{:S(2)}, u32[]{:S(2)}) collective-permute-start(f32[16,1024]{1,0:T(8,128)S(1)} %add.155), channel_id=1, source_target_pairs={{0,4},{1,5},{2,6},{3,7},{4,0},{5,1},{6,2},{7,3},{8,12},{9,13},{10,... | collective-permute-start | bytes 196616 | tf_op jit(solution)/shard_map/ppermute | solution.py:26
  118.9 14.9 %collective-permute-start.6 = (f32[16,1024]{1,0:T(8,128)S(1)}, f32[16,1024]{1,0:T(8,128)S(1)}, u32[]{:S(2)}, u32[]{:S(2)}) collective-permute-start(f32[16,1024]{1,0:T(8,128)S(1)} %add.156), channel_id=1, source_target_pairs={{0,1},{1,0},{2,3},{3,2},{4,5},{5,4},{6,7},{7,6},{8,9},{9,8},{10,11... | collective-permute-start | bytes 196616 | tf_op jit(solution)/shard_map/ppermute | solution.py:26
  133.8 12.5 %collective-permute-start.8 = (f32[2,1024]{1,0:T(2,128)S(1)}, f32[2,1024]{1,0:T(2,128)S(1)}, u32[]{:S(2)}, u32[]{:S(2)}) collective-permute-start(f32[2,1024]{1,0:T(2,128)S(1)} %get-tuple-element.27), channel_id=1, source_target_pairs={{8,16},{24,32},{40,48},{56,64},{72,80},{88,96},{104,112},{120,128}... | collective-permute-start | bytes 24584 | tf_op jit(solution)/shard_map/ppermute | solution.py:17
  138.7 7.6 %collective-permute-start.7 = (f32[2,1024]{1,0:T(2,128)S(1)}, f32[2,1024]{1,0:T(2,128)S(1)}, u32[]{:S(2)}, u32[]{:S(2)}) collective-permute-start(f32[2,1024]{1,0:T(2,128)S(1)} %get-tuple-element.28), channel_id=1, source_target_pairs={{0,8},{8,0},{16,24},{24,16},{32,40},{40,32},{48,56},{56,48},{64,72... | collective-permute-start | bytes 24584 | tf_op jit(solution)/shard_map/ppermute | solution.py:16

commit v14 on v12

--- a/solution.py
+++ b/solution.py
@@ -237,13 +237,23 @@
         c_s[j] = zero
         d_s[j] = zero
     ext = tile_cells + 2
-    for side, ref, adj, sec in ((0, zlo_ref, 1, 0), (4, zhi_ref, 6, 7)):
-        u_s[adj, wide] = ref[0:ext]
-        c_s[adj, wide] = ref[ext:2 * ext]
-        u_s[sec, own] = ref[2 * ext:2 * ext + tile_cells]
-        c_s[sec, own] = ref[2 * ext + tile_cells:2 * ext + 2 * tile_cells]
-    d_s[0, own] = zlo_ref[2 * ext + 2 * tile_cells:2 * ext + 3 * tile_cells]
-    d_s[7, own] = zhi_ref[2 * ext + 2 * tile_cells:2 * ext + 3 * tile_cells]
+    def place_halo(lo_ref, hi_ref):
+        for ref, adj, sec in ((lo_ref, 1, 0), (hi_ref, 6, 7)):
+            u_s[adj, wide] = ref[0:ext]
+            c_s[adj, wide] = ref[ext:2 * ext]
+            u_s[sec, own] = ref[2 * ext:2 * ext + tile_cells]
+            c_s[sec, own] = ref[2 * ext + tile_cells:2 * ext + 2 * tile_cells]
+        d_s[0, own] = lo_ref[2 * ext + 2 * tile_cells:2 * ext + 3 * tile_cells]
+        d_s[7, own] = hi_ref[2 * ext + 2 * tile_cells:2 * ext + 3 * tile_cells]
+
+    @pl.when(ids_ref[2] == 0)
+    def _():
+        place_halo(zhi_ref, zlo_ref)
+
+    @pl.when(ids_ref[2] == 1)
+    def _():
+        place_halo(zlo_ref, zhi_ref)
+
     dz = 4 * depth_cells
     for slot, z in ((2, 0), (3, 1), (4, depth_cells - 2), (5, depth_cells - 1)):
         dk = dmg_ref[z]
@@ -319,7 +329,7 @@
     p_ext = jnp.concatenate([lo_x[dz + depth_cells:dz + depth_cells + 2], pressure, hi_x[dz + depth_cells:dz + depth_cells + 2]])
     m_ext = jnp.concatenate([lo_x[dz + depth_cells + 2:], mask_f, hi_x[dz + depth_cells + 2:]])
     load_all = jnp.pad(4.0 * m_ext[1:-1] * p_ext[1:-1], ((X0 - 1, X0 - 1), (0, 0)))
-    ids = jnp.stack([depth_start, tile_start]).astype(jnp.int32)
+    ids = jnp.stack([depth_start, tile_start, lax.axis_index("depth") % 2]).astype(jnp.int32)
 
     def depth_face(adj, sec):
         u_adj = jnp.concatenate([lo_x[2 * adj + 1:2 * adj + 2], displacement[adj], hi_x[2 * adj:2 * adj + 1]])
@@ -329,7 +339,14 @@
         )
         return jnp.concatenate([u_adj, c_adj, displacement[sec], stiff_of(damage[sec], modulus[sec]), damage[adj]])
 
-    lo_z, hi_z = halo_swap(depth_face(0, 1), depth_face(depth_cells - 1, depth_cells - 2), "depth")
+    depths = lax.axis_size("depth")
+    even_z = lax.axis_index("depth") % 2 == 0
+    z_lo_face, z_hi_face = depth_face(0, 1), depth_face(depth_cells - 1, depth_cells - 2)
+    zgot_a = lax.ppermute(jnp.where(even_z, z_hi_face, z_lo_face), "depth", [(i, i ^ 1) for i in range(depths)])
+    zgot_b = lax.ppermute(
+        jnp.where(even_z, z_lo_face, z_hi_face), "depth",
+        [(i, i + 1) for i in range(1, depths - 1, 2)] + [(i + 1, i) for i in range(1, depths - 1, 2)],
+    )
 
     vmem = pl.BlockSpec(memory_space=pltpu.VMEM)
     smem = pl.BlockSpec(memory_space=pltpu.SMEM)
@@ -353,7 +370,7 @@
         in_specs=[smem] + [end_lo, end_hi] * 4 + [vmem] * 7,
         out_specs=vmem,
         scratch_shapes=[pltpu.VMEM((8, rows_all, width), f32)] * 4,
-    )(ids, displacement, displacement, damage, damage, modulus, modulus, toughness, toughness, lo_x, hi_x, lo_z, hi_z,
+    )(ids, displacement, displacement, damage, damage, modulus, modulus, toughness, toughness, lo_x, hi_x, zgot_a, zgot_b,
       edge, part_in, load_all)
 
     aperture = 0.5 + butterfly_sum(partial_open, "depth")

time: 148 us -> 148 us (level)
  the two profiles are of different devices: /device:TPU:30 before, /device:TPU:14 now
where the time goes in v14:
time: 148 us; the launch traced here: 147 us
  waiting for transfers between devices  75.8 us (51%)
  starting transfers between devices  46 us (31%)
  Pallas kernels  17.3 us (12%)
  other arithmetic  5.17 us (3%)
  local copies, waits for them, and re-layouts  2.95 us (2%)
    ppermute x1, waiting for transfers between devices, on_device(): lax.ppermute(jnp.where(even_z, z_lo_face, z_hi_face), 'depth', [(i, i + 1...  30.8 us
    ppermute x3, waiting for transfers between devices, butterfly_sum(): part = part + lax.ppermute(part, axis, pairs)  18.9 us
    ppermute x1, waiting for transfers between devices, on_device(): lax.ppermute(jnp.where(even_z, z_hi_face, z_lo_face), 'depth', [(i, i ^ 1...  15.4 us
    ppermute x1, starting transfers between devices, on_device(): lax.ppermute(send_b, 'tile', [(i, i + 1) for i in range(1, tiles - 1, 2)]...  12.8 us
    ppermute x1, starting transfers between devices, on_device(): lax.ppermute(jnp.where(even_z, z_lo_face, z_hi_face), 'depth', [(i, i + 1...  11 us
    ppermute x3, starting transfers between devices, butterfly_sum(): part = part + lax.ppermute(part, axis, pairs)  10.3 us
    pallas_call x1, Pallas kernels, on_device(): pl.pallas_call(functools.partial(interior_kernel, total_depth, total_rows...  9.67 us
    ppermute x1, waiting for transfers between devices, halo_swap(): got_b = lax.ppermute(jnp.where(even, lo_face, hi_face), axis, pairs_b)  7.09 us
  transfers between devices with their start and end apart: 9, of which 7 were waited for; matrix products, arithmetic and copies ran while one was open for 3% of the time, Pallas kernels for 7%

profile of v14, /device:TPU:14, one launch (start us, length us, event | category | flops | bytes accessed | tf_op | source)
XLA Modules:
  0.0 147.4 jit_solution(7225627807430008944)
XLA Ops:
  0.0 3.1 %shard_map.82 = (f32[84,1024]{1,0:T(8,128)}, f32[84,1024]{1,0:T(8,128)}) custom-call(s32[1]{0:T(128)} %bitcast.3.par_ref, f32[16,16,1024]{2,1,0:T(8,128)} %u_hi.3, f32[16,16,1024]{2,1,0:T(8,128)} %u_hi.3, f32[16,16,1024]{2,1,0:T(8,128)} %d_hi.3, f32[16,16,1024]{2,1,0:T(8,128)} %d_hi.3, f32[16,16,1024]{2,1,0:T(8,128)} %mod_hi.1, f32[16,16,1024]{2,1,0:T(8,128)} %mod_hi.1, ...), custom_call_target="tpu_custom_call" | custom-call | tf_op jit(solution)/shard_map/pallas_call | solution.py:314
  3.1 12.8 %collective-permute-start = (f32[84,1024]{1,0:T(8,128)}, f32[84,1024]{1,0:T(8,128)S(1)}, u32[]{:S(2)}, u32[]{:S(2)}) collective-permute-start(f32[84,1024]{1,0:T(8,128)} %get-tuple-element.9), channel_id=1, source_target_pairs={{8,16},{24,32},{40,48},{56,64},{72,80},{88,96},{104,112},{120,128}... | collective-permute-start | bytes 1032200 | tf_op jit(solution)/shard_map/ppermute | solution.py:324
  16.0 1.9 %collective-permute-start.1 = (f32[84,1024]{1,0:T(8,128)}, f32[84,1024]{1,0:T(8,128)S(1)}, u32[]{:S(2)}, u32[]{:S(2)}) collective-permute-start(f32[84,1024]{1,0:T(8,128)} %get-tuple-element.10), channel_id=1, source_target_pairs={{0,8},{8,0},{16,24},{24,16},{32,40},{40,32},{48,56},{56,48},{64,72... | collective-permute-start | bytes 1032200 | tf_op jit(solution)/shard_map/ppermute | solution.py:323
  17.9 1.0 bitcast_multiply_fusion
  18.9 0.6 pad_add_fusion.ids_ref
  19.5 1.2 multiply_bitcast_fusion
  20.7 3.6 %collective-permute-done = f32[84,1024]{1,0:T(8,128)S(1)} collective-permute-done((f32[84,1024]{1,0:T(8,128)}, f32[84,1024]{1,0:T(8,128)S(1)}, u32[]{:S(2)}, u32[]{:S(2)}) %collective-permute-start) | collective-permute-done | bytes 344096 | tf_op jit(solution)/shard_map/ppermute | solution.py:324
  24.4 0.7 concatenate.30
  25.2 0.7 concatenate.29
  26.0 0.1 broadcast_select_fusion
  26.0 11.0 %collective-permute-start.3 = (f32[84,1024]{1,0:T(8,128)S(1)}, f32[84,1024]{1,0:T(8,128)S(1)}, u32[]{:S(2)}, u32[]{:S(2)}) collective-permute-start(f32[84,1024]{1,0:T(8,128)S(1)} %get-tuple-element.23), channel_id=1, source_target_pairs={{1,2},{3,4},{5,6},{2,1},{4,3},{6,5},{9,10},{11,12},{13,14},{10,9},... | collective-permute-start | bytes 1032200 | tf_op jit(solution)/shard_map/ppermute | solution.py:346
  37.0 4.6 %collective-permute-start.2 = (f32[84,1024]{1,0:T(8,128)S(1)}, f32[84,1024]{1,0:T(8,128)S(1)}, u32[]{:S(2)}, u32[]{:S(2)}) collective-permute-start(f32[84,1024]{1,0:T(8,128)S(1)} %get-tuple-element.24), channel_id=1, source_target_pairs={{0,1},{1,0},{2,3},{3,2},{4,5},{5,4},{6,7},{7,6},{8,9},{9,8},{10,11... | collective-permute-start | bytes 1032200 | tf_op jit(solution)/shard_map/ppermute | solution.py:345
  41.7 0.7 pad.15.load_ref
  42.4 9.7 %shard_map.83 = (f32[16,1024]{1,0:T(8,128)}, f32[4,32,1024]{2,1,0:T(8,128)}) custom-call(s32[3]{0:T(128)} %pad_add_fusion.ids_ref, f32[16,16,1024]{2,1,0:T(8,128)} %u_hi.3, f32[16,16,1024]{2,1,0:T(8,128)} %d_hi.3, f32[16,16,1024]{2,1,0:T(8,128)} %mod_hi.1, f32[16,16,1024]{2,1,0:T(8,128)} %tgh_hi.1, f32[84,1024]{1,0:T(8,128)} %copy-done, ...), custom_call_target="tpu_custom_call" | custom-call | tf_op jit(solution)/shard_map/pallas_call | solution.py:354
  52.1 30.8 %collective-permute-done.3.zhi_ref = f32[84,1024]{1,0:T(8,128)S(1)} collective-permute-done((f32[84,1024]{1,0:T(8,128)S(1)}, f32[84,1024]{1,0:T(8,128)S(1)}, u32[]{:S(2)}, u32[]{:S(2)}) %collective-permute-start.3) | collective-permute-done | bytes 344096 | tf_op jit(solution)/shard_map/ppermute | solution.py:346
  82.8 15.4 %collective-permute-done.2.zlo_ref = f32[84,1024]{1,0:T(8,128)S(1)} collective-permute-done((f32[84,1024]{1,0:T(8,128)S(1)}, f32[84,1024]{1,0:T(8,128)S(1)}, u32[]{:S(2)}, u32[]{:S(2)}) %collective-permute-start.2) | collective-permute-done | bytes 344096 | tf_op jit(solution)/shard_map/ppermute | solution.py:345
  98.2 0.7 copy-done.5
  98.9 4.5 %shard_map.84 = f32[16,1024]{1,0:T(8,128)} custom-call(s32[3]{0:T(128)} %pad_add_fusion.ids_ref, f32[16,16,1024]{2,1,0:T(8,128)} %u_hi.3, f32[16,16,1024]{2,1,0:T(8,128)} %u_hi.3, f32[16,16,1024]{2,1,0:T(8,128)} %d_hi.3, f32[16,16,1024]{2,1,0:T(8,128)} %d_hi.3, f32[16,16,1024]{2,1,0:T(8,128)} %mod_hi.1, f32[16,16,1024]{2,1,0:T(8,128)} %mod_hi.1, ...), custom_call_target="tpu_custom_call" | custom-call | tf_op jit(solution)/shard_map/pallas_call | solution.py:366
  103.4 1.9 %collective-permute-start.4 = (f32[16,1024]{1,0:T(8,128)}, f32[16,1024]{1,0:T(8,128)S(1)}, u32[]{:S(2)}, u32[]{:S(2)}) collective-permute-start(f32[16,1024]{1,0:T(8,128)} %shard_map.84), channel_id=1, source_target_pairs={{0,2},{1,3},{2,0},{3,1},{4,6},{5,7},{6,4},{7,5},{8,10},{9,11},{10,... | collective-permute-start | bytes 196616 | tf_op jit(solution)/shard_map/ppermute | solution.py:26
  105.3 4.4 %collective-permute-done.4 = f32[16,1024]{1,0:T(8,128)S(1)} collective-permute-done((f32[16,1024]{1,0:T(8,128)}, f32[16,1024]{1,0:T(8,128)S(1)}, u32[]{:S(2)}, u32[]{:S(2)}) %collective-permute-start.4) | collective-permute-done | bytes 65568 | tf_op jit(solution)/shard_map/ppermute | solution.py:26
  109.8 0.8 add.170
  110.6 2.9 %collective-permute-start.5 = (f32[16,1024]{1,0:T(8,128)S(1)}, f32[16,1024]{1,0:T(8,128)S(1)}, u32[]{:S(2)}, u32[]{:S(2)}) collective-permute-start(f32[16,1024]{1,0:T(8,128)S(1)} %add.170), channel_id=1, source_target_pairs={{0,4},{1,5},{2,6},{3,7},{4,0},{5,1},{6,2},{7,3},{8,12},{9,13},{10,... | collective-permute-start | bytes 196616 | tf_op jit(solution)/shard_map/ppermute | solution.py:26
  113.5 0.1 iota_add_fusion
  113.6 4.7 %collective-permute-done.5 = f32[16,1024]{1,0:T(8,128)S(1)} collective-permute-done((f32[16,1024]{1,0:T(8,128)S(1)}, f32[16,1024]{1,0:T(8,128)S(1)}, u32[]{:S(2)}, u32[]{:S(2)}) %collective-permute-start.5) | collective-permute-done | bytes 65568 | tf_op jit(solution)/shard_map/ppermute | solution.py:26
  118.3 5.5 %collective-permute-start.6 = (f32[16,1024]{1,0:T(8,128)S(1)}, f32[16,1024]{1,0:T(8,128)S(1)}, u32[]{:S(2)}, u32[]{:S(2)}) collective-permute-start(f32[16,1024]{1,0:T(8,128)S(1)} %add.171), channel_id=1, source_target_pairs={{0,1},{1,0},{2,3},{3,2},{4,5},{5,4},{6,7},{7,6},{8,9},{9,8},{10,11... | collective-permute-start | bytes 196616 | tf_op jit(solution)/shard_map/ppermute | solution.py:26
  123.8 0.3 select_reduce_fusion
  124.1 9.8 %collective-permute-done.6 = f32[16,1024]{1,0:T(8,128)S(1)} collective-permute-done((f32[16,1024]{1,0:T(8,128)S(1)}, f32[16,1024]{1,0:T(8,128)S(1)}, u32[]{:S(2)}, u32[]{:S(2)}) %collective-permute-start.6) | collective-permute-done | bytes 65568 | tf_op jit(solution)/shard_map/ppermute | solution.py:26
  133.9 3.4 %collective-permute-start.8 = (f32[2,1024]{1,0:T(2,128)S(1)}, f32[2,1024]{1,0:T(2,128)S(1)}, u32[]{:S(2)}, u32[]{:S(2)}) collective-permute-start(f32[2,1024]{1,0:T(2,128)S(1)} %get-tuple-element.41), channel_id=1, source_target_pairs={{8,16},{24,32},{40,48},{56,64},{72,80},{88,96},{104,112},{120,128}... | collective-permute-start | bytes 24584 | tf_op jit(solution)/shard_map/ppermute | solution.py:17
  137.4 1.9 %collective-permute-start.7 = (f32[2,1024]{1,0:T(2,128)S(1)}, f32[2,1024]{1,0:T(2,128)S(1)}, u32[]{:S(2)}, u32[]{:S(2)}) collective-permute-start(f32[2,1024]{1,0:T(2,128)S(1)} %get-tuple-element.42), channel_id=1, source_target_pairs={{0,8},{8,0},{16,24},{24,16},{32,40},{40,32},{48,56},{56,48},{64,72... | collective-permute-start | bytes 24584 | tf_op jit(solution)/shard_map/ppermute | solution.py:16
  139.3 7.1 %collective-permute-done.8 = f32[2,1024]{1,0:T(2,128)S(1)} collective-permute-done((f32[2,1024]{1,0:T(2,128)S(1)}, f32[2,1024]{1,0:T(2,128)S(1)}, u32[]{:S(2)}, u32[]{:S(2)}) %collective-permute-start.8) | collective-permute-done | bytes 8224 | tf_op jit(solution)/shard_map/ppermute | solution.py:17
  146.4 0.2 broadcast_multiply_fusion
  146.6 0.8 fusion.33
  (30 shorter events, 0.3 us)
Async XLA Ops:
  0.0 17.9 %copy-start.3 = (s32[16,1024]{1,0:T(8,128)S(1)}, s32[16,1024]{1,0:T(8,128)}, u32[]{:S(2)}) copy-start(s32[16,1024]{1,0:T(8,128)} %k_ref.1) | copy-start | bytes 196612
  3.1 21.2 %collective-permute-start = (f32[84,1024]{1,0:T(8,128)}, f32[84,1024]{1,0:T(8,128)S(1)}, u32[]{:S(2)}, u32[]{:S(2)}) collective-permute-start(f32[84,1024]{1,0:T(8,128)} %get-tuple-element.9), channel_id=1, source_target_pairs={{8,16},{24,32},{40,48},{56,64},{72,80},{88,96},{104,112},{120,128}... | collective-permute-start | bytes 1032200 | tf_op jit(solution)/shard_map/ppermute | solution.py:324
  16.0 8.3 %collective-permute-start.1 = (f32[84,1024]{1,0:T(8,128)}, f32[84,1024]{1,0:T(8,128)S(1)}, u32[]{:S(2)}, u32[]{:S(2)}) collective-permute-start(f32[84,1024]{1,0:T(8,128)} %get-tuple-element.10), channel_id=1, source_target_pairs={{0,8},{8,0},{16,24},{24,16},{32,40},{40,32},{48,56},{56,48},{64,72... | collective-permute-start | bytes 1032200 | tf_op jit(solution)/shard_map/ppermute | solution.py:323
  24.4 17.2 %copy-start = (f32[84,1024]{1,0:T(8,128)}, f32[84,1024]{1,0:T(8,128)S(1)}, u32[]{:S(2)}) copy-start(f32[84,1024]{1,0:T(8,128)S(1)} %get-tuple-element.25.xlo_ref) | copy-start | bytes 1032196
  24.4 17.2 %copy-start.1 = (f32[84,1024]{1,0:T(8,128)}, f32[84,1024]{1,0:T(8,128)S(1)}, u32[]{:S(2)}) copy-start(f32[84,1024]{1,0:T(8,128)S(1)} %get-tuple-element.26.xhi_ref) | copy-start | bytes 1032196
  25.2 16.5 %copy-start.2 = (f32[16,1024]{1,0:T(8,128)S(1)}, f32[16,1024]{1,0:T(8,128)}, u32[]{:S(2)}) copy-start(f32[16,1024]{1,0:T(8,128)} %p_ref.1) | copy-start | bytes 196612
  26.0 56.8 %collective-permute-start.3 = (f32[84,1024]{1,0:T(8,128)S(1)}, f32[84,1024]{1,0:T(8,128)S(1)}, u32[]{:S(2)}, u32[]{:S(2)}) collective-permute-start(f32[84,1024]{1,0:T(8,128)S(1)} %get-tuple-element.23), channel_id=1, source_target_pairs={{1,2},{3,4},{5,6},{2,1},{4,3},{6,5},{9,10},{11,12},{13,14},{10,9},... | collective-permute-start | bytes 1032200 | tf_op jit(solution)/shard_map/ppermute | solution.py:346
  37.0 61.2 %collective-permute-start.2 = (f32[84,1024]{1,0:T(8,128)S(1)}, f32[84,1024]{1,0:T(8,128)S(1)}, u32[]{:S(2)}, u32[]{:S(2)}) collective-permute-start(f32[84,1024]{1,0:T(8,128)S(1)} %get-tuple-element.24), channel_id=1, source_target_pairs={{0,1},{1,0},{2,3},{3,2},{4,5},{5,4},{6,7},{7,6},{8,9},{9,8},{10,11... | collective-permute-start | bytes 1032200 | tf_op jit(solution)/shard_map/ppermute | solution.py:345
  82.8 15.4 %copy-start.4 = (f32[84,1024]{1,0:T(8,128)}, f32[84,1024]{1,0:T(8,128)S(1)}, u32[]{:S(2)}) copy-start(f32[84,1024]{1,0:T(8,128)S(1)} %collective-permute-done.3.zhi_ref) | copy-start | bytes 1032196
  98.2 0.7 copy-start.5
  98.9 24.8 %copy-start.6 = (f32[16]{0:T(128)S(1)}, f32[16]{0:T(128)}, u32[]{:S(2)}) copy-start(f32[16]{0:T(128)} %param.15) | copy-start | bytes 196
  98.9 24.8 %copy-start.7 = (s32[16]{0:T(128)S(1)}, s32[16]{0:T(128)}, u32[]{:S(2)}) copy-start(s32[16]{0:T(128)} %param.14) | copy-start | bytes 196
  103.4 6.4 %collective-permute-start.4 = (f32[16,1024]{1,0:T(8,128)}, f32[16,1024]{1,0:T(8,128)S(1)}, u32[]{:S(2)}, u32[]{:S(2)}) collective-permute-start(f32[16,1024]{1,0:T(8,128)} %shard_map.84), channel_id=1, source_target_pairs={{0,2},{1,3},{2,0},{3,1},{4,6},{5,7},{6,4},{7,5},{8,10},{9,11},{10,... | collective-permute-start | bytes 196616 | tf_op jit(solution)/shard_map/ppermute | solution.py:26
  110.6 7.7 %collective-permute-start.5 = (f32[16,1024]{1,0:T(8,128)S(1)}, f32[16,1024]{1,0:T(8,128)S(1)}, u32[]{:S(2)}, u32[]{:S(2)}) collective-permute-start(f32[16,1024]{1,0:T(8,128)S(1)} %add.170), channel_id=1, source_target_pairs={{0,4},{1,5},{2,6},{3,7},{4,0},{5,1},{6,2},{7,3},{8,12},{9,13},{10,... | collective-permute-start | bytes 196616 | tf_op jit(solution)/shard_map/ppermute | solution.py:26
  118.3 15.6 %collective-permute-start.6 = (f32[16,1024]{1,0:T(8,128)S(1)}, f32[16,1024]{1,0:T(8,128)S(1)}, u32[]{:S(2)}, u32[]{:S(2)}) collective-permute-start(f32[16,1024]{1,0:T(8,128)S(1)} %add.171), channel_id=1, source_target_pairs={{0,1},{1,0},{2,3},{3,2},{4,5},{5,4},{6,7},{7,6},{8,9},{9,8},{10,11... | collective-permute-start | bytes 196616 | tf_op jit(solution)/shard_map/ppermute | solution.py:26
  133.9 12.5 %collective-permute-start.8 = (f32[2,1024]{1,0:T(2,128)S(1)}, f32[2,1024]{1,0:T(2,128)S(1)}, u32[]{:S(2)}, u32[]{:S(2)}) collective-permute-start(f32[2,1024]{1,0:T(2,128)S(1)} %get-tuple-element.41), channel_id=1, source_target_pairs={{8,16},{24,32},{40,48},{56,64},{72,80},{88,96},{104,112},{120,128}... | collective-permute-start | bytes 24584 | tf_op jit(solution)/shard_map/ppermute | solution.py:17
  137.4 9.0 %collective-permute-start.7 = (f32[2,1024]{1,0:T(2,128)S(1)}, f32[2,1024]{1,0:T(2,128)S(1)}, u32[]{:S(2)}, u32[]{:S(2)}) collective-permute-start(f32[2,1024]{1,0:T(2,128)S(1)} %get-tuple-element.42), channel_id=1, source_target_pairs={{0,8},{8,0},{16,24},{24,16},{32,40},{40,32},{48,56},{56,48},{64,72... | collective-permute-start | bytes 24584 | tf_op jit(solution)/shard_map/ppermute | solution.py:16
